TPU v7x, 32 devices: a whole 2x2x4 slice. The times are simulated.
32 devices in a mesh: cell: 8 (over z, core), energy: 4 (over y, x).
Axes of the slice: x: 2, y: 2, z: 4, core: 2. Of those that a mesh axis runs over, the one named last changes fastest.
Arguments:
- modes: bfloat16 [8, 256, 256], P('cell'), may hold values from -0.375 to 0.375
- levels: float32 [8, 256], P('cell'), may hold values from -0.25 to 0.25
- level_shift: float32 [8, 8, 256], P('cell', 'energy'), may hold values from -0.25 to 0.25
- broadening: float32 [8, 8, 256], P('cell', 'energy'), may hold values from 0.02 to 0.3
- injection: float32 [8, 8, 256], P('cell', 'energy'), may hold values from 0.1 to 1
- coupling: bfloat16 [8, 256, 64], P('cell'), may hold values from -0.625 to 0.625
- row_mask: int32 [8, 4], P('cell'), may hold values 0 or 1
- interface: int32 [8], P('cell'), may hold values from 0 to 3
- screened: bfloat16 [8, 2, 8, 256, 256], P('cell', None, None, 'energy'), may hold values from -18 to 18
- offsets: int32 [8], replicated, may hold values from -2 to 2, as said below
Outputs:
- density: float32 [8, 8, 256], P('cell', 'energy')
- sigma_lesser: bfloat16 [8, 2, 8, 256, 256], P('cell', None, None, 'energy')
Inputs may be any that keep to these rules, and one draw needn't show every extreme that they name: interface[i] names one of the 4 blocks of 64 orbitals of cell i - 1. `offsets`: both ends of the range are taken.
All inputs are finite; a program needn't handle non-finite values. No bound on the sum of `row_mask` on one device may be relied on, other than what follows from the above.
Results may differ from a plain program's by a relative error of at most 0.014.
Values may be sent and summed in bfloat16 or wider, within the bound.
No kernel may reach another device: no remote copies, remote signals or barrier semaphores. Data moves between devices by JAX's collectives and lax.ppermute only.
A program may use at most 128 MiB of HBM per device.

v0:
```python
from functools import partial
from functools import reduce
import math

import jax
import jax.numpy as jnp
from jax import lax
from jax.sharding import PartitionSpec as P

broaden_base = 1.0
energy_low = -0.25
energy_span = 0.5
highest = lax.Precision.HIGHEST


def entering(x, axis, join, neutral):
    place = lax.axis_index(axis)
    gathered = jax.tree.map(
        lambda a, kind: lax.all_gather(a.astype(kind), axis),
        x,
        jax.tree.map(lambda a: jnp.bfloat16 if a.dtype == jnp.float32 else a.dtype, x),
    )
    state = jax.tree.map(lambda a, e: jnp.zeros_like(a) + jnp.asarray(e, a.dtype), x, neutral)

    def one(lap, state):
        return join(
            state,
            jax.tree.map(
                lambda a, own: lax.dynamic_index_in_dim(a, lap, 0, False).astype(own.dtype),
                gathered,
                x,
            ),
        )

    return lax.fori_loop(0, place, one, state)


def from_behind(block, axis, distance):
    devices = range(lax.axis_size(axis))
    route = [(i - distance, i) for i in devices if i - distance in devices]
    return lax.ppermute(block, axis, route)


def complex_product(left_re, left_im, right_re, right_im):
    einsum_high = partial(jnp.einsum, "eij,ejk->eik", precision=highest)
    return (
        einsum_high(left_re, right_re) - einsum_high(left_im, right_im),
        einsum_high(left_re, right_im) + einsum_high(left_im, right_re),
    )


def complex_adjoint(left_re, left_im, right_re, right_im):
    einsum_high = partial(jnp.einsum, "eik,ejk->eij", precision=highest)
    return (
        einsum_high(left_re, right_re) + einsum_high(left_im, right_im),
        einsum_high(left_im, right_re) - einsum_high(left_re, right_im),
    )


def adjoint_halves(left_re, left_im, right_re, right_im):
    einsum_low = partial(jnp.einsum, "eik,ejk->eij", preferred_element_type=jnp.float32)
    return (
        einsum_low(left_re, right_re) + einsum_low(left_im, right_im),
        einsum_low(left_im, right_re) - einsum_low(left_re, right_im),
    )


def compose(earlier, latter):
    forward_re, forward_im = complex_product(latter[0], latter[1], earlier[0], earlier[1])
    backward_re, backward_im = complex_product(earlier[2], earlier[3], latter[2], latter[3])
    middle_re, middle_im = complex_product(latter[0], latter[1], earlier[4], earlier[5])
    retard_re, retard_im = complex_product(middle_re, middle_im, latter[2], latter[3])
    leading_re, leading_im = complex_product(latter[0], latter[1], earlier[6], earlier[7])
    lesser_re, lesser_im = complex_adjoint(leading_re, leading_im, latter[0], latter[1])
    return (
        forward_re,
        forward_im,
        backward_re,
        backward_im,
        latter[4] + retard_re,
        latter[5] + retard_im,
        latter[6] + lesser_re,
        latter[7] + lesser_im,
    )


def block_of(values, chosen, extent, axis_dim):
    return lax.dynamic_slice_in_dim(values, chosen * extent, extent, axis_dim)


def square_rows(root_re, root_im):
    inner_dot = partial(jnp.einsum, "eik,ejk->eij", preferred_element_type=jnp.float32)
    return (
        inner_dot(root_re, root_re) + inner_dot(root_im, root_im),
        inner_dot(root_im, root_re) - inner_dot(root_re, root_im),
    )


def prepare(
    mode_mat,
    level_row,
    shift_rows,
    broad_rows,
    inject_rows,
    link_cols,
    mask_row,
    energy_grid,
    chosen,
):
    extent = link_cols.shape[1]
    detune = energy_grid[:, None] - level_row[None, :] - shift_rows
    damping = broaden_base + broad_rows
    denominator = detune * detune + damping * damping
    flipped = mode_mat.T[None]
    scaled_re = ((detune / denominator)[:, :, None] * flipped).astype(jnp.bfloat16)
    scaled_im = ((-damping / denominator)[:, :, None] * flipped).astype(jnp.bfloat16)
    free_re = jnp.einsum("mn,enk->emk", mode_mat, scaled_re, preferred_element_type=jnp.float32)
    free_im = jnp.einsum("mn,enk->emk", mode_mat, scaled_im, preferred_element_type=jnp.float32)
    half_re = free_re.astype(jnp.bfloat16)
    half_im = free_im.astype(jnp.bfloat16)
    spread = jnp.repeat(mask_row, extent).astype(jnp.bfloat16)
    link_mat = link_cols * spread[:, None]
    left_re = jnp.einsum("emn,nk->emk", half_re, link_mat, preferred_element_type=jnp.float32)
    left_im = jnp.einsum("emn,nk->emk", half_im, link_mat, preferred_element_type=jnp.float32)
    right_re = jnp.einsum("nk,enm->ekm", link_mat, half_re, preferred_element_type=jnp.float32)
    right_im = jnp.einsum("nk,enm->ekm", link_mat, half_im, preferred_element_type=jnp.float32)
    weight_root = jnp.sqrt(inject_rows)[:, None, :]
    root_re = (free_re * weight_root).astype(jnp.bfloat16)
    root_im = (free_im * weight_root).astype(jnp.bfloat16)
    handover = (
        block_of(left_re, chosen, extent, 1),
        block_of(left_im, chosen, extent, 1),
        block_of(right_re, chosen, extent, 2),
        block_of(right_im, chosen, extent, 2),
        block_of(block_of(free_re, chosen, extent, 1), chosen, extent, 2),
        block_of(block_of(free_im, chosen, extent, 1), chosen, extent, 2),
    )
    local_re, local_im = square_rows(root_re, root_im)
    lesser_block = (
        block_of(block_of(local_re, chosen, extent, 1), chosen, extent, 2),
        block_of(block_of(local_im, chosen, extent, 1), chosen, extent, 2),
    )
    details = {
        "free_im": free_im,
        "left_re": left_re,
        "left_im": left_im,
        "right_re_h": right_re.astype(jnp.bfloat16),
        "right_im_h": right_im.astype(jnp.bfloat16),
        "root_re": root_re,
        "root_im": root_im,
        "local_re": local_re,
        "local_im": local_im,
    }
    return (handover + lesser_block, details)


def finish(details, carried):
    left_re, left_im = (details["left_re"], details["left_im"])
    pz_re, pz_im = complex_product(left_re, left_im, carried[4], carried[5])
    pz_re = pz_re.astype(jnp.bfloat16)
    pz_im = pz_im.astype(jnp.bfloat16)
    diag_im = jnp.einsum(
        "enk,ekn->en", pz_re, details["right_im_h"], preferred_element_type=jnp.float32
    ) + jnp.einsum("enk,ekn->en", pz_im, details["right_re_h"], preferred_element_type=jnp.float32)
    density = -(jnp.diagonal(details["free_im"], axis1=1, axis2=2) + diag_im) / math.pi
    local_re, local_im = (details["local_re"], details["local_im"])
    pl_re, pl_im = complex_product(left_re, left_im, carried[6], carried[7])
    chain_re, chain_im = adjoint_halves(
        pl_re.astype(jnp.bfloat16),
        pl_im.astype(jnp.bfloat16),
        left_re.astype(jnp.bfloat16),
        left_im.astype(jnp.bfloat16),
    )
    lesser = jnp.stack([chain_re + local_re, chain_im + local_im]).astype(jnp.bfloat16)
    return (density, lesser)


def convolve(lesser, screen, offsets):
    overall = lesser.shape[-3]
    ndims = lesser.ndim
    widths = [(0, 0)] * (ndims - 3) + [(overall, overall), (0, 0), (0, 0)]
    padded = jnp.pad(lesser, widths)
    accum_re = jnp.zeros(lesser[..., 0, :, :, :].shape, jnp.float32)
    accum_im = jnp.zeros(lesser[..., 0, :, :, :].shape, jnp.float32)
    for position in range(screen.shape[-3]):
        start_row = (overall - offsets[position]).astype(jnp.int32)
        shifted = lax.dynamic_slice_in_dim(padded, start_row, overall, ndims - 3)
        shifted_re = shifted[..., 0, :, :, :].astype(jnp.float32)
        shifted_im = shifted[..., 1, :, :, :].astype(jnp.float32)
        screen_re = screen[..., 0, position, :, :][..., None, :, :].astype(jnp.float32)
        screen_im = screen[..., 1, position, :, :][..., None, :, :].astype(jnp.float32)
        accum_re = accum_re - (screen_re * shifted_im + screen_im * shifted_re)
        accum_im = accum_im + (screen_re * shifted_re - screen_im * shifted_im)
    return jnp.stack([accum_re, accum_im], axis=ndims - 4).astype(jnp.bfloat16)


def run_front(
    modes, levels, shift_all, broad_all, inject_all, coupling, row_mask, ahead_list, energy_grid
):
    extent = coupling.shape[2]
    energy_count = energy_grid.shape[0]
    position = 0
    handover, details = prepare(
        modes[position],
        levels[position],
        shift_all[position],
        broad_all[position],
        inject_all[position],
        coupling[position],
        row_mask[position],
        energy_grid,
        ahead_list[position],
    )
    cell_maps = [handover]
    stored = [details]
    device_map = reduce(compose, cell_maps)
    unit_block = jnp.broadcast_to(
        jnp.eye(extent, dtype=jnp.float32), (energy_count, extent, extent)
    )
    zero_block = jnp.zeros((energy_count, extent, extent), jnp.float32)
    identity = (
        unit_block,
        zero_block,
        unit_block,
        zero_block,
        zero_block,
        zero_block,
        zero_block,
        zero_block,
    )
    carried = entering(
        (
            device_map[0],
            device_map[1],
            device_map[2],
            device_map[3],
            device_map[4],
            device_map[5],
            device_map[6],
            device_map[7],
        ),
        "cell",
        compose,
        identity,
    )
    position = 0
    density, lesser = finish(stored[position], carried)
    densities = [density]
    lessers = [lesser]
    stacked = jnp.stack(lessers)
    exchanged = lax.all_to_all(stacked, "energy", split_axis=3, concat_axis=2, tiled=True)
    return (jnp.stack(densities), exchanged)


def body(
    modes,
    levels,
    level_shift,
    broadening,
    injection,
    coupling,
    row_mask,
    interface,
    screened,
    offsets,
):
    energies = level_shift.shape[1]
    groups = lax.axis_size("energy")
    overall = energies * groups
    first_energy = lax.axis_index("energy") * energies
    energy_grid = (
        energy_low
        + energy_span * ((first_energy + jnp.arange(energies)).astype(jnp.float32) + 0.5) / overall
    )
    following = from_behind(interface, "cell", -1)
    ahead_list = jnp.concatenate([interface[1:], following])
    density, exchanged = run_front(
        modes,
        levels,
        level_shift,
        broadening,
        injection,
        coupling,
        row_mask,
        ahead_list,
        energy_grid,
    )
    dens_parts = [density]
    density = jnp.concatenate(dens_parts, axis=1)
    sigma_out = convolve(exchanged, screened, offsets)
    return (density, sigma_out)


def solution(mesh):
    placed = (
        P("cell", None, None),
        P("cell", None),
        P("cell", "energy", None),
        P("cell", "energy", None),
        P("cell", "energy", None),
        P("cell", None, None),
        P("cell", None),
        P("cell"),
        P("cell", None, None, "energy", None),
        P(),
    )
    return jax.shard_map(
        body,
        mesh=mesh,
        in_specs=placed,
        out_specs=(P("cell", "energy", None), P("cell", None, None, "energy", None)),
        check_vma=False,
    )
```

profile of v0, /device:TPU:25, one launch (start us, length us, event | category | flops | bytes accessed | tf_op | source)
XLA Modules:
  0.0 208.5 jit_solution(5486309041721272976)
XLA Ops:
  0.6 3.3 %collective-permute-start = (s32[1]{0:T(128)}, s32[1]{0:T(128)}, u32[]{:S(2)}, u32[]{:S(2)}) collective-permute-start(s32[1]{0:T(128)} %param.19), channel_id=1, source_target_pairs={{4,0},{8,4},{12,8},{16,12},{20,16},{24,20},{28,24},{5,1},{9,5},{13... | collective-permute-start | bytes 20 | tf_op jit(solution)/shard_map/ppermute | solution.py:41
  7.1 1.2 multiply_convert_fusion.1
  10.2 1.2 multiply_convert_fusion
  12.3 1.0 fusion.124
  13.3 1.6 fusion.153
  24.8 16.6 %copy.54 = f32[2,256,256]{0,2,1:T(8,128)} copy(f32[2,256,256]{1,2,0:T(8,128)S(1)} %bitcast.359) | data formatting | bytes 1048576 | tf_op jit(solution)/shard_map/mn,enk->emk/transpose | solution.py:118
  42.6 1.0 bitcast_convert_fusion.15
  43.5 3.0 %gather_fusion = f32[256,2]{1,0:T(8,128)} fusion(f32[2,256,256]{0,2,1:T(8,128)} %copy.54, s32[256]{0:T(256)S(1)} %bitcast.358), kind=kCustom, calls=%fused_computation | custom fusion | bytes 6144 | tf_op jit(solution)/shard_map/jit(diagonal)/gather | solution.py:165
  47.4 13.9 %all-gather = bf16[16,64,64]{2,1,0:T(8,128)(2,1)S(1)} all-gather(bf16[2,64,64]{2,1,0:T(8,128)(2,1)S(1)} %copy.56), channel_id=2, replica_groups=mesh['cell'=8,'energy'=4] {'cell'}, dimensions={0}, use_global_device_ids=true | all-gather | bytes 147456 | tf_op jit(solution)/shard_map/all_gather | solution.py:19
  61.5 14.2 %all-gather.1 = bf16[16,64,64]{2,1,0:T(8,128)(2,1)S(1)} all-gather(bf16[2,64,64]{2,1,0:T(8,128)(2,1)S(1)} %copy.57), channel_id=3, replica_groups=mesh['cell'=8,'energy'=4] {'cell'}, dimensions={0}, use_global_device_ids=true | all-gather | bytes 147456 | tf_op jit(solution)/shard_map/all_gather | solution.py:19
  76.0 14.2 %all-gather.2 = bf16[16,64,64]{2,1,0:T(8,128)(2,1)S(1)} all-gather(bf16[2,64,64]{2,1,0:T(8,128)(2,1)S(1)} %copy.59), channel_id=4, replica_groups=mesh['cell'=8,'energy'=4] {'cell'}, dimensions={0}, use_global_device_ids=true | all-gather | bytes 147456 | tf_op jit(solution)/shard_map/all_gather | solution.py:19
  90.3 14.2 %all-gather.3 = bf16[16,64,64]{2,1,0:T(8,128)(2,1)S(1)} all-gather(bf16[2,64,64]{2,1,0:T(8,128)(2,1)S(1)} %fusion.131), channel_id=5, replica_groups=mesh['cell'=8,'energy'=4] {'cell'}, dimensions={0}, use_global_device_ids=true | all-gather | bytes 147456 | tf_op jit(solution)/shard_map/all_gather | solution.py:19
  104.6 14.2 %all-gather.4 = bf16[16,64,64]{2,1,0:T(8,128)(2,1)S(1)} all-gather(bf16[2,64,64]{2,1,0:T(8,128)(2,1)S(1)} %fusion.132), channel_id=6, replica_groups=mesh['cell'=8,'energy'=4] {'cell'}, dimensions={0}, use_global_device_ids=true | all-gather | bytes 147456 | tf_op jit(solution)/shard_map/all_gather | solution.py:19
  118.9 14.2 %all-gather.5 = bf16[16,64,64]{2,1,0:T(8,128)(2,1)S(1)} all-gather(bf16[2,64,64]{2,1,0:T(8,128)(2,1)S(1)} %copy.62), channel_id=7, replica_groups=mesh['cell'=8,'energy'=4] {'cell'}, dimensions={0}, use_global_device_ids=true | all-gather | bytes 147456 | tf_op jit(solution)/shard_map/all_gather | solution.py:19
  133.2 14.2 %all-gather.6 = bf16[16,64,64]{2,1,0:T(8,128)(2,1)S(1)} all-gather(bf16[2,64,64]{2,1,0:T(8,128)(2,1)S(1)} %dynamic-slice_convert_fusion.1), channel_id=8, replica_groups=mesh['cell'=8,'energy'=4] {'cell'}, dimensions={0}, use_global_device_ids=true | all-gather | bytes 147456 | tf_op jit(solution)/shard_map/all_gather | solution.py:19
  147.5 15.3 %all-gather.7 = bf16[16,64,64]{2,1,0:T(8,128)(2,1)} all-gather(bf16[2,64,64]{2,1,0:T(8,128)(2,1)S(1)} %dynamic-slice_convert_fusion), channel_id=9, replica_groups=mesh['cell'=8,'energy'=4] {'cell'}, dimensions={0}, use_global_device_ids=true | all-gather | bytes 147456 | tf_op jit(solution)/shard_map/all_gather | solution.py:19
  162.9 25.4 %while.22 = (s32[]{:T(128)}, f32[2,64,64]{2,1,0:T(8,128)S(1)}, f32[2,64,64]{2,1,0:T(8,128)S(1)}, f32[2,64,64]{2,1,0:T(8,128)S(1)}, f32[2,64,64]{2,1,0:T(8,128)S(...) while((s32[]{:T(128)}, f32[2,64,64]{2,1,0:T(8,128)S(1)}, ...), condition=%wide.region_1.2_spmd, body=%wide.region_0.1_spmd.sunk | while | flops 100794368 | bytes 2740471 | solution.py:35
  191.4 1.3 copy.77
  192.8 3.7 %all-to-all-start = ((bf16[1,2,2,256,256]{4,2,1,0,3:T(2,128)(2,1)}), bf16[1,2,2,256,256]{4,2,1,0,3:T(2,128)(2,1)S(1)}, u32[]{:S(2)}, u32[]{:S(2)}) async-start(bf16[1,2,2,256,256]{4,2,1,0,3:T(2,128)(2,1)} %copy.77), calls=%async_computation | async-start | bytes 1048576 | tf_op jit(solution)/shard_map/all_to_all | solution.py:251
  196.4 1.2 fusion.75
  197.8 1.2 fusion.74
  200.7 1.2 all-to-all-done
  202.0 2.8 %fusion.94 = bf16[1,1,8,64,256]{4,3,2,1,0:T(8,128)(2,1)S(1)} fusion(f32[64,256]{1,0:T(8,128)} %get-tuple-element.242, f32[64,256]{1,0:T(8,128)} %get-tuple-element.243, f32[64,256]{1,0:T(8,128)S(1)} %get-tuple-element.229, f32[64,256]{1,0:T(8,128)} %get-tuple-element.230, f32[64,256]{1,0:T(8,128)} %get-tuple-element.231, f32[64,256]{1,0:T(8,128)} %get-tuple-element.232, ...), kind=kLoop, calls=%fused_computation.159 | loop fusion | flops 6291456 | bytes 1835044 | tf_op jit(solution)/shard_map/convert.22
  204.8 2.8 %fusion.85 = bf16[1,1,8,64,256]{4,3,2,1,0:T(8,128)(2,1)S(1)} fusion(f32[64,256]{1,0:T(8,128)} %get-tuple-element.242, f32[64,256]{1,0:T(8,128)} %get-tuple-element.243, f32[64,256]{1,0:T(8,128)S(1)} %get-tuple-element.229, f32[64,256]{1,0:T(8,128)} %get-tuple-element.230, f32[64,256]{1,0:T(8,128)} %get-tuple-element.231, f32[64,256]{1,0:T(8,128)} %get-tuple-element.232, ...), kind=kLoop, calls=%fused_computation.150 | loop fusion | flops 6422528 | bytes 1835044 | tf_op jit(solution)/shard_map/convert.21
  (167 shorter events, 38.5 us)
Async XLA Ops:
  0.6 41.9 %copy-start = (bf16[1,2,8,64,256]{4,3,2,1,0:T(8,128)(2,1)S(1)}, bf16[1,2,8,64,256]{4,3,2,1,0:T(8,128)(2,1)}, u32[]{:S(2)}) copy-start(bf16[1,2,8,64,256]{4,3,2,1,0:T(8,128)(2,1)} %param.20) | copy-start | bytes 1572868
  0.6 45.9 %collective-permute-start = (s32[1]{0:T(128)}, s32[1]{0:T(128)}, u32[]{:S(2)}, u32[]{:S(2)}) collective-permute-start(s32[1]{0:T(128)} %param.19), channel_id=1, source_target_pairs={{4,0},{8,4},{12,8},{16,12},{20,16},{24,20},{28,24},{5,1},{9,5},{13... | collective-permute-start | bytes 20 | tf_op jit(solution)/shard_map/ppermute | solution.py:41
  10.2 122.9 %copy-start.1 = (bf16[2,256,64]{1,2,0:T(8,128)(2,1)}, bf16[2,256,64]{1,2,0:T(8,128)(2,1)S(1)}, u32[]{:S(2)}) copy-start(bf16[2,256,64]{1,2,0:T(8,128)(2,1)S(1)} %fusion.111) | copy-start | bytes 196612
  13.3 119.8 %copy-start.2 = (bf16[2,256,64]{1,2,0:T(8,128)(2,1)}, bf16[2,256,64]{1,2,0:T(8,128)(2,1)S(1)}, u32[]{:S(2)}) copy-start(bf16[2,256,64]{1,2,0:T(8,128)(2,1)S(1)} %fusion.124) | copy-start | bytes 196612
  192.8 9.2 %all-to-all-start = ((bf16[1,2,2,256,256]{4,2,1,0,3:T(2,128)(2,1)}), bf16[1,2,2,256,256]{4,2,1,0,3:T(2,128)(2,1)S(1)}, u32[]{:S(2)}, u32[]{:S(2)}) async-start(bf16[1,2,2,256,256]{4,2,1,0,3:T(2,128)(2,1)} %copy.77), calls=%async_computation | async-start | bytes 1048576 | tf_op jit(solution)/shard_map/all_to_all | solution.py:251
where the time goes:
time: 210 us; the launch traced here: 209 us
  blocking collectives  115 us (55%)
  matrix products  37 us (18%)
  local copies, waits for them, and re-layouts  25.5 us (12%)
  between operations  11.4 us (5%)
  other arithmetic  10.9 us (5%)
  starting transfers between devices  6.91 us (3%)
    all_gather x8, blocking collectives, entering(): lax.all_gather(a.astype(kind), axis)  115 us
    transpose x1, local copies, waits for them, and re-layouts, prepare(): jnp.einsum('mn,enk->emk', mode_mat, scaled_im, preferred_element_type=jnp...  16.6 us
    dot_general x7, matrix products, complex_adjoint(): einsum_high(left_re, right_im)  6.61 us
    another operation x2, other arithmetic  5.66 us
    dot_general x23, matrix products, complex_product(): einsum_high(left_im, right_re)  5.03 us
    dot_general x23, matrix products, complex_product(): einsum_high(left_im, right_im)  5.02 us
  transfers between devices with their start and end apart: 2, of which 1 were waited for; matrix products, arithmetic and copies ran while one was open for 18% of the time, Pallas kernels for 0%

commit v1 on v0

v1 whole, which is shorter than its diff:
```python
from functools import partial
import math

import jax
import jax.numpy as jnp
from jax import lax
from jax.experimental import pallas as pl
from jax.experimental.pallas import tpu as pltpu
from jax.sharding import PartitionSpec as P

broaden_base = 1.0
energy_low = -0.25
energy_span = 0.5
f32 = jnp.float32
bf16 = jnp.bfloat16

VMEM = pl.BlockSpec(memory_space=pltpu.VMEM)
SMEM = pl.BlockSpec(memory_space=pltpu.SMEM)


def dot_last(a, b, precision=None):
    return lax.dot_general(
        a, b, (((1,), (1,)), ((), ())), precision=precision, preferred_element_type=f32
    )


def dot_mat(a, b):
    return lax.dot_general(a, b, (((1,), (0,)), ((), ())), preferred_element_type=f32)


def signs(width, left_sign):
    lane = lax.broadcasted_iota(jnp.int32, (1, width), 1)
    return jnp.where(lane < width // 2, left_sign, -left_sign).astype(f32)


def swap_halves(x):
    return pltpu.roll(x, x.shape[1] // 2, 1)


def full(x):
    x = x.astype(f32)
    return jnp.concatenate([x, swap_halves(x) * signs(x.shape[1], -1.0)], axis=0).astype(bf16)


def full_conj(x):
    x = x.astype(f32)
    return jnp.concatenate([x * signs(x.shape[1], 1.0), swap_halves(x)], axis=0).astype(bf16)


def resolvent(levels, shift, broad, index, overall):
    eps = energy_low + energy_span * (index.astype(f32) + 0.5) / overall
    detune = eps - levels - shift
    damping = broaden_base + broad
    inverse = 1.0 / (detune * detune + damping * damping)
    return detune * inverse, -damping * inverse


def masked_link(coupling_ref, mask_ref, link2_ref):
    rows, extent = coupling_ref.shape[1:]
    count = mask_ref.shape[1]
    size = rows // count
    link2_ref[...] = jnp.zeros_like(link2_ref)
    for block in range(count):
        keep = mask_ref[0, block].astype(f32)
        piece = (coupling_ref[0, block * size : (block + 1) * size, :].astype(f32) * keep).astype(bf16)
        link2_ref[block * size : (block + 1) * size, 0:extent] = piece
        link2_ref[rows + block * size : rows + (block + 1) * size, extent : 2 * extent] = piece


def maps_kernel(overall, ahead_ref, mask_ref, modes_ref, levels_ref, params_ref, coupling_ref, out_ref, link2_ref):
    energies = params_ref.shape[1]
    extent = coupling_ref.shape[2]
    first = lax.axis_index("energy") * energies
    masked_link(coupling_ref, mask_ref, link2_ref)
    link2 = link2_ref[...]
    chosen = pl.multiple_of(ahead_ref[0] * extent, extent)
    modes = modes_ref[0]
    rows = modes_ref[0, pl.ds(chosen, extent), :]
    rows_f = rows.astype(f32)
    none = jnp.zeros_like(rows)
    rows2 = jnp.concatenate(
        [jnp.concatenate([rows, none], axis=1), jnp.concatenate([none, rows], axis=1)], axis=0
    )
    for e in range(energies):
        dr, di = resolvent(
            levels_ref[...], params_ref[0, e : e + 1, :], params_ref[1, e : e + 1, :], first + e, overall
        )
        scaled_re = (rows_f * dr).astype(bf16)
        scaled_im = (rows_f * di).astype(bf16)
        both = dot_last(jnp.concatenate([scaled_re, scaled_im], axis=0), modes)
        free_re, free_im = both[:extent], both[extent:]
        halves = jnp.concatenate([free_re.astype(bf16), free_im.astype(bf16)], axis=1)
        out_ref[e, 0] = dot_mat(halves, link2).astype(bf16)
        out_ref[e, 1] = dot_last(jnp.concatenate([scaled_re, scaled_im], axis=1), rows2).astype(bf16)
        weight = jnp.sqrt(params_ref[2, e : e + 1, :])
        root_re, root_im = free_re * weight, free_im * weight
        straight = jnp.concatenate([root_re, root_im], axis=1).astype(bf16)
        turned = jnp.concatenate([-root_im, root_re], axis=1).astype(bf16)
        out_ref[e, 2] = dot_last(straight, jnp.concatenate([straight, turned], axis=0)).astype(bf16)


def rows_kernel(
    overall, hop, share, mask_ref, modes_ref, levels_ref, params_ref, coupling_ref, left_ref, local_ref, link2_ref
):
    energies = params_ref.shape[1]
    group = lax.axis_index("energy")
    first = jnp.bitwise_xor(group, hop) * energies
    masked_link(coupling_ref, mask_ref, link2_ref)
    link2 = link2_ref[...]
    modes = modes_ref[0]
    modes_f = modes.astype(f32)
    mine = pl.multiple_of(group * share, share)
    rows_f = modes_ref[0, pl.ds(mine, share), :].astype(f32)
    for e in range(energies):
        dr, di = resolvent(
            levels_ref[...], params_ref[0, e : e + 1, :], params_ref[1, e : e + 1, :], first + e, overall
        )
        free_re = dot_last((modes_f * dr).astype(bf16), modes)
        free_im = dot_last((modes_f * di).astype(bf16), modes)
        halves = jnp.concatenate([free_re.astype(bf16), free_im.astype(bf16)], axis=1)
        left_ref[e] = dot_mat(halves, link2).astype(bf16)
        weight = jnp.sqrt(params_ref[2, e : e + 1, :])
        straight = jnp.concatenate([free_re * weight, free_im * weight], axis=1).astype(bf16)
        turned = jnp.concatenate([-(free_im * weight), free_re * weight], axis=1).astype(bf16)
        own_re = dot_last((rows_f * dr).astype(bf16), modes) * weight
        own_im = dot_last((rows_f * di).astype(bf16), modes) * weight
        own = jnp.concatenate([own_re, own_im], axis=1).astype(bf16)
        local_ref[e, 0] = dot_last(own, straight).astype(bf16)
        local_ref[e, 1] = dot_last(own, turned).astype(bf16)


def pushed(step, state):
    first = dot_mat(step[0], jnp.concatenate([full(state[0]), full(state[1])], axis=1)).astype(bf16)
    width = step[0].shape[1]
    return (
        dot_last(first[:, :width], full_conj(step[0])),
        dot_last(first[:, width:], full(step[0])),
    )


def compose(earlier, latter):
    retarded, lesser = pushed(latter, earlier[1:])
    return (
        dot_mat(latter[0], full(earlier[0])),
        latter[1].astype(f32) + retarded,
        latter[2].astype(f32) + lesser,
    )


def pick(flag, yes, no):
    return tuple(jnp.where(flag, a, b) for a, b in zip(yes, no))


def neutral(extent, width):
    row = lax.broadcasted_iota(jnp.int32, (extent, width), 0)
    lane = lax.broadcasted_iota(jnp.int32, (extent, width), 1)
    zero = jnp.zeros((extent, width), f32)
    return (jnp.where(row == lane, 1.0, 0.0).astype(bf16), zero.astype(bf16), zero.astype(bf16))


def read(ref, e):
    return tuple(ref[e, part] for part in range(ref.shape[1]))


def join_kernel(level, *refs):
    total_ref, other_ref = refs[:2]
    enter_ref = refs[2] if level else None
    new_total_ref, new_enter_ref = refs[-2:]
    energies, _, extent, width = total_ref.shape
    place = lax.axis_index("cell")
    upper = jnp.bitwise_and(jnp.right_shift(place, level), 1) == 1
    parts = new_total_ref.shape[1]
    for e in range(energies):
        total, other = read(total_ref, e), read(other_ref, e)
        joined = compose(pick(upper, other, total), pick(upper, total, other))
        for part in range(parts):
            new_total_ref[e, part] = joined[part + 3 - parts].astype(bf16)
        if level:
            enter = read(enter_ref, e)
            longer = compose(other, enter)
            longer = tuple(x.astype(bf16) for x in longer)
            enter = pick(upper, longer, enter)
        else:
            enter = pick(upper, other, neutral(extent, width))
        for part in range(3):
            new_enter_ref[e, part] = enter[part]


def arrive_kernel(enter_ref, state_ref, retarded_ref, lesser_ref):
    for e in range(enter_ref.shape[0]):
        enter = read(enter_ref, e)
        retarded, lesser = pushed(enter, read(state_ref, e))
        retarded_ref[e] = (enter[1].astype(f32) + retarded).astype(bf16)
        lesser_ref[e] = (enter[2].astype(f32) + lesser).astype(bf16)


def density_kernel(overall, modes_ref, levels_ref, params_ref, left_ref, retarded_ref, out_ref):
    energies = params_ref.shape[1]
    first = lax.axis_index("energy") * energies
    modes = modes_ref[0].astype(f32)
    for e in range(energies):
        _, di = resolvent(
            levels_ref[...], params_ref[0, e : e + 1, :], params_ref[1, e : e + 1, :], first + e, overall
        )
        plain = modes * (modes * di).astype(bf16).astype(f32)
        left = left_ref[e]
        pz = dot_mat(left, full(retarded_ref[e])).astype(bf16).astype(f32)
        turned = pz * swap_halves(left.astype(f32))
        highest = lax.Precision.HIGHEST
        total = dot_last(jnp.ones((8, plain.shape[1]), f32), plain, highest) + dot_last(
            jnp.ones((8, turned.shape[1]), f32), turned, highest
        )
        out_ref[0, e : e + 1, :] = -total[0:1] / math.pi


def convolve_kernel(groups, reach, offsets_ref, screen_ref, *refs):
    lefts, locals_, lessers = refs[:groups], refs[groups : 2 * groups], refs[2 * groups : 3 * groups]
    out_ref, g_re, g_im = refs[3 * groups :]
    energies = lefts[0].shape[0]
    overall = energies * groups
    share, width = out_ref.shape[3:]
    group = lax.axis_index("energy")
    mine = pl.multiple_of(group * share, share)
    blank = jnp.zeros((share, width), f32)
    for e in range(reach):
        g_re[e] = blank
        g_im[e] = blank
        g_re[overall + reach + e] = blank
        g_im[overall + reach + e] = blank
    for hop in range(groups):
        base = jnp.bitwise_xor(group, hop) * energies + reach
        for e in range(energies):
            left = lefts[hop][e]
            own = lefts[hop][e, pl.ds(mine, share), :]
            pl_hat = dot_mat(own, full(lessers[hop][e]))
            turned = swap_halves(pl_hat) * signs(pl_hat.shape[1], 1.0)
            chain = dot_last(jnp.concatenate([pl_hat, turned], axis=0).astype(bf16), left)
            g_re[base + e] = chain[:share] + locals_[hop][e, 0].astype(f32)
            g_im[base + e] = chain[share:] + locals_[hop][e, 1].astype(f32)
    points = screen_ref.shape[2]
    lanes, height, batch = 128, 16, min(8, overall)

    def rows_of(step, _):
        top = pl.multiple_of(step * height, height)
        for lane in range(0, width, lanes):
            for e0 in range(0, overall, batch):
                sums = [None] * batch
                for k in range(points):
                    start = e0 + reach - offsets_ref[k]
                    w_re = screen_ref[0, 0, k, pl.ds(top, height), lane : lane + lanes].astype(f32)
                    w_im = screen_ref[0, 1, k, pl.ds(top, height), lane : lane + lanes].astype(f32)
                    for e in range(batch):
                        x_re = g_re[start + e, pl.ds(top, height), lane : lane + lanes]
                        x_im = g_im[start + e, pl.ds(top, height), lane : lane + lanes]
                        re = w_re * x_im + w_im * x_re
                        im = w_re * x_re - w_im * x_im
                        sums[e] = (re, im) if k == 0 else (sums[e][0] + re, sums[e][1] + im)
                for e in range(batch):
                    out_ref[0, 0, e0 + e, pl.ds(top, height), lane : lane + lanes] = (-sums[e][0]).astype(bf16)
                    out_ref[0, 1, e0 + e, pl.ds(top, height), lane : lane + lanes] = sums[e][1].astype(bf16)
        return 0

    lax.fori_loop(0, share // height, rows_of, 0)


def call(kernel, out_shape, in_specs, scratch=(), flops=1_000_000, size=1_000_000):
    outs = jax.tree.map(lambda _: VMEM, out_shape)
    return pl.pallas_call(
        kernel,
        out_shape=out_shape,
        in_specs=in_specs,
        out_specs=outs,
        scratch_shapes=list(scratch),
        cost_estimate=pl.CostEstimate(flops=flops, bytes_accessed=size, transcendentals=0),
    )


def body(
    modes,
    levels,
    level_shift,
    broadening,
    injection,
    coupling,
    row_mask,
    interface,
    screened,
    offsets,
):
    cells = lax.axis_size("cell")
    groups = lax.axis_size("energy")
    rounds = cells.bit_length() - 1
    assert cells == 1 << rounds and groups & (groups - 1) == 0
    energies = level_shift.shape[1]
    overall = energies * groups
    orbitals, extent = coupling.shape[1:]
    width = 2 * extent
    share = orbitals // groups
    sds = jax.ShapeDtypeStruct

    ahead = lax.ppermute(interface, "cell", [(i + 1, i) for i in range(cells - 1)])
    params = jnp.concatenate([level_shift, broadening, injection], axis=0)
    all_params = [params] + [
        lax.ppermute(params, "energy", [(i, i ^ hop) for i in range(groups)]) for hop in range(1, groups)
    ]
    link2 = pltpu.VMEM((2 * orbitals, width), bf16)

    total = call(
        partial(maps_kernel, overall),
        sds((energies, 3, extent, width), bf16),
        [SMEM, SMEM, VMEM, VMEM, VMEM, VMEM],
        [link2],
    )(ahead, row_mask, modes, levels, params, coupling)

    lefts, locals_ = [], []
    for hop in range(groups):
        left, local = call(
            partial(rows_kernel, overall, hop, share),
            (sds((energies, orbitals, width), bf16), sds((energies, 2, share, orbitals), bf16)),
            [SMEM, VMEM, VMEM, VMEM, VMEM],
            [link2],
        )(row_mask, modes, levels, all_params[hop], coupling)
        lefts.append(left)
        locals_.append(local)

    enter = None
    for level in range(rounds - 1):
        other = lax.ppermute(total, "cell", [(i, i ^ (1 << level)) for i in range(cells)])
        parts = 3 if level < rounds - 2 else 2
        given = [total, other] + ([enter] if level else [])
        total, enter = call(
            partial(join_kernel, level),
            (sds((energies, parts, extent, width), bf16), sds((energies, 3, extent, width), bf16)),
            [VMEM] * len(given),
        )(*given)
    half = cells // 2
    state = lax.ppermute(total, "cell", [(i, i + half) for i in range(half)])
    retarded, lesser = call(
        arrive_kernel,
        (sds((energies, extent, width), bf16), sds((energies, extent, width), bf16)),
        [VMEM, VMEM],
    )(enter, state)

    lessers = [lesser] + [
        lax.ppermute(lesser, "energy", [(i, i ^ hop) for i in range(groups)]) for hop in range(1, groups)
    ]
    density = call(
        partial(density_kernel, overall),
        sds((1, energies, orbitals), f32),
        [VMEM] * 5,
    )(modes, levels, params, lefts[0], retarded)

    reach = overall // 4
    spread = pltpu.VMEM((overall + 2 * reach, share, orbitals), f32)
    sigma = call(
        partial(convolve_kernel, groups, reach),
        sds((1, 2, overall, share, orbitals), bf16),
        [SMEM, VMEM] + [VMEM] * (3 * groups),
        [spread, spread],
    )(offsets, screened, *lefts, *locals_, *lessers)
    return (density, sigma)


def solution(mesh):
    placed = (
        P("cell", None, None),
        P("cell", None),
        P("cell", "energy", None),
        P("cell", "energy", None),
        P("cell", "energy", None),
        P("cell", None, None),
        P("cell", None),
        P("cell"),
        P("cell", None, None, "energy", None),
        P(),
    )
    return jax.shard_map(
        body,
        mesh=mesh,
        in_specs=placed,
        out_specs=(P("cell", "energy", None), P("cell", None, None, "energy", None)),
        check_vma=False,
    )
```

time: 210 us -> 62.8 us (0.30)
  the two profiles are of different devices: /device:TPU:25 before, /device:TPU:0 now
where the time goes in v1:
time: 62.8 us; the launch traced here: 62.3 us
  Pallas kernels  27.6 us (44%)
  starting transfers between devices  18.3 us (29%)
  waiting for transfers between devices  8.55 us (14%)
  local copies, waits for them, and re-layouts  7.16 us (11%)
  between operations  0.7 us (1%)
    pallas_call x4, Pallas kernels, body(): call(partial(rows_kernel, overall, hop, share), (sds((energies, orbitals,...  10.8 us
    unnamed x29, local copies, waits for them, and re-layouts  7.15 us
    ppermute x1, starting transfers between devices, body(): state = lax.ppermute(total, 'cell', [(i, i + half) for i in range(half)])  5.01 us
    pallas_call x1, Pallas kernels, body(): call(partial(convolve_kernel, groups, reach), sds((1, 2, overall, share,...  4.82 us
    ppermute x2, waiting for transfers between devices, body(): lax.ppermute(total, 'cell', [(i, i ^ 1 << level) for i in range(cells)])  4.68 us
    pallas_call x2, Pallas kernels, body(): call(partial(join_kernel, level), (sds((energies, parts, extent, width),...  4.48 us
    ppermute x3, starting transfers between devices, body(): lax.ppermute(params, 'energy', [(i, i ^ hop) for i in range(groups)])  4.36 us
    ppermute x2, starting transfers between devices, body(): lax.ppermute(total, 'cell', [(i, i ^ 1 << level) for i in range(cells)])  4.18 us
  transfers between devices with their start and end apart: 10, of which 4 were waited for; matrix products, arithmetic and copies ran while one was open for 4% of the time, Pallas kernels for 21%

profile of v1, /device:TPU:0, one launch (start us, length us, event | category | flops | bytes accessed | tf_op | source)
XLA Modules:
  0.0 62.3 jit_solution(5229912743513731043)
XLA Ops:
  0.6 1.3 %collective-permute-start = (s32[1]{0:T(128)}, s32[1]{0:T(128)}, u32[]{:S(2)}, u32[]{:S(2)}) collective-permute-start(s32[1]{0:T(128)} %param.17), channel_id=1, source_target_pairs={{4,0},{8,4},{12,8},{16,12},{20,16},{24,20},{28,24},{5,1},{9,5},{13... | collective-permute-start | bytes 20 | tf_op jit(solution)/shard_map/ppermute | solution.py:301
  1.9 0.7 %constant_dynamic-update-slice_fusion.2 = f32[3,2,256]{2,1,0:T(2,128)S(1)} fusion(f32[1,2,256]{2,1,0:T(2,128)} %param.12), kind=kLoop, calls=%fused_computation.2 | loop fusion | bytes 4096
  2.6 1.5 %copy.12.coupling_ref = bf16[1,256,64]{2,1,0:T(8,128)(2,1)} copy(bf16[1,256,64]{1,2,0:T(8,128)(2,1)} %param.15) | data formatting | bytes 65536 | tf_op args[5]
  4.1 0.7 %copy-done.12 = f32[1,2,256]{2,1,0:T(2,128)S(1)} copy-done((f32[1,2,256]{2,1,0:T(2,128)S(1)}, f32[1,2,256]{2,1,0:T(2,128)}, u32[]{:S(2)}) %copy-start.12) | copy-done | bytes 2072
  5.4 2.9 %shard_map.114.refs_0_ = bf16[2,3,64,128]{3,2,1,0:T(8,128)(2,1)} custom-call(s32[1]{0:T(128)} %collective-permute-done.ahead_ref, s32[1,4]{1,0:T(1,128)} %mask_ref.9, bf16[1,256,256]{2,1,0:T(8,128)(2,1)} %modes_ref.11, f32[1,256]{1,0:T(1,128)} %levels_ref.11, f32[3,2,256]{2,1,0:T(2,128)} %copy-done.2, bf16[1,256,64]{2,1,0:T(8,128)(2,1)} %copy.12.coupling_ref), custom_call_target="tpu_custom_call" | custom-call | flops 1000000 | bytes 1000000 | tf_op jit(solution)/shard_map/pallas_call | solution.py:308
  8.3 1.6 %collective-permute-start.1 = (bf16[2,3,64,128]{3,2,1,0:T(8,128)(2,1)}, bf16[2,3,64,128]{3,2,1,0:T(8,128)(2,1)S(1)}, u32[]{:S(2)}, u32[]{:S(2)}) collective-permute-start(bf16[2,3,64,128]{3,2,1,0:T(8,128)(2,1)} %shard_map.114.refs_0_), channel_id=1, source_target_pairs={{0,4},{4,0},{8,12},{12,8},{16,20},{20,16},{24,28},{28,24},{1,5},{5... | collective-permute-start | bytes 294920 | tf_op jit(solution)/shard_map/ppermute | solution.py:328
  9.9 1.2 %collective-permute-done.1.refs_1_ = bf16[2,3,64,128]{3,2,1,0:T(8,128)(2,1)S(1)} collective-permute-done((bf16[2,3,64,128]{3,2,1,0:T(8,128)(2,1)}, bf16[2,3,64,128]{3,2,1,0:T(8,128)(2,1)S(1)}, u32[]{:S(2)}, u32[]{:S(2)}) %collective-permute-start.1) | collective-permute-done | bytes 98336 | tf_op jit(solution)/shard_map/ppermute | solution.py:328
  11.7 2.1 %shard_map.115 = (bf16[2,3,64,128]{3,2,1,0:T(8,128)(2,1)}, bf16[2,3,64,128]{3,2,1,0:T(8,128)(2,1)}) custom-call(bf16[2,3,64,128]{3,2,1,0:T(8,128)(2,1)} %shard_map.114.refs_0_, bf16[2,3,64,128]{3,2,1,0:T(8,128)(2,1)} %copy-done), custom_call_target="tpu_custom_call" | custom-call | flops 1000000 | bytes 1000000 | tf_op jit(solution)/shard_map/pallas_call | solution.py:331
  13.8 2.5 %collective-permute-start.2 = (bf16[2,3,64,128]{3,2,1,0:T(8,128)(2,1)}, bf16[2,3,64,128]{3,2,1,0:T(8,128)(2,1)S(1)}, u32[]{:S(2)}, u32[]{:S(2)}) collective-permute-start(bf16[2,3,64,128]{3,2,1,0:T(8,128)(2,1)} %get-tuple-element.17.refs_0_), channel_id=1, source_target_pairs={{0,8},{4,12},{8,0},{12,4},{16,24},{20,28},{24,16},{28,20},{1,9},{5... | collective-permute-start | bytes 294920 | tf_op jit(solution)/shard_map/ppermute | solution.py:328
  16.3 3.5 %collective-permute-done.2.refs_1_ = bf16[2,3,64,128]{3,2,1,0:T(8,128)(2,1)S(1)} collective-permute-done((bf16[2,3,64,128]{3,2,1,0:T(8,128)(2,1)}, bf16[2,3,64,128]{3,2,1,0:T(8,128)(2,1)S(1)}, u32[]{:S(2)}, u32[]{:S(2)}) %collective-permute-start.2) | collective-permute-done | bytes 98336 | tf_op jit(solution)/shard_map/ppermute | solution.py:328
  20.5 2.4 %shard_map.116 = (bf16[2,2,64,128]{3,2,1,0:T(8,128)(2,1)}, bf16[2,3,64,128]{3,2,1,0:T(8,128)(2,1)}) custom-call(bf16[2,3,64,128]{3,2,1,0:T(8,128)(2,1)} %get-tuple-element.17.refs_0_, bf16[2,3,64,128]{3,2,1,0:T(8,128)(2,1)} %copy-done.1, bf16[2,3,64,128]{3,2,1,0:T(8,128)(2,1)} %get-tuple-element.18.refs_2_), custom_call_target="tpu_custom_call" | custom-call | flops 1000000 | bytes 1000000 | tf_op jit(solution)/shard_map/pallas_call | solution.py:331
  22.9 5.0 %collective-permute-start.3 = (bf16[2,2,64,128]{3,2,1,0:T(8,128)(2,1)}, bf16[2,2,64,128]{3,2,1,0:T(8,128)(2,1)S(1)}, u32[]{:S(2)}, u32[]{:S(2)}) collective-permute-start(bf16[2,2,64,128]{3,2,1,0:T(8,128)(2,1)} %get-tuple-element.20), channel_id=1, source_target_pairs={{0,16},{4,20},{8,24},{12,28},{1,17},{5,21},{9,25},{13,29},{2,18},{... | collective-permute-start | bytes 196616 | tf_op jit(solution)/shard_map/ppermute | solution.py:337
  27.9 2.2 %collective-permute-done.3.state_ref = bf16[2,2,64,128]{3,2,1,0:T(8,128)(2,1)S(1)} collective-permute-done((bf16[2,2,64,128]{3,2,1,0:T(8,128)(2,1)}, bf16[2,2,64,128]{3,2,1,0:T(8,128)(2,1)S(1)}, u32[]{:S(2)}, u32[]{:S(2)}) %collective-permute-start.3) | collective-permute-done | bytes 65568 | tf_op jit(solution)/shard_map/ppermute | solution.py:337
  30.7 2.0 %shard_map.117 = (bf16[2,64,128]{2,1,0:T(8,128)(2,1)}, bf16[2,64,128]{2,1,0:T(8,128)(2,1)}) custom-call(bf16[2,3,64,128]{3,2,1,0:T(8,128)(2,1)} %get-tuple-element.19.enter_ref, bf16[2,2,64,128]{3,2,1,0:T(8,128)(2,1)} %copy-done.4), custom_call_target="tpu_custom_call" | custom-call | flops 1000000 | bytes 1000000 | tf_op jit(solution)/shard_map/pallas_call | solution.py:338
  32.7 2.4 %collective-permute-start.9 = (bf16[2,64,128]{2,1,0:T(8,128)(2,1)}, bf16[2,64,128]{2,1,0:T(8,128)(2,1)S(1)}, u32[]{:S(2)}, u32[]{:S(2)}) collective-permute-start(bf16[2,64,128]{2,1,0:T(8,128)(2,1)} %get-tuple-element.29.refs_8_), channel_id=1, source_target_pairs={{0,3},{1,2},{2,1},{3,0},{4,7},{5,6},{6,5},{7,4},{8,11},{9,10},{10,... | collective-permute-start | bytes 98312 | tf_op jit(solution)/shard_map/ppermute | solution.py:345
  36.2 2.4 %collective-permute-start.6 = (f32[3,2,256]{2,1,0:T(2,128)S(1)}, f32[3,2,256]{2,1,0:T(2,128)S(1)}, u32[]{:S(2)}, u32[]{:S(2)}) collective-permute-start(f32[3,2,256]{2,1,0:T(2,128)S(1)} %copy-done.3), channel_id=1, source_target_pairs={{0,3},{1,2},{2,1},{3,0},{4,7},{5,6},{6,5},{7,4},{8,11},{9,10},{10,... | collective-permute-start | bytes 18440 | tf_op jit(solution)/shard_map/ppermute | solution.py:304
  39.2 1.7 %collective-permute-done.6.params_ref = f32[3,2,256]{2,1,0:T(2,128)S(1)} collective-permute-done((f32[3,2,256]{2,1,0:T(2,128)S(1)}, f32[3,2,256]{2,1,0:T(2,128)S(1)}, u32[]{:S(2)}, u32[]{:S(2)}) %collective-permute-start.6) | collective-permute-done | bytes 6176 | tf_op jit(solution)/shard_map/ppermute | solution.py:304
  40.8 1.4 %collective-permute-start.4 = (f32[3,2,256]{2,1,0:T(2,128)S(1)}, f32[3,2,256]{2,1,0:T(2,128)S(1)}, u32[]{:S(2)}, u32[]{:S(2)}) collective-permute-start(f32[3,2,256]{2,1,0:T(2,128)S(1)} %copy-done.3), channel_id=1, source_target_pairs={{0,1},{1,0},{2,3},{3,2},{4,5},{5,4},{6,7},{7,6},{8,9},{9,8},{10,11... | collective-permute-start | bytes 18440 | tf_op jit(solution)/shard_map/ppermute | solution.py:304
  42.2 2.7 %shard_map.113 = (bf16[2,256,128]{2,1,0:T(8,128)(2,1)}, bf16[2,2,64,256]{3,2,1,0:T(8,128)(2,1)}) custom-call(s32[1,4]{1,0:T(1,128)} %mask_ref.9, bf16[1,256,256]{2,1,0:T(8,128)(2,1)} %modes_ref.11, f32[1,256]{1,0:T(1,128)} %levels_ref.11, f32[3,2,256]{2,1,0:T(2,128)} %copy-done.2, bf16[1,256,64]{2,1,0:T(8,128)(2,1)} %copy.12.coupling_ref), custom_call_target="tpu_custom_call" | custom-call | flops 1000000 | bytes 1000000 | tf_op jit(solution)/shard_map/pallas_call | solution.py:317
  45.0 2.7 %shard_map.121 = (bf16[2,256,128]{2,1,0:T(8,128)(2,1)}, bf16[2,2,64,256]{3,2,1,0:T(8,128)(2,1)}) custom-call(s32[1,4]{1,0:T(1,128)} %mask_ref.9, bf16[1,256,256]{2,1,0:T(8,128)(2,1)} %modes_ref.11, f32[1,256]{1,0:T(1,128)} %levels_ref.11, f32[3,2,256]{2,1,0:T(2,128)} %copy-done.10, bf16[1,256,64]{2,1,0:T(8,128)(2,1)} %copy.12.coupling_ref), custom_call_target="tpu_custom_call" | custom-call | flops 1000000 | bytes 1000000 | tf_op jit(solution)/shard_map/pallas_call | solution.py:317
  48.3 2.7 %shard_map.120 = (bf16[2,256,128]{2,1,0:T(8,128)(2,1)}, bf16[2,2,64,256]{3,2,1,0:T(8,128)(2,1)}) custom-call(s32[1,4]{1,0:T(1,128)} %mask_ref.9, bf16[1,256,256]{2,1,0:T(8,128)(2,1)} %modes_ref.11, f32[1,256]{1,0:T(1,128)} %levels_ref.11, f32[3,2,256]{2,1,0:T(2,128)} %copy-done.9, bf16[1,256,64]{2,1,0:T(8,128)(2,1)} %copy.12.coupling_ref), custom_call_target="tpu_custom_call" | custom-call | flops 1000000 | bytes 1000000 | tf_op jit(solution)/shard_map/pallas_call | solution.py:317
  51.6 2.7 %shard_map.119 = (bf16[2,256,128]{2,1,0:T(8,128)(2,1)}, bf16[2,2,64,256]{3,2,1,0:T(8,128)(2,1)}) custom-call(s32[1,4]{1,0:T(1,128)} %mask_ref.9, bf16[1,256,256]{2,1,0:T(8,128)(2,1)} %modes_ref.11, f32[1,256]{1,0:T(1,128)} %levels_ref.11, f32[3,2,256]{2,1,0:T(2,128)} %copy-done.8, bf16[1,256,64]{2,1,0:T(8,128)(2,1)} %copy.12.coupling_ref), custom_call_target="tpu_custom_call" | custom-call | flops 1000000 | bytes 1000000 | tf_op jit(solution)/shard_map/pallas_call | solution.py:317
  54.3 2.6 %shard_map.118 = f32[1,2,256]{2,1,0:T(2,128)} custom-call(bf16[1,256,256]{2,1,0:T(8,128)(2,1)} %modes_ref.11, f32[1,256]{1,0:T(1,128)} %levels_ref.11, f32[3,2,256]{2,1,0:T(2,128)} %copy-done.2, bf16[2,256,128]{2,1,0:T(8,128)(2,1)} %get-tuple-element.16.left_ref.refs_0_, bf16[2,64,128]{2,1,0:T(8,128)(2,1)} %get-tuple-element.21.retarded_ref), custom_call_target="tpu_custom_call" | custom-call | flops 1000000 | bytes 1000000 | tf_op jit(solution)/shard_map/pallas_call | solution.py:347
  57.5 4.8 %shard_map.122 = bf16[1,2,8,64,256]{4,3,2,1,0:T(8,128)(2,1)} custom-call(s32[8]{0:T(128)} %offsets_ref.1, bf16[1,2,8,64,256]{4,3,2,1,0:T(8,128)(2,1)} %screen_ref.1, bf16[2,256,128]{2,1,0:T(8,128)(2,1)} %get-tuple-element.16.left_ref.refs_0_, bf16[2,256,128]{2,1,0:T(8,128)(2,1)} %get-tuple-element.22.refs_1_, ...), custom_call_target="tpu_custom_call" | custom-call | flops 1000000 | bytes 1000000 | tf_op jit(solution)/shard_map/pallas_call | solution.py:355
  (36 shorter events, 5.9 us)
Async XLA Ops:
  0.6 4.2 %collective-permute-start = (s32[1]{0:T(128)}, s32[1]{0:T(128)}, u32[]{:S(2)}, u32[]{:S(2)}) collective-permute-start(s32[1]{0:T(128)} %param.17), channel_id=1, source_target_pairs={{4,0},{8,4},{12,8},{16,12},{20,16},{24,20},{28,24},{5,1},{9,5},{13... | collective-permute-start | bytes 20 | tf_op jit(solution)/shard_map/ppermute | solution.py:301
  2.6 1.5 %copy-start.11 = (f32[1,2,256]{2,1,0:T(2,128)S(1)}, f32[1,2,256]{2,1,0:T(2,128)}, u32[]{:S(2)}) copy-start(f32[1,2,256]{2,1,0:T(2,128)} %param.13) | copy-start | bytes 6148
  4.1 0.7 %copy-start.12 = (f32[1,2,256]{2,1,0:T(2,128)S(1)}, f32[1,2,256]{2,1,0:T(2,128)}, u32[]{:S(2)}) copy-start(f32[1,2,256]{2,1,0:T(2,128)} %param.14) | copy-start | bytes 6148
  4.8 0.6 copy-start.2
  8.3 2.8 %collective-permute-start.1 = (bf16[2,3,64,128]{3,2,1,0:T(8,128)(2,1)}, bf16[2,3,64,128]{3,2,1,0:T(8,128)(2,1)S(1)}, u32[]{:S(2)}, u32[]{:S(2)}) collective-permute-start(bf16[2,3,64,128]{3,2,1,0:T(8,128)(2,1)} %shard_map.114.refs_0_), channel_id=1, source_target_pairs={{0,4},{4,0},{8,12},{12,8},{16,20},{20,16},{24,28},{28,24},{1,5},{5... | collective-permute-start | bytes 294920 | tf_op jit(solution)/shard_map/ppermute | solution.py:328
  11.1 0.6 %copy-start = (bf16[2,3,64,128]{3,2,1,0:T(8,128)(2,1)}, bf16[2,3,64,128]{3,2,1,0:T(8,128)(2,1)S(1)}, u32[]{:S(2)}) copy-start(bf16[2,3,64,128]{3,2,1,0:T(8,128)(2,1)S(1)} %collective-permute-done.1.refs_1_) | copy-start | bytes 294916
  13.8 6.1 %collective-permute-start.2 = (bf16[2,3,64,128]{3,2,1,0:T(8,128)(2,1)}, bf16[2,3,64,128]{3,2,1,0:T(8,128)(2,1)S(1)}, u32[]{:S(2)}, u32[]{:S(2)}) collective-permute-start(bf16[2,3,64,128]{3,2,1,0:T(8,128)(2,1)} %get-tuple-element.17.refs_0_), channel_id=1, source_target_pairs={{0,8},{4,12},{8,0},{12,4},{16,24},{20,28},{24,16},{28,20},{1,9},{5... | collective-permute-start | bytes 294920 | tf_op jit(solution)/shard_map/ppermute | solution.py:328
  19.9 0.6 %copy-start.1 = (bf16[2,3,64,128]{3,2,1,0:T(8,128)(2,1)}, bf16[2,3,64,128]{3,2,1,0:T(8,128)(2,1)S(1)}, u32[]{:S(2)}) copy-start(bf16[2,3,64,128]{3,2,1,0:T(8,128)(2,1)S(1)} %collective-permute-done.2.refs_1_) | copy-start | bytes 294916
  22.9 7.2 %collective-permute-start.3 = (bf16[2,2,64,128]{3,2,1,0:T(8,128)(2,1)}, bf16[2,2,64,128]{3,2,1,0:T(8,128)(2,1)S(1)}, u32[]{:S(2)}, u32[]{:S(2)}) collective-permute-start(bf16[2,2,64,128]{3,2,1,0:T(8,128)(2,1)} %get-tuple-element.20), channel_id=1, source_target_pairs={{0,16},{4,20},{8,24},{12,28},{1,17},{5,21},{9,25},{13,29},{2,18},{... | collective-permute-start | bytes 196616 | tf_op jit(solution)/shard_map/ppermute | solution.py:337
  30.1 0.6 %copy-start.4 = (bf16[2,2,64,128]{3,2,1,0:T(8,128)(2,1)}, bf16[2,2,64,128]{3,2,1,0:T(8,128)(2,1)S(1)}, u32[]{:S(2)}) copy-start(bf16[2,2,64,128]{3,2,1,0:T(8,128)(2,1)S(1)} %collective-permute-done.3.state_ref) | copy-start | bytes 196612
  30.7 5.5 %copy-start.3 = (f32[3,2,256]{2,1,0:T(2,128)S(1)}, f32[3,2,256]{2,1,0:T(2,128)}, u32[]{:S(2)}) copy-start(f32[3,2,256]{2,1,0:T(2,128)} %copy-done.2) | copy-start | bytes 18436
  32.7 24.1 %collective-permute-start.9 = (bf16[2,64,128]{2,1,0:T(8,128)(2,1)}, bf16[2,64,128]{2,1,0:T(8,128)(2,1)S(1)}, u32[]{:S(2)}, u32[]{:S(2)}) collective-permute-start(bf16[2,64,128]{2,1,0:T(8,128)(2,1)} %get-tuple-element.29.refs_8_), channel_id=1, source_target_pairs={{0,3},{1,2},{2,1},{3,0},{4,7},{5,6},{6,5},{7,4},{8,11},{9,10},{10,... | collective-permute-start | bytes 98312 | tf_op jit(solution)/shard_map/ppermute | solution.py:345
  35.2 21.7 %collective-permute-start.8 = (bf16[2,64,128]{2,1,0:T(8,128)(2,1)}, bf16[2,64,128]{2,1,0:T(8,128)(2,1)S(1)}, u32[]{:S(2)}, u32[]{:S(2)}) collective-permute-start(bf16[2,64,128]{2,1,0:T(8,128)(2,1)} %get-tuple-element.29.refs_8_), channel_id=1, source_target_pairs={{0,2},{1,3},{2,0},{3,1},{4,6},{5,7},{6,4},{7,5},{8,10},{9,11},{10,... | collective-permute-start | bytes 98312 | tf_op jit(solution)/shard_map/ppermute | solution.py:345
  35.7 21.2 %collective-permute-start.7 = (bf16[2,64,128]{2,1,0:T(8,128)(2,1)}, bf16[2,64,128]{2,1,0:T(8,128)(2,1)S(1)}, u32[]{:S(2)}, u32[]{:S(2)}) collective-permute-start(bf16[2,64,128]{2,1,0:T(8,128)(2,1)} %get-tuple-element.29.refs_8_), channel_id=1, source_target_pairs={{0,1},{1,0},{2,3},{3,2},{4,5},{5,4},{6,7},{7,6},{8,9},{9,8},{10,11... | collective-permute-start | bytes 98312 | tf_op jit(solution)/shard_map/ppermute | solution.py:345
  36.2 4.6 %collective-permute-start.6 = (f32[3,2,256]{2,1,0:T(2,128)S(1)}, f32[3,2,256]{2,1,0:T(2,128)S(1)}, u32[]{:S(2)}, u32[]{:S(2)}) collective-permute-start(f32[3,2,256]{2,1,0:T(2,128)S(1)} %copy-done.3), channel_id=1, source_target_pairs={{0,3},{1,2},{2,1},{3,0},{4,7},{5,6},{6,5},{7,4},{8,11},{9,10},{10,... | collective-permute-start | bytes 18440 | tf_op jit(solution)/shard_map/ppermute | solution.py:304
  38.7 9.0 %collective-permute-start.5 = (f32[3,2,256]{2,1,0:T(2,128)S(1)}, f32[3,2,256]{2,1,0:T(2,128)S(1)}, u32[]{:S(2)}, u32[]{:S(2)}) collective-permute-start(f32[3,2,256]{2,1,0:T(2,128)S(1)} %copy-done.3), channel_id=1, source_target_pairs={{0,2},{1,3},{2,0},{3,1},{4,6},{5,7},{6,4},{7,5},{8,10},{9,11},{10,... | collective-permute-start | bytes 18440 | tf_op jit(solution)/shard_map/ppermute | solution.py:304
  40.8 4.1 %copy-start.10 = (f32[3,2,256]{2,1,0:T(2,128)}, f32[3,2,256]{2,1,0:T(2,128)S(1)}, u32[]{:S(2)}) copy-start(f32[3,2,256]{2,1,0:T(2,128)S(1)} %collective-permute-done.6.params_ref) | copy-start | bytes 18436
  40.8 10.1 %collective-permute-start.4 = (f32[3,2,256]{2,1,0:T(2,128)S(1)}, f32[3,2,256]{2,1,0:T(2,128)S(1)}, u32[]{:S(2)}, u32[]{:S(2)}) collective-permute-start(f32[3,2,256]{2,1,0:T(2,128)S(1)} %copy-done.3), channel_id=1, source_target_pairs={{0,1},{1,0},{2,3},{3,2},{4,5},{5,4},{6,7},{7,6},{8,9},{9,8},{10,11... | collective-permute-start | bytes 18440 | tf_op jit(solution)/shard_map/ppermute | solution.py:304
  47.7 0.6 copy-start.9
  51.0 0.6 copy-start.8
  56.8 0.6 copy-start.5
  56.9 0.6 copy-start.6
  56.9 0.6 copy-start.7

commit v2 on v1

--- a/solution.py
+++ b/solution.py
@@ -8,6 +8,7 @@
 from jax.experimental.pallas import tpu as pltpu
 from jax.sharding import PartitionSpec as P
 
+
 broaden_base = 1.0
 energy_low = -0.25
 energy_span = 0.5
@@ -56,53 +57,81 @@
 
 
 def masked_link(coupling_ref, mask_ref, link2_ref):
-    rows, extent = coupling_ref.shape[1:]
+    extent, rows = coupling_ref.shape[1:]
     count = mask_ref.shape[1]
-    size = rows // count
-    link2_ref[...] = jnp.zeros_like(link2_ref)
-    for block in range(count):
-        keep = mask_ref[0, block].astype(f32)
-        piece = (coupling_ref[0, block * size : (block + 1) * size, :].astype(f32) * keep).astype(bf16)
-        link2_ref[block * size : (block + 1) * size, 0:extent] = piece
-        link2_ref[rows + block * size : rows + (block + 1) * size, extent : 2 * extent] = piece
-
-
-def maps_kernel(overall, ahead_ref, mask_ref, modes_ref, levels_ref, params_ref, coupling_ref, out_ref, link2_ref):
-    energies = params_ref.shape[1]
-    extent = coupling_ref.shape[2]
+    block = lax.broadcasted_iota(jnp.int32, (1, rows), 1) // (rows // count)
+    keep = jnp.zeros((1, rows), f32)
+    for index in range(count):
+        keep = jnp.where(block == index, mask_ref[0, index].astype(f32), keep)
+    link = (coupling_ref[0].astype(f32) * keep).astype(bf16)
+    none = jnp.zeros_like(link)
+    link2_ref[0:extent, 0:rows] = link
+    link2_ref[0:extent, rows:] = none
+    link2_ref[extent:, 0:rows] = none
+    link2_ref[extent:, rows:] = link
+
+
+def resolvents(overall, first, e, levels_ref, shift_ref, broad_ref):
+    return resolvent(levels_ref[...], shift_ref[0, e : e + 1, :], broad_ref[0, e : e + 1, :], first + e, overall)
+
+
+def three_parts(refs):
+    return refs if len(refs) == 3 else tuple(refs[0].at[i : i + 1] for i in range(3))
+
+
+def maps_kernel(
+    overall,
+    ahead_ref,
+    modes_ref,
+    levels_ref,
+    shift_ref,
+    broad_ref,
+    inject_ref,
+    left_ref,
+    free_ref,
+    out_ref,
+):
+    energies = shift_ref.shape[1]
+    extent = out_ref.shape[2]
     first = lax.axis_index("energy") * energies
-    masked_link(coupling_ref, mask_ref, link2_ref)
-    link2 = link2_ref[...]
     chosen = pl.multiple_of(ahead_ref[0] * extent, extent)
-    modes = modes_ref[0]
     rows = modes_ref[0, pl.ds(chosen, extent), :]
+    width = rows.shape[1]
     rows_f = rows.astype(f32)
     none = jnp.zeros_like(rows)
     rows2 = jnp.concatenate(
         [jnp.concatenate([rows, none], axis=1), jnp.concatenate([none, rows], axis=1)], axis=0
     )
     for e in range(energies):
-        dr, di = resolvent(
-            levels_ref[...], params_ref[0, e : e + 1, :], params_ref[1, e : e + 1, :], first + e, overall
-        )
-        scaled_re = (rows_f * dr).astype(bf16)
-        scaled_im = (rows_f * di).astype(bf16)
-        both = dot_last(jnp.concatenate([scaled_re, scaled_im], axis=0), modes)
-        free_re, free_im = both[:extent], both[extent:]
-        halves = jnp.concatenate([free_re.astype(bf16), free_im.astype(bf16)], axis=1)
-        out_ref[e, 0] = dot_mat(halves, link2).astype(bf16)
-        out_ref[e, 1] = dot_last(jnp.concatenate([scaled_re, scaled_im], axis=1), rows2).astype(bf16)
-        weight = jnp.sqrt(params_ref[2, e : e + 1, :])
-        root_re, root_im = free_re * weight, free_im * weight
-        straight = jnp.concatenate([root_re, root_im], axis=1).astype(bf16)
-        turned = jnp.concatenate([-root_im, root_re], axis=1).astype(bf16)
-        out_ref[e, 2] = dot_last(straight, jnp.concatenate([straight, turned], axis=0)).astype(bf16)
+        dr, di = resolvents(overall, first, e, levels_ref, shift_ref, broad_ref)
+        scaled = jnp.concatenate([(rows_f * dr).astype(bf16), (rows_f * di).astype(bf16)], axis=1)
+        out_ref[e, 0] = left_ref[e, pl.ds(chosen, extent), :]
+        out_ref[e, 1] = dot_last(scaled, rows2).astype(bf16)
+        free = free_ref[e, pl.ds(chosen, extent), :]
+        free_f = free.astype(f32)
+        weight = inject_ref[0, e : e + 1, :]
+        weighted = jnp.concatenate([free_f[:, :width] * weight, free_f[:, width:] * weight], axis=1)
+        turned = jnp.concatenate([-free_f[:, width:], free_f[:, :width]], axis=1)
+        out_ref[e, 2] = dot_last(
+            weighted.astype(bf16), jnp.concatenate([free, turned.astype(bf16)], axis=0)
+        ).astype(bf16)
 
 
 def rows_kernel(
-    overall, hop, share, mask_ref, modes_ref, levels_ref, params_ref, coupling_ref, left_ref, local_ref, link2_ref
+    overall,
+    hop,
+    share,
+    mask_ref,
+    modes_ref,
+    levels_ref,
+    coupling_ref,
+    *rest,
 ):
-    energies = params_ref.shape[1]
+    given = 3 if hop == 0 else 1
+    shift_ref, broad_ref, inject_ref = three_parts(rest[:given])
+    left_ref, local_ref, *rest = rest[given:]
+    link2_ref = rest[-1]
+    energies = shift_ref.shape[1]
     group = lax.axis_index("energy")
     first = jnp.bitwise_xor(group, hop) * energies
     masked_link(coupling_ref, mask_ref, link2_ref)
@@ -112,21 +141,22 @@
     mine = pl.multiple_of(group * share, share)
     rows_f = modes_ref[0, pl.ds(mine, share), :].astype(f32)
     for e in range(energies):
-        dr, di = resolvent(
-            levels_ref[...], params_ref[0, e : e + 1, :], params_ref[1, e : e + 1, :], first + e, overall
-        )
+        dr, di = resolvents(overall, first, e, levels_ref, shift_ref, broad_ref)
         free_re = dot_last((modes_f * dr).astype(bf16), modes)
         free_im = dot_last((modes_f * di).astype(bf16), modes)
-        halves = jnp.concatenate([free_re.astype(bf16), free_im.astype(bf16)], axis=1)
-        left_ref[e] = dot_mat(halves, link2).astype(bf16)
-        weight = jnp.sqrt(params_ref[2, e : e + 1, :])
-        straight = jnp.concatenate([free_re * weight, free_im * weight], axis=1).astype(bf16)
-        turned = jnp.concatenate([-(free_im * weight), free_re * weight], axis=1).astype(bf16)
-        own_re = dot_last((rows_f * dr).astype(bf16), modes) * weight
-        own_im = dot_last((rows_f * di).astype(bf16), modes) * weight
-        own = jnp.concatenate([own_re, own_im], axis=1).astype(bf16)
-        local_ref[e, 0] = dot_last(own, straight).astype(bf16)
-        local_ref[e, 1] = dot_last(own, turned).astype(bf16)
+        free = jnp.concatenate([free_re.astype(bf16), free_im.astype(bf16)], axis=1)
+        if hop == 0:
+            rest[0][e] = free
+        left_ref[e] = dot_last(free, link2).astype(bf16)
+        weight = inject_ref[0, e : e + 1, :]
+        own = dot_last(jnp.concatenate([rows_f * dr, rows_f * di], axis=0).astype(bf16), modes) * weight
+        own_re, own_im = own[:share], own[share:]
+        own = jnp.concatenate(
+            [jnp.concatenate([own_re, own_im], axis=1), jnp.concatenate([own_im, -own_re], axis=1)], axis=0
+        )
+        local = dot_last(own.astype(bf16), free)
+        local_ref[e, 0] = local[:share].astype(bf16)
+        local_ref[e, 1] = local[share:].astype(bf16)
 
 
 def pushed(step, state):
@@ -186,22 +216,22 @@
             new_enter_ref[e, part] = enter[part]
 
 
-def arrive_kernel(enter_ref, state_ref, retarded_ref, lesser_ref):
+def arrive_kernel(level, enter_ref, state_ref, retarded_ref, lesser_ref):
+    upper = jnp.right_shift(lax.axis_index("cell"), level) == 1
     for e in range(enter_ref.shape[0]):
         enter = read(enter_ref, e)
-        retarded, lesser = pushed(enter, read(state_ref, e))
+        state = pick(upper, read(state_ref, e), (jnp.zeros_like(enter[1]), jnp.zeros_like(enter[2])))
+        retarded, lesser = pushed(enter, state)
         retarded_ref[e] = (enter[1].astype(f32) + retarded).astype(bf16)
         lesser_ref[e] = (enter[2].astype(f32) + lesser).astype(bf16)
 
 
-def density_kernel(overall, modes_ref, levels_ref, params_ref, left_ref, retarded_ref, out_ref):
-    energies = params_ref.shape[1]
+def density_kernel(overall, modes_ref, levels_ref, shift_ref, broad_ref, left_ref, retarded_ref, out_ref):
+    energies = shift_ref.shape[1]
     first = lax.axis_index("energy") * energies
     modes = modes_ref[0].astype(f32)
     for e in range(energies):
-        _, di = resolvent(
-            levels_ref[...], params_ref[0, e : e + 1, :], params_ref[1, e : e + 1, :], first + e, overall
-        )
+        _, di = resolvents(overall, first, e, levels_ref, shift_ref, broad_ref)
         plain = modes * (modes * di).astype(bf16).astype(f32)
         left = left_ref[e]
         pz = dot_mat(left, full(retarded_ref[e])).astype(bf16).astype(f32)
@@ -271,6 +301,7 @@
         in_specs=in_specs,
         out_specs=outs,
         scratch_shapes=list(scratch),
+        compiler_params=pltpu.CompilerParams(vmem_limit_bytes=16 << 20),
         cost_estimate=pl.CostEstimate(flops=flops, bytes_accessed=size, transcendentals=0),
     )
 
@@ -298,34 +329,47 @@
     share = orbitals // groups
     sds = jax.ShapeDtypeStruct
 
+    def swapped(x, axis, distance):
+        return lax.ppermute(x, axis, [(i, i ^ distance) for i in range(lax.axis_size(axis))])
+
+    def others(x):
+        got = [x]
+        for hop in range(1, groups):
+            got.append(swapped(x, "energy", hop))
+        return got
+
+    coupling = jnp.swapaxes(coupling, 1, 2)
     ahead = lax.ppermute(interface, "cell", [(i + 1, i) for i in range(cells - 1)])
-    params = jnp.concatenate([level_shift, broadening, injection], axis=0)
-    all_params = [params] + [
-        lax.ppermute(params, "energy", [(i, i ^ hop) for i in range(groups)]) for hop in range(1, groups)
-    ]
-    link2 = pltpu.VMEM((2 * orbitals, width), bf16)
+    params = others(jnp.concatenate([level_shift, broadening, injection], axis=0))
+
+    lefts, locals_ = [], []
+    for hop in range(groups):
+        outs = (sds((energies, orbitals, width), bf16), sds((energies, 2, share, orbitals), bf16))
+        given = (level_shift, broadening, injection)
+        if hop == 0:
+            outs += (sds((energies, orbitals, 2 * orbitals), bf16),)
+        else:
+            given = (params[hop],)
+        left, local, *rest = call(
+            partial(rows_kernel, overall, hop, share),
+            outs,
+            [SMEM] + [VMEM] * (3 + len(given)),
+            [pltpu.VMEM((width, 2 * orbitals), bf16)],
+        )(row_mask, modes, levels, coupling, *given)
+        if hop == 0:
+            free = rest[0]
+        lefts.append(left)
+        locals_.append(local)
 
     total = call(
         partial(maps_kernel, overall),
         sds((energies, 3, extent, width), bf16),
-        [SMEM, SMEM, VMEM, VMEM, VMEM, VMEM],
-        [link2],
-    )(ahead, row_mask, modes, levels, params, coupling)
-
-    lefts, locals_ = [], []
-    for hop in range(groups):
-        left, local = call(
-            partial(rows_kernel, overall, hop, share),
-            (sds((energies, orbitals, width), bf16), sds((energies, 2, share, orbitals), bf16)),
-            [SMEM, VMEM, VMEM, VMEM, VMEM],
-            [link2],
-        )(row_mask, modes, levels, all_params[hop], coupling)
-        lefts.append(left)
-        locals_.append(local)
+        [SMEM] + [VMEM] * 7,
+    )(ahead, modes, levels, level_shift, broadening, injection, lefts[0], free)
 
     enter = None
     for level in range(rounds - 1):
-        other = lax.ppermute(total, "cell", [(i, i ^ (1 << level)) for i in range(cells)])
+        other = swapped(total, "cell", 1 << level)
         parts = 3 if level < rounds - 2 else 2
         given = [total, other] + ([enter] if level else [])
         total, enter = call(
@@ -333,22 +377,19 @@
             (sds((energies, parts, extent, width), bf16), sds((energies, 3, extent, width), bf16)),
             [VMEM] * len(given),
         )(*given)
-    half = cells // 2
-    state = lax.ppermute(total, "cell", [(i, i + half) for i in range(half)])
+    state = swapped(total, "cell", cells // 2)
     retarded, lesser = call(
-        arrive_kernel,
+        partial(arrive_kernel, rounds - 1),
         (sds((energies, extent, width), bf16), sds((energies, extent, width), bf16)),
         [VMEM, VMEM],
     )(enter, state)
 
-    lessers = [lesser] + [
-        lax.ppermute(lesser, "energy", [(i, i ^ hop) for i in range(groups)]) for hop in range(1, groups)
-    ]
+    lessers = others(lesser)
     density = call(
         partial(density_kernel, overall),
         sds((1, energies, orbitals), f32),
-        [VMEM] * 5,
-    )(modes, levels, params, lefts[0], retarded)
+        [VMEM] * 6,
+    )(modes, levels, level_shift, broadening, lefts[0], retarded)
 
     reach = overall // 4
     spread = pltpu.VMEM((overall + 2 * reach, share, orbitals), f32)

time: 62.8 us -> 45.5 us (0.72)
  Pallas kernels: 27.6 us -> 13.5 us
  local copies, waits for them, and re-layouts: 7.16 us -> 4.39 us
    pallas_call x5, Pallas kernels: 12.8 us -> 5.93 us  [the longest x4 5.46 us: body(): call(partial(rows_kernel, overall, hop, share), outs, [SMEM] + [VMEM] * (...]
    pallas_call x2, Pallas kernels: 4.48 us -> 1.27 us  [body(): call(partial(join_kernel, level), (sds((energies, parts, extent, width),...]
    unnamed x29 -> x30, local copies, waits for them, and re-layouts: 7.15 us -> 4.38 us
    pallas_call x1, Pallas kernels: 2.88 us -> 0.89 us  [body(): call(partial(maps_kernel, overall), sds((energies, 3, extent, width), bf1...]
    pallas_call x1, Pallas kernels: 2.55 us -> 1.57 us  [body(): call(partial(density_kernel, overall), sds((1, energies, orbitals), f32),...]
    pallas_call x1, Pallas kernels: 4.82 us -> 3.87 us  [body(): call(partial(convolve_kernel, groups, reach), sds((1, 2, overall, share,...]
  transfers between devices with their start and end apart: 10 -> 10, of which waited for: 4 -> 4; matrix products, arithmetic and copies ran while one was open for 4% -> 0% of each run, Pallas kernels for 21% -> 16%
where the time goes in v2:
time: 45.5 us; the launch traced here: 45.2 us
  starting transfers between devices  17.9 us (39%)
  Pallas kernels  13.5 us (30%)
  waiting for transfers between devices  8.52 us (19%)
  local copies, waits for them, and re-layouts  4.39 us (10%)
  between operations  0.81 us (2%)
    ppermute x9, starting transfers between devices, swapped(): lax.ppermute(x, axis, [(i, i ^ distance) for i in range(lax.axis_size(axi...  16.5 us
    ppermute x9, waiting for transfers between devices, swapped(): lax.ppermute(x, axis, [(i, i ^ distance) for i in range(lax.axis_size(axi...  8.51 us
    pallas_call x4, Pallas kernels, body(): call(partial(rows_kernel, overall, hop, share), outs, [SMEM] + [VMEM] * (...  5.46 us
    unnamed x30, local copies, waits for them, and re-layouts  4.38 us
    pallas_call x1, Pallas kernels, body(): call(partial(convolve_kernel, groups, reach), sds((1, 2, overall, share,...  3.87 us
    pallas_call x1, Pallas kernels, body(): call(partial(density_kernel, overall), sds((1, energies, orbitals), f32),...  1.57 us
    ppermute x1, starting transfers between devices, body(): lax.ppermute(interface, 'cell', [(i + 1, i) for i in range(cells - 1)])  1.42 us
    pallas_call x2, Pallas kernels, body(): call(partial(join_kernel, level), (sds((energies, parts, extent, width),...  1.27 us
  transfers between devices with their start and end apart: 10, of which 4 were waited for; matrix products, arithmetic and copies ran while one was open for 0% of the time, Pallas kernels for 16%

profile of v2, /device:TPU:0, one launch (start us, length us, event | category | flops | bytes accessed | tf_op | source)
XLA Modules:
  0.0 45.2 jit_solution(8791862098520948324)
XLA Ops:
  0.7 1.4 %collective-permute-start = (s32[1]{0:T(128)}, s32[1]{0:T(128)}, u32[]{:S(2)}, u32[]{:S(2)}) collective-permute-start(s32[1]{0:T(128)} %param.17), channel_id=1, source_target_pairs={{4,0},{8,4},{12,8},{16,12},{20,16},{24,20},{28,24},{5,1},{9,5},{13... | collective-permute-start | bytes 20 | tf_op jit(solution)/shard_map/ppermute | solution.py:342
  2.1 0.9 %copy-done = bf16[1,256,256]{2,1,0:T(8,128)(2,1)S(1)} copy-done((bf16[1,256,256]{2,1,0:T(8,128)(2,1)S(1)}, bf16[1,256,256]{2,1,0:T(8,128)(2,1)}, u32[]{:S(2)}) %copy-start) | copy-done | bytes 131096
  3.0 0.8 %copy-done.3 = bf16[1,256,64]{1,2,0:T(8,128)(2,1)S(1)} copy-done((bf16[1,256,64]{1,2,0:T(8,128)(2,1)S(1)}, bf16[1,256,64]{1,2,0:T(8,128)(2,1)}, u32[]{:S(2)}) %copy-start.3) | copy-done | bytes 32792
  3.8 0.7 %copy-done.6 = f32[1,2,256]{2,1,0:T(2,128)S(1)} copy-done((f32[1,2,256]{2,1,0:T(2,128)S(1)}, f32[1,2,256]{2,1,0:T(2,128)}, u32[]{:S(2)}) %copy-start.6) | copy-done | bytes 2072
  4.5 0.7 %copy-done.8 = f32[1,2,256]{2,1,0:T(2,128)S(1)} copy-done((f32[1,2,256]{2,1,0:T(2,128)S(1)}, f32[1,2,256]{2,1,0:T(2,128)}, u32[]{:S(2)}) %copy-start.8) | copy-done | bytes 2072
  5.1 0.7 %copy-done.10 = f32[1,2,256]{2,1,0:T(2,128)S(1)} copy-done((f32[1,2,256]{2,1,0:T(2,128)S(1)}, f32[1,2,256]{2,1,0:T(2,128)}, u32[]{:S(2)}) %copy-start.10) | copy-done | bytes 2072
  5.8 1.4 %shard_map.113 = (bf16[2,256,128]{2,1,0:T(8,128)(2,1)S(1)}, bf16[2,2,64,256]{3,2,1,0:T(8,128)(2,1)S(1)}, bf16[2,256,512]{2,1,0:T(8,128)(2,1)S(1)}) custom-call(s32[1,4]{1,0:T(1,128)S(1)} %copy-done.12, bf16[1,256,256]{2,1,0:T(8,128)(2,1)S(1)} %copy-done, f32[1,256]{1,0:T(1,128)S(1)} %copy-done.5, bf16[1,64,256]{2,1,0:T(8,128)(2,1)S(1)} %bitcast.1, ...), custom_call_target="tpu_custom_call" | custom-call | flops 1000000 | bytes 1000000 | tf_op jit(solution)/shard_map/pallas_call | solution.py:353
  7.2 0.9 %shard_map.114.refs_0_ = bf16[2,3,64,128]{3,2,1,0:T(8,128)(2,1)S(1)} custom-call(s32[1]{0:T(128)} %collective-permute-done.ahead_ref, bf16[1,256,256]{2,1,0:T(8,128)(2,1)S(1)} %copy-done.1, f32[1,256]{1,0:T(1,128)S(1)} %copy-done.5, f32[1,2,256]{2,1,0:T(2,128)S(1)} %copy-done.6, f32[1,2,256]{2,1,0:T(2,128)S(1)} %copy-done.8, f32[1,2,256]{2,1,0:T(2,128)S(1)} %copy-done.10, ...), custom_call_target="tpu_custom_call" | custom-call | flops 1000000 | bytes 1000000 | tf_op jit(solution)/shard_map/pallas_call | solution.py:364
  8.1 1.2 %collective-permute-start.1 = (bf16[2,3,64,128]{3,2,1,0:T(8,128)(2,1)S(1)}, bf16[2,3,64,128]{3,2,1,0:T(8,128)(2,1)S(1)}, u32[]{:S(2)}, u32[]{:S(2)}) collective-permute-start(bf16[2,3,64,128]{3,2,1,0:T(8,128)(2,1)S(1)} %shard_map.114.refs_0_), channel_id=1, source_target_pairs={{0,4},{4,0},{8,12},{12,8},{16,20},{20,16},{24,28},{28,24},{1,5},{5... | collective-permute-start | bytes 294920 | tf_op jit(solution)/shard_map/ppermute | solution.py:333
  9.3 0.9 %collective-permute-done.1.refs_1_ = bf16[2,3,64,128]{3,2,1,0:T(8,128)(2,1)S(1)} collective-permute-done((bf16[2,3,64,128]{3,2,1,0:T(8,128)(2,1)S(1)}, bf16[2,3,64,128]{3,2,1,0:T(8,128)(2,1)S(1)}, u32[]{:S(2)}, u32[]{:S(2)}) %collective-permute-start.1) | collective-permute-done | bytes 98336 | tf_op jit(solution)/shard_map/ppermute | solution.py:333
  10.7 3.1 %collective-permute-start.2 = (bf16[2,3,64,128]{3,2,1,0:T(8,128)(2,1)S(1)}, bf16[2,3,64,128]{3,2,1,0:T(8,128)(2,1)S(1)}, u32[]{:S(2)}, u32[]{:S(2)}) collective-permute-start(bf16[2,3,64,128]{3,2,1,0:T(8,128)(2,1)S(1)} %get-tuple-element.19.refs_0_), channel_id=1, source_target_pairs={{0,8},{4,12},{8,0},{12,4},{16,24},{20,28},{24,16},{28,20},{1,9},{5... | collective-permute-start | bytes 294920 | tf_op jit(solution)/shard_map/ppermute | solution.py:333
  13.9 3.3 %collective-permute-done.2.refs_1_ = bf16[2,3,64,128]{3,2,1,0:T(8,128)(2,1)S(1)} collective-permute-done((bf16[2,3,64,128]{3,2,1,0:T(8,128)(2,1)S(1)}, bf16[2,3,64,128]{3,2,1,0:T(8,128)(2,1)S(1)}, u32[]{:S(2)}, u32[]{:S(2)}) %collective-permute-start.2) | collective-permute-done | bytes 98336 | tf_op jit(solution)/shard_map/ppermute | solution.py:333
  17.2 0.8 %shard_map.116 = (bf16[2,2,64,128]{3,2,1,0:T(8,128)(2,1)S(1)}, bf16[2,3,64,128]{3,2,1,0:T(8,128)(2,1)S(1)}) custom-call(bf16[2,3,64,128]{3,2,1,0:T(8,128)(2,1)S(1)} %get-tuple-element.19.refs_0_, bf16[2,3,64,128]{3,2,1,0:T(8,128)(2,1)S(1)} %collective-permute-done.2.refs_1_, bf16[2,3,64,128]{3,2,1,0:T(8,128)(2,1)S(1)} %get-tuple-element.20.refs_2_), custom_call_target="tpu_custom_call" | custom-call | flops 1000000 | bytes 1000000 | tf_op jit(solution)/shard_map/pallas_call | solution.py:375
  18.0 3.2 %collective-permute-start.3 = (bf16[2,2,64,128]{3,2,1,0:T(8,128)(2,1)S(1)}, bf16[2,2,64,128]{3,2,1,0:T(8,128)(2,1)S(1)}, u32[]{:S(2)}, u32[]{:S(2)}) collective-permute-start(bf16[2,2,64,128]{3,2,1,0:T(8,128)(2,1)S(1)} %get-tuple-element.22), channel_id=1, source_target_pairs={{0,16},{4,20},{8,24},{12,28},{16,0},{20,4},{24,8},{28,12},{1,17},{... | collective-permute-start | bytes 196616 | tf_op jit(solution)/shard_map/ppermute | solution.py:333
  21.2 3.6 %collective-permute-done.3.state_ref = bf16[2,2,64,128]{3,2,1,0:T(8,128)(2,1)S(1)} collective-permute-done((bf16[2,2,64,128]{3,2,1,0:T(8,128)(2,1)S(1)}, bf16[2,2,64,128]{3,2,1,0:T(8,128)(2,1)S(1)}, u32[]{:S(2)}, u32[]{:S(2)}) %collective-permute-start.3) | collective-permute-done | bytes 65568 | tf_op jit(solution)/shard_map/ppermute | solution.py:333
  25.3 2.5 %collective-permute-start.9 = (bf16[2,64,128]{2,1,0:T(8,128)(2,1)S(1)}, bf16[2,64,128]{2,1,0:T(8,128)(2,1)S(1)}, u32[]{:S(2)}, u32[]{:S(2)}) collective-permute-start(bf16[2,64,128]{2,1,0:T(8,128)(2,1)S(1)} %get-tuple-element.31.refs_8_), channel_id=1, source_target_pairs={{0,3},{1,2},{2,1},{3,0},{4,7},{5,6},{6,5},{7,4},{8,11},{9,10},{10,... | collective-permute-start | bytes 98312 | tf_op jit(solution)/shard_map/ppermute | solution.py:333
  28.8 1.5 %collective-permute-start.4 = (f32[3,2,256]{2,1,0:T(2,128)S(1)}, f32[3,2,256]{2,1,0:T(2,128)S(1)}, u32[]{:S(2)}, u32[]{:S(2)}) collective-permute-start(f32[3,2,256]{2,1,0:T(2,128)S(1)} %constant_dynamic-update-slice_fusion), channel_id=1, source_target_pairs={{0,1},{1,0},{2,3},{3,2},{4,5},{5,4},{6,7},{7,6},{8,9},{9,8},{10,11... | collective-permute-start | bytes 18440 | tf_op jit(solution)/shard_map/ppermute | solution.py:333
  30.3 1.5 %collective-permute-start.5 = (f32[3,2,256]{2,1,0:T(2,128)S(1)}, f32[3,2,256]{2,1,0:T(2,128)S(1)}, u32[]{:S(2)}, u32[]{:S(2)}) collective-permute-start(f32[3,2,256]{2,1,0:T(2,128)S(1)} %constant_dynamic-update-slice_fusion), channel_id=1, source_target_pairs={{0,2},{1,3},{2,0},{3,1},{4,6},{5,7},{6,4},{7,5},{8,10},{9,11},{10,... | collective-permute-start | bytes 18440 | tf_op jit(solution)/shard_map/ppermute | solution.py:333
  32.5 2.4 %collective-permute-start.6 = (f32[3,2,256]{2,1,0:T(2,128)S(1)}, f32[3,2,256]{2,1,0:T(2,128)S(1)}, u32[]{:S(2)}, u32[]{:S(2)}) collective-permute-start(f32[3,2,256]{2,1,0:T(2,128)S(1)} %constant_dynamic-update-slice_fusion), channel_id=1, source_target_pairs={{0,3},{1,2},{2,1},{3,0},{4,7},{5,6},{6,5},{7,4},{8,11},{9,10},{10,... | collective-permute-start | bytes 18440 | tf_op jit(solution)/shard_map/ppermute | solution.py:333
  34.9 1.4 %shard_map.119 = (bf16[2,256,128]{2,1,0:T(8,128)(2,1)S(1)}, bf16[2,2,64,256]{3,2,1,0:T(8,128)(2,1)S(1)}) custom-call(s32[1,4]{1,0:T(1,128)S(1)} %copy-done.12, bf16[1,256,256]{2,1,0:T(8,128)(2,1)S(1)} %copy-done.1, f32[1,256]{1,0:T(1,128)S(1)} %copy-done.5, bf16[1,64,256]{2,1,0:T(8,128)(2,1)S(1)} %bitcast.2, f32[3,2,256]{2,1,0:T(2,128)S(1)} %collective-permute-done.4.rest_0_), custom_call_target="tpu_custom_call" | custom-call | flops 1000000 | bytes 1000000 | tf_op jit(solution)/shard_map/pallas_call | solution.py:353
  36.3 1.4 %shard_map.120 = (bf16[2,256,128]{2,1,0:T(8,128)(2,1)S(1)}, bf16[2,2,64,256]{3,2,1,0:T(8,128)(2,1)S(1)}) custom-call(s32[1,4]{1,0:T(1,128)S(1)} %copy-done.12, bf16[1,256,256]{2,1,0:T(8,128)(2,1)S(1)} %copy-done.1, f32[1,256]{1,0:T(1,128)S(1)} %copy-done.5, bf16[1,64,256]{2,1,0:T(8,128)(2,1)S(1)} %bitcast.3, f32[3,2,256]{2,1,0:T(2,128)S(1)} %collective-permute-done.5.rest_0_), custom_call_target="tpu_custom_call" | custom-call | flops 1000000 | bytes 1000000 | tf_op jit(solution)/shard_map/pallas_call | solution.py:353
  37.7 1.4 %shard_map.121 = (bf16[2,256,128]{2,1,0:T(8,128)(2,1)S(1)}, bf16[2,2,64,256]{3,2,1,0:T(8,128)(2,1)S(1)}) custom-call(s32[1,4]{1,0:T(1,128)S(1)} %copy-done.12, bf16[1,256,256]{2,1,0:T(8,128)(2,1)S(1)} %copy-done.1, f32[1,256]{1,0:T(1,128)S(1)} %copy-done.5, bf16[1,64,256]{2,1,0:T(8,128)(2,1)S(1)} %bitcast.4, f32[3,2,256]{2,1,0:T(2,128)S(1)} %collective-permute-done.6.rest_0_), custom_call_target="tpu_custom_call" | custom-call | flops 1000000 | bytes 1000000 | tf_op jit(solution)/shard_map/pallas_call | solution.py:353
  39.1 1.6 %shard_map.118 = f32[1,2,256]{2,1,0:T(2,128)} custom-call(bf16[1,256,256]{2,1,0:T(8,128)(2,1)S(1)} %copy-done.1, f32[1,256]{1,0:T(1,128)S(1)} %copy-done.5, f32[1,2,256]{2,1,0:T(2,128)S(1)} %copy-done.7, f32[1,2,256]{2,1,0:T(2,128)S(1)} %copy-done.9, bf16[2,256,128]{2,1,0:T(8,128)(2,1)S(1)} %get-tuple-element.17.left_ref.refs_0_, ...), custom_call_target="tpu_custom_call" | custom-call | flops 1000000 | bytes 1000000 | tf_op jit(solution)/shard_map/pallas_call | solution.py:388
  41.3 3.9 %shard_map.122 = bf16[1,2,8,64,256]{4,3,2,1,0:T(8,128)(2,1)} custom-call(s32[8]{0:T(128)S(1)} %copy-done.13, bf16[1,2,8,64,256]{4,3,2,1,0:T(8,128)(2,1)S(1)} %copy-done.2, bf16[2,256,128]{2,1,0:T(8,128)(2,1)S(1)} %get-tuple-element.17.left_ref.refs_0_, bf16[2,256,128]{2,1,0:T(8,128)(2,1)S(1)} %get-tuple-element.24.refs_1_, ...), custom_call_target="tpu_custom_call" | custom-call | flops 1000000 | bytes 1000000 | tf_op jit(solution)/shard_map/pallas_call | solution.py:396
  (37 shorter events, 3.3 us)
Async XLA Ops:
  0.6 1.5 %copy-start.5 = (f32[1,256]{1,0:T(1,128)S(1)}, f32[1,256]{1,0:T(1,128)}, u32[]{:S(2)}) copy-start(f32[1,256]{1,0:T(1,128)} %levels_ref.11) | copy-start | bytes 3076
  0.6 1.5 %copy-start.12 = (s32[1,4]{1,0:T(1,128)S(1)}, s32[1,4]{1,0:T(1,128)}, u32[]{:S(2)}) copy-start(s32[1,4]{1,0:T(1,128)} %mask_ref.7) | copy-start | bytes 52
  0.7 6.5 %collective-permute-start = (s32[1]{0:T(128)}, s32[1]{0:T(128)}, u32[]{:S(2)}, u32[]{:S(2)}) collective-permute-start(s32[1]{0:T(128)} %param.17), channel_id=1, source_target_pairs={{4,0},{8,4},{12,8},{16,12},{20,16},{24,20},{28,24},{5,1},{9,5},{13... | collective-permute-start | bytes 20 | tf_op jit(solution)/shard_map/ppermute | solution.py:342
  2.1 0.9 %copy-start = (bf16[1,256,256]{2,1,0:T(8,128)(2,1)S(1)}, bf16[1,256,256]{2,1,0:T(8,128)(2,1)}, u32[]{:S(2)}) copy-start(bf16[1,256,256]{2,1,0:T(8,128)(2,1)} %modes_ref.11) | copy-start | bytes 393220
  3.0 0.8 %copy-start.3 = (bf16[1,256,64]{1,2,0:T(8,128)(2,1)S(1)}, bf16[1,256,64]{1,2,0:T(8,128)(2,1)}, u32[]{:S(2)}) copy-start(bf16[1,256,64]{1,2,0:T(8,128)(2,1)} %param.15) | copy-start | bytes 98308
  3.8 0.7 %copy-start.6 = (f32[1,2,256]{2,1,0:T(2,128)S(1)}, f32[1,2,256]{2,1,0:T(2,128)}, u32[]{:S(2)}) copy-start(f32[1,2,256]{2,1,0:T(2,128)} %shift_ref.3) | copy-start | bytes 6148
  4.4 0.7 %copy-start.8 = (f32[1,2,256]{2,1,0:T(2,128)S(1)}, f32[1,2,256]{2,1,0:T(2,128)}, u32[]{:S(2)}) copy-start(f32[1,2,256]{2,1,0:T(2,128)} %broad_ref.3) | copy-start | bytes 6148
  5.1 0.7 %copy-start.10 = (f32[1,2,256]{2,1,0:T(2,128)S(1)}, f32[1,2,256]{2,1,0:T(2,128)}, u32[]{:S(2)}) copy-start(f32[1,2,256]{2,1,0:T(2,128)} %inject_ref.1) | copy-start | bytes 6148
  5.8 1.4 %copy-start.1 = (bf16[1,256,256]{2,1,0:T(8,128)(2,1)S(1)}, bf16[1,256,256]{2,1,0:T(8,128)(2,1)}, u32[]{:S(2)}) copy-start(bf16[1,256,256]{2,1,0:T(8,128)(2,1)} %modes_ref.11) | copy-start | bytes 393220
  8.1 2.1 %collective-permute-start.1 = (bf16[2,3,64,128]{3,2,1,0:T(8,128)(2,1)S(1)}, bf16[2,3,64,128]{3,2,1,0:T(8,128)(2,1)S(1)}, u32[]{:S(2)}, u32[]{:S(2)}) collective-permute-start(bf16[2,3,64,128]{3,2,1,0:T(8,128)(2,1)S(1)} %shard_map.114.refs_0_), channel_id=1, source_target_pairs={{0,4},{4,0},{8,12},{12,8},{16,20},{20,16},{24,28},{28,24},{1,5},{5... | collective-permute-start | bytes 294920 | tf_op jit(solution)/shard_map/ppermute | solution.py:333
  10.3 3.6 %copy-start.7 = (f32[1,2,256]{2,1,0:T(2,128)S(1)}, f32[1,2,256]{2,1,0:T(2,128)}, u32[]{:S(2)}) copy-start(f32[1,2,256]{2,1,0:T(2,128)} %shift_ref.3) | copy-start | bytes 6148
  10.7 6.4 %collective-permute-start.2 = (bf16[2,3,64,128]{3,2,1,0:T(8,128)(2,1)S(1)}, bf16[2,3,64,128]{3,2,1,0:T(8,128)(2,1)S(1)}, u32[]{:S(2)}, u32[]{:S(2)}) collective-permute-start(bf16[2,3,64,128]{3,2,1,0:T(8,128)(2,1)S(1)} %get-tuple-element.19.refs_0_), channel_id=1, source_target_pairs={{0,8},{4,12},{8,0},{12,4},{16,24},{20,28},{24,16},{28,20},{1,9},{5... | collective-permute-start | bytes 294920 | tf_op jit(solution)/shard_map/ppermute | solution.py:333
  17.2 4.0 %copy-start.9 = (f32[1,2,256]{2,1,0:T(2,128)S(1)}, f32[1,2,256]{2,1,0:T(2,128)}, u32[]{:S(2)}) copy-start(f32[1,2,256]{2,1,0:T(2,128)} %broad_ref.3) | copy-start | bytes 6148
  17.2 11.6 %copy-start.11 = (f32[1,2,256]{2,1,0:T(2,128)S(1)}, f32[1,2,256]{2,1,0:T(2,128)}, u32[]{:S(2)}) copy-start(f32[1,2,256]{2,1,0:T(2,128)} %inject_ref.1) | copy-start | bytes 6148
  17.2 17.7 %copy-start.4 = (bf16[1,256,64]{1,2,0:T(8,128)(2,1)S(1)}, bf16[1,256,64]{1,2,0:T(8,128)(2,1)}, u32[]{:S(2)}) copy-start(bf16[1,256,64]{1,2,0:T(8,128)(2,1)} %param.15) | copy-start | bytes 98308
  18.0 22.7 %copy-start.2 = (bf16[1,2,8,64,256]{4,3,2,1,0:T(8,128)(2,1)S(1)}, bf16[1,2,8,64,256]{4,3,2,1,0:T(8,128)(2,1)}, u32[]{:S(2)}) copy-start(bf16[1,2,8,64,256]{4,3,2,1,0:T(8,128)(2,1)} %screen_ref.1) | copy-start | bytes 1572868
  18.0 6.8 %collective-permute-start.3 = (bf16[2,2,64,128]{3,2,1,0:T(8,128)(2,1)S(1)}, bf16[2,2,64,128]{3,2,1,0:T(8,128)(2,1)S(1)}, u32[]{:S(2)}, u32[]{:S(2)}) collective-permute-start(bf16[2,2,64,128]{3,2,1,0:T(8,128)(2,1)S(1)} %get-tuple-element.22), channel_id=1, source_target_pairs={{0,16},{4,20},{8,24},{12,28},{16,0},{20,4},{24,8},{28,12},{1,17},{... | collective-permute-start | bytes 196616 | tf_op jit(solution)/shard_map/ppermute | solution.py:333
  25.3 15.4 %collective-permute-start.9 = (bf16[2,64,128]{2,1,0:T(8,128)(2,1)S(1)}, bf16[2,64,128]{2,1,0:T(8,128)(2,1)S(1)}, u32[]{:S(2)}, u32[]{:S(2)}) collective-permute-start(bf16[2,64,128]{2,1,0:T(8,128)(2,1)S(1)} %get-tuple-element.31.refs_8_), channel_id=1, source_target_pairs={{0,3},{1,2},{2,1},{3,0},{4,7},{5,6},{6,5},{7,4},{8,11},{9,10},{10,... | collective-permute-start | bytes 98312 | tf_op jit(solution)/shard_map/ppermute | solution.py:333
  27.8 12.9 %collective-permute-start.8 = (bf16[2,64,128]{2,1,0:T(8,128)(2,1)S(1)}, bf16[2,64,128]{2,1,0:T(8,128)(2,1)S(1)}, u32[]{:S(2)}, u32[]{:S(2)}) collective-permute-start(bf16[2,64,128]{2,1,0:T(8,128)(2,1)S(1)} %get-tuple-element.31.refs_8_), channel_id=1, source_target_pairs={{0,2},{1,3},{2,0},{3,1},{4,6},{5,7},{6,4},{7,5},{8,10},{9,11},{10,... | collective-permute-start | bytes 98312 | tf_op jit(solution)/shard_map/ppermute | solution.py:333
  28.3 12.3 %collective-permute-start.7 = (bf16[2,64,128]{2,1,0:T(8,128)(2,1)S(1)}, bf16[2,64,128]{2,1,0:T(8,128)(2,1)S(1)}, u32[]{:S(2)}, u32[]{:S(2)}) collective-permute-start(bf16[2,64,128]{2,1,0:T(8,128)(2,1)S(1)} %get-tuple-element.31.refs_8_), channel_id=1, source_target_pairs={{0,1},{1,0},{2,3},{3,2},{4,5},{5,4},{6,7},{7,6},{8,9},{9,8},{10,11... | collective-permute-start | bytes 98312 | tf_op jit(solution)/shard_map/ppermute | solution.py:333
  28.8 3.6 %collective-permute-start.4 = (f32[3,2,256]{2,1,0:T(2,128)S(1)}, f32[3,2,256]{2,1,0:T(2,128)S(1)}, u32[]{:S(2)}, u32[]{:S(2)}) collective-permute-start(f32[3,2,256]{2,1,0:T(2,128)S(1)} %constant_dynamic-update-slice_fusion), channel_id=1, source_target_pairs={{0,1},{1,0},{2,3},{3,2},{4,5},{5,4},{6,7},{7,6},{8,9},{9,8},{10,11... | collective-permute-start | bytes 18440 | tf_op jit(solution)/shard_map/ppermute | solution.py:333
  30.3 6.0 %collective-permute-start.5 = (f32[3,2,256]{2,1,0:T(2,128)S(1)}, f32[3,2,256]{2,1,0:T(2,128)S(1)}, u32[]{:S(2)}, u32[]{:S(2)}) collective-permute-start(f32[3,2,256]{2,1,0:T(2,128)S(1)} %constant_dynamic-update-slice_fusion), channel_id=1, source_target_pairs={{0,2},{1,3},{2,0},{3,1},{4,6},{5,7},{6,4},{7,5},{8,10},{9,11},{10,... | collective-permute-start | bytes 18440 | tf_op jit(solution)/shard_map/ppermute | solution.py:333
  32.5 5.2 %collective-permute-start.6 = (f32[3,2,256]{2,1,0:T(2,128)S(1)}, f32[3,2,256]{2,1,0:T(2,128)S(1)}, u32[]{:S(2)}, u32[]{:S(2)}) collective-permute-start(f32[3,2,256]{2,1,0:T(2,128)S(1)} %constant_dynamic-update-slice_fusion), channel_id=1, source_target_pairs={{0,3},{1,2},{2,1},{3,0},{4,7},{5,6},{6,5},{7,4},{8,11},{9,10},{10,... | collective-permute-start | bytes 18440 | tf_op jit(solution)/shard_map/ppermute | solution.py:333
  40.6 0.7 %copy-start.13 = (s32[8]{0:T(128)S(1)}, s32[8]{0:T(128)}, u32[]{:S(2)}) copy-start(s32[8]{0:T(128)} %offsets_ref.1) | copy-start | bytes 100

commit v3 on v2

--- a/solution.py
+++ b/solution.py
@@ -17,6 +17,7 @@
 
 VMEM = pl.BlockSpec(memory_space=pltpu.VMEM)
 SMEM = pl.BlockSpec(memory_space=pltpu.SMEM)
+HBM = pl.BlockSpec(memory_space=pltpu.HBM)
 
 
 def dot_last(a, b, precision=None):
@@ -56,7 +57,7 @@
     return detune * inverse, -damping * inverse
 
 
-def masked_link(coupling_ref, mask_ref, link2_ref):
+def masked_link(link2_ref, coupling_ref, mask_ref):
     extent, rows = coupling_ref.shape[1:]
     count = mask_ref.shape[1]
     block = lax.broadcasted_iota(jnp.int32, (1, rows), 1) // (rows // count)
@@ -71,30 +72,27 @@
     link2_ref[extent:, rows:] = link
 
 
-def resolvents(overall, first, e, levels_ref, shift_ref, broad_ref):
-    return resolvent(levels_ref[...], shift_ref[0, e : e + 1, :], broad_ref[0, e : e + 1, :], first + e, overall)
-
-
-def three_parts(refs):
-    return refs if len(refs) == 3 else tuple(refs[0].at[i : i + 1] for i in range(3))
+def resolvents(overall, first, e, levels_ref, params_ref):
+    return resolvent(levels_ref[...], params_ref[0, e : e + 1, :], params_ref[1, e : e + 1, :], first + e, overall)
 
 
 def maps_kernel(
     overall,
-    ahead_ref,
+    one_ref,
+    two_ref,
     modes_ref,
     levels_ref,
-    shift_ref,
-    broad_ref,
-    inject_ref,
+    params_ref,
     left_ref,
     free_ref,
     out_ref,
+    message_ref,
 ):
-    energies = shift_ref.shape[1]
+    energies = params_ref.shape[2]
     extent = out_ref.shape[2]
     first = lax.axis_index("energy") * energies
-    chosen = pl.multiple_of(ahead_ref[0] * extent, extent)
+    odd = jnp.bitwise_and(lax.axis_index("cell"), 1) == 1
+    chosen = pl.multiple_of(jnp.where(odd, two_ref[0], one_ref[0]) * extent, extent)
     rows = modes_ref[0, pl.ds(chosen, extent), :]
     width = rows.shape[1]
     rows_f = rows.astype(f32)
@@ -102,53 +100,44 @@
     rows2 = jnp.concatenate(
         [jnp.concatenate([rows, none], axis=1), jnp.concatenate([none, rows], axis=1)], axis=0
     )
+    maps = []
     for e in range(energies):
-        dr, di = resolvents(overall, first, e, levels_ref, shift_ref, broad_ref)
+        dr, di = resolvents(overall, first, e, levels_ref, params_ref.at[0])
         scaled = jnp.concatenate([(rows_f * dr).astype(bf16), (rows_f * di).astype(bf16)], axis=1)
-        out_ref[e, 0] = left_ref[e, pl.ds(chosen, extent), :]
-        out_ref[e, 1] = dot_last(scaled, rows2).astype(bf16)
         free = free_ref[e, pl.ds(chosen, extent), :]
         free_f = free.astype(f32)
-        weight = inject_ref[0, e : e + 1, :]
+        weight = params_ref[0, 2, e : e + 1, :]
         weighted = jnp.concatenate([free_f[:, :width] * weight, free_f[:, width:] * weight], axis=1)
         turned = jnp.concatenate([-free_f[:, width:], free_f[:, :width]], axis=1)
-        out_ref[e, 2] = dot_last(
-            weighted.astype(bf16), jnp.concatenate([free, turned.astype(bf16)], axis=0)
-        ).astype(bf16)
-
-
-def rows_kernel(
-    overall,
-    hop,
-    share,
-    mask_ref,
-    modes_ref,
-    levels_ref,
-    coupling_ref,
-    *rest,
-):
-    given = 3 if hop == 0 else 1
-    shift_ref, broad_ref, inject_ref = three_parts(rest[:given])
-    left_ref, local_ref, *rest = rest[given:]
-    link2_ref = rest[-1]
-    energies = shift_ref.shape[1]
+        maps.append(
+            (
+                left_ref[e, pl.ds(chosen, extent), :],
+                dot_last(scaled, rows2),
+                dot_last(weighted.astype(bf16), jnp.concatenate([free, turned.astype(bf16)], axis=0)),
+            )
+        )
+        for part in range(3):
+            out_ref[e, part] = maps[e][part].astype(bf16)
+    write_message(message_ref, maps)
+
+
+def make_rows(energies, hop, overall, share, modes_ref, levels_ref, params_ref, link2_ref, left_ref, local_ref, free_ref):
     group = lax.axis_index("energy")
     first = jnp.bitwise_xor(group, hop) * energies
-    masked_link(coupling_ref, mask_ref, link2_ref)
     link2 = link2_ref[...]
     modes = modes_ref[0]
     modes_f = modes.astype(f32)
     mine = pl.multiple_of(group * share, share)
     rows_f = modes_ref[0, pl.ds(mine, share), :].astype(f32)
     for e in range(energies):
-        dr, di = resolvents(overall, first, e, levels_ref, shift_ref, broad_ref)
+        dr, di = resolvents(overall, first, e, levels_ref, params_ref)
         free_re = dot_last((modes_f * dr).astype(bf16), modes)
         free_im = dot_last((modes_f * di).astype(bf16), modes)
         free = jnp.concatenate([free_re.astype(bf16), free_im.astype(bf16)], axis=1)
-        if hop == 0:
-            rest[0][e] = free
+        if free_ref is not None:
+            free_ref[e] = free
         left_ref[e] = dot_last(free, link2).astype(bf16)
-        weight = inject_ref[0, e : e + 1, :]
+        weight = params_ref[2, e : e + 1, :]
         own = dot_last(jnp.concatenate([rows_f * dr, rows_f * di], axis=0).astype(bf16), modes) * weight
         own_re, own_im = own[:share], own[share:]
         own = jnp.concatenate(
@@ -159,6 +148,159 @@
         local_ref[e, 1] = local[share:].astype(bf16)
 
 
+def own_rows_kernel(
+    overall,
+    share,
+    mask_hbm,
+    modes_hbm,
+    levels_hbm,
+    coupling_hbm,
+    shift_hbm,
+    broad_hbm,
+    inject_hbm,
+    left_ref,
+    local_ref,
+    free_ref,
+    link2_ref,
+    modes_ref,
+    levels_ref,
+    params_ref,
+    mask_ref,
+    coupling_ref,
+    sems,
+):
+    energies = shift_hbm.shape[1]
+    copies = [
+        pltpu.make_async_copy(source, target, sems.at[index])
+        for index, (source, target) in enumerate(
+            (
+                (mask_hbm, mask_ref),
+                (coupling_hbm, coupling_ref),
+                (shift_hbm, params_ref.at[0, 0:1]),
+                (broad_hbm, params_ref.at[0, 1:2]),
+                (inject_hbm, params_ref.at[0, 2:3]),
+                (levels_hbm, levels_ref),
+                (modes_hbm, modes_ref),
+            )
+        )
+    ]
+    for copy in copies:
+        copy.start()
+    for copy in copies:
+        copy.wait()
+    masked_link(link2_ref, coupling_ref, mask_ref)
+    make_rows(
+        energies,
+        0,
+        overall,
+        share,
+        modes_ref,
+        levels_ref,
+        params_ref.at[0],
+        link2_ref,
+        left_ref,
+        local_ref,
+        free_ref,
+    )
+
+
+def rows_kernel(overall, share, hop, slot, modes_ref, levels_ref, link2_ref, got_ref, *rest):
+    if len(rest) > 2:
+        had_ref, left_ref, local_ref, both_ref = rest
+        count = had_ref.shape[0]
+        both_ref[0:count] = had_ref[...]
+        both_ref[count:] = got_ref[...]
+    else:
+        left_ref, local_ref = rest
+    make_rows(
+        got_ref.shape[2],
+        hop,
+        overall,
+        share,
+        modes_ref,
+        levels_ref,
+        got_ref.at[slot],
+        link2_ref,
+        left_ref,
+        local_ref,
+        None,
+    )
+
+
+spare = 16
+
+
+def places(extent, width):
+    row = lax.broadcasted_iota(jnp.int32, (extent, width), 0)
+    lane = lax.broadcasted_iota(jnp.int32, (extent, width), 1)
+    return row, jnp.where(lane < extent, lane, lane - extent), lane < extent
+
+
+def pack_lesser(first, second):
+    _, _, low = places(*first.shape)
+    return jnp.where(low, first + swap_halves(first), second + swap_halves(second))
+
+
+def with_turned(x):
+    square = jnp.concatenate([x, swap_halves(x)], axis=0)
+    return square, square.T
+
+
+def unpack_lesser(packed):
+    packed = packed.astype(f32)
+    extent, width = packed.shape
+    _, _, low = places(extent, width)
+    square, turned = with_turned(packed)
+    total, change = 0.5 * (square + turned), 0.5 * (square - turned)
+    return (
+        jnp.where(low, total[:extent], change[extent:]),
+        jnp.where(low, total[extent:], change[:extent]),
+    )
+
+
+def pack_retarded(first, second):
+    row, column, _ = places(*first.shape)
+    diagonal = jnp.sum(jnp.where(row == column, second, 0.0), axis=0, keepdims=True)
+    return jnp.where(row <= column, first, second), jnp.broadcast_to(diagonal, (spare, first.shape[1]))
+
+
+def unpack_retarded(packed, diagonal):
+    packed, diagonal = packed.astype(f32), diagonal.astype(f32)
+    extent, width = packed.shape
+    row, column, _ = places(extent, width)
+    turned = with_turned(packed)[1][:extent]
+    return (
+        jnp.where(row <= column, packed, turned),
+        jnp.where(row > column, packed, jnp.where(row == column, diagonal, turned)),
+    )
+
+
+def write_message(ref, maps):
+    extent = maps[0][-1].shape[0]
+    for pair in range(ref.shape[0]):
+        first, second = maps[2 * pair], maps[2 * pair + 1]
+        shared, diagonal = pack_retarded(first[-2], second[-2])
+        ref[pair, 0:extent] = shared.astype(bf16)
+        ref[pair, extent : 2 * extent] = pack_lesser(first[-1], second[-1]).astype(bf16)
+        ref[pair, 2 * extent : 2 * extent + spare] = diagonal.astype(bf16)
+        if ref.shape[1] > 2 * extent + spare:
+            ref[pair, 2 * extent + spare : 3 * extent + spare] = first[0].astype(bf16)
+            ref[pair, 3 * extent + spare :] = second[0].astype(bf16)
+
+
+def read_message(ref):
+    extent = ref.shape[2] // 2
+    maps = []
+    for pair in range(ref.shape[0]):
+        retarded = unpack_retarded(ref[pair, 0:extent], ref[pair, 2 * extent : 2 * extent + 1])
+        lesser = unpack_lesser(ref[pair, extent : 2 * extent])
+        for which in range(2):
+            start = (2 + which) * extent + spare
+            front = (ref[pair, start : start + extent],) if ref.shape[1] > 2 * extent + spare else ()
+            maps.append(front + (retarded[which].astype(bf16), lesser[which].astype(bf16)))
+    return maps
+
+
 def pushed(step, state):
     first = dot_mat(step[0], jnp.concatenate([full(state[0]), full(state[1])], axis=1)).astype(bf16)
     width = step[0].shape[1]
@@ -195,16 +337,16 @@
 def join_kernel(level, *refs):
     total_ref, other_ref = refs[:2]
     enter_ref = refs[2] if level else None
-    new_total_ref, new_enter_ref = refs[-2:]
+    outs = refs[3 if level else 2 :]
+    new_enter_ref, message_ref = outs[:2]
     energies, _, extent, width = total_ref.shape
     place = lax.axis_index("cell")
     upper = jnp.bitwise_and(jnp.right_shift(place, level), 1) == 1
-    parts = new_total_ref.shape[1]
+    others = read_message(other_ref)
+    joined = []
     for e in range(energies):
-        total, other = read(total_ref, e), read(other_ref, e)
-        joined = compose(pick(upper, other, total), pick(upper, total, other))
-        for part in range(parts):
-            new_total_ref[e, part] = joined[part + 3 - parts].astype(bf16)
+        total, other = read(total_ref, e), others[e]
+        joined.append(compose(pick(upper, other, total), pick(upper, total, other)))
         if level:
             enter = read(enter_ref, e)
             longer = compose(other, enter)
@@ -214,24 +356,31 @@
             enter = pick(upper, other, neutral(extent, width))
         for part in range(3):
             new_enter_ref[e, part] = enter[part]
+            if len(outs) > 2:
+                outs[2][e, part] = joined[e][part].astype(bf16)
+    write_message(message_ref, joined)
 
 
 def arrive_kernel(level, enter_ref, state_ref, retarded_ref, lesser_ref):
     upper = jnp.right_shift(lax.axis_index("cell"), level) == 1
+    states = read_message(state_ref)
+    lessers = []
     for e in range(enter_ref.shape[0]):
         enter = read(enter_ref, e)
-        state = pick(upper, read(state_ref, e), (jnp.zeros_like(enter[1]), jnp.zeros_like(enter[2])))
+        state = pick(upper, states[e], (jnp.zeros_like(enter[1]), jnp.zeros_like(enter[2])))
         retarded, lesser = pushed(enter, state)
         retarded_ref[e] = (enter[1].astype(f32) + retarded).astype(bf16)
-        lesser_ref[e] = (enter[2].astype(f32) + lesser).astype(bf16)
-
-
-def density_kernel(overall, modes_ref, levels_ref, shift_ref, broad_ref, left_ref, retarded_ref, out_ref):
-    energies = shift_ref.shape[1]
+        lessers.append(enter[2].astype(f32) + lesser)
+    for pair in range(lesser_ref.shape[0]):
+        lesser_ref[pair] = pack_lesser(lessers[2 * pair], lessers[2 * pair + 1]).astype(bf16)
+
+
+def density_kernel(overall, modes_ref, levels_ref, params_ref, left_ref, retarded_ref, out_ref):
+    energies = params_ref.shape[2]
     first = lax.axis_index("energy") * energies
     modes = modes_ref[0].astype(f32)
     for e in range(energies):
-        _, di = resolvents(overall, first, e, levels_ref, shift_ref, broad_ref)
+        _, di = resolvents(overall, first, e, levels_ref, params_ref.at[0])
         plain = modes * (modes * di).astype(bf16).astype(f32)
         left = left_ref[e]
         pz = dot_mat(left, full(retarded_ref[e])).astype(bf16).astype(f32)
@@ -243,9 +392,11 @@
         out_ref[0, e : e + 1, :] = -total[0:1] / math.pi
 
 
-def convolve_kernel(groups, reach, offsets_ref, screen_ref, *refs):
+def convolve_kernel(groups, reach, offsets_hbm, screen_ref, *refs):
     lefts, locals_, lessers = refs[:groups], refs[groups : 2 * groups], refs[2 * groups : 3 * groups]
-    out_ref, g_re, g_im = refs[3 * groups :]
+    out_ref, g_re, g_im, offsets_ref, sem = refs[3 * groups :]
+    copy = pltpu.make_async_copy(offsets_hbm, offsets_ref, sem)
+    copy.start()
     energies = lefts[0].shape[0]
     overall = energies * groups
     share, width = out_ref.shape[3:]
@@ -259,14 +410,17 @@
         g_im[overall + reach + e] = blank
     for hop in range(groups):
         base = jnp.bitwise_xor(group, hop) * energies + reach
-        for e in range(energies):
-            left = lefts[hop][e]
-            own = lefts[hop][e, pl.ds(mine, share), :]
-            pl_hat = dot_mat(own, full(lessers[hop][e]))
-            turned = swap_halves(pl_hat) * signs(pl_hat.shape[1], 1.0)
-            chain = dot_last(jnp.concatenate([pl_hat, turned], axis=0).astype(bf16), left)
-            g_re[base + e] = chain[:share] + locals_[hop][e, 0].astype(f32)
-            g_im[base + e] = chain[share:] + locals_[hop][e, 1].astype(f32)
+        for pair in range(energies // 2):
+            states = unpack_lesser(lessers[hop][pair])
+            for e in (2 * pair, 2 * pair + 1):
+                left = lefts[hop][e]
+                own = lefts[hop][e, pl.ds(mine, share), :]
+                pl_hat = dot_mat(own, full(states[e - 2 * pair]))
+                turned = swap_halves(pl_hat) * signs(pl_hat.shape[1], 1.0)
+                chain = dot_last(jnp.concatenate([pl_hat, turned], axis=0).astype(bf16), left)
+                g_re[base + e] = chain[:share] + locals_[hop][e, 0].astype(f32)
+                g_im[base + e] = chain[share:] + locals_[hop][e, 1].astype(f32)
+    copy.wait()
     points = screen_ref.shape[2]
     lanes, height, batch = 128, 16, min(8, overall)
 
@@ -291,6 +445,10 @@
         return 0
 
     lax.fori_loop(0, share // height, rows_of, 0)
+
+
+def in_hbm(x):
+    return pltpu.with_memory_space_constraint(x, pltpu.HBM)
 
 
 def call(kernel, out_shape, in_specs, scratch=(), flops=1_000_000, size=1_000_000):
@@ -332,73 +490,96 @@
     def swapped(x, axis, distance):
         return lax.ppermute(x, axis, [(i, i ^ distance) for i in range(lax.axis_size(axis))])
 
-    def others(x):
-        got = [x]
-        for hop in range(1, groups):
-            got.append(swapped(x, "energy", hop))
-        return got
-
+    assert energies % 2 == 0
+    pairs = energies // 2
+    maps_shape = sds((energies, 3, extent, width), bf16)
+    message = sds((pairs, 4 * extent + spare, width), bf16)
+    state_message = sds((pairs, 2 * extent + spare, width), bf16)
     coupling = jnp.swapaxes(coupling, 1, 2)
-    ahead = lax.ppermute(interface, "cell", [(i + 1, i) for i in range(cells - 1)])
-    params = others(jnp.concatenate([level_shift, broadening, injection], axis=0))
-
-    lefts, locals_ = [], []
-    for hop in range(groups):
-        outs = (sds((energies, orbitals, width), bf16), sds((energies, 2, share, orbitals), bf16))
-        given = (level_shift, broadening, injection)
-        if hop == 0:
-            outs += (sds((energies, orbitals, 2 * orbitals), bf16),)
-        else:
-            given = (params[hop],)
-        left, local, *rest = call(
-            partial(rows_kernel, overall, hop, share),
-            outs,
-            [SMEM] + [VMEM] * (3 + len(given)),
-            [pltpu.VMEM((width, 2 * orbitals), bf16)],
-        )(row_mask, modes, levels, coupling, *given)
-        if hop == 0:
-            free = rest[0]
-        lefts.append(left)
-        locals_.append(local)
-
-    total = call(
+    one = swapped(interface, "cell", 1)
+    near = [(i, i + 1) for i in range(1, cells - 1, 2)]
+    two = lax.ppermute(interface, "cell", near + [(j, i) for i, j in near])
+
+    left_shape = sds((energies, orbitals, width), bf16)
+    local_shape = sds((energies, 2, share, orbitals), bf16)
+    params_shape = (3, energies, orbitals)
+    left, local, free, link2, modes, levels, params = call(
+        partial(own_rows_kernel, overall, share),
+        (
+            left_shape,
+            local_shape,
+            sds((energies, orbitals, 2 * orbitals), bf16),
+            sds((width, 2 * orbitals), bf16),
+            sds(modes.shape, bf16),
+            sds(levels.shape, f32),
+            sds((1,) + params_shape, f32),
+        ),
+        [HBM] * 7,
+        [
+            pltpu.SMEM(row_mask.shape, jnp.int32),
+            pltpu.VMEM(coupling.shape, bf16),
+            pltpu.SemaphoreType.DMA((7,)),
+        ],
+    )(*map(in_hbm, (row_mask, modes, levels, coupling, level_shift, broadening, injection)))
+    lefts, locals_ = [left], [local]
+
+    total, sent = call(
         partial(maps_kernel, overall),
-        sds((energies, 3, extent, width), bf16),
-        [SMEM] + [VMEM] * 7,
-    )(ahead, modes, levels, level_shift, broadening, injection, lefts[0], free)
+        (maps_shape, message),
+        [SMEM] * 2 + [VMEM] * 5,
+    )(one, two, modes, levels, params, left, free)
+
+    known = params
+    while known.shape[0] < groups:
+        count = known.shape[0]
+        got = swapped(known, "energy", count)
+        more = 2 * count < groups
+        for slot in range(count):
+            outs, given = (left_shape, local_shape), (modes, levels, link2, got)
+            if slot == 0 and more:
+                outs, given = outs + (sds((2 * count,) + params_shape, f32),), given + (known,)
+            left, local, *rest = call(
+                partial(rows_kernel, overall, share, count + slot, slot), outs, [VMEM] * len(given)
+            )(*given)
+            lefts.append(left)
+            locals_.append(local)
+            if rest:
+                both = rest[0]
+        if not more:
+            break
+        known = both
 
     enter = None
     for level in range(rounds - 1):
-        other = swapped(total, "cell", 1 << level)
-        parts = 3 if level < rounds - 2 else 2
+        other = swapped(sent, "cell", 1 << level)
+        outs = (maps_shape, message, maps_shape) if level < rounds - 2 else (maps_shape, state_message)
         given = [total, other] + ([enter] if level else [])
-        total, enter = call(
-            partial(join_kernel, level),
-            (sds((energies, parts, extent, width), bf16), sds((energies, 3, extent, width), bf16)),
-            [VMEM] * len(given),
-        )(*given)
-    state = swapped(total, "cell", cells // 2)
+        enter, sent, *rest = call(partial(join_kernel, level), outs, [VMEM] * len(given))(*given)
+        total = rest[0] if rest else None
+    state = swapped(sent, "cell", cells // 2)
     retarded, lesser = call(
         partial(arrive_kernel, rounds - 1),
-        (sds((energies, extent, width), bf16), sds((energies, extent, width), bf16)),
+        (sds((energies, extent, width), bf16), sds((pairs, extent, width), bf16)),
         [VMEM, VMEM],
     )(enter, state)
 
-    lessers = others(lesser)
+    lessers = [lesser]
+    for hop in range(1, groups):
+        lessers.append(swapped(lesser, "energy", hop))
     density = call(
         partial(density_kernel, overall),
         sds((1, energies, orbitals), f32),
-        [VMEM] * 6,
-    )(modes, levels, level_shift, broadening, lefts[0], retarded)
+        [VMEM] * 5,
+    )(modes, levels, params, lefts[0], retarded)
 
     reach = overall // 4
     spread = pltpu.VMEM((overall + 2 * reach, share, orbitals), f32)
     sigma = call(
         partial(convolve_kernel, groups, reach),
         sds((1, 2, overall, share, orbitals), bf16),
-        [SMEM, VMEM] + [VMEM] * (3 * groups),
-        [spread, spread],
-    )(offsets, screened, *lefts, *locals_, *lessers)
+        [HBM, VMEM] + [VMEM] * (3 * groups),
+        [spread, spread, pltpu.SMEM(offsets.shape, jnp.int32), pltpu.SemaphoreType.DMA],
+    )(in_hbm(offsets), screened, *lefts, *locals_, *lessers)
     return (density, sigma)
 
 

time: 45.5 us -> 37.5 us (0.82)
  local copies, waits for them, and re-layouts: 4.39 us -> 0.01 us
  starting transfers between devices: 17.9 us -> 16.2 us
  waiting for transfers between devices: 8.52 us -> 6.94 us
    unnamed x30 -> x2, local copies, waits for them, and re-layouts: 4.38 us -> 0.01 us
    ppermute x9, starting transfers between devices: 16.5 us -> 14.9 us  [swapped(): lax.ppermute(x, axis, [(i, i ^ distance) for i in range(lax.axis_size(axi...]
    ppermute x9, waiting for transfers between devices: 8.51 us -> 6.94 us  [swapped(): lax.ppermute(x, axis, [(i, i ^ distance) for i in range(lax.axis_size(axi...]
  transfers between devices with their start and end apart: 10 -> 10, of which waited for: 4 -> 4; matrix products, arithmetic and copies ran while one was open for 0% -> 0% of each run, Pallas kernels for 16% -> 18%
where the time goes in v3:
time: 37.5 us; the launch traced here: 37.3 us
  starting transfers between devices  16.2 us (43%)
  Pallas kernels  13.5 us (36%)
  waiting for transfers between devices  6.94 us (19%)
  between operations  0.72 us (2%)
    ppermute x9, starting transfers between devices, swapped(): lax.ppermute(x, axis, [(i, i ^ distance) for i in range(lax.axis_size(axi...  14.9 us
    ppermute x9, waiting for transfers between devices, swapped(): lax.ppermute(x, axis, [(i, i ^ distance) for i in range(lax.axis_size(axi...  6.94 us
    pallas_call x1, Pallas kernels, body(): call(partial(convolve_kernel, groups, reach), sds((1, 2, overall, share,...  3.54 us
    pallas_call x3, Pallas kernels, body(): call(partial(rows_kernel, overall, share, count + slot, slot), outs, [VME...  2.48 us
    pallas_call x1, Pallas kernels, body(): call(partial(own_rows_kernel, overall, share), (left_shape, local_shape,...  1.88 us
    pallas_call x1, Pallas kernels, body(): call(partial(maps_kernel, overall), (maps_shape, message), [SMEM] * 2 + [...  1.73 us
    pallas_call x2, Pallas kernels, body(): call(partial(join_kernel, level), outs, [VMEM] * len(given))(*given)  1.62 us
    pallas_call x1, Pallas kernels, body(): call(partial(density_kernel, overall), sds((1, energies, orbitals), f32),...  1.57 us
  transfers between devices with their start and end apart: 10, of which 4 were waited for; matrix products, arithmetic and copies ran while one was open for 0% of the time, Pallas kernels for 18%

profile of v3, /device:TPU:0, one launch (start us, length us, event | category | flops | bytes accessed | tf_op | source)
XLA Modules:
  0.0 37.3 jit_solution(14861619856038711803)
XLA Ops:
  0.6 1.2 %collective-permute-start.1 = (s32[1]{0:T(128)}, s32[1]{0:T(128)}, u32[]{:S(2)}, u32[]{:S(2)}) collective-permute-start(s32[1]{0:T(128)} %param.17), channel_id=1, source_target_pairs={{4,8},{12,16},{20,24},{8,4},{16,12},{24,20},{5,9},{13,17},{21,25},... | collective-permute-start | bytes 20 | tf_op jit(solution)/shard_map/ppermute | solution.py:501
  1.9 3.9 %collective-permute-start = (s32[1]{0:T(128)}, s32[1]{0:T(128)}, u32[]{:S(2)}, u32[]{:S(2)}) collective-permute-start(s32[1]{0:T(128)} %param.17), channel_id=1, source_target_pairs={{0,4},{4,0},{8,12},{12,8},{16,20},{20,16},{24,28},{28,24},{1,5},{5... | collective-permute-start | bytes 20 | tf_op jit(solution)/shard_map/ppermute | solution.py:491
  5.8 1.9 %shard_map.113 = (bf16[2,256,128]{2,1,0:T(8,128)(2,1)S(1)}, bf16[2,2,64,256]{3,2,1,0:T(8,128)(2,1)S(1)}, bf16[2,256,512]{2,1,0:T(8,128)(2,1)S(1)}, bf16[128,512]...) custom-call(s32[1,4]{1,0:T(1,128)} %mask_hbm.1, ...), custom_call_target="tpu_custom_call" | custom-call | flops 1000000 | bytes 1000000 | tf_op jit(solution)/shard_map/pallas_call | solution.py:506
  7.7 1.7 %shard_map.114 = (bf16[2,3,64,128]{3,2,1,0:T(8,128)(2,1)S(1)}, bf16[1,272,128]{2,1,0:T(8,128)(2,1)S(1)}) custom-call(s32[1]{0:T(128)} %collective-permute-done.one_ref, s32[1]{0:T(128)} %collective-permute-done.1.two_ref, bf16[1,256,256]{2,1,0:T(8,128)(2,1)S(1)} %get-tuple-element.25.modes_ref, f32[1,256]{1,0:T(1,128)S(1)} %get-tuple-element.26.levels_ref, ...), custom_call_target="tpu_custom_call" | custom-call | flops 1000000 | bytes 1000000 | tf_op jit(solution)/shard_map/pallas_call | solution.py:526
  9.4 0.1 collective-permute-start.2
  9.5 1.2 %collective-permute-done.2.refs_1_ = bf16[1,272,128]{2,1,0:T(8,128)(2,1)S(1)} collective-permute-done((bf16[1,272,128]{2,1,0:T(8,128)(2,1)S(1)}, bf16[1,272,128]{2,1,0:T(8,128)(2,1)S(1)}, u32[]{:S(2)}, u32[]{:S(2)}) %collective-permute-start.2) | collective-permute-done | bytes 69664 | tf_op jit(solution)/shard_map/ppermute | solution.py:491
  10.8 0.7 %shard_map.115 = (bf16[2,3,64,128]{3,2,1,0:T(8,128)(2,1)S(1)}, bf16[1,272,128]{2,1,0:T(8,128)(2,1)S(1)}, bf16[2,3,64,128]{3,2,1,0:T(8,128)(2,1)S(1)}) custom-call(bf16[2,3,64,128]{3,2,1,0:T(8,128)(2,1)S(1)} %get-tuple-element.30.refs_0_, bf16[1,272,128]{2,1,0:T(8,128)(2,1)S(1)} %collective-permute-done.2.refs_1_), custom_call_target="tpu_custom_call" | custom-call | flops 1000000 | bytes 1000000 | tf_op jit(solution)/shard_map/pallas_call | solution.py:557
  11.5 1.6 %collective-permute-start.3 = (bf16[1,272,128]{2,1,0:T(8,128)(2,1)S(1)}, bf16[1,272,128]{2,1,0:T(8,128)(2,1)S(1)}, u32[]{:S(2)}, u32[]{:S(2)}) collective-permute-start(bf16[1,272,128]{2,1,0:T(8,128)(2,1)S(1)} %get-tuple-element.33), channel_id=1, source_target_pairs={{0,8},{4,12},{8,0},{12,4},{16,24},{20,28},{24,16},{28,20},{1,9},{5... | collective-permute-start | bytes 208904 | tf_op jit(solution)/shard_map/ppermute | solution.py:491
  13.1 2.7 %collective-permute-done.3.refs_1_ = bf16[1,272,128]{2,1,0:T(8,128)(2,1)S(1)} collective-permute-done((bf16[1,272,128]{2,1,0:T(8,128)(2,1)S(1)}, bf16[1,272,128]{2,1,0:T(8,128)(2,1)S(1)}, u32[]{:S(2)}, u32[]{:S(2)}) %collective-permute-start.3) | collective-permute-done | bytes 69664 | tf_op jit(solution)/shard_map/ppermute | solution.py:491
  15.8 0.9 %shard_map.116 = (bf16[2,3,64,128]{3,2,1,0:T(8,128)(2,1)S(1)}, bf16[1,144,128]{2,1,0:T(8,128)(2,1)S(1)}) custom-call(bf16[2,3,64,128]{3,2,1,0:T(8,128)(2,1)S(1)} %get-tuple-element.32.refs_0_, bf16[1,272,128]{2,1,0:T(8,128)(2,1)S(1)} %collective-permute-done.3.refs_1_, bf16[2,3,64,128]{3,2,1,0:T(8,128)(2,1)S(1)} %get-tuple-element.34.refs_2_), custom_call_target="tpu_custom_call" | custom-call | flops 1000000 | bytes 1000000 | tf_op jit(solution)/shard_map/pallas_call | solution.py:557
  16.8 2.7 %collective-permute-start.4 = (bf16[1,144,128]{2,1,0:T(8,128)(2,1)S(1)}, bf16[1,144,128]{2,1,0:T(8,128)(2,1)S(1)}, u32[]{:S(2)}, u32[]{:S(2)}) collective-permute-start(bf16[1,144,128]{2,1,0:T(8,128)(2,1)S(1)} %get-tuple-element.36), channel_id=1, source_target_pairs={{0,16},{4,20},{8,24},{12,28},{16,0},{20,4},{24,8},{28,12},{1,17},{... | collective-permute-start | bytes 110600 | tf_op jit(solution)/shard_map/ppermute | solution.py:491
  19.4 1.5 %collective-permute-start.5 = (f32[1,3,2,256]{3,2,1,0:T(2,128)S(1)}, f32[1,3,2,256]{3,2,1,0:T(2,128)S(1)}, u32[]{:S(2)}, u32[]{:S(2)}) collective-permute-start(f32[1,3,2,256]{3,2,1,0:T(2,128)S(1)} %get-tuple-element.27.params_ref.rest_0_), channel_id=1, source_target_pairs={{0,1},{1,0},{2,3},{3,2},{4,5},{5,4},{6,7},{7,6},{8,9},{9,8},{10,11... | collective-permute-start | bytes 18440 | tf_op jit(solution)/shard_map/ppermute | solution.py:491
  20.9 0.8 %collective-permute-done.4.state_ref = bf16[1,144,128]{2,1,0:T(8,128)(2,1)S(1)} collective-permute-done((bf16[1,144,128]{2,1,0:T(8,128)(2,1)S(1)}, bf16[1,144,128]{2,1,0:T(8,128)(2,1)S(1)}, u32[]{:S(2)}, u32[]{:S(2)}) %collective-permute-start.4) | collective-permute-done | bytes 36896 | tf_op jit(solution)/shard_map/ppermute | solution.py:491
  21.7 0.7 %shard_map.117 = (bf16[2,64,128]{2,1,0:T(8,128)(2,1)S(1)}, bf16[1,64,128]{2,1,0:T(8,128)(2,1)S(1)}) custom-call(bf16[2,3,64,128]{3,2,1,0:T(8,128)(2,1)S(1)} %get-tuple-element.35.enter_ref, bf16[1,144,128]{2,1,0:T(8,128)(2,1)S(1)} %collective-permute-done.4.state_ref), custom_call_target="tpu_custom_call" | custom-call | flops 1000000 | bytes 1000000 | tf_op jit(solution)/shard_map/pallas_call | solution.py:560
  22.4 2.5 %collective-permute-start.9 = (bf16[1,64,128]{2,1,0:T(8,128)(2,1)S(1)}, bf16[1,64,128]{2,1,0:T(8,128)(2,1)S(1)}, u32[]{:S(2)}, u32[]{:S(2)}) collective-permute-start(bf16[1,64,128]{2,1,0:T(8,128)(2,1)S(1)} %get-tuple-element.47.refs_8_), channel_id=1, source_target_pairs={{0,3},{1,2},{2,1},{3,0},{4,7},{5,6},{6,5},{7,4},{8,11},{9,10},{10,... | collective-permute-start | bytes 49160 | tf_op jit(solution)/shard_map/ppermute | solution.py:491
  24.9 0.5 %collective-permute-start.8 = (bf16[1,64,128]{2,1,0:T(8,128)(2,1)S(1)}, bf16[1,64,128]{2,1,0:T(8,128)(2,1)S(1)}, u32[]{:S(2)}, u32[]{:S(2)}) collective-permute-start(bf16[1,64,128]{2,1,0:T(8,128)(2,1)S(1)} %get-tuple-element.47.refs_8_), channel_id=1, source_target_pairs={{0,2},{1,3},{2,0},{3,1},{4,6},{5,7},{6,4},{7,5},{8,10},{9,11},{10,... | collective-permute-start | bytes 49160 | tf_op jit(solution)/shard_map/ppermute | solution.py:491
  25.4 0.5 %collective-permute-start.7 = (bf16[1,64,128]{2,1,0:T(8,128)(2,1)S(1)}, bf16[1,64,128]{2,1,0:T(8,128)(2,1)S(1)}, u32[]{:S(2)}, u32[]{:S(2)}) collective-permute-start(bf16[1,64,128]{2,1,0:T(8,128)(2,1)S(1)} %get-tuple-element.47.refs_8_), channel_id=1, source_target_pairs={{0,1},{1,0},{2,3},{3,2},{4,5},{5,4},{6,7},{7,6},{8,9},{9,8},{10,11... | collective-permute-start | bytes 49160 | tf_op jit(solution)/shard_map/ppermute | solution.py:491
  25.9 0.8 %shard_map.119 = (bf16[2,256,128]{2,1,0:T(8,128)(2,1)S(1)}, bf16[2,2,64,256]{3,2,1,0:T(8,128)(2,1)S(1)}, f32[2,3,2,256]{3,2,1,0:T(2,128)S(1)}) custom-call(bf16[1,256,256]{2,1,0:T(8,128)(2,1)S(1)} %get-tuple-element.25.modes_ref, f32[1,256]{1,0:T(1,128)S(1)} %get-tuple-element.26.levels_ref, bf16[128,512]{1,0:T(8,128)(2,1)S(1)} %get-tuple-element.38.link2_ref, ...), custom_call_target="tpu_custom_call" | custom-call | flops 1000000 | bytes 1000000 | tf_op jit(solution)/shard_map/pallas_call | solution.py:541
  26.8 1.6 %collective-permute-start.6 = (f32[2,3,2,256]{3,2,1,0:T(2,128)S(1)}, f32[2,3,2,256]{3,2,1,0:T(2,128)S(1)}, u32[]{:S(2)}, u32[]{:S(2)}) collective-permute-start(f32[2,3,2,256]{3,2,1,0:T(2,128)S(1)} %get-tuple-element.40), channel_id=1, source_target_pairs={{0,2},{1,3},{2,0},{3,1},{4,6},{5,7},{6,4},{7,5},{8,10},{9,11},{10,... | collective-permute-start | bytes 36872 | tf_op jit(solution)/shard_map/ppermute | solution.py:491
  28.4 2.2 %collective-permute-done.6.got_ref = f32[2,3,2,256]{3,2,1,0:T(2,128)S(1)} collective-permute-done((f32[2,3,2,256]{3,2,1,0:T(2,128)S(1)}, f32[2,3,2,256]{3,2,1,0:T(2,128)S(1)}, u32[]{:S(2)}, u32[]{:S(2)}) %collective-permute-start.6) | collective-permute-done | bytes 12320 | tf_op jit(solution)/shard_map/ppermute | solution.py:491
  30.5 0.8 %shard_map.121 = (bf16[2,256,128]{2,1,0:T(8,128)(2,1)S(1)}, bf16[2,2,64,256]{3,2,1,0:T(8,128)(2,1)S(1)}) custom-call(bf16[1,256,256]{2,1,0:T(8,128)(2,1)S(1)} %get-tuple-element.25.modes_ref, f32[1,256]{1,0:T(1,128)S(1)} %get-tuple-element.26.levels_ref, bf16[128,512]{1,0:T(8,128)(2,1)S(1)} %get-tuple-element.38.link2_ref, ...), custom_call_target="tpu_custom_call" | custom-call | flops 1000000 | bytes 1000000 | tf_op jit(solution)/shard_map/pallas_call | solution.py:541
  31.4 0.8 %shard_map.120 = (bf16[2,256,128]{2,1,0:T(8,128)(2,1)S(1)}, bf16[2,2,64,256]{3,2,1,0:T(8,128)(2,1)S(1)}) custom-call(bf16[1,256,256]{2,1,0:T(8,128)(2,1)S(1)} %get-tuple-element.25.modes_ref, f32[1,256]{1,0:T(1,128)S(1)} %get-tuple-element.26.levels_ref, bf16[128,512]{1,0:T(8,128)(2,1)S(1)} %get-tuple-element.38.link2_ref, ...), custom_call_target="tpu_custom_call" | custom-call | flops 1000000 | bytes 1000000 | tf_op jit(solution)/shard_map/pallas_call | solution.py:541
  32.2 1.6 %shard_map.118 = f32[1,2,256]{2,1,0:T(2,128)} custom-call(bf16[1,256,256]{2,1,0:T(8,128)(2,1)S(1)} %get-tuple-element.25.modes_ref, f32[1,256]{1,0:T(1,128)S(1)} %get-tuple-element.26.levels_ref, f32[1,3,2,256]{3,2,1,0:T(2,128)S(1)} %get-tuple-element.27.params_ref.rest_0_, bf16[2,256,128]{2,1,0:T(8,128)(2,1)S(1)} %get-tuple-element.28.left_ref.refs_0_, ...), custom_call_target="tpu_custom_call" | custom-call | flops 1000000 | bytes 1000000 | tf_op jit(solution)/shard_map/pallas_call | solution.py:569
  33.8 3.5 %shard_map.122 = bf16[1,2,8,64,256]{4,3,2,1,0:T(8,128)(2,1)} custom-call(s32[8]{0:T(128)} %offsets_hbm.1, bf16[1,2,8,64,256]{4,3,2,1,0:T(8,128)(2,1)S(1)} %copy-done, bf16[2,256,128]{2,1,0:T(8,128)(2,1)S(1)} %get-tuple-element.28.left_ref.refs_0_, bf16[2,256,128]{2,1,0:T(8,128)(2,1)S(1)} %get-tuple-element.39.refs_1_, ...), custom_call_target="tpu_custom_call" | custom-call | flops 1000000 | bytes 1000000 | tf_op jit(solution)/shard_map/pallas_call | solution.py:577
  (8 shorter events, 0.0 us)
Async XLA Ops:
  0.6 7.0 %collective-permute-start.1 = (s32[1]{0:T(128)}, s32[1]{0:T(128)}, u32[]{:S(2)}, u32[]{:S(2)}) collective-permute-start(s32[1]{0:T(128)} %param.17), channel_id=1, source_target_pairs={{4,8},{12,16},{20,24},{8,4},{16,12},{24,20},{5,9},{13,17},{21,25},... | collective-permute-start | bytes 20 | tf_op jit(solution)/shard_map/ppermute | solution.py:501
  1.9 5.8 %collective-permute-start = (s32[1]{0:T(128)}, s32[1]{0:T(128)}, u32[]{:S(2)}, u32[]{:S(2)}) collective-permute-start(s32[1]{0:T(128)} %param.17), channel_id=1, source_target_pairs={{0,4},{4,0},{8,12},{12,8},{16,20},{20,16},{24,28},{28,24},{1,5},{5... | collective-permute-start | bytes 20 | tf_op jit(solution)/shard_map/ppermute | solution.py:491
  9.4 1.3 %collective-permute-start.2 = (bf16[1,272,128]{2,1,0:T(8,128)(2,1)S(1)}, bf16[1,272,128]{2,1,0:T(8,128)(2,1)S(1)}, u32[]{:S(2)}, u32[]{:S(2)}) collective-permute-start(bf16[1,272,128]{2,1,0:T(8,128)(2,1)S(1)} %get-tuple-element.31), channel_id=1, source_target_pairs={{0,4},{4,0},{8,12},{12,8},{16,20},{20,16},{24,28},{28,24},{1,5},{5... | collective-permute-start | bytes 208904 | tf_op jit(solution)/shard_map/ppermute | solution.py:491
  11.5 4.4 %collective-permute-start.3 = (bf16[1,272,128]{2,1,0:T(8,128)(2,1)S(1)}, bf16[1,272,128]{2,1,0:T(8,128)(2,1)S(1)}, u32[]{:S(2)}, u32[]{:S(2)}) collective-permute-start(bf16[1,272,128]{2,1,0:T(8,128)(2,1)S(1)} %get-tuple-element.33), channel_id=1, source_target_pairs={{0,8},{4,12},{8,0},{12,4},{16,24},{20,28},{24,16},{28,20},{1,9},{5... | collective-permute-start | bytes 208904 | tf_op jit(solution)/shard_map/ppermute | solution.py:491
  16.8 4.9 %collective-permute-start.4 = (bf16[1,144,128]{2,1,0:T(8,128)(2,1)S(1)}, bf16[1,144,128]{2,1,0:T(8,128)(2,1)S(1)}, u32[]{:S(2)}, u32[]{:S(2)}) collective-permute-start(bf16[1,144,128]{2,1,0:T(8,128)(2,1)S(1)} %get-tuple-element.36), channel_id=1, source_target_pairs={{0,16},{4,20},{8,24},{12,28},{16,0},{20,4},{24,8},{28,12},{1,17},{... | collective-permute-start | bytes 110600 | tf_op jit(solution)/shard_map/ppermute | solution.py:491
  19.4 6.5 %collective-permute-start.5 = (f32[1,3,2,256]{3,2,1,0:T(2,128)S(1)}, f32[1,3,2,256]{3,2,1,0:T(2,128)S(1)}, u32[]{:S(2)}, u32[]{:S(2)}) collective-permute-start(f32[1,3,2,256]{3,2,1,0:T(2,128)S(1)} %get-tuple-element.27.params_ref.rest_0_), channel_id=1, source_target_pairs={{0,1},{1,0},{2,3},{3,2},{4,5},{5,4},{6,7},{7,6},{8,9},{9,8},{10,11... | collective-permute-start | bytes 18440 | tf_op jit(solution)/shard_map/ppermute | solution.py:491
  22.4 11.4 %collective-permute-start.9 = (bf16[1,64,128]{2,1,0:T(8,128)(2,1)S(1)}, bf16[1,64,128]{2,1,0:T(8,128)(2,1)S(1)}, u32[]{:S(2)}, u32[]{:S(2)}) collective-permute-start(bf16[1,64,128]{2,1,0:T(8,128)(2,1)S(1)} %get-tuple-element.47.refs_8_), channel_id=1, source_target_pairs={{0,3},{1,2},{2,1},{3,0},{4,7},{5,6},{6,5},{7,4},{8,11},{9,10},{10,... | collective-permute-start | bytes 49160 | tf_op jit(solution)/shard_map/ppermute | solution.py:491
  24.9 8.9 %collective-permute-start.8 = (bf16[1,64,128]{2,1,0:T(8,128)(2,1)S(1)}, bf16[1,64,128]{2,1,0:T(8,128)(2,1)S(1)}, u32[]{:S(2)}, u32[]{:S(2)}) collective-permute-start(bf16[1,64,128]{2,1,0:T(8,128)(2,1)S(1)} %get-tuple-element.47.refs_8_), channel_id=1, source_target_pairs={{0,2},{1,3},{2,0},{3,1},{4,6},{5,7},{6,4},{7,5},{8,10},{9,11},{10,... | collective-permute-start | bytes 49160 | tf_op jit(solution)/shard_map/ppermute | solution.py:491
  25.4 8.4 %collective-permute-start.7 = (bf16[1,64,128]{2,1,0:T(8,128)(2,1)S(1)}, bf16[1,64,128]{2,1,0:T(8,128)(2,1)S(1)}, u32[]{:S(2)}, u32[]{:S(2)}) collective-permute-start(bf16[1,64,128]{2,1,0:T(8,128)(2,1)S(1)} %get-tuple-element.47.refs_8_), channel_id=1, source_target_pairs={{0,1},{1,0},{2,3},{3,2},{4,5},{5,4},{6,7},{7,6},{8,9},{9,8},{10,11... | collective-permute-start | bytes 49160 | tf_op jit(solution)/shard_map/ppermute | solution.py:491
  25.9 7.8 %copy-start = (bf16[1,2,8,64,256]{4,3,2,1,0:T(8,128)(2,1)S(1)}, bf16[1,2,8,64,256]{4,3,2,1,0:T(8,128)(2,1)}, u32[]{:S(2)}) copy-start(bf16[1,2,8,64,256]{4,3,2,1,0:T(8,128)(2,1)} %screen_ref.1) | copy-start | bytes 1572868
  26.8 3.8 %collective-permute-start.6 = (f32[2,3,2,256]{3,2,1,0:T(2,128)S(1)}, f32[2,3,2,256]{3,2,1,0:T(2,128)S(1)}, u32[]{:S(2)}, u32[]{:S(2)}) collective-permute-start(f32[2,3,2,256]{3,2,1,0:T(2,128)S(1)} %get-tuple-element.40), channel_id=1, source_target_pairs={{0,2},{1,3},{2,0},{3,1},{4,6},{5,7},{6,4},{7,5},{8,10},{9,11},{10,... | collective-permute-start | bytes 36872 | tf_op jit(solution)/shard_map/ppermute | solution.py:491

commit v4 on v3

--- a/solution.py
+++ b/solution.py
@@ -92,7 +92,8 @@
     extent = out_ref.shape[2]
     first = lax.axis_index("energy") * energies
     odd = jnp.bitwise_and(lax.axis_index("cell"), 1) == 1
-    chosen = pl.multiple_of(jnp.where(odd, two_ref[0], one_ref[0]) * extent, extent)
+    block = jnp.max(jnp.where(odd, two_ref[...], one_ref[...])).astype(jnp.int32)
+    chosen = pl.multiple_of(block * extent, extent)
     rows = modes_ref[0, pl.ds(chosen, extent), :]
     width = rows.shape[1]
     rows_f = rows.astype(f32)
@@ -148,9 +149,8 @@
         local_ref[e, 1] = local[share:].astype(bf16)
 
 
-def own_rows_kernel(
-    overall,
-    share,
+def front_kernel(
+    interface_ref,
     mask_hbm,
     modes_hbm,
     levels_hbm,
@@ -158,9 +158,7 @@
     shift_hbm,
     broad_hbm,
     inject_hbm,
-    left_ref,
-    local_ref,
-    free_ref,
+    block_ref,
     link2_ref,
     modes_ref,
     levels_ref,
@@ -169,7 +167,6 @@
     coupling_ref,
     sems,
 ):
-    energies = shift_hbm.shape[1]
     copies = [
         pltpu.make_async_copy(source, target, sems.at[index])
         for index, (source, target) in enumerate(
@@ -188,9 +185,13 @@
         copy.start()
     for copy in copies:
         copy.wait()
+    block_ref[...] = jnp.full(block_ref.shape, interface_ref[0].astype(f32))
     masked_link(link2_ref, coupling_ref, mask_ref)
+
+
+def own_rows_kernel(overall, share, modes_ref, levels_ref, link2_ref, params_ref, left_ref, local_ref, free_ref):
     make_rows(
-        energies,
+        params_ref.shape[2],
         0,
         overall,
         share,
@@ -375,26 +376,30 @@
         lesser_ref[pair] = pack_lesser(lessers[2 * pair], lessers[2 * pair + 1]).astype(bf16)
 
 
-def density_kernel(overall, modes_ref, levels_ref, params_ref, left_ref, retarded_ref, out_ref):
+def row_sums(x):
+    return dot_last(jnp.ones((8, x.shape[1]), bf16), x.astype(bf16))[0:1]
+
+
+def diagonal_kernel(overall, modes_ref, levels_ref, params_ref, out_ref):
     energies = params_ref.shape[2]
     first = lax.axis_index("energy") * energies
     modes = modes_ref[0].astype(f32)
     for e in range(energies):
         _, di = resolvents(overall, first, e, levels_ref, params_ref.at[0])
-        plain = modes * (modes * di).astype(bf16).astype(f32)
+        out_ref[0, e : e + 1, :] = row_sums(modes * (modes * di).astype(bf16).astype(f32))
+
+
+def density_kernel(diagonal_ref, left_ref, retarded_ref, out_ref):
+    for e in range(left_ref.shape[0]):
         left = left_ref[e]
         pz = dot_mat(left, full(retarded_ref[e])).astype(bf16).astype(f32)
-        turned = pz * swap_halves(left.astype(f32))
-        highest = lax.Precision.HIGHEST
-        total = dot_last(jnp.ones((8, plain.shape[1]), f32), plain, highest) + dot_last(
-            jnp.ones((8, turned.shape[1]), f32), turned, highest
-        )
-        out_ref[0, e : e + 1, :] = -total[0:1] / math.pi
+        total = diagonal_ref[0, e : e + 1, :] + row_sums(pz * swap_halves(left.astype(f32)))
+        out_ref[0, e : e + 1, :] = -total / math.pi
 
 
 def convolve_kernel(groups, reach, offsets_hbm, screen_ref, *refs):
     lefts, locals_, lessers = refs[:groups], refs[groups : 2 * groups], refs[2 * groups : 3 * groups]
-    out_ref, g_re, g_im, offsets_ref, sem = refs[3 * groups :]
+    out_hbm, g_re, g_im, g_sum, out_ref, offsets_ref, sem, out_sems = refs[3 * groups :]
     copy = pltpu.make_async_copy(offsets_hbm, offsets_ref, sem)
     copy.start()
     energies = lefts[0].shape[0]
@@ -404,10 +409,9 @@
     mine = pl.multiple_of(group * share, share)
     blank = jnp.zeros((share, width), f32)
     for e in range(reach):
-        g_re[e] = blank
-        g_im[e] = blank
-        g_re[overall + reach + e] = blank
-        g_im[overall + reach + e] = blank
+        for g in (g_re, g_im, g_sum):
+            g[e] = blank
+            g[overall + reach + e] = blank
     for hop in range(groups):
         base = jnp.bitwise_xor(group, hop) * energies + reach
         for pair in range(energies // 2):
@@ -418,11 +422,20 @@
                 pl_hat = dot_mat(own, full(states[e - 2 * pair]))
                 turned = swap_halves(pl_hat) * signs(pl_hat.shape[1], 1.0)
                 chain = dot_last(jnp.concatenate([pl_hat, turned], axis=0).astype(bf16), left)
-                g_re[base + e] = chain[:share] + locals_[hop][e, 0].astype(f32)
-                g_im[base + e] = chain[share:] + locals_[hop][e, 1].astype(f32)
+                re = chain[:share] + locals_[hop][e, 0].astype(f32)
+                im = chain[share:] + locals_[hop][e, 1].astype(f32)
+                g_re[base + e] = re
+                g_im[base + e] = im
+                g_sum[base + e] = re + im
     copy.wait()
     points = screen_ref.shape[2]
     lanes, height, batch = 128, 16, min(8, overall)
+
+    def out_copy(step):
+        rows = pl.ds(pl.multiple_of(step * height, height), height)
+        return pltpu.make_async_copy(
+            out_ref.at[:, :, :, rows, :], out_hbm.at[:, :, :, rows, :], out_sems.at[step]
+        )
 
     def rows_of(step, _):
         top = pl.multiple_of(step * height, height)
@@ -433,26 +446,33 @@
                     start = e0 + reach - offsets_ref[k]
                     w_re = screen_ref[0, 0, k, pl.ds(top, height), lane : lane + lanes].astype(f32)
                     w_im = screen_ref[0, 1, k, pl.ds(top, height), lane : lane + lanes].astype(f32)
+                    w_sum, w_change = w_re + w_im, w_im - w_re
                     for e in range(batch):
-                        x_re = g_re[start + e, pl.ds(top, height), lane : lane + lanes]
-                        x_im = g_im[start + e, pl.ds(top, height), lane : lane + lanes]
-                        re = w_re * x_im + w_im * x_re
-                        im = w_re * x_re - w_im * x_im
-                        sums[e] = (re, im) if k == 0 else (sums[e][0] + re, sums[e][1] + im)
+                        new = tuple(
+                            w * g[start + e, pl.ds(top, height), lane : lane + lanes]
+                            for w, g in ((w_re, g_sum), (w_sum, g_im), (w_change, g_re))
+                        )
+                        sums[e] = new if k == 0 else tuple(a + b for a, b in zip(sums[e], new))
                 for e in range(batch):
-                    out_ref[0, 0, e0 + e, pl.ds(top, height), lane : lane + lanes] = (-sums[e][0]).astype(bf16)
-                    out_ref[0, 1, e0 + e, pl.ds(top, height), lane : lane + lanes] = sums[e][1].astype(bf16)
+                    common, first, second = sums[e]
+                    where = (e0 + e, pl.ds(top, height), slice(lane, lane + lanes))
+                    out_ref[(0, 0) + where] = (-(common + second)).astype(bf16)
+                    out_ref[(0, 1) + where] = (common - first).astype(bf16)
+        out_copy(step).start()
         return 0
 
-    lax.fori_loop(0, share // height, rows_of, 0)
+    steps = share // height
+    lax.fori_loop(0, steps, rows_of, 0)
+    for step in range(steps):
+        out_copy(step).wait()
 
 
 def in_hbm(x):
     return pltpu.with_memory_space_constraint(x, pltpu.HBM)
 
 
-def call(kernel, out_shape, in_specs, scratch=(), flops=1_000_000, size=1_000_000):
-    outs = jax.tree.map(lambda _: VMEM, out_shape)
+def call(kernel, out_shape, in_specs, scratch=(), flops=1_000_000, size=1_000_000, out_specs=None):
+    outs = out_specs or jax.tree.map(lambda _: VMEM, out_shape)
     return pl.pallas_call(
         kernel,
         out_shape=out_shape,
@@ -496,38 +516,44 @@
     message = sds((pairs, 4 * extent + spare, width), bf16)
     state_message = sds((pairs, 2 * extent + spare, width), bf16)
     coupling = jnp.swapaxes(coupling, 1, 2)
-    one = swapped(interface, "cell", 1)
-    near = [(i, i + 1) for i in range(1, cells - 1, 2)]
-    two = lax.ppermute(interface, "cell", near + [(j, i) for i, j in near])
-
-    left_shape = sds((energies, orbitals, width), bf16)
-    local_shape = sds((energies, 2, share, orbitals), bf16)
-    params_shape = (3, energies, orbitals)
-    left, local, free, link2, modes, levels, params = call(
-        partial(own_rows_kernel, overall, share),
+    block, link2, modes, levels, params = call(
+        front_kernel,
         (
-            left_shape,
-            local_shape,
-            sds((energies, orbitals, 2 * orbitals), bf16),
+            sds((8, width), f32),
             sds((width, 2 * orbitals), bf16),
             sds(modes.shape, bf16),
             sds(levels.shape, f32),
-            sds((1,) + params_shape, f32),
+            sds((1, 3, energies, orbitals), f32),
         ),
-        [HBM] * 7,
+        [SMEM] + [HBM] * 7,
         [
             pltpu.SMEM(row_mask.shape, jnp.int32),
             pltpu.VMEM(coupling.shape, bf16),
             pltpu.SemaphoreType.DMA((7,)),
         ],
-    )(*map(in_hbm, (row_mask, modes, levels, coupling, level_shift, broadening, injection)))
+    )(interface, *map(in_hbm, (row_mask, modes, levels, coupling, level_shift, broadening, injection)))
+    one = swapped(block, "cell", 1)
+    near = [(i, i + 1) for i in range(1, cells - 1, 2)]
+    two = lax.ppermute(block, "cell", near + [(j, i) for i, j in near])
+
+    left_shape = sds((energies, orbitals, width), bf16)
+    local_shape = sds((energies, 2, share, orbitals), bf16)
+    params_shape = (3, energies, orbitals)
+    left, local, free = call(
+        partial(own_rows_kernel, overall, share),
+        (left_shape, local_shape, sds((energies, orbitals, 2 * orbitals), bf16)),
+        [VMEM] * 4,
+    )(modes, levels, link2, params)
     lefts, locals_ = [left], [local]
 
     total, sent = call(
         partial(maps_kernel, overall),
         (maps_shape, message),
-        [SMEM] * 2 + [VMEM] * 5,
+        [VMEM] * 7,
     )(one, two, modes, levels, params, left, free)
+    diagonal = call(
+        partial(diagonal_kernel, overall), sds((1, energies, orbitals), f32), [VMEM] * 3
+    )(modes, levels, params)
 
     known = params
     while known.shape[0] < groups:
@@ -566,19 +592,27 @@
     lessers = [lesser]
     for hop in range(1, groups):
         lessers.append(swapped(lesser, "energy", hop))
-    density = call(
-        partial(density_kernel, overall),
-        sds((1, energies, orbitals), f32),
-        [VMEM] * 5,
-    )(modes, levels, params, lefts[0], retarded)
+    density = call(density_kernel, sds((1, energies, orbitals), f32), [VMEM] * 3)(
+        diagonal, lefts[0], retarded
+    )
 
     reach = overall // 4
     spread = pltpu.VMEM((overall + 2 * reach, share, orbitals), f32)
+    out_shape = (1, 2, overall, share, orbitals)
     sigma = call(
         partial(convolve_kernel, groups, reach),
-        sds((1, 2, overall, share, orbitals), bf16),
+        sds(out_shape, bf16),
         [HBM, VMEM] + [VMEM] * (3 * groups),
-        [spread, spread, pltpu.SMEM(offsets.shape, jnp.int32), pltpu.SemaphoreType.DMA],
+        [
+            spread,
+            spread,
+            spread,
+            pltpu.VMEM(out_shape, bf16),
+            pltpu.SMEM(offsets.shape, jnp.int32),
+            pltpu.SemaphoreType.DMA,
+            pltpu.SemaphoreType.DMA((share // 16,)),
+        ],
+        out_specs=HBM,
     )(in_hbm(offsets), screened, *lefts, *locals_, *lessers)
     return (density, sigma)
 

time: 37.5 us -> 37 us (0.987)
  Pallas kernels: 13.5 us -> 11.9 us
  starting transfers between devices: 16.2 us -> 17.3 us
  waiting for transfers between devices: 6.94 us -> 6.23 us
  between operations: 0.72 us -> 1.39 us
    ppermute x9, starting transfers between devices: 14.9 us -> 16.7 us  [swapped(): lax.ppermute(x, axis, [(i, i ^ distance) for i in range(lax.axis_size(axi...]
    pallas_call x1, Pallas kernels: 1.88 us -> 0.83 us  [body(): call(partial(own_rows_kernel, overall, share), (left_shape, local_shape,...]
    ppermute x9, waiting for transfers between devices: 6.94 us -> 6.23 us  [swapped(): lax.ppermute(x, axis, [(i, i ^ distance) for i in range(lax.axis_size(axi...]
    ppermute x1, starting transfers between devices: 1.25 us -> 0.65 us  [body(): two = lax.ppermute(block, 'cell', near + [(j, i) for i, j in near])]
    pallas_call x3 -> x5, Pallas kernels: 6.84 us -> 6.27 us  [the longest x1 3.54 us: body(): call(partial(convolve_kernel, groups, reach), sds(out_shape, bf16), [HBM,...]
  transfers between devices with their start and end apart: 10 -> 10, of which waited for: 4 -> 4; matrix products, arithmetic and copies ran while one was open for 0% -> 0% of each run, Pallas kernels for 18% -> 14%
where the time goes in v4:
time: 37 us; the launch traced here: 36.8 us
  starting transfers between devices  17.3 us (47%)
  Pallas kernels  11.9 us (32%)
  waiting for transfers between devices  6.23 us (17%)
  between operations  1.39 us (4%)
    ppermute x9, starting transfers between devices, swapped(): lax.ppermute(x, axis, [(i, i ^ distance) for i in range(lax.axis_size(axi...  16.7 us
    ppermute x9, waiting for transfers between devices, swapped(): lax.ppermute(x, axis, [(i, i ^ distance) for i in range(lax.axis_size(axi...  6.23 us
    pallas_call x1, Pallas kernels, body(): call(partial(convolve_kernel, groups, reach), sds(out_shape, bf16), [HBM,...  3.54 us
    pallas_call x3, Pallas kernels, body(): call(partial(rows_kernel, overall, share, count + slot, slot), outs, [VME...  2.48 us
    pallas_call x2, Pallas kernels, body(): call(partial(join_kernel, level), outs, [VMEM] * len(given))(*given)  1.62 us
    pallas_call x1, Pallas kernels, body(): call(front_kernel, (sds((8, width), f32), sds((width, 2 * orbitals), bf16...  1.07 us
    pallas_call x1, Pallas kernels, body(): call(density_kernel, sds((1, energies, orbitals), f32), [VMEM] * 3)  0.99 us
    pallas_call x1, Pallas kernels, body(): call(partial(own_rows_kernel, overall, share), (left_shape, local_shape,...  0.83 us
  transfers between devices with their start and end apart: 10, of which 4 were waited for; matrix products, arithmetic and copies ran while one was open for 0% of the time, Pallas kernels for 14%

profile of v4, /device:TPU:0, one launch (start us, length us, event | category | flops | bytes accessed | tf_op | source)
XLA Modules:
  0.0 36.8 jit_solution(2444087979335853552)
XLA Ops:
  1.3 1.1 %shard_map.113 = (f32[8,128]{1,0:T(8,128)S(1)}, bf16[128,512]{1,0:T(8,128)(2,1)S(1)}, bf16[1,256,256]{2,1,0:T(8,128)(2,1)S(1)}, f32[1,256]{1,0:T(1,128)S(1)}, f32[1,3,2,256]{3,2,1,0:T(2,128)S(1)}) custom-call(s32[1]{0:T(128)S(6)} %copy.12.interface_ref, s32[1,4]{1,0:T(1,128)} %mask_hbm.1, bf16[1,256,256]{2,1,0:T(8,128)(2,1)} %modes_hbm.1, ...), custom_call_target="tpu_custom_call" | custom-call | flops 1000000 | bytes 1000000 | tf_op jit(solution)/shard_map/pallas_call | solution.py:519
  2.4 0.6 %collective-permute-start = (f32[8,128]{1,0:T(8,128)S(1)}, f32[8,128]{1,0:T(8,128)S(1)}, u32[]{:S(2)}, u32[]{:S(2)}) collective-permute-start(f32[8,128]{1,0:T(8,128)S(1)} %get-tuple-element.31), channel_id=1, source_target_pairs={{0,4},{4,0},{8,12},{12,8},{16,20},{20,16},{24,28},{28,24},{1,5},{5... | collective-permute-start | bytes 12296 | tf_op jit(solution)/shard_map/ppermute | solution.py:511
  2.9 0.6 %collective-permute-start.1 = (f32[8,128]{1,0:T(8,128)S(1)}, f32[8,128]{1,0:T(8,128)S(1)}, u32[]{:S(2)}, u32[]{:S(2)}) collective-permute-start(f32[8,128]{1,0:T(8,128)S(1)} %get-tuple-element.31), channel_id=1, source_target_pairs={{4,8},{12,16},{20,24},{8,4},{16,12},{24,20},{5,9},{13,17},{21,25},... | collective-permute-start | bytes 12296 | tf_op jit(solution)/shard_map/ppermute | solution.py:537
  3.6 0.8 %shard_map.115 = (bf16[2,256,128]{2,1,0:T(8,128)(2,1)S(1)}, bf16[2,2,64,256]{3,2,1,0:T(8,128)(2,1)S(1)}, bf16[2,256,512]{2,1,0:T(8,128)(2,1)S(1)}) custom-call(bf16[1,256,256]{2,1,0:T(8,128)(2,1)S(1)} %get-tuple-element.26.modes_ref, f32[1,256]{1,0:T(1,128)S(1)} %get-tuple-element.27.levels_ref, bf16[128,512]{1,0:T(8,128)(2,1)S(1)} %get-tuple-element.29.link2_ref, ...), custom_call_target="tpu_custom_call" | custom-call | flops 1000000 | bytes 1000000 | tf_op jit(solution)/shard_map/pallas_call | solution.py:542
  4.4 0.5 %shard_map.116 = (bf16[2,3,64,128]{3,2,1,0:T(8,128)(2,1)S(1)}, bf16[1,272,128]{2,1,0:T(8,128)(2,1)S(1)}) custom-call(f32[8,128]{1,0:T(8,128)S(1)} %collective-permute-done.one_ref, f32[8,128]{1,0:T(8,128)S(1)} %collective-permute-done.1.two_ref, bf16[1,256,256]{2,1,0:T(8,128)(2,1)S(1)} %get-tuple-element.26.modes_ref, ...), custom_call_target="tpu_custom_call" | custom-call | flops 1000000 | bytes 1000000 | tf_op jit(solution)/shard_map/pallas_call | solution.py:549
  4.9 4.4 %collective-permute-start.2 = (bf16[1,272,128]{2,1,0:T(8,128)(2,1)S(1)}, bf16[1,272,128]{2,1,0:T(8,128)(2,1)S(1)}, u32[]{:S(2)}, u32[]{:S(2)}) collective-permute-start(bf16[1,272,128]{2,1,0:T(8,128)(2,1)S(1)} %get-tuple-element.34), channel_id=1, source_target_pairs={{0,4},{4,0},{8,12},{12,8},{16,20},{20,16},{24,28},{28,24},{1,5},{5... | collective-permute-start | bytes 208904 | tf_op jit(solution)/shard_map/ppermute | solution.py:511
  9.3 0.9 %collective-permute-done.2.refs_1_ = bf16[1,272,128]{2,1,0:T(8,128)(2,1)S(1)} collective-permute-done((bf16[1,272,128]{2,1,0:T(8,128)(2,1)S(1)}, bf16[1,272,128]{2,1,0:T(8,128)(2,1)S(1)}, u32[]{:S(2)}, u32[]{:S(2)}) %collective-permute-start.2) | collective-permute-done | bytes 69664 | tf_op jit(solution)/shard_map/ppermute | solution.py:511
  10.2 0.7 %shard_map.117 = (bf16[2,3,64,128]{3,2,1,0:T(8,128)(2,1)S(1)}, bf16[1,272,128]{2,1,0:T(8,128)(2,1)S(1)}, bf16[2,3,64,128]{3,2,1,0:T(8,128)(2,1)S(1)}) custom-call(bf16[2,3,64,128]{3,2,1,0:T(8,128)(2,1)S(1)} %get-tuple-element.33.refs_0_, bf16[1,272,128]{2,1,0:T(8,128)(2,1)S(1)} %collective-permute-done.2.refs_1_), custom_call_target="tpu_custom_call" | custom-call | flops 1000000 | bytes 1000000 | tf_op jit(solution)/shard_map/pallas_call | solution.py:583
  10.9 2.2 %collective-permute-start.3 = (bf16[1,272,128]{2,1,0:T(8,128)(2,1)S(1)}, bf16[1,272,128]{2,1,0:T(8,128)(2,1)S(1)}, u32[]{:S(2)}, u32[]{:S(2)}) collective-permute-start(bf16[1,272,128]{2,1,0:T(8,128)(2,1)S(1)} %get-tuple-element.36), channel_id=1, source_target_pairs={{0,8},{4,12},{8,0},{12,4},{16,24},{20,28},{24,16},{28,20},{1,9},{5... | collective-permute-start | bytes 208904 | tf_op jit(solution)/shard_map/ppermute | solution.py:511
  13.1 2.7 %collective-permute-done.3.refs_1_ = bf16[1,272,128]{2,1,0:T(8,128)(2,1)S(1)} collective-permute-done((bf16[1,272,128]{2,1,0:T(8,128)(2,1)S(1)}, bf16[1,272,128]{2,1,0:T(8,128)(2,1)S(1)}, u32[]{:S(2)}, u32[]{:S(2)}) %collective-permute-start.3) | collective-permute-done | bytes 69664 | tf_op jit(solution)/shard_map/ppermute | solution.py:511
  15.8 0.9 %shard_map.118 = (bf16[2,3,64,128]{3,2,1,0:T(8,128)(2,1)S(1)}, bf16[1,144,128]{2,1,0:T(8,128)(2,1)S(1)}) custom-call(bf16[2,3,64,128]{3,2,1,0:T(8,128)(2,1)S(1)} %get-tuple-element.35.refs_0_, bf16[1,272,128]{2,1,0:T(8,128)(2,1)S(1)} %collective-permute-done.3.refs_1_, bf16[2,3,64,128]{3,2,1,0:T(8,128)(2,1)S(1)} %get-tuple-element.37.refs_2_), custom_call_target="tpu_custom_call" | custom-call | flops 1000000 | bytes 1000000 | tf_op jit(solution)/shard_map/pallas_call | solution.py:583
  16.7 2.8 %collective-permute-start.4 = (bf16[1,144,128]{2,1,0:T(8,128)(2,1)S(1)}, bf16[1,144,128]{2,1,0:T(8,128)(2,1)S(1)}, u32[]{:S(2)}, u32[]{:S(2)}) collective-permute-start(bf16[1,144,128]{2,1,0:T(8,128)(2,1)S(1)} %get-tuple-element.39), channel_id=1, source_target_pairs={{0,16},{4,20},{8,24},{12,28},{16,0},{20,4},{24,8},{28,12},{1,17},{... | collective-permute-start | bytes 110600 | tf_op jit(solution)/shard_map/ppermute | solution.py:511
  19.5 1.5 %collective-permute-start.5 = (f32[1,3,2,256]{3,2,1,0:T(2,128)S(1)}, f32[1,3,2,256]{3,2,1,0:T(2,128)S(1)}, u32[]{:S(2)}, u32[]{:S(2)}) collective-permute-start(f32[1,3,2,256]{3,2,1,0:T(2,128)S(1)} %get-tuple-element.28.params_ref.rest_0_), channel_id=1, source_target_pairs={{0,1},{1,0},{2,3},{3,2},{4,5},{5,4},{6,7},{7,6},{8,9},{9,8},{10,11... | collective-permute-start | bytes 18440 | tf_op jit(solution)/shard_map/ppermute | solution.py:511
  21.0 0.7 %collective-permute-done.4.state_ref = bf16[1,144,128]{2,1,0:T(8,128)(2,1)S(1)} collective-permute-done((bf16[1,144,128]{2,1,0:T(8,128)(2,1)S(1)}, bf16[1,144,128]{2,1,0:T(8,128)(2,1)S(1)}, u32[]{:S(2)}, u32[]{:S(2)}) %collective-permute-start.4) | collective-permute-done | bytes 36896 | tf_op jit(solution)/shard_map/ppermute | solution.py:511
  21.8 0.7 %shard_map.119 = (bf16[2,64,128]{2,1,0:T(8,128)(2,1)S(1)}, bf16[1,64,128]{2,1,0:T(8,128)(2,1)S(1)}) custom-call(bf16[2,3,64,128]{3,2,1,0:T(8,128)(2,1)S(1)} %get-tuple-element.38.enter_ref, bf16[1,144,128]{2,1,0:T(8,128)(2,1)S(1)} %collective-permute-done.4.state_ref), custom_call_target="tpu_custom_call" | custom-call | flops 1000000 | bytes 1000000 | tf_op jit(solution)/shard_map/pallas_call | solution.py:586
  22.5 1.6 %collective-permute-start.7 = (bf16[1,64,128]{2,1,0:T(8,128)(2,1)S(1)}, bf16[1,64,128]{2,1,0:T(8,128)(2,1)S(1)}, u32[]{:S(2)}, u32[]{:S(2)}) collective-permute-start(bf16[1,64,128]{2,1,0:T(8,128)(2,1)S(1)} %get-tuple-element.49.refs_8_), channel_id=1, source_target_pairs={{0,1},{1,0},{2,3},{3,2},{4,5},{5,4},{6,7},{7,6},{8,9},{9,8},{10,11... | collective-permute-start | bytes 49160 | tf_op jit(solution)/shard_map/ppermute | solution.py:511
  24.1 1.5 %collective-permute-start.8 = (bf16[1,64,128]{2,1,0:T(8,128)(2,1)S(1)}, bf16[1,64,128]{2,1,0:T(8,128)(2,1)S(1)}, u32[]{:S(2)}, u32[]{:S(2)}) collective-permute-start(bf16[1,64,128]{2,1,0:T(8,128)(2,1)S(1)} %get-tuple-element.49.refs_8_), channel_id=1, source_target_pairs={{0,2},{1,3},{2,0},{3,1},{4,6},{5,7},{6,4},{7,5},{8,10},{9,11},{10,... | collective-permute-start | bytes 49160 | tf_op jit(solution)/shard_map/ppermute | solution.py:511
  26.0 0.8 %shard_map.121 = (bf16[2,256,128]{2,1,0:T(8,128)(2,1)S(1)}, bf16[2,2,64,256]{3,2,1,0:T(8,128)(2,1)S(1)}, f32[2,3,2,256]{3,2,1,0:T(2,128)S(1)}) custom-call(bf16[1,256,256]{2,1,0:T(8,128)(2,1)S(1)} %get-tuple-element.26.modes_ref, f32[1,256]{1,0:T(1,128)S(1)} %get-tuple-element.27.levels_ref, bf16[128,512]{1,0:T(8,128)(2,1)S(1)} %get-tuple-element.29.link2_ref, ...), custom_call_target="tpu_custom_call" | custom-call | flops 1000000 | bytes 1000000 | tf_op jit(solution)/shard_map/pallas_call | solution.py:567
  26.8 1.7 %collective-permute-start.6 = (f32[2,3,2,256]{3,2,1,0:T(2,128)S(1)}, f32[2,3,2,256]{3,2,1,0:T(2,128)S(1)}, u32[]{:S(2)}, u32[]{:S(2)}) collective-permute-start(f32[2,3,2,256]{3,2,1,0:T(2,128)S(1)} %get-tuple-element.42), channel_id=1, source_target_pairs={{0,2},{1,3},{2,0},{3,1},{4,6},{5,7},{6,4},{7,5},{8,10},{9,11},{10,... | collective-permute-start | bytes 36872 | tf_op jit(solution)/shard_map/ppermute | solution.py:511
  28.7 1.9 %collective-permute-done.6.got_ref = f32[2,3,2,256]{3,2,1,0:T(2,128)S(1)} collective-permute-done((f32[2,3,2,256]{3,2,1,0:T(2,128)S(1)}, f32[2,3,2,256]{3,2,1,0:T(2,128)S(1)}, u32[]{:S(2)}, u32[]{:S(2)}) %collective-permute-start.6) | collective-permute-done | bytes 12320 | tf_op jit(solution)/shard_map/ppermute | solution.py:511
  30.6 0.8 %shard_map.122 = (bf16[2,256,128]{2,1,0:T(8,128)(2,1)S(1)}, bf16[2,2,64,256]{3,2,1,0:T(8,128)(2,1)S(1)}) custom-call(bf16[1,256,256]{2,1,0:T(8,128)(2,1)S(1)} %get-tuple-element.26.modes_ref, f32[1,256]{1,0:T(1,128)S(1)} %get-tuple-element.27.levels_ref, bf16[128,512]{1,0:T(8,128)(2,1)S(1)} %get-tuple-element.29.link2_ref, ...), custom_call_target="tpu_custom_call" | custom-call | flops 1000000 | bytes 1000000 | tf_op jit(solution)/shard_map/pallas_call | solution.py:567
  31.4 0.8 %shard_map.123 = (bf16[2,256,128]{2,1,0:T(8,128)(2,1)S(1)}, bf16[2,2,64,256]{3,2,1,0:T(8,128)(2,1)S(1)}) custom-call(bf16[1,256,256]{2,1,0:T(8,128)(2,1)S(1)} %get-tuple-element.26.modes_ref, f32[1,256]{1,0:T(1,128)S(1)} %get-tuple-element.27.levels_ref, bf16[128,512]{1,0:T(8,128)(2,1)S(1)} %get-tuple-element.29.link2_ref, ...), custom_call_target="tpu_custom_call" | custom-call | flops 1000000 | bytes 1000000 | tf_op jit(solution)/shard_map/pallas_call | solution.py:567
  32.3 1.0 %shard_map.120 = f32[1,2,256]{2,1,0:T(2,128)} custom-call(f32[1,2,256]{2,1,0:T(2,128)S(1)} %shard_map.114.diagonal_ref, bf16[2,256,128]{2,1,0:T(8,128)(2,1)S(1)} %get-tuple-element.30.left_ref.refs_0_, bf16[2,64,128]{2,1,0:T(8,128)(2,1)S(1)} %get-tuple-element.40.retarded_ref), custom_call_target="tpu_custom_call" | custom-call | flops 1000000 | bytes 1000000 | tf_op jit(solution)/shard_map/pallas_call | solution.py:595
  33.3 3.5 %shard_map.124 = bf16[1,2,8,64,256]{4,3,2,1,0:T(8,128)(2,1)} custom-call(s32[8]{0:T(128)} %offsets_hbm.1, bf16[1,2,8,64,256]{4,3,2,1,0:T(8,128)(2,1)S(1)} %copy-done, bf16[2,256,128]{2,1,0:T(8,128)(2,1)S(1)} %get-tuple-element.30.left_ref.refs_0_, bf16[2,256,128]{2,1,0:T(8,128)(2,1)S(1)} %get-tuple-element.41.refs_1_, ...), custom_call_target="tpu_custom_call" | custom-call | flops 1000000 | bytes 1000000 | tf_op jit(solution)/shard_map/pallas_call | solution.py:602
  (10 shorter events, 0.6 us)
Async XLA Ops:
  2.4 2.1 %collective-permute-start = (f32[8,128]{1,0:T(8,128)S(1)}, f32[8,128]{1,0:T(8,128)S(1)}, u32[]{:S(2)}, u32[]{:S(2)}) collective-permute-start(f32[8,128]{1,0:T(8,128)S(1)} %get-tuple-element.31), channel_id=1, source_target_pairs={{0,4},{4,0},{8,12},{12,8},{16,20},{20,16},{24,28},{28,24},{1,5},{5... | collective-permute-start | bytes 12296 | tf_op jit(solution)/shard_map/ppermute | solution.py:511
  2.9 1.5 %collective-permute-start.1 = (f32[8,128]{1,0:T(8,128)S(1)}, f32[8,128]{1,0:T(8,128)S(1)}, u32[]{:S(2)}, u32[]{:S(2)}) collective-permute-start(f32[8,128]{1,0:T(8,128)S(1)} %get-tuple-element.31), channel_id=1, source_target_pairs={{4,8},{12,16},{20,24},{8,4},{16,12},{24,20},{5,9},{13,17},{21,25},... | collective-permute-start | bytes 12296 | tf_op jit(solution)/shard_map/ppermute | solution.py:537
  4.9 5.3 %collective-permute-start.2 = (bf16[1,272,128]{2,1,0:T(8,128)(2,1)S(1)}, bf16[1,272,128]{2,1,0:T(8,128)(2,1)S(1)}, u32[]{:S(2)}, u32[]{:S(2)}) collective-permute-start(bf16[1,272,128]{2,1,0:T(8,128)(2,1)S(1)} %get-tuple-element.34), channel_id=1, source_target_pairs={{0,4},{4,0},{8,12},{12,8},{16,20},{20,16},{24,28},{28,24},{1,5},{5... | collective-permute-start | bytes 208904 | tf_op jit(solution)/shard_map/ppermute | solution.py:511
  10.9 4.9 %collective-permute-start.3 = (bf16[1,272,128]{2,1,0:T(8,128)(2,1)S(1)}, bf16[1,272,128]{2,1,0:T(8,128)(2,1)S(1)}, u32[]{:S(2)}, u32[]{:S(2)}) collective-permute-start(bf16[1,272,128]{2,1,0:T(8,128)(2,1)S(1)} %get-tuple-element.36), channel_id=1, source_target_pairs={{0,8},{4,12},{8,0},{12,4},{16,24},{20,28},{24,16},{28,20},{1,9},{5... | collective-permute-start | bytes 208904 | tf_op jit(solution)/shard_map/ppermute | solution.py:511
  16.7 5.0 %collective-permute-start.4 = (bf16[1,144,128]{2,1,0:T(8,128)(2,1)S(1)}, bf16[1,144,128]{2,1,0:T(8,128)(2,1)S(1)}, u32[]{:S(2)}, u32[]{:S(2)}) collective-permute-start(bf16[1,144,128]{2,1,0:T(8,128)(2,1)S(1)} %get-tuple-element.39), channel_id=1, source_target_pairs={{0,16},{4,20},{8,24},{12,28},{16,0},{20,4},{24,8},{28,12},{1,17},{... | collective-permute-start | bytes 110600 | tf_op jit(solution)/shard_map/ppermute | solution.py:511
  19.5 6.5 %collective-permute-start.5 = (f32[1,3,2,256]{3,2,1,0:T(2,128)S(1)}, f32[1,3,2,256]{3,2,1,0:T(2,128)S(1)}, u32[]{:S(2)}, u32[]{:S(2)}) collective-permute-start(f32[1,3,2,256]{3,2,1,0:T(2,128)S(1)} %get-tuple-element.28.params_ref.rest_0_), channel_id=1, source_target_pairs={{0,1},{1,0},{2,3},{3,2},{4,5},{5,4},{6,7},{7,6},{8,9},{9,8},{10,11... | collective-permute-start | bytes 18440 | tf_op jit(solution)/shard_map/ppermute | solution.py:511
  22.4 10.8 %copy-start = (bf16[1,2,8,64,256]{4,3,2,1,0:T(8,128)(2,1)S(1)}, bf16[1,2,8,64,256]{4,3,2,1,0:T(8,128)(2,1)}, u32[]{:S(2)}) copy-start(bf16[1,2,8,64,256]{4,3,2,1,0:T(8,128)(2,1)} %screen_ref.1) | copy-start | bytes 1572868
  22.5 10.8 %collective-permute-start.7 = (bf16[1,64,128]{2,1,0:T(8,128)(2,1)S(1)}, bf16[1,64,128]{2,1,0:T(8,128)(2,1)S(1)}, u32[]{:S(2)}, u32[]{:S(2)}) collective-permute-start(bf16[1,64,128]{2,1,0:T(8,128)(2,1)S(1)} %get-tuple-element.49.refs_8_), channel_id=1, source_target_pairs={{0,1},{1,0},{2,3},{3,2},{4,5},{5,4},{6,7},{7,6},{8,9},{9,8},{10,11... | collective-permute-start | bytes 49160 | tf_op jit(solution)/shard_map/ppermute | solution.py:511
  24.1 9.2 %collective-permute-start.8 = (bf16[1,64,128]{2,1,0:T(8,128)(2,1)S(1)}, bf16[1,64,128]{2,1,0:T(8,128)(2,1)S(1)}, u32[]{:S(2)}, u32[]{:S(2)}) collective-permute-start(bf16[1,64,128]{2,1,0:T(8,128)(2,1)S(1)} %get-tuple-element.49.refs_8_), channel_id=1, source_target_pairs={{0,2},{1,3},{2,0},{3,1},{4,6},{5,7},{6,4},{7,5},{8,10},{9,11},{10,... | collective-permute-start | bytes 49160 | tf_op jit(solution)/shard_map/ppermute | solution.py:511
  25.6 7.7 %collective-permute-start.9 = (bf16[1,64,128]{2,1,0:T(8,128)(2,1)S(1)}, bf16[1,64,128]{2,1,0:T(8,128)(2,1)S(1)}, u32[]{:S(2)}, u32[]{:S(2)}) collective-permute-start(bf16[1,64,128]{2,1,0:T(8,128)(2,1)S(1)} %get-tuple-element.49.refs_8_), channel_id=1, source_target_pairs={{0,3},{1,2},{2,1},{3,0},{4,7},{5,6},{6,5},{7,4},{8,11},{9,10},{10,... | collective-permute-start | bytes 49160 | tf_op jit(solution)/shard_map/ppermute | solution.py:511
  26.8 3.8 %collective-permute-start.6 = (f32[2,3,2,256]{3,2,1,0:T(2,128)S(1)}, f32[2,3,2,256]{3,2,1,0:T(2,128)S(1)}, u32[]{:S(2)}, u32[]{:S(2)}) collective-permute-start(f32[2,3,2,256]{3,2,1,0:T(2,128)S(1)} %get-tuple-element.42), channel_id=1, source_target_pairs={{0,2},{1,3},{2,0},{3,1},{4,6},{5,7},{6,4},{7,5},{8,10},{9,11},{10,... | collective-permute-start | bytes 36872 | tf_op jit(solution)/shard_map/ppermute | solution.py:511

commit v5 on v4

--- a/solution.py
+++ b/solution.py
@@ -76,23 +76,11 @@
     return resolvent(levels_ref[...], params_ref[0, e : e + 1, :], params_ref[1, e : e + 1, :], first + e, overall)
 
 
-def maps_kernel(
-    overall,
-    one_ref,
-    two_ref,
-    modes_ref,
-    levels_ref,
-    params_ref,
-    left_ref,
-    free_ref,
-    out_ref,
-    message_ref,
-):
-    energies = params_ref.shape[2]
-    extent = out_ref.shape[2]
+def own_maps(overall, block_ref, modes_ref, levels_ref, params_ref, left_ref, free_ref):
+    energies, _, width = left_ref.shape
+    extent = width // 2
     first = lax.axis_index("energy") * energies
-    odd = jnp.bitwise_and(lax.axis_index("cell"), 1) == 1
-    block = jnp.max(jnp.where(odd, two_ref[...], one_ref[...])).astype(jnp.int32)
+    block = jnp.max(block_ref[...]).astype(jnp.int32)
     chosen = pl.multiple_of(block * extent, extent)
     rows = modes_ref[0, pl.ds(chosen, extent), :]
     width = rows.shape[1]
@@ -117,9 +105,13 @@
                 dot_last(weighted.astype(bf16), jnp.concatenate([free, turned.astype(bf16)], axis=0)),
             )
         )
-        for part in range(3):
-            out_ref[e, part] = maps[e][part].astype(bf16)
-    write_message(message_ref, maps)
+    return maps
+
+
+def maps_kernel(overall, block_ref, modes_ref, levels_ref, params_ref, left_ref, free_ref, message_ref):
+    write_message(
+        message_ref, own_maps(overall, block_ref, modes_ref, levels_ref, params_ref, left_ref, free_ref)
+    )
 
 
 def make_rows(energies, hop, overall, share, modes_ref, levels_ref, params_ref, link2_ref, left_ref, local_ref, free_ref):
@@ -320,60 +312,48 @@
     )
 
 
-def pick(flag, yes, no):
-    return tuple(jnp.where(flag, a, b) for a, b in zip(yes, no))
-
-
-def neutral(extent, width):
-    row = lax.broadcasted_iota(jnp.int32, (extent, width), 0)
-    lane = lax.broadcasted_iota(jnp.int32, (extent, width), 1)
-    zero = jnp.zeros((extent, width), f32)
-    return (jnp.where(row == lane, 1.0, 0.0).astype(bf16), zero.astype(bf16), zero.astype(bf16))
-
-
-def read(ref, e):
-    return tuple(ref[e, part] for part in range(ref.shape[1]))
-
-
-def join_kernel(level, *refs):
-    total_ref, other_ref = refs[:2]
-    enter_ref = refs[2] if level else None
-    outs = refs[3 if level else 2 :]
-    new_enter_ref, message_ref = outs[:2]
-    energies, _, extent, width = total_ref.shape
-    place = lax.axis_index("cell")
-    upper = jnp.bitwise_and(jnp.right_shift(place, level), 1) == 1
-    others = read_message(other_ref)
+def join_kernel(
+    overall, block_ref, modes_ref, levels_ref, params_ref, left_ref, free_ref, other_ref, even_ref, *outs
+):
+    latter = own_maps(overall, block_ref, modes_ref, levels_ref, params_ref, left_ref, free_ref)
+    earlier = read_message(other_ref)
     joined = []
+    for e in range(len(latter)):
+        joined.append(compose(earlier[e], latter[e]))
+        for part in range(3):
+            even_ref[e, part] = earlier[e][part]
+    for out in outs:
+        write_message(out, joined)
+
+
+def arrive_kernel(count, even_ref, *refs):
+    hops, (keep_ref, hand_ref, retarded_ref) = refs[:count], refs[count:]
+    energies, _, extent, width = even_ref.shape
+    if hops:
+        states = [x[-2:] for x in read_message(hops[-1])]
+        for hop in reversed(hops[:-1]):
+            maps = read_message(hop)
+            states = [moved(maps[e], states[e]) for e in range(energies)]
+    else:
+        states = [(jnp.zeros((extent, width), f32),) * 2] * energies
+    nexts = [moved(tuple(even_ref[e, part] for part in range(3)), states[e]) for e in range(energies)]
+    states = [tuple(x.astype(f32) for x in state) for state in states]
+    write_message(hand_ref, states)
+    for pair in range(keep_ref.shape[0]):
+        e = 2 * pair
+        keep_ref[pair, 0:extent] = pack_lesser(states[e][1], states[e + 1][1]).astype(bf16)
+        keep_ref[pair, extent:] = pack_lesser(nexts[e][1], nexts[e + 1][1]).astype(bf16)
     for e in range(energies):
-        total, other = read(total_ref, e), others[e]
-        joined.append(compose(pick(upper, other, total), pick(upper, total, other)))
-        if level:
-            enter = read(enter_ref, e)
-            longer = compose(other, enter)
-            longer = tuple(x.astype(bf16) for x in longer)
-            enter = pick(upper, longer, enter)
-        else:
-            enter = pick(upper, other, neutral(extent, width))
-        for part in range(3):
-            new_enter_ref[e, part] = enter[part]
-            if len(outs) > 2:
-                outs[2][e, part] = joined[e][part].astype(bf16)
-    write_message(message_ref, joined)
-
-
-def arrive_kernel(level, enter_ref, state_ref, retarded_ref, lesser_ref):
-    upper = jnp.right_shift(lax.axis_index("cell"), level) == 1
-    states = read_message(state_ref)
-    lessers = []
-    for e in range(enter_ref.shape[0]):
-        enter = read(enter_ref, e)
-        state = pick(upper, states[e], (jnp.zeros_like(enter[1]), jnp.zeros_like(enter[2])))
-        retarded, lesser = pushed(enter, state)
-        retarded_ref[e] = (enter[1].astype(f32) + retarded).astype(bf16)
-        lessers.append(enter[2].astype(f32) + lesser)
-    for pair in range(lesser_ref.shape[0]):
-        lesser_ref[pair] = pack_lesser(lessers[2 * pair], lessers[2 * pair + 1]).astype(bf16)
+        retarded_ref[e] = nexts[e][0].astype(bf16)
+
+
+def moved(step, state):
+    retarded, lesser = pushed(step, state)
+    return step[1].astype(f32) + retarded, step[2].astype(f32) + lesser
+
+
+def is_odd():
+    return jnp.bitwise_and(lax.axis_index("cell"), 1) == 1
 
 
 def row_sums(x):
@@ -389,17 +369,22 @@
         out_ref[0, e : e + 1, :] = row_sums(modes * (modes * di).astype(bf16).astype(f32))
 
 
-def density_kernel(diagonal_ref, left_ref, retarded_ref, out_ref):
+def density_kernel(diagonal_ref, left_ref, retarded_ref, hand_ref, out_ref):
+    odd = is_odd()
+    given = read_message(hand_ref)
     for e in range(left_ref.shape[0]):
         left = left_ref[e]
-        pz = dot_mat(left, full(retarded_ref[e])).astype(bf16).astype(f32)
+        state = jnp.where(odd, retarded_ref[e], given[e][0])
+        pz = dot_mat(left, full(state)).astype(bf16).astype(f32)
         total = diagonal_ref[0, e : e + 1, :] + row_sums(pz * swap_halves(left.astype(f32)))
         out_ref[0, e : e + 1, :] = -total / math.pi
 
 
 def convolve_kernel(groups, reach, offsets_hbm, screen_ref, *refs):
-    lefts, locals_, lessers = refs[:groups], refs[groups : 2 * groups], refs[2 * groups : 3 * groups]
-    out_hbm, g_re, g_im, g_sum, out_ref, offsets_ref, sem, out_sems = refs[3 * groups :]
+    lefts, locals_, kept, given = (refs[part * groups : (part + 1) * groups] for part in range(4))
+    out_hbm, g_re, g_im, g_sum, out_ref, offsets_ref, sem, out_sems = refs[4 * groups :]
+    odd = is_odd()
+    extent = lefts[0].shape[2] // 2
     copy = pltpu.make_async_copy(offsets_hbm, offsets_ref, sem)
     copy.start()
     energies = lefts[0].shape[0]
@@ -415,7 +400,10 @@
     for hop in range(groups):
         base = jnp.bitwise_xor(group, hop) * energies + reach
         for pair in range(energies // 2):
-            states = unpack_lesser(lessers[hop][pair])
+            start = 0 if hop else extent
+            states = unpack_lesser(
+                jnp.where(odd, kept[hop][pair, extent : 2 * extent], given[hop][pair, start : start + extent])
+            )
             for e in (2 * pair, 2 * pair + 1):
                 left = lefts[hop][e]
                 own = lefts[hop][e, pl.ds(mine, share), :]
@@ -498,8 +486,8 @@
 ):
     cells = lax.axis_size("cell")
     groups = lax.axis_size("energy")
-    rounds = cells.bit_length() - 1
-    assert cells == 1 << rounds and groups & (groups - 1) == 0
+    chips = cells // 2
+    assert cells % 2 == 0 and groups & (groups - 1) == 0
     energies = level_shift.shape[1]
     overall = energies * groups
     orbitals, extent = coupling.shape[1:]
@@ -532,9 +520,9 @@
             pltpu.SemaphoreType.DMA((7,)),
         ],
     )(interface, *map(in_hbm, (row_mask, modes, levels, coupling, level_shift, broadening, injection)))
-    one = swapped(block, "cell", 1)
-    near = [(i, i + 1) for i in range(1, cells - 1, 2)]
-    two = lax.ppermute(block, "cell", near + [(j, i) for i, j in near])
+    odds = range(1, cells, 2)
+    one = lax.ppermute(block, "cell", [(i, i - 1) for i in odds])
+    two = lax.ppermute(block, "cell", [(i + 1, i) for i in odds if i + 1 < cells])
 
     left_shape = sds((energies, orbitals, width), bf16)
     local_shape = sds((energies, 2, share, orbitals), bf16)
@@ -546,11 +534,8 @@
     )(modes, levels, link2, params)
     lefts, locals_ = [left], [local]
 
-    total, sent = call(
-        partial(maps_kernel, overall),
-        (maps_shape, message),
-        [VMEM] * 7,
-    )(one, two, modes, levels, params, left, free)
+    sent = call(partial(maps_kernel, overall), message, [VMEM] * 6)(one, modes, levels, params, left, free)
+    other = lax.ppermute(sent, "cell", [(i - 1, i) for i in odds])
     diagonal = call(
         partial(diagonal_kernel, overall), sds((1, energies, orbitals), f32), [VMEM] * 3
     )(modes, levels, params)
@@ -575,25 +560,35 @@
             break
         known = both
 
-    enter = None
-    for level in range(rounds - 1):
-        other = swapped(sent, "cell", 1 << level)
-        outs = (maps_shape, message, maps_shape) if level < rounds - 2 else (maps_shape, state_message)
-        given = [total, other] + ([enter] if level else [])
-        enter, sent, *rest = call(partial(join_kernel, level), outs, [VMEM] * len(given))(*given)
-        total = rest[0] if rest else None
-    state = swapped(sent, "cell", cells // 2)
-    retarded, lesser = call(
-        partial(arrive_kernel, rounds - 1),
-        (sds((energies, extent, width), bf16), sds((pairs, extent, width), bf16)),
-        [VMEM, VMEM],
-    )(enter, state)
-
-    lessers = [lesser]
+    even, total, total_state = call(
+        partial(join_kernel, overall), (maps_shape, message, state_message), [VMEM] * 7
+    )(two, modes, levels, params, lefts[0], free, other)
+    hops = []
+    for hop in range(1, chips):
+        route = [(i, i + 2 * hop) for i in odds if i + 2 * hop < cells]
+        hops.append(lax.ppermute(total if hop < chips - 1 else total_state, "cell", route))
+    keep, hand, retarded = call(
+        partial(arrive_kernel, len(hops)),
+        (
+            sds((pairs, 2 * extent, width), bf16),
+            state_message,
+            sds((energies, extent, width), bf16),
+        ),
+        [VMEM] * (1 + len(hops)),
+    )(even, *hops)
+
+    def handed(x):
+        return lax.ppermute(x, "cell", [(i, i - 1) for i in odds])
+
+    kept = [keep]
     for hop in range(1, groups):
-        lessers.append(swapped(lesser, "energy", hop))
-    density = call(density_kernel, sds((1, energies, orbitals), f32), [VMEM] * 3)(
-        diagonal, lefts[0], retarded
+        route = [(i * groups + g, i * groups + (g ^ hop)) for i in odds for g in range(groups)]
+        kept.append(lax.ppermute(keep, ("cell", "energy"), route))
+    given = []
+    for hop in range(groups):
+        given.append(handed(kept[hop] if hop else hand))
+    density = call(density_kernel, sds((1, energies, orbitals), f32), [VMEM] * 4)(
+        diagonal, lefts[0], retarded, given[0]
     )
 
     reach = overall // 4
@@ -602,7 +597,7 @@
     sigma = call(
         partial(convolve_kernel, groups, reach),
         sds(out_shape, bf16),
-        [HBM, VMEM] + [VMEM] * (3 * groups),
+        [HBM, VMEM] + [VMEM] * (4 * groups),
         [
             spread,
             spread,
@@ -613,7 +608,7 @@
             pltpu.SemaphoreType.DMA((share // 16,)),
         ],
         out_specs=HBM,
-    )(in_hbm(offsets), screened, *lefts, *locals_, *lessers)
+    )(in_hbm(offsets), screened, *lefts, *locals_, *kept, *given)
     return (density, sigma)
 
 

time: 37 us -> 50.4 us (1.36)
  the two profiles are of different devices: /device:TPU:0 before, /device:TPU:25 now
where the time goes in v5:
time: 50.4 us; the launch traced here: 49.4 us
  starting transfers between devices  24.5 us (49%)
  Pallas kernels  11.9 us (24%)
  waiting for transfers between devices  11.5 us (23%)
  between operations  1.51 us (3%)
    ppermute x3, starting transfers between devices, body(): kept.append(lax.ppermute(keep, ('cell', 'energy'), route))  8.37 us
    ppermute x3, waiting for transfers between devices, body(): lax.ppermute(total if hop < chips - 1 else total_state, 'cell', route)  7.9 us
    ppermute x4, starting transfers between devices, handed(): return lax.ppermute(x, 'cell', [(i, i - 1) for i in odds])  5.17 us
    ppermute x3, starting transfers between devices, body(): lax.ppermute(total if hop < chips - 1 else total_state, 'cell', route)  3.88 us
    pallas_call x1, Pallas kernels, body(): call(partial(convolve_kernel, groups, reach), sds(out_shape, bf16), [HBM,...  3.55 us
    ppermute x2, starting transfers between devices, swapped(): lax.ppermute(x, axis, [(i, i ^ distance) for i in range(lax.axis_size(axi...  2.58 us
    ppermute x1, starting transfers between devices, body(): one = lax.ppermute(block, 'cell', [(i, i - 1) for i in odds])  2.58 us
    pallas_call x3, Pallas kernels, body(): call(partial(rows_kernel, overall, share, count + slot, slot), outs, [VME...  2.48 us
  transfers between devices with their start and end apart: 15, of which 4 were waited for; matrix products, arithmetic and copies ran while one was open for 0% of the time, Pallas kernels for 9%

profile of v5, /device:TPU:25, one launch (start us, length us, event | category | flops | bytes accessed | tf_op | source)
XLA Modules:
  0.0 49.4 jit_solution(17569465794915892964)
XLA Ops:
  1.3 1.1 %shard_map.113 = (f32[8,128]{1,0:T(8,128)S(1)}, bf16[128,512]{1,0:T(8,128)(2,1)S(1)}, bf16[1,256,256]{2,1,0:T(8,128)(2,1)S(1)}, f32[1,256]{1,0:T(1,128)S(1)}, f32[1,3,2,256]{3,2,1,0:T(2,128)S(1)}) custom-call(s32[1]{0:T(128)S(6)} %copy.12.interface_ref, s32[1,4]{1,0:T(1,128)} %mask_hbm.1, bf16[1,256,256]{2,1,0:T(8,128)(2,1)} %modes_hbm.1, ...), custom_call_target="tpu_custom_call" | custom-call | flops 1000000 | bytes 1000000 | tf_op jit(solution)/shard_map/pallas_call | solution.py:507
  2.4 2.6 %collective-permute-start.1 = (f32[8,128]{1,0:T(8,128)S(1)}, f32[8,128]{1,0:T(8,128)S(1)}, u32[]{:S(2)}, u32[]{:S(2)}) collective-permute-start(f32[8,128]{1,0:T(8,128)S(1)} %get-tuple-element.28), channel_id=1, source_target_pairs={{4,0},{12,8},{20,16},{28,24},{5,1},{13,9},{21,17},{29,25},{6,2},{1... | collective-permute-start | bytes 12296 | tf_op jit(solution)/shard_map/ppermute | solution.py:524
  4.9 0.8 %shard_map.115 = (bf16[2,256,128]{2,1,0:T(8,128)(2,1)S(1)}, bf16[2,2,64,256]{3,2,1,0:T(8,128)(2,1)S(1)}, bf16[2,256,512]{2,1,0:T(8,128)(2,1)S(1)}) custom-call(bf16[1,256,256]{2,1,0:T(8,128)(2,1)S(1)} %get-tuple-element.23.modes_ref, f32[1,256]{1,0:T(1,128)S(1)} %get-tuple-element.24.levels_ref, bf16[128,512]{1,0:T(8,128)(2,1)S(1)} %get-tuple-element.26.link2_ref, ...), custom_call_target="tpu_custom_call" | custom-call | flops 1000000 | bytes 1000000 | tf_op jit(solution)/shard_map/pallas_call | solution.py:530
  6.3 1.3 %collective-permute-start.2 = (bf16[1,272,128]{2,1,0:T(8,128)(2,1)S(1)}, bf16[1,272,128]{2,1,0:T(8,128)(2,1)S(1)}, u32[]{:S(2)}, u32[]{:S(2)}) collective-permute-start(bf16[1,272,128]{2,1,0:T(8,128)(2,1)S(1)} %shard_map.116), channel_id=1, source_target_pairs={{0,4},{8,12},{16,20},{24,28},{1,5},{9,13},{17,21},{25,29},{2,6},{1... | collective-permute-start | bytes 208904 | tf_op jit(solution)/shard_map/ppermute | solution.py:538
  8.2 1.2 %collective-permute-done.2.other_ref = bf16[1,272,128]{2,1,0:T(8,128)(2,1)S(1)} collective-permute-done((bf16[1,272,128]{2,1,0:T(8,128)(2,1)S(1)}, bf16[1,272,128]{2,1,0:T(8,128)(2,1)S(1)}, u32[]{:S(2)}, u32[]{:S(2)}) %collective-permute-start.2) | collective-permute-done | bytes 69664 | tf_op jit(solution)/shard_map/ppermute | solution.py:538
  9.4 0.9 %shard_map.117 = (bf16[2,3,64,128]{3,2,1,0:T(8,128)(2,1)S(1)}, bf16[1,272,128]{2,1,0:T(8,128)(2,1)S(1)}, bf16[1,144,128]{2,1,0:T(8,128)(2,1)S(1)}) custom-call(f32[8,128]{1,0:T(8,128)S(1)} %collective-permute-done.block_ref, bf16[1,256,256]{2,1,0:T(8,128)(2,1)S(1)} %get-tuple-element.23.modes_ref, f32[1,256]{1,0:T(1,128)S(1)} %get-tuple-element.24.levels_ref, ...), custom_call_target="tpu_custom_call" | custom-call | flops 1000000 | bytes 1000000 | tf_op jit(solution)/shard_map/pallas_call | solution.py:563
  10.3 1.3 %collective-permute-start.3 = (bf16[1,272,128]{2,1,0:T(8,128)(2,1)S(1)}, bf16[1,272,128]{2,1,0:T(8,128)(2,1)S(1)}, u32[]{:S(2)}, u32[]{:S(2)}) collective-permute-start(bf16[1,272,128]{2,1,0:T(8,128)(2,1)S(1)} %get-tuple-element.31), channel_id=1, source_target_pairs={{4,12},{12,20},{20,28},{5,13},{13,21},{21,29},{6,14},{14,22},{22,3... | collective-permute-start | bytes 208904 | tf_op jit(solution)/shard_map/ppermute | solution.py:569
  11.6 1.3 %collective-permute-start.4 = (bf16[1,272,128]{2,1,0:T(8,128)(2,1)S(1)}, bf16[1,272,128]{2,1,0:T(8,128)(2,1)S(1)}, u32[]{:S(2)}, u32[]{:S(2)}) collective-permute-start(bf16[1,272,128]{2,1,0:T(8,128)(2,1)S(1)} %get-tuple-element.31), channel_id=1, source_target_pairs={{4,20},{12,28},{5,21},{13,29},{6,22},{14,30},{7,23},{15,31}} | collective-permute-start | bytes 208904 | tf_op jit(solution)/shard_map/ppermute | solution.py:569
  12.9 1.3 %collective-permute-start.5 = (bf16[1,144,128]{2,1,0:T(8,128)(2,1)S(1)}, bf16[1,144,128]{2,1,0:T(8,128)(2,1)S(1)}, u32[]{:S(2)}, u32[]{:S(2)}) collective-permute-start(bf16[1,144,128]{2,1,0:T(8,128)(2,1)S(1)} %get-tuple-element.32), channel_id=1, source_target_pairs={{4,28},{5,29},{6,30},{7,31}} | collective-permute-start | bytes 110600 | tf_op jit(solution)/shard_map/ppermute | solution.py:569
  14.2 7.9 %collective-permute-done.5.refs_2_ = bf16[1,144,128]{2,1,0:T(8,128)(2,1)S(1)} collective-permute-done((bf16[1,144,128]{2,1,0:T(8,128)(2,1)S(1)}, bf16[1,144,128]{2,1,0:T(8,128)(2,1)S(1)}, u32[]{:S(2)}, u32[]{:S(2)}) %collective-permute-start.5) | collective-permute-done | bytes 36896 | tf_op jit(solution)/shard_map/ppermute | solution.py:569
  22.1 1.3 %shard_map.118 = (bf16[1,128,128]{2,1,0:T(8,128)(2,1)S(1)}, bf16[1,144,128]{2,1,0:T(8,128)(2,1)S(1)}, bf16[2,64,128]{2,1,0:T(8,128)(2,1)S(1)}) custom-call(bf16[2,3,64,128]{3,2,1,0:T(8,128)(2,1)S(1)} %get-tuple-element.30.even_ref, bf16[1,272,128]{2,1,0:T(8,128)(2,1)S(1)} %collective-permute-done.3.refs_0_, ...), custom_call_target="tpu_custom_call" | custom-call | flops 1000000 | bytes 1000000 | tf_op jit(solution)/shard_map/pallas_call | solution.py:570
  23.4 3.1 %collective-permute-start.9 = (bf16[1,128,128]{2,1,0:T(8,128)(2,1)S(1)}, bf16[1,128,128]{2,1,0:T(8,128)(2,1)S(1)}, u32[]{:S(2)}, u32[]{:S(2)}) collective-permute-start(bf16[1,128,128]{2,1,0:T(8,128)(2,1)S(1)} %get-tuple-element.43.refs_8_), channel_id=1, source_target_pairs={{4,5},{5,4},{6,7},{7,6},{12,13},{13,12},{14,15},{15,14},{20,21},{2... | collective-permute-start | bytes 98312 | tf_op jit(solution)/shard_map/ppermute | solution.py:586
  26.6 3.1 %collective-permute-start.10 = (bf16[1,128,128]{2,1,0:T(8,128)(2,1)S(1)}, bf16[1,128,128]{2,1,0:T(8,128)(2,1)S(1)}, u32[]{:S(2)}, u32[]{:S(2)}) collective-permute-start(bf16[1,128,128]{2,1,0:T(8,128)(2,1)S(1)} %get-tuple-element.43.refs_8_), channel_id=1, source_target_pairs={{4,6},{5,7},{6,4},{7,5},{12,14},{13,15},{14,12},{15,13},{20,22},{2... | collective-permute-start | bytes 98312 | tf_op jit(solution)/shard_map/ppermute | solution.py:586
  29.7 2.1 %collective-permute-start.11 = (bf16[1,128,128]{2,1,0:T(8,128)(2,1)S(1)}, bf16[1,128,128]{2,1,0:T(8,128)(2,1)S(1)}, u32[]{:S(2)}, u32[]{:S(2)}) collective-permute-start(bf16[1,128,128]{2,1,0:T(8,128)(2,1)S(1)} %get-tuple-element.43.refs_8_), channel_id=1, source_target_pairs={{4,7},{5,6},{6,5},{7,4},{12,15},{13,14},{14,13},{15,12},{20,23},{2... | collective-permute-start | bytes 98312 | tf_op jit(solution)/shard_map/ppermute | solution.py:586
  31.8 1.3 %collective-permute-start.6 = (bf16[1,144,128]{2,1,0:T(8,128)(2,1)S(1)}, bf16[1,144,128]{2,1,0:T(8,128)(2,1)S(1)}, u32[]{:S(2)}, u32[]{:S(2)}) collective-permute-start(bf16[1,144,128]{2,1,0:T(8,128)(2,1)S(1)} %get-tuple-element.34), channel_id=1, source_target_pairs={{4,0},{12,8},{20,16},{28,24},{5,1},{13,9},{21,17},{29,25},{6,2},{1... | collective-permute-start | bytes 110600 | tf_op jit(solution)/shard_map/ppermute | solution.py:581
  33.1 1.3 %collective-permute-start.12 = (bf16[1,128,128]{2,1,0:T(8,128)(2,1)S(1)}, bf16[1,128,128]{2,1,0:T(8,128)(2,1)S(1)}, u32[]{:S(2)}, u32[]{:S(2)}) collective-permute-start(bf16[1,128,128]{2,1,0:T(8,128)(2,1)S(1)} %collective-permute-done.9.refs_9_), channel_id=1, source_target_pairs={{4,0},{12,8},{20,16},{28,24},{5,1},{13,9},{21,17},{29,25},{6,2},{1... | collective-permute-start | bytes 98312 | tf_op jit(solution)/shard_map/ppermute | solution.py:581
  34.5 1.3 %collective-permute-start.13 = (bf16[1,128,128]{2,1,0:T(8,128)(2,1)S(1)}, bf16[1,128,128]{2,1,0:T(8,128)(2,1)S(1)}, u32[]{:S(2)}, u32[]{:S(2)}) collective-permute-start(bf16[1,128,128]{2,1,0:T(8,128)(2,1)S(1)} %collective-permute-done.10.refs_10_), channel_id=1, source_target_pairs={{4,0},{12,8},{20,16},{28,24},{5,1},{13,9},{21,17},{29,25},{6,2},{1... | collective-permute-start | bytes 98312 | tf_op jit(solution)/shard_map/ppermute | solution.py:581
  35.8 1.3 %collective-permute-start.14 = (bf16[1,128,128]{2,1,0:T(8,128)(2,1)S(1)}, bf16[1,128,128]{2,1,0:T(8,128)(2,1)S(1)}, u32[]{:S(2)}, u32[]{:S(2)}) collective-permute-start(bf16[1,128,128]{2,1,0:T(8,128)(2,1)S(1)} %collective-permute-done.11.refs_11_), channel_id=1, source_target_pairs={{4,0},{12,8},{20,16},{28,24},{5,1},{13,9},{21,17},{29,25},{6,2},{1... | collective-permute-start | bytes 98312 | tf_op jit(solution)/shard_map/ppermute | solution.py:581
  37.1 1.3 %collective-permute-start.7 = (f32[1,3,2,256]{3,2,1,0:T(2,128)S(1)}, f32[1,3,2,256]{3,2,1,0:T(2,128)S(1)}, u32[]{:S(2)}, u32[]{:S(2)}) collective-permute-start(f32[1,3,2,256]{3,2,1,0:T(2,128)S(1)} %get-tuple-element.25.params_ref.rest_0_), channel_id=1, source_target_pairs={{0,1},{1,0},{2,3},{3,2},{4,5},{5,4},{6,7},{7,6},{8,9},{9,8},{10,11... | collective-permute-start | bytes 18440 | tf_op jit(solution)/shard_map/ppermute | solution.py:499
  38.3 1.3 %collective-permute-done.7.got_ref = f32[1,3,2,256]{3,2,1,0:T(2,128)S(1)} collective-permute-done((f32[1,3,2,256]{3,2,1,0:T(2,128)S(1)}, f32[1,3,2,256]{3,2,1,0:T(2,128)S(1)}, u32[]{:S(2)}, u32[]{:S(2)}) %collective-permute-start.7) | collective-permute-done | bytes 6176 | tf_op jit(solution)/shard_map/ppermute | solution.py:499
  40.5 1.3 %collective-permute-start.8 = (f32[2,3,2,256]{3,2,1,0:T(2,128)S(1)}, f32[2,3,2,256]{3,2,1,0:T(2,128)S(1)}, u32[]{:S(2)}, u32[]{:S(2)}) collective-permute-start(f32[2,3,2,256]{3,2,1,0:T(2,128)S(1)} %get-tuple-element.36), channel_id=1, source_target_pairs={{0,2},{1,3},{2,0},{3,1},{4,6},{5,7},{6,4},{7,5},{8,10},{9,11},{10,... | collective-permute-start | bytes 36872 | tf_op jit(solution)/shard_map/ppermute | solution.py:499
  42.0 1.1 %collective-permute-done.8.got_ref = f32[2,3,2,256]{3,2,1,0:T(2,128)S(1)} collective-permute-done((f32[2,3,2,256]{3,2,1,0:T(2,128)S(1)}, f32[2,3,2,256]{3,2,1,0:T(2,128)S(1)}, u32[]{:S(2)}, u32[]{:S(2)}) %collective-permute-start.8) | collective-permute-done | bytes 12320 | tf_op jit(solution)/shard_map/ppermute | solution.py:499
  44.7 1.1 %shard_map.119 = f32[1,2,256]{2,1,0:T(2,128)} custom-call(f32[1,2,256]{2,1,0:T(2,128)S(1)} %shard_map.114.diagonal_ref, bf16[2,256,128]{2,1,0:T(8,128)(2,1)S(1)} %get-tuple-element.27.left_ref.refs_0_, bf16[2,64,128]{2,1,0:T(8,128)(2,1)S(1)} %get-tuple-element.33.retarded_ref, bf16[1,144,128]{2,1,0:T(8,128)(2,1)S(1)} %collective-permute-done.6.hand_ref.refs_12_), custom_call_target="tpu_custom_call" | custom-call | flops 1000000 | bytes 1000000 | tf_op jit(solution)/shard_map/pallas_call | solution.py:590
  45.9 3.5 %shard_map.123 = bf16[1,2,8,64,256]{4,3,2,1,0:T(8,128)(2,1)} custom-call(s32[8]{0:T(128)} %offsets_hbm.1, bf16[1,2,8,64,256]{4,3,2,1,0:T(8,128)(2,1)S(1)} %copy-done, bf16[2,256,128]{2,1,0:T(8,128)(2,1)S(1)} %get-tuple-element.27.left_ref.refs_0_, bf16[2,256,128]{2,1,0:T(8,128)(2,1)S(1)} %get-tuple-element.35.refs_1_, ...), custom_call_target="tpu_custom_call" | custom-call | flops 1000000 | bytes 1000000 | tf_op jit(solution)/shard_map/pallas_call | solution.py:597
  (19 shorter events, 3.8 us)
Async XLA Ops:
  2.4 3.4 %collective-permute-start.1 = (f32[8,128]{1,0:T(8,128)S(1)}, f32[8,128]{1,0:T(8,128)S(1)}, u32[]{:S(2)}, u32[]{:S(2)}) collective-permute-start(f32[8,128]{1,0:T(8,128)S(1)} %get-tuple-element.28), channel_id=1, source_target_pairs={{4,0},{12,8},{20,16},{28,24},{5,1},{13,9},{21,17},{29,25},{6,2},{1... | collective-permute-start | bytes 12296 | tf_op jit(solution)/shard_map/ppermute | solution.py:524
  6.3 3.2 %collective-permute-start.2 = (bf16[1,272,128]{2,1,0:T(8,128)(2,1)S(1)}, bf16[1,272,128]{2,1,0:T(8,128)(2,1)S(1)}, u32[]{:S(2)}, u32[]{:S(2)}) collective-permute-start(bf16[1,272,128]{2,1,0:T(8,128)(2,1)S(1)} %shard_map.116), channel_id=1, source_target_pairs={{0,4},{8,12},{16,20},{24,28},{1,5},{9,13},{17,21},{25,29},{2,6},{1... | collective-permute-start | bytes 208904 | tf_op jit(solution)/shard_map/ppermute | solution.py:538
  7.6 0.7 %collective-permute-start = (f32[8,128]{1,0:T(8,128)S(1)}, f32[8,128]{1,0:T(8,128)S(1)}, u32[]{:S(2)}, u32[]{:S(2)}) collective-permute-start(f32[8,128]{1,0:T(8,128)S(1)} %get-tuple-element.28), channel_id=1, source_target_pairs={{8,4},{16,12},{24,20},{9,5},{17,13},{25,21},{10,6},{18,14},{26,22}... | collective-permute-start | bytes 12296 | tf_op jit(solution)/shard_map/ppermute | solution.py:525
  10.3 11.8 %collective-permute-start.3 = (bf16[1,272,128]{2,1,0:T(8,128)(2,1)S(1)}, bf16[1,272,128]{2,1,0:T(8,128)(2,1)S(1)}, u32[]{:S(2)}, u32[]{:S(2)}) collective-permute-start(bf16[1,272,128]{2,1,0:T(8,128)(2,1)S(1)} %get-tuple-element.31), channel_id=1, source_target_pairs={{4,12},{12,20},{20,28},{5,13},{13,21},{21,29},{6,14},{14,22},{22,3... | collective-permute-start | bytes 208904 | tf_op jit(solution)/shard_map/ppermute | solution.py:569
  11.6 10.5 %collective-permute-start.4 = (bf16[1,272,128]{2,1,0:T(8,128)(2,1)S(1)}, bf16[1,272,128]{2,1,0:T(8,128)(2,1)S(1)}, u32[]{:S(2)}, u32[]{:S(2)}) collective-permute-start(bf16[1,272,128]{2,1,0:T(8,128)(2,1)S(1)} %get-tuple-element.31), channel_id=1, source_target_pairs={{4,20},{12,28},{5,21},{13,29},{6,22},{14,30},{7,23},{15,31}} | collective-permute-start | bytes 208904 | tf_op jit(solution)/shard_map/ppermute | solution.py:569
  12.9 9.2 %collective-permute-start.5 = (bf16[1,144,128]{2,1,0:T(8,128)(2,1)S(1)}, bf16[1,144,128]{2,1,0:T(8,128)(2,1)S(1)}, u32[]{:S(2)}, u32[]{:S(2)}) collective-permute-start(bf16[1,144,128]{2,1,0:T(8,128)(2,1)S(1)} %get-tuple-element.32), channel_id=1, source_target_pairs={{4,28},{5,29},{6,30},{7,31}} | collective-permute-start | bytes 110600 | tf_op jit(solution)/shard_map/ppermute | solution.py:569
  23.4 9.7 %collective-permute-start.9 = (bf16[1,128,128]{2,1,0:T(8,128)(2,1)S(1)}, bf16[1,128,128]{2,1,0:T(8,128)(2,1)S(1)}, u32[]{:S(2)}, u32[]{:S(2)}) collective-permute-start(bf16[1,128,128]{2,1,0:T(8,128)(2,1)S(1)} %get-tuple-element.43.refs_8_), channel_id=1, source_target_pairs={{4,5},{5,4},{6,7},{7,6},{12,13},{13,12},{14,15},{15,14},{20,21},{2... | collective-permute-start | bytes 98312 | tf_op jit(solution)/shard_map/ppermute | solution.py:586
  26.6 7.9 %collective-permute-start.10 = (bf16[1,128,128]{2,1,0:T(8,128)(2,1)S(1)}, bf16[1,128,128]{2,1,0:T(8,128)(2,1)S(1)}, u32[]{:S(2)}, u32[]{:S(2)}) collective-permute-start(bf16[1,128,128]{2,1,0:T(8,128)(2,1)S(1)} %get-tuple-element.43.refs_8_), channel_id=1, source_target_pairs={{4,6},{5,7},{6,4},{7,5},{12,14},{13,15},{14,12},{15,13},{20,22},{2... | collective-permute-start | bytes 98312 | tf_op jit(solution)/shard_map/ppermute | solution.py:586
  29.7 6.0 %collective-permute-start.11 = (bf16[1,128,128]{2,1,0:T(8,128)(2,1)S(1)}, bf16[1,128,128]{2,1,0:T(8,128)(2,1)S(1)}, u32[]{:S(2)}, u32[]{:S(2)}) collective-permute-start(bf16[1,128,128]{2,1,0:T(8,128)(2,1)S(1)} %get-tuple-element.43.refs_8_), channel_id=1, source_target_pairs={{4,7},{5,6},{6,5},{7,4},{12,15},{13,14},{14,13},{15,12},{20,23},{2... | collective-permute-start | bytes 98312 | tf_op jit(solution)/shard_map/ppermute | solution.py:586
  31.8 12.9 %collective-permute-start.6 = (bf16[1,144,128]{2,1,0:T(8,128)(2,1)S(1)}, bf16[1,144,128]{2,1,0:T(8,128)(2,1)S(1)}, u32[]{:S(2)}, u32[]{:S(2)}) collective-permute-start(bf16[1,144,128]{2,1,0:T(8,128)(2,1)S(1)} %get-tuple-element.34), channel_id=1, source_target_pairs={{4,0},{12,8},{20,16},{28,24},{5,1},{13,9},{21,17},{29,25},{6,2},{1... | collective-permute-start | bytes 110600 | tf_op jit(solution)/shard_map/ppermute | solution.py:581
  33.1 12.7 %collective-permute-start.12 = (bf16[1,128,128]{2,1,0:T(8,128)(2,1)S(1)}, bf16[1,128,128]{2,1,0:T(8,128)(2,1)S(1)}, u32[]{:S(2)}, u32[]{:S(2)}) collective-permute-start(bf16[1,128,128]{2,1,0:T(8,128)(2,1)S(1)} %collective-permute-done.9.refs_9_), channel_id=1, source_target_pairs={{4,0},{12,8},{20,16},{28,24},{5,1},{13,9},{21,17},{29,25},{6,2},{1... | collective-permute-start | bytes 98312 | tf_op jit(solution)/shard_map/ppermute | solution.py:581
  34.5 11.4 %collective-permute-start.13 = (bf16[1,128,128]{2,1,0:T(8,128)(2,1)S(1)}, bf16[1,128,128]{2,1,0:T(8,128)(2,1)S(1)}, u32[]{:S(2)}, u32[]{:S(2)}) collective-permute-start(bf16[1,128,128]{2,1,0:T(8,128)(2,1)S(1)} %collective-permute-done.10.refs_10_), channel_id=1, source_target_pairs={{4,0},{12,8},{20,16},{28,24},{5,1},{13,9},{21,17},{29,25},{6,2},{1... | collective-permute-start | bytes 98312 | tf_op jit(solution)/shard_map/ppermute | solution.py:581
  35.8 10.1 %collective-permute-start.14 = (bf16[1,128,128]{2,1,0:T(8,128)(2,1)S(1)}, bf16[1,128,128]{2,1,0:T(8,128)(2,1)S(1)}, u32[]{:S(2)}, u32[]{:S(2)}) collective-permute-start(bf16[1,128,128]{2,1,0:T(8,128)(2,1)S(1)} %collective-permute-done.11.refs_11_), channel_id=1, source_target_pairs={{4,0},{12,8},{20,16},{28,24},{5,1},{13,9},{21,17},{29,25},{6,2},{1... | collective-permute-start | bytes 98312 | tf_op jit(solution)/shard_map/ppermute | solution.py:581
  37.1 2.5 %collective-permute-start.7 = (f32[1,3,2,256]{3,2,1,0:T(2,128)S(1)}, f32[1,3,2,256]{3,2,1,0:T(2,128)S(1)}, u32[]{:S(2)}, u32[]{:S(2)}) collective-permute-start(f32[1,3,2,256]{3,2,1,0:T(2,128)S(1)} %get-tuple-element.25.params_ref.rest_0_), channel_id=1, source_target_pairs={{0,1},{1,0},{2,3},{3,2},{4,5},{5,4},{6,7},{7,6},{8,9},{9,8},{10,11... | collective-permute-start | bytes 18440 | tf_op jit(solution)/shard_map/ppermute | solution.py:499
  40.4 5.4 %copy-start = (bf16[1,2,8,64,256]{4,3,2,1,0:T(8,128)(2,1)S(1)}, bf16[1,2,8,64,256]{4,3,2,1,0:T(8,128)(2,1)}, u32[]{:S(2)}) copy-start(bf16[1,2,8,64,256]{4,3,2,1,0:T(8,128)(2,1)} %screen_ref.1) | copy-start | bytes 1572868
  40.5 2.6 %collective-permute-start.8 = (f32[2,3,2,256]{3,2,1,0:T(2,128)S(1)}, f32[2,3,2,256]{3,2,1,0:T(2,128)S(1)}, u32[]{:S(2)}, u32[]{:S(2)}) collective-permute-start(f32[2,3,2,256]{3,2,1,0:T(2,128)S(1)} %get-tuple-element.36), channel_id=1, source_target_pairs={{0,2},{1,3},{2,0},{3,1},{4,6},{5,7},{6,4},{7,5},{8,10},{9,11},{10,... | collective-permute-start | bytes 36872 | tf_op jit(solution)/shard_map/ppermute | solution.py:499

commit v6 on v4

--- a/solution.py
+++ b/solution.py
@@ -158,11 +158,13 @@
     shift_hbm,
     broad_hbm,
     inject_hbm,
+    offsets_hbm,
     block_ref,
     link2_ref,
     modes_ref,
     levels_ref,
     params_ref,
+    offsets_ref,
     mask_ref,
     coupling_ref,
     sems,
@@ -172,6 +174,7 @@
         for index, (source, target) in enumerate(
             (
                 (mask_hbm, mask_ref),
+                (offsets_hbm, offsets_ref),
                 (coupling_hbm, coupling_ref),
                 (shift_hbm, params_ref.at[0, 0:1]),
                 (broad_hbm, params_ref.at[0, 1:2]),
@@ -397,81 +400,77 @@
         out_ref[0, e : e + 1, :] = -total / math.pi
 
 
-def convolve_kernel(groups, reach, offsets_hbm, screen_ref, *refs):
-    lefts, locals_, lessers = refs[:groups], refs[groups : 2 * groups], refs[2 * groups : 3 * groups]
-    out_hbm, g_re, g_im, g_sum, out_ref, offsets_ref, sem, out_sems = refs[3 * groups :]
-    copy = pltpu.make_async_copy(offsets_hbm, offsets_ref, sem)
+def convolve_kernel(reach, hop, last, offsets_ref, screen_ref, lesser_ref, left_ref, local_ref, *refs):
+    if hop:
+        refs = refs[1:]
+    sums_ref, *refs = refs
+    if last:
+        out_hbm, *refs = refs
+    g_ref, picked_ref, sem, *refs = refs
+    copy = pltpu.make_async_copy(offsets_ref, picked_ref, sem)
     copy.start()
-    energies = lefts[0].shape[0]
-    overall = energies * groups
-    share, width = out_ref.shape[3:]
+    energies = left_ref.shape[0]
+    points, share, width = screen_ref.shape[2:]
+    overall = sums_ref.shape[1] - 2 * reach
     group = lax.axis_index("energy")
     mine = pl.multiple_of(group * share, share)
-    blank = jnp.zeros((share, width), f32)
-    for e in range(reach):
-        for g in (g_re, g_im, g_sum):
-            g[e] = blank
-            g[overall + reach + e] = blank
-    for hop in range(groups):
-        base = jnp.bitwise_xor(group, hop) * energies + reach
-        for pair in range(energies // 2):
-            states = unpack_lesser(lessers[hop][pair])
-            for e in (2 * pair, 2 * pair + 1):
-                left = lefts[hop][e]
-                own = lefts[hop][e, pl.ds(mine, share), :]
-                pl_hat = dot_mat(own, full(states[e - 2 * pair]))
-                turned = swap_halves(pl_hat) * signs(pl_hat.shape[1], 1.0)
-                chain = dot_last(jnp.concatenate([pl_hat, turned], axis=0).astype(bf16), left)
-                re = chain[:share] + locals_[hop][e, 0].astype(f32)
-                im = chain[share:] + locals_[hop][e, 1].astype(f32)
-                g_re[base + e] = re
-                g_im[base + e] = im
-                g_sum[base + e] = re + im
+    base = jnp.bitwise_xor(group, hop) * energies + reach
+    if hop == 0:
+        blank = jnp.zeros((share, width), f32)
+        for part in range(3):
+            for e in range(sums_ref.shape[1]):
+                sums_ref[part, e] = blank
+    for pair in range(energies // 2):
+        states = unpack_lesser(lesser_ref[pair])
+        for e in (2 * pair, 2 * pair + 1):
+            own = left_ref[e, pl.ds(mine, share), :]
+            pl_hat = dot_mat(own, full(states[e - 2 * pair]))
+            turned = swap_halves(pl_hat) * signs(pl_hat.shape[1], 1.0)
+            chain = dot_last(jnp.concatenate([pl_hat, turned], axis=0).astype(bf16), left_ref[e])
+            re = chain[:share] + local_ref[e, 0].astype(f32)
+            im = chain[share:] + local_ref[e, 1].astype(f32)
+            g_ref[0, e] = re + im
+            g_ref[1, e] = im
+            g_ref[2, e] = re
     copy.wait()
-    points = screen_ref.shape[2]
-    lanes, height, batch = 128, 16, min(8, overall)
+    height = 16
 
     def out_copy(step):
         rows = pl.ds(pl.multiple_of(step * height, height), height)
         return pltpu.make_async_copy(
-            out_ref.at[:, :, :, rows, :], out_hbm.at[:, :, :, rows, :], out_sems.at[step]
+            refs[0].at[:, :, :, rows, :], out_hbm.at[:, :, :, rows, :], refs[1].at[step]
         )
 
     def rows_of(step, _):
-        top = pl.multiple_of(step * height, height)
-        for lane in range(0, width, lanes):
-            for e0 in range(0, overall, batch):
-                sums = [None] * batch
-                for k in range(points):
-                    start = e0 + reach - offsets_ref[k]
-                    w_re = screen_ref[0, 0, k, pl.ds(top, height), lane : lane + lanes].astype(f32)
-                    w_im = screen_ref[0, 1, k, pl.ds(top, height), lane : lane + lanes].astype(f32)
-                    w_sum, w_change = w_re + w_im, w_im - w_re
-                    for e in range(batch):
-                        new = tuple(
-                            w * g[start + e, pl.ds(top, height), lane : lane + lanes]
-                            for w, g in ((w_re, g_sum), (w_sum, g_im), (w_change, g_re))
-                        )
-                        sums[e] = new if k == 0 else tuple(a + b for a, b in zip(sums[e], new))
-                for e in range(batch):
-                    common, first, second = sums[e]
-                    where = (e0 + e, pl.ds(top, height), slice(lane, lane + lanes))
-                    out_ref[(0, 0) + where] = (-(common + second)).astype(bf16)
-                    out_ref[(0, 1) + where] = (common - first).astype(bf16)
-        out_copy(step).start()
+        rows = pl.ds(pl.multiple_of(step * height, height), height)
+        for k in range(points):
+            w_re = screen_ref[0, 0, k, rows, :].astype(f32)
+            w_im = screen_ref[0, 1, k, rows, :].astype(f32)
+            factors = (w_re, w_re + w_im, w_im - w_re)
+            for e in range(energies):
+                target = base + e + picked_ref[k]
+                for part in range(3):
+                    sums_ref[part, target, rows, :] += factors[part] * g_ref[part, e, rows, :]
+        if last:
+            for e in range(overall):
+                common = sums_ref[0, reach + e, rows, :]
+                refs[0][0, 0, e, rows, :] = (-(common + sums_ref[2, reach + e, rows, :])).astype(bf16)
+                refs[0][0, 1, e, rows, :] = (common - sums_ref[1, reach + e, rows, :]).astype(bf16)
+            out_copy(step).start()
         return 0
 
     steps = share // height
     lax.fori_loop(0, steps, rows_of, 0)
-    for step in range(steps):
-        out_copy(step).wait()
+    if last:
+        for step in range(steps):
+            out_copy(step).wait()
 
 
 def in_hbm(x):
     return pltpu.with_memory_space_constraint(x, pltpu.HBM)
 
 
-def call(kernel, out_shape, in_specs, scratch=(), flops=1_000_000, size=1_000_000, out_specs=None):
+def call(kernel, out_shape, in_specs, scratch=(), flops=1_000_000, size=1_000_000, out_specs=None, aliases={}):
     outs = out_specs or jax.tree.map(lambda _: VMEM, out_shape)
     return pl.pallas_call(
         kernel,
@@ -479,6 +478,7 @@
         in_specs=in_specs,
         out_specs=outs,
         scratch_shapes=list(scratch),
+        input_output_aliases=aliases,
         compiler_params=pltpu.CompilerParams(vmem_limit_bytes=16 << 20),
         cost_estimate=pl.CostEstimate(flops=flops, bytes_accessed=size, transcendentals=0),
     )
@@ -516,7 +516,7 @@
     message = sds((pairs, 4 * extent + spare, width), bf16)
     state_message = sds((pairs, 2 * extent + spare, width), bf16)
     coupling = jnp.swapaxes(coupling, 1, 2)
-    block, link2, modes, levels, params = call(
+    block, link2, modes, levels, params, offsets = call(
         front_kernel,
         (
             sds((8, width), f32),
@@ -524,17 +524,20 @@
             sds(modes.shape, bf16),
             sds(levels.shape, f32),
             sds((1, 3, energies, orbitals), f32),
+            sds(offsets.shape, jnp.int32),
         ),
-        [SMEM] + [HBM] * 7,
+        [SMEM] + [HBM] * 8,
         [
             pltpu.SMEM(row_mask.shape, jnp.int32),
             pltpu.VMEM(coupling.shape, bf16),
-            pltpu.SemaphoreType.DMA((7,)),
+            pltpu.SemaphoreType.DMA((8,)),
         ],
-    )(interface, *map(in_hbm, (row_mask, modes, levels, coupling, level_shift, broadening, injection)))
+    )(interface, *map(in_hbm, (row_mask, modes, levels, coupling, level_shift, broadening, injection, offsets)))
     one = swapped(block, "cell", 1)
-    near = [(i, i + 1) for i in range(1, cells - 1, 2)]
-    two = lax.ppermute(block, "cell", near + [(j, i) for i, j in near])
+    mate = [i + 1 if i % 2 else i - 1 for i in range(cells)]
+    mate[0], mate[-1] = 0, cells - 1
+    route = [(i * groups + g, mate[i] * groups + (g ^ int(mate[i] == i))) for i in range(cells) for g in range(groups)]
+    two = lax.ppermute(block, ("cell", "energy"), route)
 
     left_shape = sds((energies, orbitals, width), bf16)
     local_shape = sds((energies, 2, share, orbitals), bf16)
@@ -597,23 +600,29 @@
     )
 
     reach = overall // 4
-    spread = pltpu.VMEM((overall + 2 * reach, share, orbitals), f32)
-    out_shape = (1, 2, overall, share, orbitals)
-    sigma = call(
-        partial(convolve_kernel, groups, reach),
-        sds(out_shape, bf16),
-        [HBM, VMEM] + [VMEM] * (3 * groups),
-        [
-            spread,
-            spread,
-            spread,
-            pltpu.VMEM(out_shape, bf16),
-            pltpu.SMEM(offsets.shape, jnp.int32),
-            pltpu.SemaphoreType.DMA,
-            pltpu.SemaphoreType.DMA((share // 16,)),
-        ],
-        out_specs=HBM,
-    )(in_hbm(offsets), screened, *lefts, *locals_, *lessers)
+    sums_shape = sds((3, overall + 2 * reach, share, orbitals), f32)
+    sigma_shape = sds((1, 2, overall, share, orbitals), bf16)
+    scratch = [
+        pltpu.VMEM((3, energies, share, orbitals), f32),
+        pltpu.SMEM(offsets.shape, jnp.int32),
+        pltpu.SemaphoreType.DMA,
+    ]
+    for hop in (0, *reversed(range(1, groups))):
+        last = hop == min(1, groups - 1)
+        given = (offsets, screened, lessers[hop], lefts[hop], locals_[hop]) + ((sums,) if hop else ())
+        outs, specs, extra = sums_shape, VMEM, []
+        if last:
+            outs, specs = (sums_shape, sigma_shape), (VMEM, HBM)
+            extra = [pltpu.VMEM(sigma_shape.shape, bf16), pltpu.SemaphoreType.DMA((share // 16,))]
+        sums = call(
+            partial(convolve_kernel, reach, hop, last),
+            outs,
+            [VMEM] * len(given),
+            scratch + extra,
+            out_specs=specs,
+            aliases={5: 0} if hop else {},
+        )(*given)
+    sigma = sums[1]
     return (density, sigma)
 
 

time: 37 us -> 36.9 us (level)
  starting transfers between devices: 17.3 us -> 14.8 us
  Pallas kernels: 11.9 us -> 13.6 us
  waiting for transfers between devices: 6.23 us -> 6.88 us
    ppermute x9, starting transfers between devices: 16.7 us -> 11.7 us  [swapped(): lax.ppermute(x, axis, [(i, i ^ distance) for i in range(lax.axis_size(axi...]
    ppermute x1, starting transfers between devices: 0.65 us -> 3.03 us  [body(): two = lax.ppermute(block, ('cell', 'energy'), route)]
    pallas_call x1 -> x4, Pallas kernels: 3.54 us -> 5.24 us  [body(): call(partial(convolve_kernel, reach, hop, last), outs, [VMEM] * len(given...]
    ppermute x1, waiting for transfers between devices: 0.01 us -> 0.55 us  [body(): two = lax.ppermute(block, ('cell', 'energy'), route)]
  transfers between devices with their start and end apart: 10 -> 10, of which waited for: 4 -> 5; matrix products, arithmetic and copies ran while one was open for 0% -> 0% of each run, Pallas kernels for 14% -> 23%
where the time goes in v6:
time: 36.9 us; the launch traced here: 36.7 us
  starting transfers between devices  14.8 us (40%)
  Pallas kernels  13.6 us (37%)
  waiting for transfers between devices  6.88 us (19%)
  between operations  1.46 us (4%)
    ppermute x9, starting transfers between devices, swapped(): lax.ppermute(x, axis, [(i, i ^ distance) for i in range(lax.axis_size(axi...  11.7 us
    ppermute x9, waiting for transfers between devices, swapped(): lax.ppermute(x, axis, [(i, i ^ distance) for i in range(lax.axis_size(axi...  6.33 us
    pallas_call x4, Pallas kernels, body(): call(partial(convolve_kernel, reach, hop, last), outs, [VMEM] * len(given...  5.24 us
    ppermute x1, starting transfers between devices, body(): two = lax.ppermute(block, ('cell', 'energy'), route)  3.03 us
    pallas_call x3, Pallas kernels, body(): call(partial(rows_kernel, overall, share, count + slot, slot), outs, [VME...  2.48 us
    pallas_call x2, Pallas kernels, body(): call(partial(join_kernel, level), outs, [VMEM] * len(given))(*given)  1.62 us
    pallas_call x1, Pallas kernels, body(): call(front_kernel, (sds((8, width), f32), sds((width, 2 * orbitals), bf16...  1.09 us
    pallas_call x1, Pallas kernels, body(): call(density_kernel, sds((1, energies, orbitals), f32), [VMEM] * 3)  0.99 us
  transfers between devices with their start and end apart: 10, of which 5 were waited for; matrix products, arithmetic and copies ran while one was open for 0% of the time, Pallas kernels for 23%

profile of v6, /device:TPU:0, one launch (start us, length us, event | category | flops | bytes accessed | tf_op | source)
XLA Modules:
  0.0 36.7 jit_solution(1349061692450200148)
XLA Ops:
  1.3 1.1 %shard_map.113 = (f32[8,128]{1,0:T(8,128)S(1)}, bf16[128,512]{1,0:T(8,128)(2,1)S(1)}, bf16[1,256,256]{2,1,0:T(8,128)(2,1)S(1)}, f32[1,256]{1,0:T(1,128)S(1)}, f3...) custom-call(s32[1]{0:T(128)S(6)} %copy.18.interface_ref, s32[1,4]{1,0:T(1,128)} %mask_hbm.1, bf16[1,256,256]{2,1,0:T(8,128)(2,1)} %modes_hbm.1, ...), custom_call_target="tpu_custom_call" | custom-call | flops 1000000 | bytes 1000000 | tf_op jit(solution)/shard_map/pallas_call | solution.py:519
  2.4 3.0 %collective-permute-start.1 = (f32[8,128]{1,0:T(8,128)S(1)}, f32[8,128]{1,0:T(8,128)S(1)}, u32[]{:S(2)}, u32[]{:S(2)}) collective-permute-start(f32[8,128]{1,0:T(8,128)S(1)} %get-tuple-element.33), channel_id=1, source_target_pairs={{0,1},{1,0},{2,3},{3,2},{4,8},{5,9},{6,10},{7,11},{8,4},{9,5},{10,... | collective-permute-start | bytes 12296 | tf_op jit(solution)/shard_map/ppermute | solution.py:540
  5.7 0.8 %shard_map.115 = (bf16[2,256,128]{2,1,0:T(8,128)(2,1)S(1)}, bf16[2,2,64,256]{3,2,1,0:T(8,128)(2,1)S(1)}, bf16[2,256,512]{2,1,0:T(8,128)(2,1)S(1)}) custom-call(bf16[1,256,256]{2,1,0:T(8,128)(2,1)S(1)} %get-tuple-element.28.modes_ref, f32[1,256]{1,0:T(1,128)S(1)} %get-tuple-element.29.levels_ref, bf16[128,512]{1,0:T(8,128)(2,1)S(1)} %get-tuple-element.31.link2_ref, ...), custom_call_target="tpu_custom_call" | custom-call | flops 1000000 | bytes 1000000 | tf_op jit(solution)/shard_map/pallas_call | solution.py:545
  6.5 0.6 %collective-permute-done.1.two_ref = f32[8,128]{1,0:T(8,128)S(1)} collective-permute-done((f32[8,128]{1,0:T(8,128)S(1)}, f32[8,128]{1,0:T(8,128)S(1)}, u32[]{:S(2)}, u32[]{:S(2)}) %collective-permute-start.1) | collective-permute-done | bytes 4128 | tf_op jit(solution)/shard_map/ppermute | solution.py:540
  7.7 1.1 %collective-permute-done.2.refs_1_ = bf16[1,272,128]{2,1,0:T(8,128)(2,1)S(1)} collective-permute-done((bf16[1,272,128]{2,1,0:T(8,128)(2,1)S(1)}, bf16[1,272,128]{2,1,0:T(8,128)(2,1)S(1)}, u32[]{:S(2)}, u32[]{:S(2)}) %collective-permute-start.2) | collective-permute-done | bytes 69664 | tf_op jit(solution)/shard_map/ppermute | solution.py:511
  8.9 0.7 %shard_map.117 = (bf16[2,3,64,128]{3,2,1,0:T(8,128)(2,1)S(1)}, bf16[1,272,128]{2,1,0:T(8,128)(2,1)S(1)}, bf16[2,3,64,128]{3,2,1,0:T(8,128)(2,1)S(1)}) custom-call(bf16[2,3,64,128]{3,2,1,0:T(8,128)(2,1)S(1)} %get-tuple-element.35.refs_0_, bf16[1,272,128]{2,1,0:T(8,128)(2,1)S(1)} %collective-permute-done.2.refs_1_), custom_call_target="tpu_custom_call" | custom-call | flops 1000000 | bytes 1000000 | tf_op jit(solution)/shard_map/pallas_call | solution.py:586
  9.6 1.6 %collective-permute-start.3 = (bf16[1,272,128]{2,1,0:T(8,128)(2,1)S(1)}, bf16[1,272,128]{2,1,0:T(8,128)(2,1)S(1)}, u32[]{:S(2)}, u32[]{:S(2)}) collective-permute-start(bf16[1,272,128]{2,1,0:T(8,128)(2,1)S(1)} %get-tuple-element.38), channel_id=1, source_target_pairs={{0,8},{4,12},{8,0},{12,4},{16,24},{20,28},{24,16},{28,20},{1,9},{5... | collective-permute-start | bytes 208904 | tf_op jit(solution)/shard_map/ppermute | solution.py:511
  11.2 2.8 %collective-permute-done.3.refs_1_ = bf16[1,272,128]{2,1,0:T(8,128)(2,1)S(1)} collective-permute-done((bf16[1,272,128]{2,1,0:T(8,128)(2,1)S(1)}, bf16[1,272,128]{2,1,0:T(8,128)(2,1)S(1)}, u32[]{:S(2)}, u32[]{:S(2)}) %collective-permute-start.3) | collective-permute-done | bytes 69664 | tf_op jit(solution)/shard_map/ppermute | solution.py:511
  13.9 0.9 %shard_map.118 = (bf16[2,3,64,128]{3,2,1,0:T(8,128)(2,1)S(1)}, bf16[1,144,128]{2,1,0:T(8,128)(2,1)S(1)}) custom-call(bf16[2,3,64,128]{3,2,1,0:T(8,128)(2,1)S(1)} %get-tuple-element.37.refs_0_, bf16[1,272,128]{2,1,0:T(8,128)(2,1)S(1)} %collective-permute-done.3.refs_1_, bf16[2,3,64,128]{3,2,1,0:T(8,128)(2,1)S(1)} %get-tuple-element.39.refs_2_), custom_call_target="tpu_custom_call" | custom-call | flops 1000000 | bytes 1000000 | tf_op jit(solution)/shard_map/pallas_call | solution.py:586
  14.9 2.6 %collective-permute-start.4 = (bf16[1,144,128]{2,1,0:T(8,128)(2,1)S(1)}, bf16[1,144,128]{2,1,0:T(8,128)(2,1)S(1)}, u32[]{:S(2)}, u32[]{:S(2)}) collective-permute-start(bf16[1,144,128]{2,1,0:T(8,128)(2,1)S(1)} %get-tuple-element.41), channel_id=1, source_target_pairs={{0,16},{4,20},{8,24},{12,28},{16,0},{20,4},{24,8},{28,12},{1,17},{... | collective-permute-start | bytes 110600 | tf_op jit(solution)/shard_map/ppermute | solution.py:511
  17.5 1.5 %collective-permute-start.6 = (f32[1,3,2,256]{3,2,1,0:T(2,128)S(1)}, f32[1,3,2,256]{3,2,1,0:T(2,128)S(1)}, u32[]{:S(2)}, u32[]{:S(2)}) collective-permute-start(f32[1,3,2,256]{3,2,1,0:T(2,128)S(1)} %get-tuple-element.30.params_ref.rest_0_), channel_id=1, source_target_pairs={{0,1},{1,0},{2,3},{3,2},{4,5},{5,4},{6,7},{7,6},{8,9},{9,8},{10,11... | collective-permute-start | bytes 18440 | tf_op jit(solution)/shard_map/ppermute | solution.py:511
  19.0 0.8 %collective-permute-done.4.state_ref = bf16[1,144,128]{2,1,0:T(8,128)(2,1)S(1)} collective-permute-done((bf16[1,144,128]{2,1,0:T(8,128)(2,1)S(1)}, bf16[1,144,128]{2,1,0:T(8,128)(2,1)S(1)}, u32[]{:S(2)}, u32[]{:S(2)}) %collective-permute-start.4) | collective-permute-done | bytes 36896 | tf_op jit(solution)/shard_map/ppermute | solution.py:511
  19.8 0.7 %shard_map.119 = (bf16[2,64,128]{2,1,0:T(8,128)(2,1)S(1)}, bf16[1,64,128]{2,1,0:T(8,128)(2,1)S(1)}) custom-call(bf16[2,3,64,128]{3,2,1,0:T(8,128)(2,1)S(1)} %get-tuple-element.40.enter_ref, bf16[1,144,128]{2,1,0:T(8,128)(2,1)S(1)} %collective-permute-done.4.state_ref), custom_call_target="tpu_custom_call" | custom-call | flops 1000000 | bytes 1000000 | tf_op jit(solution)/shard_map/pallas_call | solution.py:589
  20.5 3.0 %collective-permute-start.9 = (bf16[1,64,128]{2,1,0:T(8,128)(2,1)S(1)}, bf16[1,64,128]{2,1,0:T(8,128)(2,1)S(1)}, u32[]{:S(2)}, u32[]{:S(2)}) collective-permute-start(bf16[1,64,128]{2,1,0:T(8,128)(2,1)S(1)} %get-tuple-element.44.lesser_ref), channel_id=1, source_target_pairs={{0,3},{1,2},{2,1},{3,0},{4,7},{5,6},{6,5},{7,4},{8,11},{9,10},{10,... | collective-permute-start | bytes 49160 | tf_op jit(solution)/shard_map/ppermute | solution.py:511
  24.2 0.8 %shard_map.121 = (bf16[2,256,128]{2,1,0:T(8,128)(2,1)S(1)}, bf16[2,2,64,256]{3,2,1,0:T(8,128)(2,1)S(1)}, f32[2,3,2,256]{3,2,1,0:T(2,128)S(1)}) custom-call(bf16[1,256,256]{2,1,0:T(8,128)(2,1)S(1)} %get-tuple-element.28.modes_ref, f32[1,256]{1,0:T(1,128)S(1)} %get-tuple-element.29.levels_ref, bf16[128,512]{1,0:T(8,128)(2,1)S(1)} %get-tuple-element.31.link2_ref, ...), custom_call_target="tpu_custom_call" | custom-call | flops 1000000 | bytes 1000000 | tf_op jit(solution)/shard_map/pallas_call | solution.py:570
  25.0 2.0 %collective-permute-start.8 = (f32[2,3,2,256]{3,2,1,0:T(2,128)S(1)}, f32[2,3,2,256]{3,2,1,0:T(2,128)S(1)}, u32[]{:S(2)}, u32[]{:S(2)}) collective-permute-start(f32[2,3,2,256]{3,2,1,0:T(2,128)S(1)} %get-tuple-element.47), channel_id=1, source_target_pairs={{0,2},{1,3},{2,0},{3,1},{4,6},{5,7},{6,4},{7,5},{8,10},{9,11},{10,... | collective-permute-start | bytes 36872 | tf_op jit(solution)/shard_map/ppermute | solution.py:511
  27.2 1.6 %collective-permute-done.8.got_ref = f32[2,3,2,256]{3,2,1,0:T(2,128)S(1)} collective-permute-done((f32[2,3,2,256]{3,2,1,0:T(2,128)S(1)}, f32[2,3,2,256]{3,2,1,0:T(2,128)S(1)}, u32[]{:S(2)}, u32[]{:S(2)}) %collective-permute-start.8) | collective-permute-done | bytes 12320 | tf_op jit(solution)/shard_map/ppermute | solution.py:511
  28.8 0.8 %shard_map.123 = (bf16[2,256,128]{2,1,0:T(8,128)(2,1)S(1)}, bf16[2,2,64,256]{3,2,1,0:T(8,128)(2,1)S(1)}) custom-call(bf16[1,256,256]{2,1,0:T(8,128)(2,1)S(1)} %get-tuple-element.28.modes_ref, f32[1,256]{1,0:T(1,128)S(1)} %get-tuple-element.29.levels_ref, bf16[128,512]{1,0:T(8,128)(2,1)S(1)} %get-tuple-element.31.link2_ref, ...), custom_call_target="tpu_custom_call" | custom-call | flops 1000000 | bytes 1000000 | tf_op jit(solution)/shard_map/pallas_call | solution.py:570
  29.6 0.8 %shard_map.122 = (bf16[2,256,128]{2,1,0:T(8,128)(2,1)S(1)}, bf16[2,2,64,256]{3,2,1,0:T(8,128)(2,1)S(1)}) custom-call(bf16[1,256,256]{2,1,0:T(8,128)(2,1)S(1)} %get-tuple-element.28.modes_ref, f32[1,256]{1,0:T(1,128)S(1)} %get-tuple-element.29.levels_ref, bf16[128,512]{1,0:T(8,128)(2,1)S(1)} %get-tuple-element.31.link2_ref, ...), custom_call_target="tpu_custom_call" | custom-call | flops 1000000 | bytes 1000000 | tf_op jit(solution)/shard_map/pallas_call | solution.py:570
  30.4 1.0 %shard_map.120 = f32[1,2,256]{2,1,0:T(2,128)} custom-call(f32[1,2,256]{2,1,0:T(2,128)S(1)} %shard_map.114.diagonal_ref, bf16[2,256,128]{2,1,0:T(8,128)(2,1)S(1)} %get-tuple-element.32.left_ref, bf16[2,64,128]{2,1,0:T(8,128)(2,1)S(1)} %get-tuple-element.42.retarded_ref), custom_call_target="tpu_custom_call" | custom-call | flops 1000000 | bytes 1000000 | tf_op jit(solution)/shard_map/pallas_call | solution.py:598
  31.4 1.2 %shard_map.124.refs_0_ = f32[3,12,64,256]{3,2,1,0:T(8,128)S(1)} custom-call(s32[8]{0:T(128)S(1)} %get-tuple-element.43.offsets_ref, bf16[1,2,8,64,256]{4,3,2,1,0:T(8,128)(2,1)S(1)} %copy-done, bf16[1,64,128]{2,1,0:T(8,128)(2,1)S(1)} %get-tuple-element.44.lesser_ref, bf16[2,256,128]{2,1,0:T(8,128)(2,1)S(1)} %get-tuple-element.32.left_ref, ...), custom_call_target="tpu_custom_call" | custom-call | flops 1000000 | bytes 1000000 | tf_op jit(solution)/shard_map/pallas_call | solution.py:617
  32.6 1.1 %shard_map.125.refs_0_ = f32[3,12,64,256]{3,2,1,0:T(8,128)S(1)} custom-call(s32[8]{0:T(128)S(1)} %get-tuple-element.43.offsets_ref, bf16[1,2,8,64,256]{4,3,2,1,0:T(8,128)(2,1)S(1)} %copy-done, bf16[1,64,128]{2,1,0:T(8,128)(2,1)S(1)} %collective-permute-done.9.lesser_ref, ...), custom_call_target="tpu_custom_call", output_to_operand_aliasing={{}: (5, {})} | custom-call | flops 1000000 | bytes 1000000 | tf_op jit(solution)/shard_map/pallas_call | solution.py:617
  33.7 1.1 %shard_map.126.refs_0_ = f32[3,12,64,256]{3,2,1,0:T(8,128)S(1)} custom-call(s32[8]{0:T(128)S(1)} %get-tuple-element.43.offsets_ref, bf16[1,2,8,64,256]{4,3,2,1,0:T(8,128)(2,1)S(1)} %copy-done, bf16[1,64,128]{2,1,0:T(8,128)(2,1)S(1)} %collective-permute-done.7.lesser_ref, ...), custom_call_target="tpu_custom_call", output_to_operand_aliasing={{}: (5, {})} | custom-call | flops 1000000 | bytes 1000000 | tf_op jit(solution)/shard_map/pallas_call | solution.py:617
  34.8 1.9 %shard_map.127 = (f32[3,12,64,256]{3,2,1,0:T(8,128)S(1)}, bf16[1,2,8,64,256]{4,3,2,1,0:T(8,128)(2,1)}) custom-call(s32[8]{0:T(128)S(1)} %get-tuple-element.43.offsets_ref, bf16[1,2,8,64,256]{4,3,2,1,0:T(8,128)(2,1)S(1)} %copy-done, bf16[1,64,128]{2,1,0:T(8,128)(2,1)S(1)} %collective-permute-done.5.lesser_ref, ...), custom_call_target="tpu_custom_call", output_to_operand_aliasing={{0}: (5, {})} | custom-call | flops 1000000 | bytes 1000000 | tf_op jit(solution)/shard_map/pallas_call | solution.py:617
  (13 shorter events, 1.7 us)
Async XLA Ops:
  0.6 30.8 %copy-start = (bf16[1,2,8,64,256]{4,3,2,1,0:T(8,128)(2,1)S(1)}, bf16[1,2,8,64,256]{4,3,2,1,0:T(8,128)(2,1)}, u32[]{:S(2)}) copy-start(bf16[1,2,8,64,256]{4,3,2,1,0:T(8,128)(2,1)} %screen_ref.7) | copy-start | bytes 1572868
  2.4 4.6 %collective-permute-start.1 = (f32[8,128]{1,0:T(8,128)S(1)}, f32[8,128]{1,0:T(8,128)S(1)}, u32[]{:S(2)}, u32[]{:S(2)}) collective-permute-start(f32[8,128]{1,0:T(8,128)S(1)} %get-tuple-element.33), channel_id=1, source_target_pairs={{0,1},{1,0},{2,3},{3,2},{4,8},{5,9},{6,10},{7,11},{8,4},{9,5},{10,... | collective-permute-start | bytes 12296 | tf_op jit(solution)/shard_map/ppermute | solution.py:540
  5.5 1.6 %collective-permute-start = (f32[8,128]{1,0:T(8,128)S(1)}, f32[8,128]{1,0:T(8,128)S(1)}, u32[]{:S(2)}, u32[]{:S(2)}) collective-permute-start(f32[8,128]{1,0:T(8,128)S(1)} %get-tuple-element.33), channel_id=1, source_target_pairs={{0,4},{4,0},{8,12},{12,8},{16,20},{20,16},{24,28},{28,24},{1,5},{5... | collective-permute-start | bytes 12296 | tf_op jit(solution)/shard_map/ppermute | solution.py:511
  7.5 1.3 %collective-permute-start.2 = (bf16[1,272,128]{2,1,0:T(8,128)(2,1)S(1)}, bf16[1,272,128]{2,1,0:T(8,128)(2,1)S(1)}, u32[]{:S(2)}, u32[]{:S(2)}) collective-permute-start(bf16[1,272,128]{2,1,0:T(8,128)(2,1)S(1)} %get-tuple-element.36), channel_id=1, source_target_pairs={{0,4},{4,0},{8,12},{12,8},{16,20},{20,16},{24,28},{28,24},{1,5},{5... | collective-permute-start | bytes 208904 | tf_op jit(solution)/shard_map/ppermute | solution.py:511
  9.6 4.4 %collective-permute-start.3 = (bf16[1,272,128]{2,1,0:T(8,128)(2,1)S(1)}, bf16[1,272,128]{2,1,0:T(8,128)(2,1)S(1)}, u32[]{:S(2)}, u32[]{:S(2)}) collective-permute-start(bf16[1,272,128]{2,1,0:T(8,128)(2,1)S(1)} %get-tuple-element.38), channel_id=1, source_target_pairs={{0,8},{4,12},{8,0},{12,4},{16,24},{20,28},{24,16},{28,20},{1,9},{5... | collective-permute-start | bytes 208904 | tf_op jit(solution)/shard_map/ppermute | solution.py:511
  14.9 4.9 %collective-permute-start.4 = (bf16[1,144,128]{2,1,0:T(8,128)(2,1)S(1)}, bf16[1,144,128]{2,1,0:T(8,128)(2,1)S(1)}, u32[]{:S(2)}, u32[]{:S(2)}) collective-permute-start(bf16[1,144,128]{2,1,0:T(8,128)(2,1)S(1)} %get-tuple-element.41), channel_id=1, source_target_pairs={{0,16},{4,20},{8,24},{12,28},{16,0},{20,4},{24,8},{28,12},{1,17},{... | collective-permute-start | bytes 110600 | tf_op jit(solution)/shard_map/ppermute | solution.py:511
  17.5 6.7 %collective-permute-start.6 = (f32[1,3,2,256]{3,2,1,0:T(2,128)S(1)}, f32[1,3,2,256]{3,2,1,0:T(2,128)S(1)}, u32[]{:S(2)}, u32[]{:S(2)}) collective-permute-start(f32[1,3,2,256]{3,2,1,0:T(2,128)S(1)} %get-tuple-element.30.params_ref.rest_0_), channel_id=1, source_target_pairs={{0,1},{1,0},{2,3},{3,2},{4,5},{5,4},{6,7},{7,6},{8,9},{9,8},{10,11... | collective-permute-start | bytes 18440 | tf_op jit(solution)/shard_map/ppermute | solution.py:511
  20.5 12.1 %collective-permute-start.9 = (bf16[1,64,128]{2,1,0:T(8,128)(2,1)S(1)}, bf16[1,64,128]{2,1,0:T(8,128)(2,1)S(1)}, u32[]{:S(2)}, u32[]{:S(2)}) collective-permute-start(bf16[1,64,128]{2,1,0:T(8,128)(2,1)S(1)} %get-tuple-element.44.lesser_ref), channel_id=1, source_target_pairs={{0,3},{1,2},{2,1},{3,0},{4,7},{5,6},{6,5},{7,4},{8,11},{9,10},{10,... | collective-permute-start | bytes 49160 | tf_op jit(solution)/shard_map/ppermute | solution.py:511
  23.5 10.2 %collective-permute-start.7 = (bf16[1,64,128]{2,1,0:T(8,128)(2,1)S(1)}, bf16[1,64,128]{2,1,0:T(8,128)(2,1)S(1)}, u32[]{:S(2)}, u32[]{:S(2)}) collective-permute-start(bf16[1,64,128]{2,1,0:T(8,128)(2,1)S(1)} %get-tuple-element.44.lesser_ref), channel_id=1, source_target_pairs={{0,2},{1,3},{2,0},{3,1},{4,6},{5,7},{6,4},{7,5},{8,10},{9,11},{10,... | collective-permute-start | bytes 49160 | tf_op jit(solution)/shard_map/ppermute | solution.py:511
  24.0 10.8 %collective-permute-start.5 = (bf16[1,64,128]{2,1,0:T(8,128)(2,1)S(1)}, bf16[1,64,128]{2,1,0:T(8,128)(2,1)S(1)}, u32[]{:S(2)}, u32[]{:S(2)}) collective-permute-start(bf16[1,64,128]{2,1,0:T(8,128)(2,1)S(1)} %get-tuple-element.44.lesser_ref), channel_id=1, source_target_pairs={{0,1},{1,0},{2,3},{3,2},{4,5},{5,4},{6,7},{7,6},{8,9},{9,8},{10,11... | collective-permute-start | bytes 49160 | tf_op jit(solution)/shard_map/ppermute | solution.py:511
  25.0 3.8 %collective-permute-start.8 = (f32[2,3,2,256]{3,2,1,0:T(2,128)S(1)}, f32[2,3,2,256]{3,2,1,0:T(2,128)S(1)}, u32[]{:S(2)}, u32[]{:S(2)}) collective-permute-start(f32[2,3,2,256]{3,2,1,0:T(2,128)S(1)} %get-tuple-element.47), channel_id=1, source_target_pairs={{0,2},{1,3},{2,0},{3,1},{4,6},{5,7},{6,4},{7,5},{8,10},{9,11},{10,... | collective-permute-start | bytes 36872 | tf_op jit(solution)/shard_map/ppermute | solution.py:511

commit v7 on v6

--- a/solution.py
+++ b/solution.py
@@ -149,8 +149,11 @@
         local_ref[e, 1] = local[share:].astype(bf16)
 
 
+def tile_kernel(interface_ref, block_ref):
+    block_ref[...] = jnp.full(block_ref.shape, interface_ref[0].astype(f32))
+
+
 def front_kernel(
-    interface_ref,
     mask_hbm,
     modes_hbm,
     levels_hbm,
@@ -159,7 +162,6 @@
     broad_hbm,
     inject_hbm,
     offsets_hbm,
-    block_ref,
     link2_ref,
     modes_ref,
     levels_ref,
@@ -188,7 +190,6 @@
         copy.start()
     for copy in copies:
         copy.wait()
-    block_ref[...] = jnp.full(block_ref.shape, interface_ref[0].astype(f32))
     masked_link(link2_ref, coupling_ref, mask_ref)
 
 
@@ -338,31 +339,41 @@
     return tuple(ref[e, part] for part in range(ref.shape[1]))
 
 
-def join_kernel(level, *refs):
-    total_ref, other_ref = refs[:2]
-    enter_ref = refs[2] if level else None
-    outs = refs[3 if level else 2 :]
-    new_enter_ref, message_ref = outs[:2]
-    energies, _, extent, width = total_ref.shape
-    place = lax.axis_index("cell")
-    upper = jnp.bitwise_and(jnp.right_shift(place, level), 1) == 1
+def upper_half(level):
+    return jnp.bitwise_and(jnp.right_shift(lax.axis_index("cell"), level), 1) == 1
+
+
+def join_kernel(level, total_ref, other_ref, message_ref, *new_total_ref):
+    upper = upper_half(level)
     others = read_message(other_ref)
     joined = []
-    for e in range(energies):
+    for e in range(total_ref.shape[0]):
         total, other = read(total_ref, e), others[e]
-        joined.append(compose(pick(upper, other, total), pick(upper, total, other)))
+        pair = pick(upper, other, total), pick(upper, total, other)
+        joined.append(compose(*pair) if new_total_ref else moved(pair[1], pair[0][1:]))
+        for ref in new_total_ref:
+            for part in range(3):
+                ref[e, part] = joined[e][part].astype(bf16)
+    write_message(message_ref, joined)
+
+
+def enter_kernel(level, other_ref, *refs):
+    upper = upper_half(level)
+    others = read_message(other_ref)
+    out_ref = refs[-1]
+    for e in range(out_ref.shape[0]):
         if level:
-            enter = read(enter_ref, e)
-            longer = compose(other, enter)
-            longer = tuple(x.astype(bf16) for x in longer)
-            enter = pick(upper, longer, enter)
+            old = read(refs[0], e)
+            new = pick(upper, tuple(x.astype(bf16) for x in compose(others[e], old)), old)
         else:
-            enter = pick(upper, other, neutral(extent, width))
+            new = pick(upper, others[e], neutral(*out_ref.shape[2:]))
         for part in range(3):
-            new_enter_ref[e, part] = enter[part]
-            if len(outs) > 2:
-                outs[2][e, part] = joined[e][part].astype(bf16)
-    write_message(message_ref, joined)
+            out_ref[e, part] = new[part]
+
+
+def moved(step, state):
+    retarded, lesser = pushed(step, state)
+    return step[1].astype(f32) + retarded, step[2].astype(f32) + lesser
 
 
 def arrive_kernel(level, enter_ref, state_ref, retarded_ref, lesser_ref):
@@ -383,16 +394,20 @@
     return dot_last(jnp.ones((8, x.shape[1]), bf16), x.astype(bf16))[0:1]
 
 
-def diagonal_kernel(overall, modes_ref, levels_ref, params_ref, out_ref):
+def diagonal_kernel(overall, modes_ref, levels_ref, params_ref, out_ref, sums_ref):
     energies = params_ref.shape[2]
     first = lax.axis_index("energy") * energies
     modes = modes_ref[0].astype(f32)
     for e in range(energies):
         _, di = resolvents(overall, first, e, levels_ref, params_ref.at[0])
         out_ref[0, e : e + 1, :] = row_sums(modes * (modes * di).astype(bf16).astype(f32))
-
-
-def density_kernel(diagonal_ref, left_ref, retarded_ref, out_ref):
+    blank = jnp.zeros(sums_ref.shape[2:], f32)
+    for part in range(sums_ref.shape[0]):
+        for e in range(sums_ref.shape[1]):
+            sums_ref[part, e] = blank
+
+
+def density_of(diagonal_ref, left_ref, retarded_ref, out_ref):
     for e in range(left_ref.shape[0]):
         left = left_ref[e]
         pz = dot_mat(left, full(retarded_ref[e])).astype(bf16).astype(f32)
@@ -400,26 +415,23 @@
         out_ref[0, e : e + 1, :] = -total / math.pi
 
 
-def convolve_kernel(reach, hop, last, offsets_ref, screen_ref, lesser_ref, left_ref, local_ref, *refs):
-    if hop:
-        refs = refs[1:]
+def convolve_kernel(reach, hop, last, offsets_ref, screen_ref, lesser_ref, left_ref, local_ref, _, *refs):
+    if hop == 0:
+        diagonal_ref, retarded_ref, *refs = refs
     sums_ref, *refs = refs
+    if hop == 0:
+        density_of(diagonal_ref, left_ref, retarded_ref, refs.pop(0))
     if last:
         out_hbm, *refs = refs
     g_ref, picked_ref, sem, *refs = refs
     copy = pltpu.make_async_copy(offsets_ref, picked_ref, sem)
     copy.start()
     energies = left_ref.shape[0]
-    points, share, width = screen_ref.shape[2:]
+    points, share, _ = screen_ref.shape[2:]
     overall = sums_ref.shape[1] - 2 * reach
     group = lax.axis_index("energy")
     mine = pl.multiple_of(group * share, share)
     base = jnp.bitwise_xor(group, hop) * energies + reach
-    if hop == 0:
-        blank = jnp.zeros((share, width), f32)
-        for part in range(3):
-            for e in range(sums_ref.shape[1]):
-                sums_ref[part, e] = blank
     for pair in range(energies // 2):
         states = unpack_lesser(lesser_ref[pair])
         for e in (2 * pair, 2 * pair + 1):
@@ -516,29 +528,29 @@
     message = sds((pairs, 4 * extent + spare, width), bf16)
     state_message = sds((pairs, 2 * extent + spare, width), bf16)
     coupling = jnp.swapaxes(coupling, 1, 2)
-    block, link2, modes, levels, params, offsets = call(
+    block = call(tile_kernel, sds((8, width), f32), [SMEM])(interface)
+    one = swapped(block, "cell", 1)
+    mate = [i + 1 if i % 2 else i - 1 for i in range(cells)]
+    mate[0], mate[-1] = 0, cells - 1
+    route = [(i * groups + g, mate[i] * groups + (g ^ int(mate[i] == i))) for i in range(cells) for g in range(groups)]
+    two = lax.ppermute(block, ("cell", "energy"), route)
+
+    link2, modes, levels, params, offsets = call(
         front_kernel,
         (
-            sds((8, width), f32),
             sds((width, 2 * orbitals), bf16),
             sds(modes.shape, bf16),
             sds(levels.shape, f32),
             sds((1, 3, energies, orbitals), f32),
             sds(offsets.shape, jnp.int32),
         ),
-        [SMEM] + [HBM] * 8,
+        [HBM] * 8,
         [
             pltpu.SMEM(row_mask.shape, jnp.int32),
             pltpu.VMEM(coupling.shape, bf16),
             pltpu.SemaphoreType.DMA((8,)),
         ],
-    )(interface, *map(in_hbm, (row_mask, modes, levels, coupling, level_shift, broadening, injection, offsets)))
-    one = swapped(block, "cell", 1)
-    mate = [i + 1 if i % 2 else i - 1 for i in range(cells)]
-    mate[0], mate[-1] = 0, cells - 1
-    route = [(i * groups + g, mate[i] * groups + (g ^ int(mate[i] == i))) for i in range(cells) for g in range(groups)]
-    two = lax.ppermute(block, ("cell", "energy"), route)
-
+    )(*map(in_hbm, (row_mask, modes, levels, coupling, level_shift, broadening, injection, offsets)))
     left_shape = sds((energies, orbitals, width), bf16)
     local_shape = sds((energies, 2, share, orbitals), bf16)
     params_shape = (3, energies, orbitals)
@@ -554,8 +566,12 @@
         (maps_shape, message),
         [VMEM] * 7,
     )(one, two, modes, levels, params, left, free)
-    diagonal = call(
-        partial(diagonal_kernel, overall), sds((1, energies, orbitals), f32), [VMEM] * 3
+    reach = overall // 4
+    sums_shape = sds((3, overall + 2 * reach, share, orbitals), f32)
+    sigma_shape = sds((1, 2, overall, share, orbitals), bf16)
+    density_shape = sds((1, energies, orbitals), f32)
+    diagonal, sums = call(
+        partial(diagonal_kernel, overall), (density_shape, sums_shape), [VMEM] * 3
     )(modes, levels, params)
 
     known = params
@@ -581,10 +597,11 @@
     enter = None
     for level in range(rounds - 1):
         other = swapped(sent, "cell", 1 << level)
-        outs = (maps_shape, message, maps_shape) if level < rounds - 2 else (maps_shape, state_message)
-        given = [total, other] + ([enter] if level else [])
-        enter, sent, *rest = call(partial(join_kernel, level), outs, [VMEM] * len(given))(*given)
+        outs = (message, maps_shape) if level < rounds - 2 else (state_message,)
+        sent, *rest = call(partial(join_kernel, level), outs, [VMEM] * 2)(total, other)
         total = rest[0] if rest else None
+        given = (other, enter) if level else (other,)
+        enter = call(partial(enter_kernel, level), maps_shape, [VMEM] * len(given))(*given)
     state = swapped(sent, "cell", cells // 2)
     retarded, lesser = call(
         partial(arrive_kernel, rounds - 1),
@@ -595,34 +612,32 @@
     lessers = [lesser]
     for hop in range(1, groups):
         lessers.append(swapped(lesser, "energy", hop))
-    density = call(density_kernel, sds((1, energies, orbitals), f32), [VMEM] * 3)(
-        diagonal, lefts[0], retarded
-    )
-
-    reach = overall // 4
-    sums_shape = sds((3, overall + 2 * reach, share, orbitals), f32)
-    sigma_shape = sds((1, 2, overall, share, orbitals), bf16)
     scratch = [
         pltpu.VMEM((3, energies, share, orbitals), f32),
         pltpu.SMEM(offsets.shape, jnp.int32),
         pltpu.SemaphoreType.DMA,
     ]
-    for hop in (0, *reversed(range(1, groups))):
-        last = hop == min(1, groups - 1)
-        given = (offsets, screened, lessers[hop], lefts[hop], locals_[hop]) + ((sums,) if hop else ())
-        outs, specs, extra = sums_shape, VMEM, []
+    for hop in range(groups):
+        last = hop == groups - 1
+        given = (offsets, screened, lessers[hop], lefts[hop], locals_[hop], sums)
+        outs, specs, extra = (sums_shape,), (VMEM,), []
+        if hop == 0:
+            given += (diagonal, retarded)
+            outs, specs = outs + (density_shape,), specs + (VMEM,)
         if last:
-            outs, specs = (sums_shape, sigma_shape), (VMEM, HBM)
+            outs, specs = outs + (sigma_shape,), specs + (HBM,)
             extra = [pltpu.VMEM(sigma_shape.shape, bf16), pltpu.SemaphoreType.DMA((share // 16,))]
-        sums = call(
+        sums, *rest = call(
             partial(convolve_kernel, reach, hop, last),
             outs,
             [VMEM] * len(given),
             scratch + extra,
             out_specs=specs,
-            aliases={5: 0} if hop else {},
+            aliases={5: 0},
         )(*given)
-    sigma = sums[1]
+        if hop == 0:
+            density = rest[0]
+    sigma = rest[-1]
     return (density, sigma)
 
 

time: 36.9 us -> 35.2 us (0.954)
  waiting for transfers between devices: 6.88 us -> 5.75 us
  starting transfers between devices: 14.8 us -> 14.3 us
    ppermute x9, waiting for transfers between devices: 6.33 us -> 5.75 us  [swapped(): lax.ppermute(x, axis, [(i, i ^ distance) for i in range(lax.axis_size(axi...]
    ppermute x1, waiting for transfers between devices: 0.55 us -> 0.01 us  [body(): two = lax.ppermute(block, ('cell', 'energy'), route)]
    ppermute x1, starting transfers between devices: 3.03 us -> 2.55 us  [body(): two = lax.ppermute(block, ('cell', 'energy'), route)]
    pallas_call x5 -> x7, Pallas kernels: 3.9 us -> 3.51 us  [the longest x2 1.39 us: body(): call(partial(join_kernel, level), outs, [VMEM] * 2)(total, other)]
  transfers between devices with their start and end apart: 10 -> 10, of which waited for: 5 -> 3; matrix products, arithmetic and copies ran while one was open for 0% -> 0% of each run, Pallas kernels for 23% -> 28%
where the time goes in v7:
time: 35.2 us; the launch traced here: 35.1 us
  starting transfers between devices  14.3 us (41%)
  Pallas kernels  13.5 us (38%)
  waiting for transfers between devices  5.75 us (16%)
  between operations  1.51 us (4%)
    ppermute x9, starting transfers between devices, swapped(): lax.ppermute(x, axis, [(i, i ^ distance) for i in range(lax.axis_size(axi...  11.7 us
    ppermute x9, waiting for transfers between devices, swapped(): lax.ppermute(x, axis, [(i, i ^ distance) for i in range(lax.axis_size(axi...  5.75 us
    pallas_call x4, Pallas kernels, body(): call(partial(convolve_kernel, reach, hop, last), outs, [VMEM] * len(given...  5.55 us
    ppermute x1, starting transfers between devices, body(): two = lax.ppermute(block, ('cell', 'energy'), route)  2.55 us
    pallas_call x3, Pallas kernels, body(): call(partial(rows_kernel, overall, share, count + slot, slot), outs, [VME...  2.48 us
    pallas_call x2, Pallas kernels, body(): call(partial(join_kernel, level), outs, [VMEM] * 2)(total, other)  1.39 us
    pallas_call x1, Pallas kernels, body(): call(front_kernel, (sds((width, 2 * orbitals), bf16), sds(modes.shape, bf...  1.09 us
    pallas_call x1, Pallas kernels, body(): call(partial(own_rows_kernel, overall, share), (left_shape, local_shape,...  0.83 us
  transfers between devices with their start and end apart: 10, of which 3 were waited for; matrix products, arithmetic and copies ran while one was open for 0% of the time, Pallas kernels for 28%

profile of v7, /device:TPU:0, one launch (start us, length us, event | category | flops | bytes accessed | tf_op | source)
XLA Modules:
  0.0 35.1 jit_solution(7492533686902869048)
XLA Ops:
  1.4 0.6 %collective-permute-start = (f32[8,128]{1,0:T(8,128)S(1)}, f32[8,128]{1,0:T(8,128)S(1)}, u32[]{:S(2)}, u32[]{:S(2)}) collective-permute-start(f32[8,128]{1,0:T(8,128)S(1)} %shard_map.114), channel_id=1, source_target_pairs={{0,4},{4,0},{8,12},{12,8},{16,20},{20,16},{24,28},{28,24},{1,5},{5... | collective-permute-start | bytes 12296 | tf_op jit(solution)/shard_map/ppermute | solution.py:523
  1.9 2.6 %collective-permute-start.1 = (f32[8,128]{1,0:T(8,128)S(1)}, f32[8,128]{1,0:T(8,128)S(1)}, u32[]{:S(2)}, u32[]{:S(2)}) collective-permute-start(f32[8,128]{1,0:T(8,128)S(1)} %shard_map.114), channel_id=1, source_target_pairs={{0,1},{1,0},{2,3},{3,2},{4,8},{5,9},{6,10},{7,11},{8,4},{9,5},{10,... | collective-permute-start | bytes 12296 | tf_op jit(solution)/shard_map/ppermute | solution.py:536
  4.5 1.1 %shard_map.113 = (bf16[128,512]{1,0:T(8,128)(2,1)S(1)}, bf16[1,256,256]{2,1,0:T(8,128)(2,1)S(1)}, f32[1,256]{1,0:T(1,128)S(1)}, f32[1,3,2,256]{3,2,1,0:T(2,128)S(1)}, s32[8]{0:T(128)S(1)}) custom-call(s32[1,4]{1,0:T(1,128)} %mask_hbm.1, bf16[1,256,256]{2,1,0:T(8,128)(2,1)} %modes_hbm.1, f32[1,256]{1,0:T(1,128)} %levels_hbm.1, bf16[1,64,256]{2,1,0:T(8,128)(2,1)} %bitcast.1, ...), custom_call_target="tpu_custom_call" | custom-call | flops 1000000 | bytes 1000000 | tf_op jit(solution)/shard_map/pallas_call | solution.py:538
  5.6 0.8 %shard_map.115 = (bf16[2,256,128]{2,1,0:T(8,128)(2,1)S(1)}, bf16[2,2,64,256]{3,2,1,0:T(8,128)(2,1)S(1)}, bf16[2,256,512]{2,1,0:T(8,128)(2,1)S(1)}) custom-call(bf16[1,256,256]{2,1,0:T(8,128)(2,1)S(1)} %get-tuple-element.29.modes_ref, f32[1,256]{1,0:T(1,128)S(1)} %get-tuple-element.30.levels_ref, bf16[128,512]{1,0:T(8,128)(2,1)S(1)} %get-tuple-element.32.link2_ref, ...), custom_call_target="tpu_custom_call" | custom-call | flops 1000000 | bytes 1000000 | tf_op jit(solution)/shard_map/pallas_call | solution.py:557
  7.2 1.1 %collective-permute-done.2.other_ref = bf16[1,272,128]{2,1,0:T(8,128)(2,1)S(1)} collective-permute-done((bf16[1,272,128]{2,1,0:T(8,128)(2,1)S(1)}, bf16[1,272,128]{2,1,0:T(8,128)(2,1)S(1)}, u32[]{:S(2)}, u32[]{:S(2)}) %collective-permute-start.2) | collective-permute-done | bytes 69664 | tf_op jit(solution)/shard_map/ppermute | solution.py:523
  8.2 0.7 %shard_map.117 = (bf16[1,272,128]{2,1,0:T(8,128)(2,1)S(1)}, bf16[2,3,64,128]{3,2,1,0:T(8,128)(2,1)S(1)}) custom-call(bf16[2,3,64,128]{3,2,1,0:T(8,128)(2,1)S(1)} %get-tuple-element.35.total_ref, bf16[1,272,128]{2,1,0:T(8,128)(2,1)S(1)} %collective-permute-done.2.other_ref), custom_call_target="tpu_custom_call" | custom-call | flops 1000000 | bytes 1000000 | tf_op jit(solution)/shard_map/pallas_call | solution.py:601
  8.9 1.5 %collective-permute-start.3 = (bf16[1,272,128]{2,1,0:T(8,128)(2,1)S(1)}, bf16[1,272,128]{2,1,0:T(8,128)(2,1)S(1)}, u32[]{:S(2)}, u32[]{:S(2)}) collective-permute-start(bf16[1,272,128]{2,1,0:T(8,128)(2,1)S(1)} %get-tuple-element.37), channel_id=1, source_target_pairs={{0,8},{4,12},{8,0},{12,4},{16,24},{20,28},{24,16},{28,20},{1,9},{5... | collective-permute-start | bytes 208904 | tf_op jit(solution)/shard_map/ppermute | solution.py:523
  10.4 2.9 %collective-permute-done.3.other_ref = bf16[1,272,128]{2,1,0:T(8,128)(2,1)S(1)} collective-permute-done((bf16[1,272,128]{2,1,0:T(8,128)(2,1)S(1)}, bf16[1,272,128]{2,1,0:T(8,128)(2,1)S(1)}, u32[]{:S(2)}, u32[]{:S(2)}) %collective-permute-start.3) | collective-permute-done | bytes 69664 | tf_op jit(solution)/shard_map/ppermute | solution.py:523
  13.3 0.7 %shard_map.120 = bf16[1,144,128]{2,1,0:T(8,128)(2,1)S(1)} custom-call(bf16[2,3,64,128]{3,2,1,0:T(8,128)(2,1)S(1)} %get-tuple-element.38.total_ref, bf16[1,272,128]{2,1,0:T(8,128)(2,1)S(1)} %collective-permute-done.3.other_ref), custom_call_target="tpu_custom_call" | custom-call | flops 1000000 | bytes 1000000 | tf_op jit(solution)/shard_map/pallas_call | solution.py:601
  14.0 2.6 %collective-permute-start.4 = (bf16[1,144,128]{2,1,0:T(8,128)(2,1)S(1)}, bf16[1,144,128]{2,1,0:T(8,128)(2,1)S(1)}, u32[]{:S(2)}, u32[]{:S(2)}) collective-permute-start(bf16[1,144,128]{2,1,0:T(8,128)(2,1)S(1)} %shard_map.120), channel_id=1, source_target_pairs={{0,16},{4,20},{8,24},{12,28},{16,0},{20,4},{24,8},{28,12},{1,17},{... | collective-permute-start | bytes 110600 | tf_op jit(solution)/shard_map/ppermute | solution.py:523
  16.6 1.5 %collective-permute-start.6 = (f32[1,3,2,256]{3,2,1,0:T(2,128)S(1)}, f32[1,3,2,256]{3,2,1,0:T(2,128)S(1)}, u32[]{:S(2)}, u32[]{:S(2)}) collective-permute-start(f32[1,3,2,256]{3,2,1,0:T(2,128)S(1)} %get-tuple-element.31.params_ref.rest_0_), channel_id=1, source_target_pairs={{0,1},{1,0},{2,3},{3,2},{4,5},{5,4},{6,7},{7,6},{8,9},{9,8},{10,11... | collective-permute-start | bytes 18440 | tf_op jit(solution)/shard_map/ppermute | solution.py:523
  18.3 0.6 %shard_map.119.enter_ref = bf16[2,3,64,128]{3,2,1,0:T(8,128)(2,1)S(1)} custom-call(bf16[1,272,128]{2,1,0:T(8,128)(2,1)S(1)} %collective-permute-done.3.other_ref, bf16[2,3,64,128]{3,2,1,0:T(8,128)(2,1)S(1)} %shard_map.118.refs_0_), custom_call_target="tpu_custom_call" | custom-call | flops 1000000 | bytes 1000000 | tf_op jit(solution)/shard_map/pallas_call | solution.py:604
  18.9 0.7 %shard_map.121 = (bf16[2,64,128]{2,1,0:T(8,128)(2,1)S(1)}, bf16[1,64,128]{2,1,0:T(8,128)(2,1)S(1)}) custom-call(bf16[2,3,64,128]{3,2,1,0:T(8,128)(2,1)S(1)} %shard_map.119.enter_ref, bf16[1,144,128]{2,1,0:T(8,128)(2,1)S(1)} %collective-permute-done.4.state_ref), custom_call_target="tpu_custom_call" | custom-call | flops 1000000 | bytes 1000000 | tf_op jit(solution)/shard_map/pallas_call | solution.py:606
  19.6 1.7 %collective-permute-start.9 = (bf16[1,64,128]{2,1,0:T(8,128)(2,1)S(1)}, bf16[1,64,128]{2,1,0:T(8,128)(2,1)S(1)}, u32[]{:S(2)}, u32[]{:S(2)}) collective-permute-start(bf16[1,64,128]{2,1,0:T(8,128)(2,1)S(1)} %get-tuple-element.39.lesser_ref), channel_id=1, source_target_pairs={{0,1},{1,0},{2,3},{3,2},{4,5},{5,4},{6,7},{7,6},{8,9},{9,8},{10,11... | collective-permute-start | bytes 49160 | tf_op jit(solution)/shard_map/ppermute | solution.py:523
  21.3 1.5 %collective-permute-start.8 = (bf16[1,64,128]{2,1,0:T(8,128)(2,1)S(1)}, bf16[1,64,128]{2,1,0:T(8,128)(2,1)S(1)}, u32[]{:S(2)}, u32[]{:S(2)}) collective-permute-start(bf16[1,64,128]{2,1,0:T(8,128)(2,1)S(1)} %get-tuple-element.39.lesser_ref), channel_id=1, source_target_pairs={{0,2},{1,3},{2,0},{3,1},{4,6},{5,7},{6,4},{7,5},{8,10},{9,11},{10,... | collective-permute-start | bytes 49160 | tf_op jit(solution)/shard_map/ppermute | solution.py:523
  23.2 0.8 %shard_map.124 = (bf16[2,256,128]{2,1,0:T(8,128)(2,1)S(1)}, bf16[2,2,64,256]{3,2,1,0:T(8,128)(2,1)S(1)}, f32[2,3,2,256]{3,2,1,0:T(2,128)S(1)}) custom-call(bf16[1,256,256]{2,1,0:T(8,128)(2,1)S(1)} %get-tuple-element.29.modes_ref, f32[1,256]{1,0:T(1,128)S(1)} %get-tuple-element.30.levels_ref, bf16[128,512]{1,0:T(8,128)(2,1)S(1)} %get-tuple-element.32.link2_ref, ...), custom_call_target="tpu_custom_call" | custom-call | flops 1000000 | bytes 1000000 | tf_op jit(solution)/shard_map/pallas_call | solution.py:586
  24.0 1.7 %collective-permute-start.7 = (f32[2,3,2,256]{3,2,1,0:T(2,128)S(1)}, f32[2,3,2,256]{3,2,1,0:T(2,128)S(1)}, u32[]{:S(2)}, u32[]{:S(2)}) collective-permute-start(f32[2,3,2,256]{3,2,1,0:T(2,128)S(1)} %get-tuple-element.45), channel_id=1, source_target_pairs={{0,2},{1,3},{2,0},{3,1},{4,6},{5,7},{6,4},{7,5},{8,10},{9,11},{10,... | collective-permute-start | bytes 36872 | tf_op jit(solution)/shard_map/ppermute | solution.py:523
  26.0 1.8 %collective-permute-done.7.got_ref = f32[2,3,2,256]{3,2,1,0:T(2,128)S(1)} collective-permute-done((f32[2,3,2,256]{3,2,1,0:T(2,128)S(1)}, f32[2,3,2,256]{3,2,1,0:T(2,128)S(1)}, u32[]{:S(2)}, u32[]{:S(2)}) %collective-permute-start.7) | collective-permute-done | bytes 12320 | tf_op jit(solution)/shard_map/ppermute | solution.py:523
  27.8 0.8 %shard_map.126 = (bf16[2,256,128]{2,1,0:T(8,128)(2,1)S(1)}, bf16[2,2,64,256]{3,2,1,0:T(8,128)(2,1)S(1)}) custom-call(bf16[1,256,256]{2,1,0:T(8,128)(2,1)S(1)} %get-tuple-element.29.modes_ref, f32[1,256]{1,0:T(1,128)S(1)} %get-tuple-element.30.levels_ref, bf16[128,512]{1,0:T(8,128)(2,1)S(1)} %get-tuple-element.32.link2_ref, ...), custom_call_target="tpu_custom_call" | custom-call | flops 1000000 | bytes 1000000 | tf_op jit(solution)/shard_map/pallas_call | solution.py:586
  28.6 0.8 %shard_map.125 = (bf16[2,256,128]{2,1,0:T(8,128)(2,1)S(1)}, bf16[2,2,64,256]{3,2,1,0:T(8,128)(2,1)S(1)}) custom-call(bf16[1,256,256]{2,1,0:T(8,128)(2,1)S(1)} %get-tuple-element.29.modes_ref, f32[1,256]{1,0:T(1,128)S(1)} %get-tuple-element.30.levels_ref, bf16[128,512]{1,0:T(8,128)(2,1)S(1)} %get-tuple-element.32.link2_ref, ...), custom_call_target="tpu_custom_call" | custom-call | flops 1000000 | bytes 1000000 | tf_op jit(solution)/shard_map/pallas_call | solution.py:586
  29.4 1.6 %shard_map.123 = (f32[3,12,64,256]{3,2,1,0:T(8,128)S(1)}, f32[1,2,256]{2,1,0:T(2,128)}) custom-call(s32[8]{0:T(128)S(1)} %get-tuple-element.28.offsets_ref, bf16[1,2,8,64,256]{4,3,2,1,0:T(8,128)(2,1)S(1)} %copy-done, bf16[1,64,128]{2,1,0:T(8,128)(2,1)S(1)} %get-tuple-element.39.lesser_ref, ...), custom_call_target="tpu_custom_call", output_to_operand_aliasing={{0}: (5, {})} | custom-call | flops 1000000 | bytes 1000000 | tf_op jit(solution)/shard_map/pallas_call | solution.py:630
  31.0 1.1 %shard_map.127._ = f32[3,12,64,256]{3,2,1,0:T(8,128)S(1)} custom-call(s32[8]{0:T(128)S(1)} %get-tuple-element.28.offsets_ref, bf16[1,2,8,64,256]{4,3,2,1,0:T(8,128)(2,1)S(1)} %copy-done, bf16[1,64,128]{2,1,0:T(8,128)(2,1)S(1)} %collective-permute-done.9.lesser_ref, ...), custom_call_target="tpu_custom_call", output_to_operand_aliasing={{}: (5, {})} | custom-call | flops 1000000 | bytes 1000000 | tf_op jit(solution)/shard_map/pallas_call | solution.py:630
  32.1 1.1 %shard_map.128._ = f32[3,12,64,256]{3,2,1,0:T(8,128)S(1)} custom-call(s32[8]{0:T(128)S(1)} %get-tuple-element.28.offsets_ref, bf16[1,2,8,64,256]{4,3,2,1,0:T(8,128)(2,1)S(1)} %copy-done, bf16[1,64,128]{2,1,0:T(8,128)(2,1)S(1)} %collective-permute-done.8.lesser_ref, ...), custom_call_target="tpu_custom_call", output_to_operand_aliasing={{}: (5, {})} | custom-call | flops 1000000 | bytes 1000000 | tf_op jit(solution)/shard_map/pallas_call | solution.py:630
  33.2 1.8 %shard_map.129 = (f32[3,12,64,256]{3,2,1,0:T(8,128)S(1)}, bf16[1,2,8,64,256]{4,3,2,1,0:T(8,128)(2,1)}) custom-call(s32[8]{0:T(128)S(1)} %get-tuple-element.28.offsets_ref, bf16[1,2,8,64,256]{4,3,2,1,0:T(8,128)(2,1)S(1)} %copy-done, bf16[1,64,128]{2,1,0:T(8,128)(2,1)S(1)} %collective-permute-done.5.lesser_ref, ...), custom_call_target="tpu_custom_call", output_to_operand_aliasing={{0}: (5, {})} | custom-call | flops 1000000 | bytes 1000000 | tf_op jit(solution)/shard_map/pallas_call | solution.py:630
  (15 shorter events, 1.5 us)
Async XLA Ops:
  0.6 28.8 %copy-start = (bf16[1,2,8,64,256]{4,3,2,1,0:T(8,128)(2,1)S(1)}, bf16[1,2,8,64,256]{4,3,2,1,0:T(8,128)(2,1)}, u32[]{:S(2)}) copy-start(bf16[1,2,8,64,256]{4,3,2,1,0:T(8,128)(2,1)} %screen_ref.7) | copy-start | bytes 1572868
  1.4 5.0 %collective-permute-start = (f32[8,128]{1,0:T(8,128)S(1)}, f32[8,128]{1,0:T(8,128)S(1)}, u32[]{:S(2)}, u32[]{:S(2)}) collective-permute-start(f32[8,128]{1,0:T(8,128)S(1)} %shard_map.114), channel_id=1, source_target_pairs={{0,4},{4,0},{8,12},{12,8},{16,20},{20,16},{24,28},{28,24},{1,5},{5... | collective-permute-start | bytes 12296 | tf_op jit(solution)/shard_map/ppermute | solution.py:523
  1.9 4.5 %collective-permute-start.1 = (f32[8,128]{1,0:T(8,128)S(1)}, f32[8,128]{1,0:T(8,128)S(1)}, u32[]{:S(2)}, u32[]{:S(2)}) collective-permute-start(f32[8,128]{1,0:T(8,128)S(1)} %shard_map.114), channel_id=1, source_target_pairs={{0,1},{1,0},{2,3},{3,2},{4,8},{5,9},{6,10},{7,11},{8,4},{9,5},{10,... | collective-permute-start | bytes 12296 | tf_op jit(solution)/shard_map/ppermute | solution.py:536
  6.9 1.3 %collective-permute-start.2 = (bf16[1,272,128]{2,1,0:T(8,128)(2,1)S(1)}, bf16[1,272,128]{2,1,0:T(8,128)(2,1)S(1)}, u32[]{:S(2)}, u32[]{:S(2)}) collective-permute-start(bf16[1,272,128]{2,1,0:T(8,128)(2,1)S(1)} %get-tuple-element.36), channel_id=1, source_target_pairs={{0,4},{4,0},{8,12},{12,8},{16,20},{20,16},{24,28},{28,24},{1,5},{5... | collective-permute-start | bytes 208904 | tf_op jit(solution)/shard_map/ppermute | solution.py:523
  8.9 4.4 %collective-permute-start.3 = (bf16[1,272,128]{2,1,0:T(8,128)(2,1)S(1)}, bf16[1,272,128]{2,1,0:T(8,128)(2,1)S(1)}, u32[]{:S(2)}, u32[]{:S(2)}) collective-permute-start(bf16[1,272,128]{2,1,0:T(8,128)(2,1)S(1)} %get-tuple-element.37), channel_id=1, source_target_pairs={{0,8},{4,12},{8,0},{12,4},{16,24},{20,28},{24,16},{28,20},{1,9},{5... | collective-permute-start | bytes 208904 | tf_op jit(solution)/shard_map/ppermute | solution.py:523
  14.0 4.9 %collective-permute-start.4 = (bf16[1,144,128]{2,1,0:T(8,128)(2,1)S(1)}, bf16[1,144,128]{2,1,0:T(8,128)(2,1)S(1)}, u32[]{:S(2)}, u32[]{:S(2)}) collective-permute-start(bf16[1,144,128]{2,1,0:T(8,128)(2,1)S(1)} %shard_map.120), channel_id=1, source_target_pairs={{0,16},{4,20},{8,24},{12,28},{16,0},{20,4},{24,8},{28,12},{1,17},{... | collective-permute-start | bytes 110600 | tf_op jit(solution)/shard_map/ppermute | solution.py:523
  16.6 6.6 %collective-permute-start.6 = (f32[1,3,2,256]{3,2,1,0:T(2,128)S(1)}, f32[1,3,2,256]{3,2,1,0:T(2,128)S(1)}, u32[]{:S(2)}, u32[]{:S(2)}) collective-permute-start(f32[1,3,2,256]{3,2,1,0:T(2,128)S(1)} %get-tuple-element.31.params_ref.rest_0_), channel_id=1, source_target_pairs={{0,1},{1,0},{2,3},{3,2},{4,5},{5,4},{6,7},{7,6},{8,9},{9,8},{10,11... | collective-permute-start | bytes 18440 | tf_op jit(solution)/shard_map/ppermute | solution.py:523
  19.6 11.4 %collective-permute-start.9 = (bf16[1,64,128]{2,1,0:T(8,128)(2,1)S(1)}, bf16[1,64,128]{2,1,0:T(8,128)(2,1)S(1)}, u32[]{:S(2)}, u32[]{:S(2)}) collective-permute-start(bf16[1,64,128]{2,1,0:T(8,128)(2,1)S(1)} %get-tuple-element.39.lesser_ref), channel_id=1, source_target_pairs={{0,1},{1,0},{2,3},{3,2},{4,5},{5,4},{6,7},{7,6},{8,9},{9,8},{10,11... | collective-permute-start | bytes 49160 | tf_op jit(solution)/shard_map/ppermute | solution.py:523
  21.3 10.8 %collective-permute-start.8 = (bf16[1,64,128]{2,1,0:T(8,128)(2,1)S(1)}, bf16[1,64,128]{2,1,0:T(8,128)(2,1)S(1)}, u32[]{:S(2)}, u32[]{:S(2)}) collective-permute-start(bf16[1,64,128]{2,1,0:T(8,128)(2,1)S(1)} %get-tuple-element.39.lesser_ref), channel_id=1, source_target_pairs={{0,2},{1,3},{2,0},{3,1},{4,6},{5,7},{6,4},{7,5},{8,10},{9,11},{10,... | collective-permute-start | bytes 49160 | tf_op jit(solution)/shard_map/ppermute | solution.py:523
  22.8 10.4 %collective-permute-start.5 = (bf16[1,64,128]{2,1,0:T(8,128)(2,1)S(1)}, bf16[1,64,128]{2,1,0:T(8,128)(2,1)S(1)}, u32[]{:S(2)}, u32[]{:S(2)}) collective-permute-start(bf16[1,64,128]{2,1,0:T(8,128)(2,1)S(1)} %get-tuple-element.39.lesser_ref), channel_id=1, source_target_pairs={{0,3},{1,2},{2,1},{3,0},{4,7},{5,6},{6,5},{7,4},{8,11},{9,10},{10,... | collective-permute-start | bytes 49160 | tf_op jit(solution)/shard_map/ppermute | solution.py:523
  24.0 3.8 %collective-permute-start.7 = (f32[2,3,2,256]{3,2,1,0:T(2,128)S(1)}, f32[2,3,2,256]{3,2,1,0:T(2,128)S(1)}, u32[]{:S(2)}, u32[]{:S(2)}) collective-permute-start(f32[2,3,2,256]{3,2,1,0:T(2,128)S(1)} %get-tuple-element.45), channel_id=1, source_target_pairs={{0,2},{1,3},{2,0},{3,1},{4,6},{5,7},{6,4},{7,5},{8,10},{9,11},{10,... | collective-permute-start | bytes 36872 | tf_op jit(solution)/shard_map/ppermute | solution.py:523

commit v8 on v7

--- a/solution.py
+++ b/solution.py
@@ -209,14 +209,13 @@
     )
 
 
-def rows_kernel(overall, share, hop, slot, modes_ref, levels_ref, link2_ref, got_ref, *rest):
-    if len(rest) > 2:
-        had_ref, left_ref, local_ref, both_ref = rest
-        count = had_ref.shape[0]
-        both_ref[0:count] = had_ref[...]
-        both_ref[count:] = got_ref[...]
-    else:
-        left_ref, local_ref = rest
+def both_kernel(had_ref, got_ref, both_ref):
+    count = had_ref.shape[0]
+    both_ref[0:count] = had_ref[...]
+    both_ref[count:] = got_ref[...]
+
+
+def rows_kernel(overall, share, hop, slot, modes_ref, levels_ref, link2_ref, got_ref, left_ref, local_ref):
     make_rows(
         got_ref.shape[2],
         hop,
@@ -455,6 +454,7 @@
 
     def rows_of(step, _):
         rows = pl.ds(pl.multiple_of(step * height, height), height)
+        held = [[g_ref[part, e, rows, :] for part in range(3)] for e in range(energies)]
         for k in range(points):
             w_re = screen_ref[0, 0, k, rows, :].astype(f32)
             w_im = screen_ref[0, 1, k, rows, :].astype(f32)
@@ -462,7 +462,7 @@
             for e in range(energies):
                 target = base + e + picked_ref[k]
                 for part in range(3):
-                    sums_ref[part, target, rows, :] += factors[part] * g_ref[part, e, rows, :]
+                    sums_ref[part, target, rows, :] += factors[part] * held[e][part]
         if last:
             for e in range(overall):
                 common = sums_ref[0, reach + e, rows, :]
@@ -578,21 +578,16 @@
     while known.shape[0] < groups:
         count = known.shape[0]
         got = swapped(known, "energy", count)
-        more = 2 * count < groups
+        if 2 * count < groups:
+            known = call(both_kernel, sds((2 * count,) + params_shape, f32), [VMEM] * 2)(known, got)
         for slot in range(count):
-            outs, given = (left_shape, local_shape), (modes, levels, link2, got)
-            if slot == 0 and more:
-                outs, given = outs + (sds((2 * count,) + params_shape, f32),), given + (known,)
-            left, local, *rest = call(
-                partial(rows_kernel, overall, share, count + slot, slot), outs, [VMEM] * len(given)
-            )(*given)
+            left, local = call(
+                partial(rows_kernel, overall, share, count + slot, slot), (left_shape, local_shape), [VMEM] * 4
+            )(modes, levels, link2, got)
             lefts.append(left)
             locals_.append(local)
-            if rest:
-                both = rest[0]
-        if not more:
+        if 2 * count >= groups:
             break
-        known = both
 
     enter = None
     for level in range(rounds - 1):

time: 35.2 us -> 33.9 us (0.963)
  waiting for transfers between devices: 5.75 us -> 4.92 us
  Pallas kernels: 13.5 us -> 13.1 us
    ppermute x9, waiting for transfers between devices: 5.75 us -> 4.91 us  [swapped(): lax.ppermute(x, axis, [(i, i ^ distance) for i in range(lax.axis_size(axi...]
    pallas_call x4, Pallas kernels: 5.55 us -> 5.13 us  [body(): call(partial(convolve_kernel, reach, hop, last), outs, [VMEM] * len(given...]
    pallas_call x3 -> x4, Pallas kernels: 2.48 us -> 2.48 us  [the longest x3 2.48 us: body(): call(partial(rows_kernel, overall, share, count + slot, slot), (left_shap...]
where the time goes in v8:
time: 33.9 us; the launch traced here: 33.7 us
  starting transfers between devices  14.2 us (42%)
  Pallas kernels  13.1 us (39%)
  waiting for transfers between devices  4.92 us (15%)
  between operations  1.51 us (4%)
    ppermute x9, starting transfers between devices, swapped(): lax.ppermute(x, axis, [(i, i ^ distance) for i in range(lax.axis_size(axi...  11.6 us
    pallas_call x4, Pallas kernels, body(): call(partial(convolve_kernel, reach, hop, last), outs, [VMEM] * len(given...  5.13 us
    ppermute x9, waiting for transfers between devices, swapped(): lax.ppermute(x, axis, [(i, i ^ distance) for i in range(lax.axis_size(axi...  4.91 us
    ppermute x1, starting transfers between devices, body(): two = lax.ppermute(block, ('cell', 'energy'), route)  2.55 us
    pallas_call x3, Pallas kernels, body(): call(partial(rows_kernel, overall, share, count + slot, slot), (left_shap...  2.48 us
    pallas_call x2, Pallas kernels, body(): call(partial(join_kernel, level), outs, [VMEM] * 2)(total, other)  1.39 us
    pallas_call x1, Pallas kernels, body(): call(front_kernel, (sds((width, 2 * orbitals), bf16), sds(modes.shape, bf...  1.09 us
    pallas_call x1, Pallas kernels, body(): call(partial(own_rows_kernel, overall, share), (left_shape, local_shape,...  0.83 us
  transfers between devices with their start and end apart: 10, of which 3 were waited for; matrix products, arithmetic and copies ran while one was open for 0% of the time, Pallas kernels for 28%

profile of v8, /device:TPU:0, one launch (start us, length us, event | category | flops | bytes accessed | tf_op | source)
XLA Modules:
  0.0 33.7 jit_solution(3362749648841508638)
XLA Ops:
  1.4 0.6 %collective-permute-start = (f32[8,128]{1,0:T(8,128)S(1)}, f32[8,128]{1,0:T(8,128)S(1)}, u32[]{:S(2)}, u32[]{:S(2)}) collective-permute-start(f32[8,128]{1,0:T(8,128)S(1)} %shard_map.114), channel_id=1, source_target_pairs={{0,4},{4,0},{8,12},{12,8},{16,20},{20,16},{24,28},{28,24},{1,5},{5... | collective-permute-start | bytes 12296 | tf_op jit(solution)/shard_map/ppermute | solution.py:523
  1.9 2.6 %collective-permute-start.1 = (f32[8,128]{1,0:T(8,128)S(1)}, f32[8,128]{1,0:T(8,128)S(1)}, u32[]{:S(2)}, u32[]{:S(2)}) collective-permute-start(f32[8,128]{1,0:T(8,128)S(1)} %shard_map.114), channel_id=1, source_target_pairs={{0,1},{1,0},{2,3},{3,2},{4,8},{5,9},{6,10},{7,11},{8,4},{9,5},{10,... | collective-permute-start | bytes 12296 | tf_op jit(solution)/shard_map/ppermute | solution.py:536
  4.5 1.1 %shard_map.113 = (bf16[128,512]{1,0:T(8,128)(2,1)S(1)}, bf16[1,256,256]{2,1,0:T(8,128)(2,1)S(1)}, f32[1,256]{1,0:T(1,128)S(1)}, f32[1,3,2,256]{3,2,1,0:T(2,128)S(1)}, s32[8]{0:T(128)S(1)}) custom-call(s32[1,4]{1,0:T(1,128)} %mask_hbm.1, bf16[1,256,256]{2,1,0:T(8,128)(2,1)} %modes_hbm.1, f32[1,256]{1,0:T(1,128)} %levels_hbm.1, bf16[1,64,256]{2,1,0:T(8,128)(2,1)} %bitcast.1, ...), custom_call_target="tpu_custom_call" | custom-call | flops 1000000 | bytes 1000000 | tf_op jit(solution)/shard_map/pallas_call | solution.py:538
  5.6 0.8 %shard_map.115 = (bf16[2,256,128]{2,1,0:T(8,128)(2,1)S(1)}, bf16[2,2,64,256]{3,2,1,0:T(8,128)(2,1)S(1)}, bf16[2,256,512]{2,1,0:T(8,128)(2,1)S(1)}) custom-call(bf16[1,256,256]{2,1,0:T(8,128)(2,1)S(1)} %get-tuple-element.28.modes_ref, f32[1,256]{1,0:T(1,128)S(1)} %get-tuple-element.29.levels_ref, bf16[128,512]{1,0:T(8,128)(2,1)S(1)} %get-tuple-element.31.link2_ref, ...), custom_call_target="tpu_custom_call" | custom-call | flops 1000000 | bytes 1000000 | tf_op jit(solution)/shard_map/pallas_call | solution.py:557
  7.2 1.1 %collective-permute-done.2.other_ref = bf16[1,272,128]{2,1,0:T(8,128)(2,1)S(1)} collective-permute-done((bf16[1,272,128]{2,1,0:T(8,128)(2,1)S(1)}, bf16[1,272,128]{2,1,0:T(8,128)(2,1)S(1)}, u32[]{:S(2)}, u32[]{:S(2)}) %collective-permute-start.2) | collective-permute-done | bytes 69664 | tf_op jit(solution)/shard_map/ppermute | solution.py:523
  8.2 0.7 %shard_map.117 = (bf16[1,272,128]{2,1,0:T(8,128)(2,1)S(1)}, bf16[2,3,64,128]{3,2,1,0:T(8,128)(2,1)S(1)}) custom-call(bf16[2,3,64,128]{3,2,1,0:T(8,128)(2,1)S(1)} %get-tuple-element.34.total_ref, bf16[1,272,128]{2,1,0:T(8,128)(2,1)S(1)} %collective-permute-done.2.other_ref), custom_call_target="tpu_custom_call" | custom-call | flops 1000000 | bytes 1000000 | tf_op jit(solution)/shard_map/pallas_call | solution.py:596
  8.9 1.5 %collective-permute-start.3 = (bf16[1,272,128]{2,1,0:T(8,128)(2,1)S(1)}, bf16[1,272,128]{2,1,0:T(8,128)(2,1)S(1)}, u32[]{:S(2)}, u32[]{:S(2)}) collective-permute-start(bf16[1,272,128]{2,1,0:T(8,128)(2,1)S(1)} %get-tuple-element.36), channel_id=1, source_target_pairs={{0,8},{4,12},{8,0},{12,4},{16,24},{20,28},{24,16},{28,20},{1,9},{5... | collective-permute-start | bytes 208904 | tf_op jit(solution)/shard_map/ppermute | solution.py:523
  10.4 2.9 %collective-permute-done.3.other_ref = bf16[1,272,128]{2,1,0:T(8,128)(2,1)S(1)} collective-permute-done((bf16[1,272,128]{2,1,0:T(8,128)(2,1)S(1)}, bf16[1,272,128]{2,1,0:T(8,128)(2,1)S(1)}, u32[]{:S(2)}, u32[]{:S(2)}) %collective-permute-start.3) | collective-permute-done | bytes 69664 | tf_op jit(solution)/shard_map/ppermute | solution.py:523
  13.3 0.7 %shard_map.120 = bf16[1,144,128]{2,1,0:T(8,128)(2,1)S(1)} custom-call(bf16[2,3,64,128]{3,2,1,0:T(8,128)(2,1)S(1)} %get-tuple-element.37.total_ref, bf16[1,272,128]{2,1,0:T(8,128)(2,1)S(1)} %collective-permute-done.3.other_ref), custom_call_target="tpu_custom_call" | custom-call | flops 1000000 | bytes 1000000 | tf_op jit(solution)/shard_map/pallas_call | solution.py:596
  14.0 2.6 %collective-permute-start.4 = (bf16[1,144,128]{2,1,0:T(8,128)(2,1)S(1)}, bf16[1,144,128]{2,1,0:T(8,128)(2,1)S(1)}, u32[]{:S(2)}, u32[]{:S(2)}) collective-permute-start(bf16[1,144,128]{2,1,0:T(8,128)(2,1)S(1)} %shard_map.120), channel_id=1, source_target_pairs={{0,16},{4,20},{8,24},{12,28},{16,0},{20,4},{24,8},{28,12},{1,17},{... | collective-permute-start | bytes 110600 | tf_op jit(solution)/shard_map/ppermute | solution.py:523
  16.6 1.5 %collective-permute-start.6 = (f32[1,3,2,256]{3,2,1,0:T(2,128)S(1)}, f32[1,3,2,256]{3,2,1,0:T(2,128)S(1)}, u32[]{:S(2)}, u32[]{:S(2)}) collective-permute-start(f32[1,3,2,256]{3,2,1,0:T(2,128)S(1)} %get-tuple-element.30.params_ref.had_ref), channel_id=1, source_target_pairs={{0,1},{1,0},{2,3},{3,2},{4,5},{5,4},{6,7},{7,6},{8,9},{9,8},{10,11... | collective-permute-start | bytes 18440 | tf_op jit(solution)/shard_map/ppermute | solution.py:523
  18.3 0.6 %shard_map.119.enter_ref = bf16[2,3,64,128]{3,2,1,0:T(8,128)(2,1)S(1)} custom-call(bf16[1,272,128]{2,1,0:T(8,128)(2,1)S(1)} %collective-permute-done.3.other_ref, bf16[2,3,64,128]{3,2,1,0:T(8,128)(2,1)S(1)} %shard_map.118.refs_0_), custom_call_target="tpu_custom_call" | custom-call | flops 1000000 | bytes 1000000 | tf_op jit(solution)/shard_map/pallas_call | solution.py:599
  18.9 0.7 %shard_map.121 = (bf16[2,64,128]{2,1,0:T(8,128)(2,1)S(1)}, bf16[1,64,128]{2,1,0:T(8,128)(2,1)S(1)}) custom-call(bf16[2,3,64,128]{3,2,1,0:T(8,128)(2,1)S(1)} %shard_map.119.enter_ref, bf16[1,144,128]{2,1,0:T(8,128)(2,1)S(1)} %collective-permute-done.4.state_ref), custom_call_target="tpu_custom_call" | custom-call | flops 1000000 | bytes 1000000 | tf_op jit(solution)/shard_map/pallas_call | solution.py:601
  19.6 1.7 %collective-permute-start.9 = (bf16[1,64,128]{2,1,0:T(8,128)(2,1)S(1)}, bf16[1,64,128]{2,1,0:T(8,128)(2,1)S(1)}, u32[]{:S(2)}, u32[]{:S(2)}) collective-permute-start(bf16[1,64,128]{2,1,0:T(8,128)(2,1)S(1)} %get-tuple-element.38.lesser_ref), channel_id=1, source_target_pairs={{0,1},{1,0},{2,3},{3,2},{4,5},{5,4},{6,7},{7,6},{8,9},{9,8},{10,11... | collective-permute-start | bytes 49160 | tf_op jit(solution)/shard_map/ppermute | solution.py:523
  21.3 1.5 %collective-permute-start.8 = (bf16[1,64,128]{2,1,0:T(8,128)(2,1)S(1)}, bf16[1,64,128]{2,1,0:T(8,128)(2,1)S(1)}, u32[]{:S(2)}, u32[]{:S(2)}) collective-permute-start(bf16[1,64,128]{2,1,0:T(8,128)(2,1)S(1)} %get-tuple-element.38.lesser_ref), channel_id=1, source_target_pairs={{0,2},{1,3},{2,0},{3,1},{4,6},{5,7},{6,4},{7,5},{8,10},{9,11},{10,... | collective-permute-start | bytes 49160 | tf_op jit(solution)/shard_map/ppermute | solution.py:523
  23.2 1.7 %collective-permute-start.7 = (f32[2,3,2,256]{3,2,1,0:T(2,128)S(1)}, f32[2,3,2,256]{3,2,1,0:T(2,128)S(1)}, u32[]{:S(2)}, u32[]{:S(2)}) collective-permute-start(f32[2,3,2,256]{3,2,1,0:T(2,128)S(1)} %shard_map.124), channel_id=1, source_target_pairs={{0,2},{1,3},{2,0},{3,1},{4,6},{5,7},{6,4},{7,5},{8,10},{9,11},{10,... | collective-permute-start | bytes 36872 | tf_op jit(solution)/shard_map/ppermute | solution.py:523
  25.1 0.8 %shard_map.127 = (bf16[2,256,128]{2,1,0:T(8,128)(2,1)S(1)}, bf16[2,2,64,256]{3,2,1,0:T(8,128)(2,1)S(1)}) custom-call(bf16[1,256,256]{2,1,0:T(8,128)(2,1)S(1)} %get-tuple-element.28.modes_ref, f32[1,256]{1,0:T(1,128)S(1)} %get-tuple-element.29.levels_ref, bf16[128,512]{1,0:T(8,128)(2,1)S(1)} %get-tuple-element.31.link2_ref, ...), custom_call_target="tpu_custom_call" | custom-call | flops 1000000 | bytes 1000000 | tf_op jit(solution)/shard_map/pallas_call | solution.py:584
  25.9 0.9 %collective-permute-done.7.got_ref = f32[2,3,2,256]{3,2,1,0:T(2,128)S(1)} collective-permute-done((f32[2,3,2,256]{3,2,1,0:T(2,128)S(1)}, f32[2,3,2,256]{3,2,1,0:T(2,128)S(1)}, u32[]{:S(2)}, u32[]{:S(2)}) %collective-permute-start.7) | collective-permute-done | bytes 12320 | tf_op jit(solution)/shard_map/ppermute | solution.py:523
  26.9 0.8 %shard_map.126 = (bf16[2,256,128]{2,1,0:T(8,128)(2,1)S(1)}, bf16[2,2,64,256]{3,2,1,0:T(8,128)(2,1)S(1)}) custom-call(bf16[1,256,256]{2,1,0:T(8,128)(2,1)S(1)} %get-tuple-element.28.modes_ref, f32[1,256]{1,0:T(1,128)S(1)} %get-tuple-element.29.levels_ref, bf16[128,512]{1,0:T(8,128)(2,1)S(1)} %get-tuple-element.31.link2_ref, ...), custom_call_target="tpu_custom_call" | custom-call | flops 1000000 | bytes 1000000 | tf_op jit(solution)/shard_map/pallas_call | solution.py:584
  27.7 0.8 %shard_map.125 = (bf16[2,256,128]{2,1,0:T(8,128)(2,1)S(1)}, bf16[2,2,64,256]{3,2,1,0:T(8,128)(2,1)S(1)}) custom-call(bf16[1,256,256]{2,1,0:T(8,128)(2,1)S(1)} %get-tuple-element.28.modes_ref, f32[1,256]{1,0:T(1,128)S(1)} %get-tuple-element.29.levels_ref, bf16[128,512]{1,0:T(8,128)(2,1)S(1)} %get-tuple-element.31.link2_ref, ...), custom_call_target="tpu_custom_call" | custom-call | flops 1000000 | bytes 1000000 | tf_op jit(solution)/shard_map/pallas_call | solution.py:584
  28.6 1.5 %shard_map.123 = (f32[3,12,64,256]{3,2,1,0:T(8,128)S(1)}, f32[1,2,256]{2,1,0:T(2,128)}) custom-call(s32[8]{0:T(128)S(1)} %get-tuple-element.27.offsets_ref, bf16[1,2,8,64,256]{4,3,2,1,0:T(8,128)(2,1)S(1)} %copy-done, bf16[1,64,128]{2,1,0:T(8,128)(2,1)S(1)} %get-tuple-element.38.lesser_ref, ...), custom_call_target="tpu_custom_call", output_to_operand_aliasing={{0}: (5, {})} | custom-call | flops 1000000 | bytes 1000000 | tf_op jit(solution)/shard_map/pallas_call | solution.py:625
  30.0 1.0 %shard_map.128._ = f32[3,12,64,256]{3,2,1,0:T(8,128)S(1)} custom-call(s32[8]{0:T(128)S(1)} %get-tuple-element.27.offsets_ref, bf16[1,2,8,64,256]{4,3,2,1,0:T(8,128)(2,1)S(1)} %copy-done, bf16[1,64,128]{2,1,0:T(8,128)(2,1)S(1)} %collective-permute-done.9.lesser_ref, ...), custom_call_target="tpu_custom_call", output_to_operand_aliasing={{}: (5, {})} | custom-call | flops 1000000 | bytes 1000000 | tf_op jit(solution)/shard_map/pallas_call | solution.py:625
  31.0 1.0 %shard_map.129._ = f32[3,12,64,256]{3,2,1,0:T(8,128)S(1)} custom-call(s32[8]{0:T(128)S(1)} %get-tuple-element.27.offsets_ref, bf16[1,2,8,64,256]{4,3,2,1,0:T(8,128)(2,1)S(1)} %copy-done, bf16[1,64,128]{2,1,0:T(8,128)(2,1)S(1)} %collective-permute-done.8.lesser_ref, ...), custom_call_target="tpu_custom_call", output_to_operand_aliasing={{}: (5, {})} | custom-call | flops 1000000 | bytes 1000000 | tf_op jit(solution)/shard_map/pallas_call | solution.py:625
  32.0 1.7 %shard_map.130 = (f32[3,12,64,256]{3,2,1,0:T(8,128)S(1)}, bf16[1,2,8,64,256]{4,3,2,1,0:T(8,128)(2,1)}) custom-call(s32[8]{0:T(128)S(1)} %get-tuple-element.27.offsets_ref, bf16[1,2,8,64,256]{4,3,2,1,0:T(8,128)(2,1)S(1)} %copy-done, bf16[1,64,128]{2,1,0:T(8,128)(2,1)S(1)} %collective-permute-done.5.lesser_ref, ...), custom_call_target="tpu_custom_call", output_to_operand_aliasing={{0}: (5, {})} | custom-call | flops 1000000 | bytes 1000000 | tf_op jit(solution)/shard_map/pallas_call | solution.py:625
  (16 shorter events, 1.5 us)
Async XLA Ops:
  0.6 27.9 %copy-start = (bf16[1,2,8,64,256]{4,3,2,1,0:T(8,128)(2,1)S(1)}, bf16[1,2,8,64,256]{4,3,2,1,0:T(8,128)(2,1)}, u32[]{:S(2)}) copy-start(bf16[1,2,8,64,256]{4,3,2,1,0:T(8,128)(2,1)} %screen_ref.7) | copy-start | bytes 1572868
  1.4 5.0 %collective-permute-start = (f32[8,128]{1,0:T(8,128)S(1)}, f32[8,128]{1,0:T(8,128)S(1)}, u32[]{:S(2)}, u32[]{:S(2)}) collective-permute-start(f32[8,128]{1,0:T(8,128)S(1)} %shard_map.114), channel_id=1, source_target_pairs={{0,4},{4,0},{8,12},{12,8},{16,20},{20,16},{24,28},{28,24},{1,5},{5... | collective-permute-start | bytes 12296 | tf_op jit(solution)/shard_map/ppermute | solution.py:523
  1.9 4.5 %collective-permute-start.1 = (f32[8,128]{1,0:T(8,128)S(1)}, f32[8,128]{1,0:T(8,128)S(1)}, u32[]{:S(2)}, u32[]{:S(2)}) collective-permute-start(f32[8,128]{1,0:T(8,128)S(1)} %shard_map.114), channel_id=1, source_target_pairs={{0,1},{1,0},{2,3},{3,2},{4,8},{5,9},{6,10},{7,11},{8,4},{9,5},{10,... | collective-permute-start | bytes 12296 | tf_op jit(solution)/shard_map/ppermute | solution.py:536
  6.9 1.3 %collective-permute-start.2 = (bf16[1,272,128]{2,1,0:T(8,128)(2,1)S(1)}, bf16[1,272,128]{2,1,0:T(8,128)(2,1)S(1)}, u32[]{:S(2)}, u32[]{:S(2)}) collective-permute-start(bf16[1,272,128]{2,1,0:T(8,128)(2,1)S(1)} %get-tuple-element.35), channel_id=1, source_target_pairs={{0,4},{4,0},{8,12},{12,8},{16,20},{20,16},{24,28},{28,24},{1,5},{5... | collective-permute-start | bytes 208904 | tf_op jit(solution)/shard_map/ppermute | solution.py:523
  8.9 4.4 %collective-permute-start.3 = (bf16[1,272,128]{2,1,0:T(8,128)(2,1)S(1)}, bf16[1,272,128]{2,1,0:T(8,128)(2,1)S(1)}, u32[]{:S(2)}, u32[]{:S(2)}) collective-permute-start(bf16[1,272,128]{2,1,0:T(8,128)(2,1)S(1)} %get-tuple-element.36), channel_id=1, source_target_pairs={{0,8},{4,12},{8,0},{12,4},{16,24},{20,28},{24,16},{28,20},{1,9},{5... | collective-permute-start | bytes 208904 | tf_op jit(solution)/shard_map/ppermute | solution.py:523
  14.0 4.9 %collective-permute-start.4 = (bf16[1,144,128]{2,1,0:T(8,128)(2,1)S(1)}, bf16[1,144,128]{2,1,0:T(8,128)(2,1)S(1)}, u32[]{:S(2)}, u32[]{:S(2)}) collective-permute-start(bf16[1,144,128]{2,1,0:T(8,128)(2,1)S(1)} %shard_map.120), channel_id=1, source_target_pairs={{0,16},{4,20},{8,24},{12,28},{16,0},{20,4},{24,8},{28,12},{1,17},{... | collective-permute-start | bytes 110600 | tf_op jit(solution)/shard_map/ppermute | solution.py:523
  16.6 6.6 %collective-permute-start.6 = (f32[1,3,2,256]{3,2,1,0:T(2,128)S(1)}, f32[1,3,2,256]{3,2,1,0:T(2,128)S(1)}, u32[]{:S(2)}, u32[]{:S(2)}) collective-permute-start(f32[1,3,2,256]{3,2,1,0:T(2,128)S(1)} %get-tuple-element.30.params_ref.had_ref), channel_id=1, source_target_pairs={{0,1},{1,0},{2,3},{3,2},{4,5},{5,4},{6,7},{7,6},{8,9},{9,8},{10,11... | collective-permute-start | bytes 18440 | tf_op jit(solution)/shard_map/ppermute | solution.py:523
  19.6 10.4 %collective-permute-start.9 = (bf16[1,64,128]{2,1,0:T(8,128)(2,1)S(1)}, bf16[1,64,128]{2,1,0:T(8,128)(2,1)S(1)}, u32[]{:S(2)}, u32[]{:S(2)}) collective-permute-start(bf16[1,64,128]{2,1,0:T(8,128)(2,1)S(1)} %get-tuple-element.38.lesser_ref), channel_id=1, source_target_pairs={{0,1},{1,0},{2,3},{3,2},{4,5},{5,4},{6,7},{7,6},{8,9},{9,8},{10,11... | collective-permute-start | bytes 49160 | tf_op jit(solution)/shard_map/ppermute | solution.py:523
  21.3 9.7 %collective-permute-start.8 = (bf16[1,64,128]{2,1,0:T(8,128)(2,1)S(1)}, bf16[1,64,128]{2,1,0:T(8,128)(2,1)S(1)}, u32[]{:S(2)}, u32[]{:S(2)}) collective-permute-start(bf16[1,64,128]{2,1,0:T(8,128)(2,1)S(1)} %get-tuple-element.38.lesser_ref), channel_id=1, source_target_pairs={{0,2},{1,3},{2,0},{3,1},{4,6},{5,7},{6,4},{7,5},{8,10},{9,11},{10,... | collective-permute-start | bytes 49160 | tf_op jit(solution)/shard_map/ppermute | solution.py:523
  22.8 9.1 %collective-permute-start.5 = (bf16[1,64,128]{2,1,0:T(8,128)(2,1)S(1)}, bf16[1,64,128]{2,1,0:T(8,128)(2,1)S(1)}, u32[]{:S(2)}, u32[]{:S(2)}) collective-permute-start(bf16[1,64,128]{2,1,0:T(8,128)(2,1)S(1)} %get-tuple-element.38.lesser_ref), channel_id=1, source_target_pairs={{0,3},{1,2},{2,1},{3,0},{4,7},{5,6},{6,5},{7,4},{8,11},{9,10},{10,... | collective-permute-start | bytes 49160 | tf_op jit(solution)/shard_map/ppermute | solution.py:523
  23.2 3.7 %collective-permute-start.7 = (f32[2,3,2,256]{3,2,1,0:T(2,128)S(1)}, f32[2,3,2,256]{3,2,1,0:T(2,128)S(1)}, u32[]{:S(2)}, u32[]{:S(2)}) collective-permute-start(f32[2,3,2,256]{3,2,1,0:T(2,128)S(1)} %shard_map.124), channel_id=1, source_target_pairs={{0,2},{1,3},{2,0},{3,1},{4,6},{5,7},{6,4},{7,5},{8,10},{9,11},{10,... | collective-permute-start | bytes 36872 | tf_op jit(solution)/shard_map/ppermute | solution.py:523

commit v9 on v8

--- a/solution.py
+++ b/solution.py
@@ -57,36 +57,26 @@
     return detune * inverse, -damping * inverse
 
 
-def masked_link(link2_ref, coupling_ref, mask_ref):
-    extent, rows = coupling_ref.shape[1:]
+def masked_link(coupling_ref, mask_ref):
+    _, rows = coupling_ref.shape[1:]
     count = mask_ref.shape[1]
     block = lax.broadcasted_iota(jnp.int32, (1, rows), 1) // (rows // count)
     keep = jnp.zeros((1, rows), f32)
     for index in range(count):
         keep = jnp.where(block == index, mask_ref[0, index].astype(f32), keep)
-    link = (coupling_ref[0].astype(f32) * keep).astype(bf16)
-    none = jnp.zeros_like(link)
-    link2_ref[0:extent, 0:rows] = link
-    link2_ref[0:extent, rows:] = none
-    link2_ref[extent:, 0:rows] = none
-    link2_ref[extent:, rows:] = link
+    return (coupling_ref[0].astype(f32) * keep).astype(bf16)
 
 
 def resolvents(overall, first, e, levels_ref, params_ref):
     return resolvent(levels_ref[...], params_ref[0, e : e + 1, :], params_ref[1, e : e + 1, :], first + e, overall)
 
 
+def both_scaled(x, dr, di, axis):
+    return jnp.concatenate([x * dr, x * di], axis=axis).astype(bf16)
+
+
 def maps_kernel(
-    overall,
-    one_ref,
-    two_ref,
-    modes_ref,
-    levels_ref,
-    params_ref,
-    left_ref,
-    free_ref,
-    out_ref,
-    message_ref,
+    overall, one_ref, two_ref, modes_ref, levels_ref, params_ref, mixed_ref, out_ref
 ):
     energies = params_ref.shape[2]
     extent = out_ref.shape[2]
@@ -94,59 +84,52 @@
     odd = jnp.bitwise_and(lax.axis_index("cell"), 1) == 1
     block = jnp.max(jnp.where(odd, two_ref[...], one_ref[...])).astype(jnp.int32)
     chosen = pl.multiple_of(block * extent, extent)
+    modes = modes_ref[0]
     rows = modes_ref[0, pl.ds(chosen, extent), :]
-    width = rows.shape[1]
     rows_f = rows.astype(f32)
     none = jnp.zeros_like(rows)
     rows2 = jnp.concatenate(
         [jnp.concatenate([rows, none], axis=1), jnp.concatenate([none, rows], axis=1)], axis=0
     )
-    maps = []
+    mixed = mixed_ref[...]
     for e in range(energies):
         dr, di = resolvents(overall, first, e, levels_ref, params_ref.at[0])
-        scaled = jnp.concatenate([(rows_f * dr).astype(bf16), (rows_f * di).astype(bf16)], axis=1)
-        free = free_ref[e, pl.ds(chosen, extent), :]
-        free_f = free.astype(f32)
+        free = dot_last(both_scaled(rows_f, dr, di, 0), modes)
+        re, im = free[:extent], free[extent:]
         weight = params_ref[0, 2, e : e + 1, :]
-        weighted = jnp.concatenate([free_f[:, :width] * weight, free_f[:, width:] * weight], axis=1)
-        turned = jnp.concatenate([-free_f[:, width:], free_f[:, :width]], axis=1)
-        maps.append(
-            (
-                left_ref[e, pl.ds(chosen, extent), :],
-                dot_last(scaled, rows2),
-                dot_last(weighted.astype(bf16), jnp.concatenate([free, turned.astype(bf16)], axis=0)),
-            )
-        )
-        for part in range(3):
-            out_ref[e, part] = maps[e][part].astype(bf16)
-    write_message(message_ref, maps)
-
-
-def make_rows(energies, hop, overall, share, modes_ref, levels_ref, params_ref, link2_ref, left_ref, local_ref, free_ref):
+        weighted = jnp.concatenate([re * weight, im * weight], axis=1).astype(bf16)
+        straight = jnp.concatenate([re, im], axis=1)
+        turned = jnp.concatenate([-im, re], axis=1)
+        out_ref[e, 0] = dot_last(rows, both_scaled(mixed, dr, di, 0)).astype(bf16)
+        out_ref[e, 1] = dot_last(both_scaled(rows_f, dr, di, 1), rows2).astype(bf16)
+        out_ref[e, 2] = dot_last(weighted, jnp.concatenate([straight, turned], axis=0).astype(bf16)).astype(bf16)
+
+
+def rows_kernel(overall, share, hop, slot, modes_ref, levels_ref, mixed_ref, params_ref, left_ref, local_ref):
+    energies = params_ref.shape[2]
     group = lax.axis_index("energy")
     first = jnp.bitwise_xor(group, hop) * energies
-    link2 = link2_ref[...]
     modes = modes_ref[0]
-    modes_f = modes.astype(f32)
+    mixed = mixed_ref[...]
     mine = pl.multiple_of(group * share, share)
     rows_f = modes_ref[0, pl.ds(mine, share), :].astype(f32)
-    for e in range(energies):
-        dr, di = resolvents(overall, first, e, levels_ref, params_ref)
-        free_re = dot_last((modes_f * dr).astype(bf16), modes)
-        free_im = dot_last((modes_f * di).astype(bf16), modes)
-        free = jnp.concatenate([free_re.astype(bf16), free_im.astype(bf16)], axis=1)
-        if free_ref is not None:
-            free_ref[e] = free
-        left_ref[e] = dot_last(free, link2).astype(bf16)
-        weight = params_ref[2, e : e + 1, :]
-        own = dot_last(jnp.concatenate([rows_f * dr, rows_f * di], axis=0).astype(bf16), modes) * weight
-        own_re, own_im = own[:share], own[share:]
-        own = jnp.concatenate(
-            [jnp.concatenate([own_re, own_im], axis=1), jnp.concatenate([own_im, -own_re], axis=1)], axis=0
-        )
-        local = dot_last(own.astype(bf16), free)
-        local_ref[e, 0] = local[:share].astype(bf16)
-        local_ref[e, 1] = local[share:].astype(bf16)
+    given = [resolvents(overall, first, e, levels_ref, params_ref.at[slot]) for e in range(energies)]
+    own = dot_last(jnp.concatenate([both_scaled(rows_f, dr, di, 0) for dr, di in given], axis=0), modes)
+    weighted = [
+        own[2 * share * e : 2 * share * (e + 1)] * params_ref[slot, 2, e : e + 1, :] for e in range(energies)
+    ]
+    back = dot_mat(jnp.concatenate(weighted, axis=0).astype(bf16), modes)
+    parts = []
+    for e, (dr, di) in enumerate(given):
+        re = back[2 * share * e : 2 * share * e + share]
+        im = back[2 * share * e + share : 2 * share * (e + 1)]
+        parts += [re * dr + im * di, im * dr - re * di]
+    local = dot_last(jnp.concatenate(parts, axis=0).astype(bf16), modes)
+    for e, (dr, di) in enumerate(given):
+        left_ref[e] = dot_last(modes, both_scaled(mixed, dr, di, 0)).astype(bf16)
+        for part in range(2):
+            start = (2 * e + part) * share
+            local_ref[e, part] = local[start : start + share].astype(bf16)
 
 
 def tile_kernel(interface_ref, block_ref):
@@ -162,7 +145,7 @@
     broad_hbm,
     inject_hbm,
     offsets_hbm,
-    link2_ref,
+    mixed_ref,
     modes_ref,
     levels_ref,
     params_ref,
@@ -190,45 +173,13 @@
         copy.start()
     for copy in copies:
         copy.wait()
-    masked_link(link2_ref, coupling_ref, mask_ref)
-
-
-def own_rows_kernel(overall, share, modes_ref, levels_ref, link2_ref, params_ref, left_ref, local_ref, free_ref):
-    make_rows(
-        params_ref.shape[2],
-        0,
-        overall,
-        share,
-        modes_ref,
-        levels_ref,
-        params_ref.at[0],
-        link2_ref,
-        left_ref,
-        local_ref,
-        free_ref,
-    )
+    mixed_ref[...] = dot_mat(masked_link(coupling_ref, mask_ref), modes_ref[0])
 
 
 def both_kernel(had_ref, got_ref, both_ref):
     count = had_ref.shape[0]
     both_ref[0:count] = had_ref[...]
     both_ref[count:] = got_ref[...]
-
-
-def rows_kernel(overall, share, hop, slot, modes_ref, levels_ref, link2_ref, got_ref, left_ref, local_ref):
-    make_rows(
-        got_ref.shape[2],
-        hop,
-        overall,
-        share,
-        modes_ref,
-        levels_ref,
-        got_ref.at[slot],
-        link2_ref,
-        left_ref,
-        local_ref,
-        None,
-    )
 
 
 spare = 16
@@ -292,6 +243,12 @@
             ref[pair, 3 * extent + spare :] = second[0].astype(bf16)
 
 
+def read_maps(ref):
+    if len(ref.shape) == 4:
+        return [read(ref, e) for e in range(ref.shape[0])]
+    return read_message(ref)
+
+
 def read_message(ref):
     extent = ref.shape[2] // 2
     maps = []
@@ -344,7 +301,7 @@
 
 def join_kernel(level, total_ref, other_ref, message_ref, *new_total_ref):
     upper = upper_half(level)
-    others = read_message(other_ref)
+    others = read_maps(other_ref)
     joined = []
     for e in range(total_ref.shape[0]):
         total, other = read(total_ref, e), others[e]
@@ -358,7 +315,7 @@
 
 def enter_kernel(level, other_ref, *refs):
     upper = upper_half(level)
-    others = read_message(other_ref)
+    others = read_maps(other_ref)
     out_ref = refs[-1]
     for e in range(out_ref.shape[0]):
         if level:
@@ -535,10 +492,10 @@
     route = [(i * groups + g, mate[i] * groups + (g ^ int(mate[i] == i))) for i in range(cells) for g in range(groups)]
     two = lax.ppermute(block, ("cell", "energy"), route)
 
-    link2, modes, levels, params, offsets = call(
+    mixed, modes, levels, params, offsets = call(
         front_kernel,
         (
-            sds((width, 2 * orbitals), bf16),
+            sds((extent, orbitals), f32),
             sds(modes.shape, bf16),
             sds(levels.shape, f32),
             sds((1, 3, energies, orbitals), f32),
@@ -554,18 +511,13 @@
     left_shape = sds((energies, orbitals, width), bf16)
     local_shape = sds((energies, 2, share, orbitals), bf16)
     params_shape = (3, energies, orbitals)
-    left, local, free = call(
-        partial(own_rows_kernel, overall, share),
-        (left_shape, local_shape, sds((energies, orbitals, 2 * orbitals), bf16)),
-        [VMEM] * 4,
-    )(modes, levels, link2, params)
+    left, local = call(partial(rows_kernel, overall, share, 0, 0), (left_shape, local_shape), [VMEM] * 4)(
+        modes, levels, mixed, params
+    )
     lefts, locals_ = [left], [local]
 
-    total, sent = call(
-        partial(maps_kernel, overall),
-        (maps_shape, message),
-        [VMEM] * 7,
-    )(one, two, modes, levels, params, left, free)
+    total = call(partial(maps_kernel, overall), maps_shape, [VMEM] * 6)(one, two, modes, levels, params, mixed)
+    sent = total
     reach = overall // 4
     sums_shape = sds((3, overall + 2 * reach, share, orbitals), f32)
     sigma_shape = sds((1, 2, overall, share, orbitals), bf16)
@@ -583,7 +535,7 @@
         for slot in range(count):
             left, local = call(
                 partial(rows_kernel, overall, share, count + slot, slot), (left_shape, local_shape), [VMEM] * 4
-            )(modes, levels, link2, got)
+            )(modes, levels, mixed, got)
             lefts.append(left)
             locals_.append(local)
         if 2 * count >= groups:

time: 33.9 us -> 33.1 us (0.976)
  Pallas kernels: 13.1 us -> 12 us
  starting transfers between devices: 14.2 us -> 14.8 us
    pallas_call x3, Pallas kernels: 2.48 us -> 1.71 us  [body(): call(partial(rows_kernel, overall, share, count + slot, slot), (left_shap...]
    ppermute x9, waiting for transfers between devices: 4.91 us -> 4.32 us  [swapped(): lax.ppermute(x, axis, [(i, i ^ distance) for i in range(lax.axis_size(axi...]
    ppermute x9, starting transfers between devices: 11.6 us -> 12.2 us  [swapped(): lax.ppermute(x, axis, [(i, i ^ distance) for i in range(lax.axis_size(axi...]
  transfers between devices with their start and end apart: 10 -> 10, of which waited for: 3 -> 4; matrix products, arithmetic and copies ran while one was open for 0% -> 0% of each run, Pallas kernels for 28% -> 26%
where the time goes in v9:
time: 33.1 us; the launch traced here: 32.9 us
  starting transfers between devices  14.8 us (45%)
  Pallas kernels  12 us (36%)
  waiting for transfers between devices  4.67 us (14%)
  between operations  1.48 us (4%)
    ppermute x9, starting transfers between devices, swapped(): lax.ppermute(x, axis, [(i, i ^ distance) for i in range(lax.axis_size(axi...  12.2 us
    pallas_call x4, Pallas kernels, body(): call(partial(convolve_kernel, reach, hop, last), outs, [VMEM] * len(given...  5.09 us
    ppermute x9, waiting for transfers between devices, swapped(): lax.ppermute(x, axis, [(i, i ^ distance) for i in range(lax.axis_size(axi...  4.32 us
    ppermute x1, starting transfers between devices, body(): two = lax.ppermute(block, ('cell', 'energy'), route)  2.55 us
    pallas_call x3, Pallas kernels, body(): call(partial(rows_kernel, overall, share, count + slot, slot), (left_shap...  1.71 us
    pallas_call x2, Pallas kernels, body(): call(partial(join_kernel, level), outs, [VMEM] * 2)(total, other)  1.24 us
    pallas_call x1, Pallas kernels, body(): call(front_kernel, (sds((extent, orbitals), f32), sds(modes.shape, bf16),...  1.23 us
    pallas_call x1, Pallas kernels, body(): call(partial(arrive_kernel, rounds - 1), (sds((energies, extent, width),...  0.69 us
  transfers between devices with their start and end apart: 10, of which 4 were waited for; matrix products, arithmetic and copies ran while one was open for 0% of the time, Pallas kernels for 26%

profile of v9, /device:TPU:0, one launch (start us, length us, event | category | flops | bytes accessed | tf_op | source)
XLA Modules:
  0.0 32.9 jit_solution(12221231090755158266)
XLA Ops:
  1.4 0.6 %collective-permute-start = (f32[8,128]{1,0:T(8,128)S(1)}, f32[8,128]{1,0:T(8,128)S(1)}, u32[]{:S(2)}, u32[]{:S(2)}) collective-permute-start(f32[8,128]{1,0:T(8,128)S(1)} %shard_map.114), channel_id=1, source_target_pairs={{0,4},{4,0},{8,12},{12,8},{16,20},{20,16},{24,28},{28,24},{1,5},{5... | collective-permute-start | bytes 12296 | tf_op jit(solution)/shard_map/ppermute | solution.py:480
  1.9 2.6 %collective-permute-start.1 = (f32[8,128]{1,0:T(8,128)S(1)}, f32[8,128]{1,0:T(8,128)S(1)}, u32[]{:S(2)}, u32[]{:S(2)}) collective-permute-start(f32[8,128]{1,0:T(8,128)S(1)} %shard_map.114), channel_id=1, source_target_pairs={{0,1},{1,0},{2,3},{3,2},{4,8},{5,9},{6,10},{7,11},{8,4},{9,5},{10,... | collective-permute-start | bytes 12296 | tf_op jit(solution)/shard_map/ppermute | solution.py:493
  4.5 1.2 %shard_map.113 = (f32[64,256]{1,0:T(8,128)S(1)}, bf16[1,256,256]{2,1,0:T(8,128)(2,1)S(1)}, f32[1,256]{1,0:T(1,128)S(1)}, f32[1,3,2,256]{3,2,1,0:T(2,128)S(1)}, s32[8]{0:T(128)S(1)}) custom-call(s32[1,4]{1,0:T(1,128)} %mask_hbm.1, bf16[1,256,256]{2,1,0:T(8,128)(2,1)} %modes_hbm.1, f32[1,256]{1,0:T(1,128)} %levels_hbm.1, bf16[1,64,256]{2,1,0:T(8,128)(2,1)} %bitcast.1, ...), custom_call_target="tpu_custom_call" | custom-call | flops 1000000 | bytes 1000000 | tf_op jit(solution)/shard_map/pallas_call | solution.py:495
  6.1 0.6 %shard_map.115.total_ref = bf16[2,3,64,128]{3,2,1,0:T(8,128)(2,1)S(1)} custom-call(f32[8,128]{1,0:T(8,128)S(1)} %collective-permute-done.one_ref, f32[8,128]{1,0:T(8,128)S(1)} %collective-permute-done.1.two_ref, bf16[1,256,256]{2,1,0:T(8,128)(2,1)S(1)} %get-tuple-element.25.modes_ref, f32[1,256]{1,0:T(1,128)S(1)} %get-tuple-element.26.levels_ref, ...), custom_call_target="tpu_custom_call" | custom-call | flops 1000000 | bytes 1000000 | tf_op jit(solution)/shard_map/pallas_call | solution.py:519
  6.8 1.2 %collective-permute-done.2.other_ref = bf16[2,3,64,128]{3,2,1,0:T(8,128)(2,1)S(1)} collective-permute-done((bf16[2,3,64,128]{3,2,1,0:T(8,128)(2,1)S(1)}, bf16[2,3,64,128]{3,2,1,0:T(8,128)(2,1)S(1)}, u32[]{:S(2)}, u32[]{:S(2)}) %collective-permute-start.2) | collective-permute-done | bytes 98336 | tf_op jit(solution)/shard_map/ppermute | solution.py:480
  8.0 0.5 %shard_map.116 = (bf16[1,272,128]{2,1,0:T(8,128)(2,1)S(1)}, bf16[2,3,64,128]{3,2,1,0:T(8,128)(2,1)S(1)}) custom-call(bf16[2,3,64,128]{3,2,1,0:T(8,128)(2,1)S(1)} %shard_map.115.total_ref, bf16[2,3,64,128]{3,2,1,0:T(8,128)(2,1)S(1)} %collective-permute-done.2.other_ref), custom_call_target="tpu_custom_call" | custom-call | flops 1000000 | bytes 1000000 | tf_op jit(solution)/shard_map/pallas_call | solution.py:548
  8.6 1.7 %collective-permute-start.3 = (bf16[1,272,128]{2,1,0:T(8,128)(2,1)S(1)}, bf16[1,272,128]{2,1,0:T(8,128)(2,1)S(1)}, u32[]{:S(2)}, u32[]{:S(2)}) collective-permute-start(bf16[1,272,128]{2,1,0:T(8,128)(2,1)S(1)} %get-tuple-element.29), channel_id=1, source_target_pairs={{0,8},{4,12},{8,0},{12,4},{16,24},{20,28},{24,16},{28,20},{1,9},{5... | collective-permute-start | bytes 208904 | tf_op jit(solution)/shard_map/ppermute | solution.py:480
  10.2 2.7 %collective-permute-done.3.other_ref = bf16[1,272,128]{2,1,0:T(8,128)(2,1)S(1)} collective-permute-done((bf16[1,272,128]{2,1,0:T(8,128)(2,1)S(1)}, bf16[1,272,128]{2,1,0:T(8,128)(2,1)S(1)}, u32[]{:S(2)}, u32[]{:S(2)}) %collective-permute-start.3) | collective-permute-done | bytes 69664 | tf_op jit(solution)/shard_map/ppermute | solution.py:480
  12.9 0.7 %shard_map.119 = bf16[1,144,128]{2,1,0:T(8,128)(2,1)S(1)} custom-call(bf16[2,3,64,128]{3,2,1,0:T(8,128)(2,1)S(1)} %get-tuple-element.30.total_ref, bf16[1,272,128]{2,1,0:T(8,128)(2,1)S(1)} %collective-permute-done.3.other_ref), custom_call_target="tpu_custom_call" | custom-call | flops 1000000 | bytes 1000000 | tf_op jit(solution)/shard_map/pallas_call | solution.py:548
  13.6 2.8 %collective-permute-start.4 = (bf16[1,144,128]{2,1,0:T(8,128)(2,1)S(1)}, bf16[1,144,128]{2,1,0:T(8,128)(2,1)S(1)}, u32[]{:S(2)}, u32[]{:S(2)}) collective-permute-start(bf16[1,144,128]{2,1,0:T(8,128)(2,1)S(1)} %shard_map.119), channel_id=1, source_target_pairs={{0,16},{4,20},{8,24},{12,28},{16,0},{20,4},{24,8},{28,12},{1,17},{... | collective-permute-start | bytes 110600 | tf_op jit(solution)/shard_map/ppermute | solution.py:480
  16.5 1.5 %collective-permute-start.6 = (f32[1,3,2,256]{3,2,1,0:T(2,128)S(1)}, f32[1,3,2,256]{3,2,1,0:T(2,128)S(1)}, u32[]{:S(2)}, u32[]{:S(2)}) collective-permute-start(f32[1,3,2,256]{3,2,1,0:T(2,128)S(1)} %get-tuple-element.27.params_ref.had_ref), channel_id=1, source_target_pairs={{0,1},{1,0},{2,3},{3,2},{4,5},{5,4},{6,7},{7,6},{8,9},{9,8},{10,11... | collective-permute-start | bytes 18440 | tf_op jit(solution)/shard_map/ppermute | solution.py:480
  18.0 0.6 %shard_map.118.enter_ref = bf16[2,3,64,128]{3,2,1,0:T(8,128)(2,1)S(1)} custom-call(bf16[1,272,128]{2,1,0:T(8,128)(2,1)S(1)} %collective-permute-done.3.other_ref, bf16[2,3,64,128]{3,2,1,0:T(8,128)(2,1)S(1)} %shard_map.117.refs_0_), custom_call_target="tpu_custom_call" | custom-call | flops 1000000 | bytes 1000000 | tf_op jit(solution)/shard_map/pallas_call | solution.py:551
  18.7 0.7 %shard_map.120 = (bf16[2,64,128]{2,1,0:T(8,128)(2,1)S(1)}, bf16[1,64,128]{2,1,0:T(8,128)(2,1)S(1)}) custom-call(bf16[2,3,64,128]{3,2,1,0:T(8,128)(2,1)S(1)} %shard_map.118.enter_ref, bf16[1,144,128]{2,1,0:T(8,128)(2,1)S(1)} %collective-permute-done.4.state_ref), custom_call_target="tpu_custom_call" | custom-call | flops 1000000 | bytes 1000000 | tf_op jit(solution)/shard_map/pallas_call | solution.py:553
  19.4 2.0 %collective-permute-start.9 = (bf16[1,64,128]{2,1,0:T(8,128)(2,1)S(1)}, bf16[1,64,128]{2,1,0:T(8,128)(2,1)S(1)}, u32[]{:S(2)}, u32[]{:S(2)}) collective-permute-start(bf16[1,64,128]{2,1,0:T(8,128)(2,1)S(1)} %get-tuple-element.31.lesser_ref), channel_id=1, source_target_pairs={{0,1},{1,0},{2,3},{3,2},{4,5},{5,4},{6,7},{7,6},{8,9},{9,8},{10,11... | collective-permute-start | bytes 49160 | tf_op jit(solution)/shard_map/ppermute | solution.py:480
  21.3 1.5 %collective-permute-start.8 = (bf16[1,64,128]{2,1,0:T(8,128)(2,1)S(1)}, bf16[1,64,128]{2,1,0:T(8,128)(2,1)S(1)}, u32[]{:S(2)}, u32[]{:S(2)}) collective-permute-start(bf16[1,64,128]{2,1,0:T(8,128)(2,1)S(1)} %get-tuple-element.31.lesser_ref), channel_id=1, source_target_pairs={{0,2},{1,3},{2,0},{3,1},{4,6},{5,7},{6,4},{7,5},{8,10},{9,11},{10,... | collective-permute-start | bytes 49160 | tf_op jit(solution)/shard_map/ppermute | solution.py:480
  22.9 2.0 %collective-permute-start.7 = (f32[2,3,2,256]{3,2,1,0:T(2,128)S(1)}, f32[2,3,2,256]{3,2,1,0:T(2,128)S(1)}, u32[]{:S(2)}, u32[]{:S(2)}) collective-permute-start(f32[2,3,2,256]{3,2,1,0:T(2,128)S(1)} %shard_map.124), channel_id=1, source_target_pairs={{0,2},{1,3},{2,0},{3,1},{4,6},{5,7},{6,4},{7,5},{8,10},{9,11},{10,... | collective-permute-start | bytes 36872 | tf_op jit(solution)/shard_map/ppermute | solution.py:480
  24.9 0.6 %shard_map.121 = (bf16[2,256,128]{2,1,0:T(8,128)(2,1)S(1)}, bf16[2,2,64,256]{3,2,1,0:T(8,128)(2,1)S(1)}) custom-call(bf16[1,256,256]{2,1,0:T(8,128)(2,1)S(1)} %get-tuple-element.25.modes_ref, f32[1,256]{1,0:T(1,128)S(1)} %get-tuple-element.26.levels_ref, f32[64,256]{1,0:T(8,128)S(1)} %get-tuple-element.28.mixed_ref, ...), custom_call_target="tpu_custom_call" | custom-call | flops 1000000 | bytes 1000000 | tf_op jit(solution)/shard_map/pallas_call | solution.py:514
  25.7 0.6 %shard_map.127 = (bf16[2,256,128]{2,1,0:T(8,128)(2,1)S(1)}, bf16[2,2,64,256]{3,2,1,0:T(8,128)(2,1)S(1)}) custom-call(bf16[1,256,256]{2,1,0:T(8,128)(2,1)S(1)} %get-tuple-element.25.modes_ref, f32[1,256]{1,0:T(1,128)S(1)} %get-tuple-element.26.levels_ref, f32[64,256]{1,0:T(8,128)S(1)} %get-tuple-element.28.mixed_ref, ...), custom_call_target="tpu_custom_call" | custom-call | flops 1000000 | bytes 1000000 | tf_op jit(solution)/shard_map/pallas_call | solution.py:536
  26.6 0.6 %shard_map.126 = (bf16[2,256,128]{2,1,0:T(8,128)(2,1)S(1)}, bf16[2,2,64,256]{3,2,1,0:T(8,128)(2,1)S(1)}) custom-call(bf16[1,256,256]{2,1,0:T(8,128)(2,1)S(1)} %get-tuple-element.25.modes_ref, f32[1,256]{1,0:T(1,128)S(1)} %get-tuple-element.26.levels_ref, f32[64,256]{1,0:T(8,128)S(1)} %get-tuple-element.28.mixed_ref, ...), custom_call_target="tpu_custom_call" | custom-call | flops 1000000 | bytes 1000000 | tf_op jit(solution)/shard_map/pallas_call | solution.py:536
  27.2 0.6 %shard_map.125 = (bf16[2,256,128]{2,1,0:T(8,128)(2,1)S(1)}, bf16[2,2,64,256]{3,2,1,0:T(8,128)(2,1)S(1)}) custom-call(bf16[1,256,256]{2,1,0:T(8,128)(2,1)S(1)} %get-tuple-element.25.modes_ref, f32[1,256]{1,0:T(1,128)S(1)} %get-tuple-element.26.levels_ref, f32[64,256]{1,0:T(8,128)S(1)} %get-tuple-element.28.mixed_ref, ...), custom_call_target="tpu_custom_call" | custom-call | flops 1000000 | bytes 1000000 | tf_op jit(solution)/shard_map/pallas_call | solution.py:536
  27.8 1.4 %shard_map.123 = (f32[3,12,64,256]{3,2,1,0:T(8,128)S(1)}, f32[1,2,256]{2,1,0:T(2,128)}) custom-call(s32[8]{0:T(128)S(1)} %get-tuple-element.24.offsets_ref, bf16[1,2,8,64,256]{4,3,2,1,0:T(8,128)(2,1)S(1)} %copy-done, bf16[1,64,128]{2,1,0:T(8,128)(2,1)S(1)} %get-tuple-element.31.lesser_ref, ...), custom_call_target="tpu_custom_call", output_to_operand_aliasing={{0}: (5, {})} | custom-call | flops 1000000 | bytes 1000000 | tf_op jit(solution)/shard_map/pallas_call | solution.py:577
  29.3 1.0 %shard_map.128._ = f32[3,12,64,256]{3,2,1,0:T(8,128)S(1)} custom-call(s32[8]{0:T(128)S(1)} %get-tuple-element.24.offsets_ref, bf16[1,2,8,64,256]{4,3,2,1,0:T(8,128)(2,1)S(1)} %copy-done, bf16[1,64,128]{2,1,0:T(8,128)(2,1)S(1)} %collective-permute-done.9.lesser_ref, ...), custom_call_target="tpu_custom_call", output_to_operand_aliasing={{}: (5, {})} | custom-call | flops 1000000 | bytes 1000000 | tf_op jit(solution)/shard_map/pallas_call | solution.py:577
  30.2 1.0 %shard_map.129._ = f32[3,12,64,256]{3,2,1,0:T(8,128)S(1)} custom-call(s32[8]{0:T(128)S(1)} %get-tuple-element.24.offsets_ref, bf16[1,2,8,64,256]{4,3,2,1,0:T(8,128)(2,1)S(1)} %copy-done, bf16[1,64,128]{2,1,0:T(8,128)(2,1)S(1)} %collective-permute-done.8.lesser_ref, ...), custom_call_target="tpu_custom_call", output_to_operand_aliasing={{}: (5, {})} | custom-call | flops 1000000 | bytes 1000000 | tf_op jit(solution)/shard_map/pallas_call | solution.py:577
  31.2 1.7 %shard_map.130 = (f32[3,12,64,256]{3,2,1,0:T(8,128)S(1)}, bf16[1,2,8,64,256]{4,3,2,1,0:T(8,128)(2,1)}) custom-call(s32[8]{0:T(128)S(1)} %get-tuple-element.24.offsets_ref, bf16[1,2,8,64,256]{4,3,2,1,0:T(8,128)(2,1)S(1)} %copy-done, bf16[1,64,128]{2,1,0:T(8,128)(2,1)S(1)} %collective-permute-done.5.lesser_ref, ...), custom_call_target="tpu_custom_call", output_to_operand_aliasing={{0}: (5, {})} | custom-call | flops 1000000 | bytes 1000000 | tf_op jit(solution)/shard_map/pallas_call | solution.py:577
  (16 shorter events, 1.3 us)
Async XLA Ops:
  0.6 27.2 %copy-start = (bf16[1,2,8,64,256]{4,3,2,1,0:T(8,128)(2,1)S(1)}, bf16[1,2,8,64,256]{4,3,2,1,0:T(8,128)(2,1)}, u32[]{:S(2)}) copy-start(bf16[1,2,8,64,256]{4,3,2,1,0:T(8,128)(2,1)} %screen_ref.7) | copy-start | bytes 1572868
  1.4 4.3 %collective-permute-start = (f32[8,128]{1,0:T(8,128)S(1)}, f32[8,128]{1,0:T(8,128)S(1)}, u32[]{:S(2)}, u32[]{:S(2)}) collective-permute-start(f32[8,128]{1,0:T(8,128)S(1)} %shard_map.114), channel_id=1, source_target_pairs={{0,4},{4,0},{8,12},{12,8},{16,20},{20,16},{24,28},{28,24},{1,5},{5... | collective-permute-start | bytes 12296 | tf_op jit(solution)/shard_map/ppermute | solution.py:480
  1.9 4.1 %collective-permute-start.1 = (f32[8,128]{1,0:T(8,128)S(1)}, f32[8,128]{1,0:T(8,128)S(1)}, u32[]{:S(2)}, u32[]{:S(2)}) collective-permute-start(f32[8,128]{1,0:T(8,128)S(1)} %shard_map.114), channel_id=1, source_target_pairs={{0,1},{1,0},{2,3},{3,2},{4,8},{5,9},{6,10},{7,11},{8,4},{9,5},{10,... | collective-permute-start | bytes 12296 | tf_op jit(solution)/shard_map/ppermute | solution.py:493
  6.6 1.4 %collective-permute-start.2 = (bf16[2,3,64,128]{3,2,1,0:T(8,128)(2,1)S(1)}, bf16[2,3,64,128]{3,2,1,0:T(8,128)(2,1)S(1)}, u32[]{:S(2)}, u32[]{:S(2)}) collective-permute-start(bf16[2,3,64,128]{3,2,1,0:T(8,128)(2,1)S(1)} %shard_map.115.total_ref), channel_id=1, source_target_pairs={{0,4},{4,0},{8,12},{12,8},{16,20},{20,16},{24,28},{28,24},{1,5},{5... | collective-permute-start | bytes 294920 | tf_op jit(solution)/shard_map/ppermute | solution.py:480
  8.6 4.4 %collective-permute-start.3 = (bf16[1,272,128]{2,1,0:T(8,128)(2,1)S(1)}, bf16[1,272,128]{2,1,0:T(8,128)(2,1)S(1)}, u32[]{:S(2)}, u32[]{:S(2)}) collective-permute-start(bf16[1,272,128]{2,1,0:T(8,128)(2,1)S(1)} %get-tuple-element.29), channel_id=1, source_target_pairs={{0,8},{4,12},{8,0},{12,4},{16,24},{20,28},{24,16},{28,20},{1,9},{5... | collective-permute-start | bytes 208904 | tf_op jit(solution)/shard_map/ppermute | solution.py:480
  13.6 5.0 %collective-permute-start.4 = (bf16[1,144,128]{2,1,0:T(8,128)(2,1)S(1)}, bf16[1,144,128]{2,1,0:T(8,128)(2,1)S(1)}, u32[]{:S(2)}, u32[]{:S(2)}) collective-permute-start(bf16[1,144,128]{2,1,0:T(8,128)(2,1)S(1)} %shard_map.119), channel_id=1, source_target_pairs={{0,16},{4,20},{8,24},{12,28},{16,0},{20,4},{24,8},{28,12},{1,17},{... | collective-permute-start | bytes 110600 | tf_op jit(solution)/shard_map/ppermute | solution.py:480
  16.5 6.5 %collective-permute-start.6 = (f32[1,3,2,256]{3,2,1,0:T(2,128)S(1)}, f32[1,3,2,256]{3,2,1,0:T(2,128)S(1)}, u32[]{:S(2)}, u32[]{:S(2)}) collective-permute-start(f32[1,3,2,256]{3,2,1,0:T(2,128)S(1)} %get-tuple-element.27.params_ref.had_ref), channel_id=1, source_target_pairs={{0,1},{1,0},{2,3},{3,2},{4,5},{5,4},{6,7},{7,6},{8,9},{9,8},{10,11... | collective-permute-start | bytes 18440 | tf_op jit(solution)/shard_map/ppermute | solution.py:480
  19.4 9.9 %collective-permute-start.9 = (bf16[1,64,128]{2,1,0:T(8,128)(2,1)S(1)}, bf16[1,64,128]{2,1,0:T(8,128)(2,1)S(1)}, u32[]{:S(2)}, u32[]{:S(2)}) collective-permute-start(bf16[1,64,128]{2,1,0:T(8,128)(2,1)S(1)} %get-tuple-element.31.lesser_ref), channel_id=1, source_target_pairs={{0,1},{1,0},{2,3},{3,2},{4,5},{5,4},{6,7},{7,6},{8,9},{9,8},{10,11... | collective-permute-start | bytes 49160 | tf_op jit(solution)/shard_map/ppermute | solution.py:480
  21.3 8.9 %collective-permute-start.8 = (bf16[1,64,128]{2,1,0:T(8,128)(2,1)S(1)}, bf16[1,64,128]{2,1,0:T(8,128)(2,1)S(1)}, u32[]{:S(2)}, u32[]{:S(2)}) collective-permute-start(bf16[1,64,128]{2,1,0:T(8,128)(2,1)S(1)} %get-tuple-element.31.lesser_ref), channel_id=1, source_target_pairs={{0,2},{1,3},{2,0},{3,1},{4,6},{5,7},{6,4},{7,5},{8,10},{9,11},{10,... | collective-permute-start | bytes 49160 | tf_op jit(solution)/shard_map/ppermute | solution.py:480
  22.9 8.3 %collective-permute-start.5 = (bf16[1,64,128]{2,1,0:T(8,128)(2,1)S(1)}, bf16[1,64,128]{2,1,0:T(8,128)(2,1)S(1)}, u32[]{:S(2)}, u32[]{:S(2)}) collective-permute-start(bf16[1,64,128]{2,1,0:T(8,128)(2,1)S(1)} %get-tuple-element.31.lesser_ref), channel_id=1, source_target_pairs={{0,3},{1,2},{2,1},{3,0},{4,7},{5,6},{6,5},{7,4},{8,11},{9,10},{10,... | collective-permute-start | bytes 49160 | tf_op jit(solution)/shard_map/ppermute | solution.py:480
  22.9 3.7 %collective-permute-start.7 = (f32[2,3,2,256]{3,2,1,0:T(2,128)S(1)}, f32[2,3,2,256]{3,2,1,0:T(2,128)S(1)}, u32[]{:S(2)}, u32[]{:S(2)}) collective-permute-start(f32[2,3,2,256]{3,2,1,0:T(2,128)S(1)} %shard_map.124), channel_id=1, source_target_pairs={{0,2},{1,3},{2,0},{3,1},{4,6},{5,7},{6,4},{7,5},{8,10},{9,11},{10,... | collective-permute-start | bytes 36872 | tf_op jit(solution)/shard_map/ppermute | solution.py:480

commit v10 on v9

--- a/solution.py
+++ b/solution.py
@@ -213,6 +213,19 @@
     )
 
 
+def unpack_full_lesser(packed):
+    packed = packed.astype(f32)
+    extent, width = packed.shape
+    _, _, low = places(extent, width)
+    square, turned = with_turned(packed)
+    total, change = 0.5 * (square + turned), 0.5 * (square - turned)
+    upper, lower = (total[:extent], change[:extent]), (total[extent:], change[extent:])
+    return tuple(
+        jnp.concatenate([jnp.where(low, a[0], b[1]), jnp.where(low, -a[1], b[0])], axis=0).astype(bf16)
+        for a, b in ((upper, lower), (lower, upper))
+    )
+
+
 def pack_retarded(first, second):
     row, column, _ = places(*first.shape)
     diagonal = jnp.sum(jnp.where(row == column, second, 0.0), axis=0, keepdims=True)
@@ -299,17 +312,41 @@
     return jnp.bitwise_and(jnp.right_shift(lax.axis_index("cell"), level), 1) == 1
 
 
-def join_kernel(level, total_ref, other_ref, message_ref, *new_total_ref):
+def join_kernel(level, total_ref, other_ref, message_ref, new_total_ref):
     upper = upper_half(level)
     others = read_maps(other_ref)
     joined = []
     for e in range(total_ref.shape[0]):
         total, other = read(total_ref, e), others[e]
-        pair = pick(upper, other, total), pick(upper, total, other)
-        joined.append(compose(*pair) if new_total_ref else moved(pair[1], pair[0][1:]))
-        for ref in new_total_ref:
-            for part in range(3):
-                ref[e, part] = joined[e][part].astype(bf16)
+        joined.append(compose(pick(upper, other, total), pick(upper, total, other)))
+        for part in range(3):
+            new_total_ref[e, part] = joined[e][part].astype(bf16)
+    write_message(message_ref, joined)
+
+
+def last_join_kernel(level, total_ref, other_ref, message_ref):
+    upper = upper_half(level)
+    extent = total_ref.shape[2]
+    joined = []
+    for pair in range(message_ref.shape[0]):
+        fulls = (
+            unpack_full_retarded(
+                other_ref[pair, 0:extent], other_ref[pair, 2 * extent : 2 * extent + 1]
+            ),
+            unpack_full_lesser(other_ref[pair, extent : 2 * extent]),
+        )
+        for which in range(2):
+            e = 2 * pair + which
+            start = (2 + which) * extent + spare
+            step = jnp.where(upper, total_ref[e, 0], other_ref[pair, start : start + extent])
+            sums = []
+            for part, turn in ((1, full_conj), (2, full)):
+                other = fulls[part - 1][which]
+                own = total_ref[e, part]
+                before = jnp.where(upper, other, full(own))
+                after = jnp.where(upper, own, other[:extent]).astype(f32)
+                sums.append(after + dot_last(dot_mat(step, before).astype(bf16), turn(step)))
+            joined.append(sums)
     write_message(message_ref, joined)
 
 
@@ -327,23 +364,44 @@
             out_ref[e, part] = new[part]
 
 
-def moved(step, state):
-    retarded, lesser = pushed(step, state)
-    return step[1].astype(f32) + retarded, step[2].astype(f32) + lesser
+def unpack_full_retarded(packed, diagonal):
+    packed, diagonal = packed.astype(f32), diagonal.astype(f32)
+    extent, width = packed.shape
+    row, column, low = places(extent, width)
+    square, turned = with_turned(packed)
+    swapped_diagonal = swap_halves(jnp.broadcast_to(diagonal, (8, width)))[0:1]
+    first = [jnp.where(row <= column, square[k : k + extent], turned[:extent] if k == 0 else turned[extent:]) for k in (0, extent)]
+    second = [
+        jnp.where(
+            row > column,
+            square[k : k + extent],
+            jnp.where(row == column, diagonal if k == 0 else swapped_diagonal, turned[:extent] if k == 0 else turned[extent:]),
+        )
+        for k in (0, extent)
+    ]
+    return tuple(
+        jnp.concatenate([top, jnp.where(low, -bottom, bottom)], axis=0).astype(bf16) for top, bottom in (first, second)
+    )
 
 
 def arrive_kernel(level, enter_ref, state_ref, retarded_ref, lesser_ref):
     upper = jnp.right_shift(lax.axis_index("cell"), level) == 1
-    states = read_message(state_ref)
-    lessers = []
-    for e in range(enter_ref.shape[0]):
-        enter = read(enter_ref, e)
-        state = pick(upper, states[e], (jnp.zeros_like(enter[1]), jnp.zeros_like(enter[2])))
-        retarded, lesser = pushed(enter, state)
-        retarded_ref[e] = (enter[1].astype(f32) + retarded).astype(bf16)
-        lessers.append(enter[2].astype(f32) + lesser)
+    extent = enter_ref.shape[2]
     for pair in range(lesser_ref.shape[0]):
-        lesser_ref[pair] = pack_lesser(lessers[2 * pair], lessers[2 * pair + 1]).astype(bf16)
+        both = unpack_full_lesser(state_ref[pair, extent : 2 * extent])
+        lessers = []
+        for e in (2 * pair, 2 * pair + 1):
+            step = enter_ref[e, 0]
+            state = jnp.where(upper, both[e % 2], jnp.zeros_like(both[0]))
+            middle = dot_mat(step, state).astype(bf16)
+            lessers.append(enter_ref[e, 2].astype(f32) + dot_last(middle, full(step)))
+        lesser_ref[pair] = pack_lesser(*lessers).astype(bf16)
+        both = unpack_full_retarded(state_ref[pair, 0:extent], state_ref[pair, 2 * extent : 2 * extent + 1])
+        for e in (2 * pair, 2 * pair + 1):
+            step = enter_ref[e, 0]
+            state = jnp.where(upper, both[e % 2], jnp.zeros_like(both[0]))
+            middle = dot_mat(step, state).astype(bf16)
+            retarded_ref[e] = (enter_ref[e, 1].astype(f32) + dot_last(middle, full_conj(step))).astype(bf16)
 
 
 def row_sums(x):
@@ -389,10 +447,10 @@
     mine = pl.multiple_of(group * share, share)
     base = jnp.bitwise_xor(group, hop) * energies + reach
     for pair in range(energies // 2):
-        states = unpack_lesser(lesser_ref[pair])
+        states = unpack_full_lesser(lesser_ref[pair])
         for e in (2 * pair, 2 * pair + 1):
             own = left_ref[e, pl.ds(mine, share), :]
-            pl_hat = dot_mat(own, full(states[e - 2 * pair]))
+            pl_hat = dot_mat(own, states[e - 2 * pair])
             turned = swap_halves(pl_hat) * signs(pl_hat.shape[1], 1.0)
             chain = dot_last(jnp.concatenate([pl_hat, turned], axis=0).astype(bf16), left_ref[e])
             re = chain[:share] + local_ref[e, 0].astype(f32)
@@ -468,7 +526,7 @@
     cells = lax.axis_size("cell")
     groups = lax.axis_size("energy")
     rounds = cells.bit_length() - 1
-    assert cells == 1 << rounds and groups & (groups - 1) == 0
+    assert cells == 1 << rounds and rounds > 2 and groups & (groups - 1) == 0
     energies = level_shift.shape[1]
     overall = energies * groups
     orbitals, extent = coupling.shape[1:]
@@ -544,8 +602,11 @@
     enter = None
     for level in range(rounds - 1):
         other = swapped(sent, "cell", 1 << level)
-        outs = (message, maps_shape) if level < rounds - 2 else (state_message,)
-        sent, *rest = call(partial(join_kernel, level), outs, [VMEM] * 2)(total, other)
+        if level < rounds - 2:
+            kernel, outs = join_kernel, (message, maps_shape)
+        else:
+            kernel, outs = last_join_kernel, (state_message,)
+        sent, *rest = call(partial(kernel, level), outs, [VMEM] * 2)(total, other)
         total = rest[0] if rest else None
         given = (other, enter) if level else (other,)
         enter = call(partial(enter_kernel, level), maps_shape, [VMEM] * len(given))(*given)
@@ -564,8 +625,9 @@
         pltpu.SMEM(offsets.shape, jnp.int32),
         pltpu.SemaphoreType.DMA,
     ]
-    for hop in range(groups):
-        last = hop == groups - 1
+    order = [h ^ (h >> 1) for h in range(groups)]
+    for hop in order:
+        last = hop == order[-1]
         given = (offsets, screened, lessers[hop], lefts[hop], locals_[hop], sums)
         outs, specs, extra = (sums_shape,), (VMEM,), []
         if hop == 0:

time: 33.1 us -> 32.8 us (level)
  Pallas kernels: 12 us -> 11.6 us
  transfers between devices with their start and end apart: 10 -> 10, of which waited for: 4 -> 4; matrix products, arithmetic and copies ran while one was open for 0% -> 0% of each run, Pallas kernels for 26% -> 25%
where the time goes in v10:
time: 32.8 us; the launch traced here: 32.6 us
  starting transfers between devices  14.8 us (45%)
  Pallas kernels  11.6 us (35%)
  waiting for transfers between devices  4.74 us (14%)
  between operations  1.48 us (5%)
    ppermute x9, starting transfers between devices, swapped(): lax.ppermute(x, axis, [(i, i ^ distance) for i in range(lax.axis_size(axi...  12.2 us
    pallas_call x4, Pallas kernels, body(): call(partial(convolve_kernel, reach, hop, last), outs, [VMEM] * len(given...  4.9 us
    ppermute x9, waiting for transfers between devices, swapped(): lax.ppermute(x, axis, [(i, i ^ distance) for i in range(lax.axis_size(axi...  4.39 us
    ppermute x1, starting transfers between devices, body(): two = lax.ppermute(block, ('cell', 'energy'), route)  2.55 us
    pallas_call x3, Pallas kernels, body(): call(partial(rows_kernel, overall, share, count + slot, slot), (left_shap...  1.7 us
    pallas_call x1, Pallas kernels, body(): call(front_kernel, (sds((extent, orbitals), f32), sds(modes.shape, bf16),...  1.23 us
    pallas_call x2, Pallas kernels, body(): sent, *rest = call(partial(kernel, level), outs, [VMEM] * 2)(total, other)  1.16 us
  transfers between devices with their start and end apart: 10, of which 4 were waited for; matrix products, arithmetic and copies ran while one was open for 0% of the time, Pallas kernels for 25%

profile of v10, /device:TPU:0, one launch (start us, length us, event | category | flops | bytes accessed | tf_op | source)
XLA Modules:
  0.0 32.6 jit_solution(153628090200211751)
XLA Ops:
  1.4 0.6 %collective-permute-start = (f32[8,128]{1,0:T(8,128)S(1)}, f32[8,128]{1,0:T(8,128)S(1)}, u32[]{:S(2)}, u32[]{:S(2)}) collective-permute-start(f32[8,128]{1,0:T(8,128)S(1)} %shard_map.114), channel_id=1, source_target_pairs={{0,4},{4,0},{8,12},{12,8},{16,20},{20,16},{24,28},{28,24},{1,5},{5... | collective-permute-start | bytes 12296 | tf_op jit(solution)/shard_map/ppermute | solution.py:538
  1.9 2.6 %collective-permute-start.1 = (f32[8,128]{1,0:T(8,128)S(1)}, f32[8,128]{1,0:T(8,128)S(1)}, u32[]{:S(2)}, u32[]{:S(2)}) collective-permute-start(f32[8,128]{1,0:T(8,128)S(1)} %shard_map.114), channel_id=1, source_target_pairs={{0,1},{1,0},{2,3},{3,2},{4,8},{5,9},{6,10},{7,11},{8,4},{9,5},{10,... | collective-permute-start | bytes 12296 | tf_op jit(solution)/shard_map/ppermute | solution.py:551
  4.5 1.2 %shard_map.113 = (f32[64,256]{1,0:T(8,128)S(1)}, bf16[1,256,256]{2,1,0:T(8,128)(2,1)S(1)}, f32[1,256]{1,0:T(1,128)S(1)}, f32[1,3,2,256]{3,2,1,0:T(2,128)S(1)}, s32[8]{0:T(128)S(1)}) custom-call(s32[1,4]{1,0:T(1,128)} %mask_hbm.1, bf16[1,256,256]{2,1,0:T(8,128)(2,1)} %modes_hbm.1, f32[1,256]{1,0:T(1,128)} %levels_hbm.1, bf16[1,64,256]{2,1,0:T(8,128)(2,1)} %bitcast.1, ...), custom_call_target="tpu_custom_call" | custom-call | flops 1000000 | bytes 1000000 | tf_op jit(solution)/shard_map/pallas_call | solution.py:553
  6.1 0.6 %shard_map.115.total_ref = bf16[2,3,64,128]{3,2,1,0:T(8,128)(2,1)S(1)} custom-call(f32[8,128]{1,0:T(8,128)S(1)} %collective-permute-done.one_ref, f32[8,128]{1,0:T(8,128)S(1)} %collective-permute-done.1.two_ref, bf16[1,256,256]{2,1,0:T(8,128)(2,1)S(1)} %get-tuple-element.25.modes_ref, f32[1,256]{1,0:T(1,128)S(1)} %get-tuple-element.26.levels_ref, ...), custom_call_target="tpu_custom_call" | custom-call | flops 1000000 | bytes 1000000 | tf_op jit(solution)/shard_map/pallas_call | solution.py:577
  6.8 1.2 %collective-permute-done.2.other_ref = bf16[2,3,64,128]{3,2,1,0:T(8,128)(2,1)S(1)} collective-permute-done((bf16[2,3,64,128]{3,2,1,0:T(8,128)(2,1)S(1)}, bf16[2,3,64,128]{3,2,1,0:T(8,128)(2,1)S(1)}, u32[]{:S(2)}, u32[]{:S(2)}) %collective-permute-start.2) | collective-permute-done | bytes 98336 | tf_op jit(solution)/shard_map/ppermute | solution.py:538
  8.0 0.5 %shard_map.116 = (bf16[1,272,128]{2,1,0:T(8,128)(2,1)S(1)}, bf16[2,3,64,128]{3,2,1,0:T(8,128)(2,1)S(1)}) custom-call(bf16[2,3,64,128]{3,2,1,0:T(8,128)(2,1)S(1)} %shard_map.115.total_ref, bf16[2,3,64,128]{3,2,1,0:T(8,128)(2,1)S(1)} %collective-permute-done.2.other_ref), custom_call_target="tpu_custom_call" | custom-call | flops 1000000 | bytes 1000000 | tf_op jit(solution)/shard_map/pallas_call | solution.py:609
  8.6 1.7 %collective-permute-start.3 = (bf16[1,272,128]{2,1,0:T(8,128)(2,1)S(1)}, bf16[1,272,128]{2,1,0:T(8,128)(2,1)S(1)}, u32[]{:S(2)}, u32[]{:S(2)}) collective-permute-start(bf16[1,272,128]{2,1,0:T(8,128)(2,1)S(1)} %get-tuple-element.29), channel_id=1, source_target_pairs={{0,8},{4,12},{8,0},{12,4},{16,24},{20,28},{24,16},{28,20},{1,9},{5... | collective-permute-start | bytes 208904 | tf_op jit(solution)/shard_map/ppermute | solution.py:538
  10.2 2.7 %collective-permute-done.3.other_ref = bf16[1,272,128]{2,1,0:T(8,128)(2,1)S(1)} collective-permute-done((bf16[1,272,128]{2,1,0:T(8,128)(2,1)S(1)}, bf16[1,272,128]{2,1,0:T(8,128)(2,1)S(1)}, u32[]{:S(2)}, u32[]{:S(2)}) %collective-permute-start.3) | collective-permute-done | bytes 69664 | tf_op jit(solution)/shard_map/ppermute | solution.py:538
  12.9 0.6 %shard_map.119 = bf16[1,144,128]{2,1,0:T(8,128)(2,1)S(1)} custom-call(bf16[2,3,64,128]{3,2,1,0:T(8,128)(2,1)S(1)} %get-tuple-element.30.total_ref, bf16[1,272,128]{2,1,0:T(8,128)(2,1)S(1)} %collective-permute-done.3.other_ref), custom_call_target="tpu_custom_call" | custom-call | flops 1000000 | bytes 1000000 | tf_op jit(solution)/shard_map/pallas_call | solution.py:609
  13.6 2.8 %collective-permute-start.4 = (bf16[1,144,128]{2,1,0:T(8,128)(2,1)S(1)}, bf16[1,144,128]{2,1,0:T(8,128)(2,1)S(1)}, u32[]{:S(2)}, u32[]{:S(2)}) collective-permute-start(bf16[1,144,128]{2,1,0:T(8,128)(2,1)S(1)} %shard_map.119), channel_id=1, source_target_pairs={{0,16},{4,20},{8,24},{12,28},{16,0},{20,4},{24,8},{28,12},{1,17},{... | collective-permute-start | bytes 110600 | tf_op jit(solution)/shard_map/ppermute | solution.py:538
  16.4 1.5 %collective-permute-start.6 = (f32[1,3,2,256]{3,2,1,0:T(2,128)S(1)}, f32[1,3,2,256]{3,2,1,0:T(2,128)S(1)}, u32[]{:S(2)}, u32[]{:S(2)}) collective-permute-start(f32[1,3,2,256]{3,2,1,0:T(2,128)S(1)} %get-tuple-element.27.params_ref.had_ref), channel_id=1, source_target_pairs={{0,1},{1,0},{2,3},{3,2},{4,5},{5,4},{6,7},{7,6},{8,9},{9,8},{10,11... | collective-permute-start | bytes 18440 | tf_op jit(solution)/shard_map/ppermute | solution.py:538
  17.9 0.6 %shard_map.118.enter_ref = bf16[2,3,64,128]{3,2,1,0:T(8,128)(2,1)S(1)} custom-call(bf16[1,272,128]{2,1,0:T(8,128)(2,1)S(1)} %collective-permute-done.3.other_ref, bf16[2,3,64,128]{3,2,1,0:T(8,128)(2,1)S(1)} %shard_map.117.refs_0_), custom_call_target="tpu_custom_call" | custom-call | flops 1000000 | bytes 1000000 | tf_op jit(solution)/shard_map/pallas_call | solution.py:612
  18.6 0.6 %shard_map.120 = (bf16[2,64,128]{2,1,0:T(8,128)(2,1)S(1)}, bf16[1,64,128]{2,1,0:T(8,128)(2,1)S(1)}) custom-call(bf16[2,3,64,128]{3,2,1,0:T(8,128)(2,1)S(1)} %shard_map.118.enter_ref, bf16[1,144,128]{2,1,0:T(8,128)(2,1)S(1)} %collective-permute-done.4.state_ref), custom_call_target="tpu_custom_call" | custom-call | flops 1000000 | bytes 1000000 | tf_op jit(solution)/shard_map/pallas_call | solution.py:614
  19.1 2.0 %collective-permute-start.9 = (bf16[1,64,128]{2,1,0:T(8,128)(2,1)S(1)}, bf16[1,64,128]{2,1,0:T(8,128)(2,1)S(1)}, u32[]{:S(2)}, u32[]{:S(2)}) collective-permute-start(bf16[1,64,128]{2,1,0:T(8,128)(2,1)S(1)} %get-tuple-element.31.lesser_ref), channel_id=1, source_target_pairs={{0,1},{1,0},{2,3},{3,2},{4,5},{5,4},{6,7},{7,6},{8,9},{9,8},{10,11... | collective-permute-start | bytes 49160 | tf_op jit(solution)/shard_map/ppermute | solution.py:538
  21.1 1.5 %collective-permute-start.8 = (bf16[1,64,128]{2,1,0:T(8,128)(2,1)S(1)}, bf16[1,64,128]{2,1,0:T(8,128)(2,1)S(1)}, u32[]{:S(2)}, u32[]{:S(2)}) collective-permute-start(bf16[1,64,128]{2,1,0:T(8,128)(2,1)S(1)} %get-tuple-element.31.lesser_ref), channel_id=1, source_target_pairs={{0,3},{1,2},{2,1},{3,0},{4,7},{5,6},{6,5},{7,4},{8,11},{9,10},{10,... | collective-permute-start | bytes 49160 | tf_op jit(solution)/shard_map/ppermute | solution.py:538
  22.7 2.0 %collective-permute-start.7 = (f32[2,3,2,256]{3,2,1,0:T(2,128)S(1)}, f32[2,3,2,256]{3,2,1,0:T(2,128)S(1)}, u32[]{:S(2)}, u32[]{:S(2)}) collective-permute-start(f32[2,3,2,256]{3,2,1,0:T(2,128)S(1)} %shard_map.124), channel_id=1, source_target_pairs={{0,2},{1,3},{2,0},{3,1},{4,6},{5,7},{6,4},{7,5},{8,10},{9,11},{10,... | collective-permute-start | bytes 36872 | tf_op jit(solution)/shard_map/ppermute | solution.py:538
  24.6 0.6 %shard_map.121 = (bf16[2,256,128]{2,1,0:T(8,128)(2,1)S(1)}, bf16[2,2,64,256]{3,2,1,0:T(8,128)(2,1)S(1)}) custom-call(bf16[1,256,256]{2,1,0:T(8,128)(2,1)S(1)} %get-tuple-element.25.modes_ref, f32[1,256]{1,0:T(1,128)S(1)} %get-tuple-element.26.levels_ref, f32[64,256]{1,0:T(8,128)S(1)} %get-tuple-element.28.mixed_ref, ...), custom_call_target="tpu_custom_call" | custom-call | flops 1000000 | bytes 1000000 | tf_op jit(solution)/shard_map/pallas_call | solution.py:572
  25.5 0.6 %shard_map.127 = (bf16[2,256,128]{2,1,0:T(8,128)(2,1)S(1)}, bf16[2,2,64,256]{3,2,1,0:T(8,128)(2,1)S(1)}) custom-call(bf16[1,256,256]{2,1,0:T(8,128)(2,1)S(1)} %get-tuple-element.25.modes_ref, f32[1,256]{1,0:T(1,128)S(1)} %get-tuple-element.26.levels_ref, f32[64,256]{1,0:T(8,128)S(1)} %get-tuple-element.28.mixed_ref, ...), custom_call_target="tpu_custom_call" | custom-call | flops 1000000 | bytes 1000000 | tf_op jit(solution)/shard_map/pallas_call | solution.py:594
  26.5 0.6 %shard_map.126 = (bf16[2,256,128]{2,1,0:T(8,128)(2,1)S(1)}, bf16[2,2,64,256]{3,2,1,0:T(8,128)(2,1)S(1)}) custom-call(bf16[1,256,256]{2,1,0:T(8,128)(2,1)S(1)} %get-tuple-element.25.modes_ref, f32[1,256]{1,0:T(1,128)S(1)} %get-tuple-element.26.levels_ref, f32[64,256]{1,0:T(8,128)S(1)} %get-tuple-element.28.mixed_ref, ...), custom_call_target="tpu_custom_call" | custom-call | flops 1000000 | bytes 1000000 | tf_op jit(solution)/shard_map/pallas_call | solution.py:594
  27.1 0.6 %shard_map.125 = (bf16[2,256,128]{2,1,0:T(8,128)(2,1)S(1)}, bf16[2,2,64,256]{3,2,1,0:T(8,128)(2,1)S(1)}) custom-call(bf16[1,256,256]{2,1,0:T(8,128)(2,1)S(1)} %get-tuple-element.25.modes_ref, f32[1,256]{1,0:T(1,128)S(1)} %get-tuple-element.26.levels_ref, f32[64,256]{1,0:T(8,128)S(1)} %get-tuple-element.28.mixed_ref, ...), custom_call_target="tpu_custom_call" | custom-call | flops 1000000 | bytes 1000000 | tf_op jit(solution)/shard_map/pallas_call | solution.py:594
  27.6 1.4 %shard_map.123 = (f32[3,12,64,256]{3,2,1,0:T(8,128)S(1)}, f32[1,2,256]{2,1,0:T(2,128)}) custom-call(s32[8]{0:T(128)S(1)} %get-tuple-element.24.offsets_ref, bf16[1,2,8,64,256]{4,3,2,1,0:T(8,128)(2,1)S(1)} %copy-done, bf16[1,64,128]{2,1,0:T(8,128)(2,1)S(1)} %get-tuple-element.31.lesser_ref, ...), custom_call_target="tpu_custom_call", output_to_operand_aliasing={{0}: (5, {})} | custom-call | flops 1000000 | bytes 1000000 | tf_op jit(solution)/shard_map/pallas_call | solution.py:639
  29.1 0.9 %shard_map.128._ = f32[3,12,64,256]{3,2,1,0:T(8,128)S(1)} custom-call(s32[8]{0:T(128)S(1)} %get-tuple-element.24.offsets_ref, bf16[1,2,8,64,256]{4,3,2,1,0:T(8,128)(2,1)S(1)} %copy-done, bf16[1,64,128]{2,1,0:T(8,128)(2,1)S(1)} %collective-permute-done.9.lesser_ref, ...), custom_call_target="tpu_custom_call", output_to_operand_aliasing={{}: (5, {})} | custom-call | flops 1000000 | bytes 1000000 | tf_op jit(solution)/shard_map/pallas_call | solution.py:639
  30.0 0.9 %shard_map.129._ = f32[3,12,64,256]{3,2,1,0:T(8,128)S(1)} custom-call(s32[8]{0:T(128)S(1)} %get-tuple-element.24.offsets_ref, bf16[1,2,8,64,256]{4,3,2,1,0:T(8,128)(2,1)S(1)} %copy-done, bf16[1,64,128]{2,1,0:T(8,128)(2,1)S(1)} %collective-permute-done.8.lesser_ref, ...), custom_call_target="tpu_custom_call", output_to_operand_aliasing={{}: (5, {})} | custom-call | flops 1000000 | bytes 1000000 | tf_op jit(solution)/shard_map/pallas_call | solution.py:639
  30.9 1.7 %shard_map.130 = (f32[3,12,64,256]{3,2,1,0:T(8,128)S(1)}, bf16[1,2,8,64,256]{4,3,2,1,0:T(8,128)(2,1)}) custom-call(s32[8]{0:T(128)S(1)} %get-tuple-element.24.offsets_ref, bf16[1,2,8,64,256]{4,3,2,1,0:T(8,128)(2,1)S(1)} %copy-done, bf16[1,64,128]{2,1,0:T(8,128)(2,1)S(1)} %collective-permute-done.5.lesser_ref, ...), custom_call_target="tpu_custom_call", output_to_operand_aliasing={{0}: (5, {})} | custom-call | flops 1000000 | bytes 1000000 | tf_op jit(solution)/shard_map/pallas_call | solution.py:639
  (16 shorter events, 1.4 us)
Async XLA Ops:
  0.6 27.0 %copy-start = (bf16[1,2,8,64,256]{4,3,2,1,0:T(8,128)(2,1)S(1)}, bf16[1,2,8,64,256]{4,3,2,1,0:T(8,128)(2,1)}, u32[]{:S(2)}) copy-start(bf16[1,2,8,64,256]{4,3,2,1,0:T(8,128)(2,1)} %screen_ref.7) | copy-start | bytes 1572868
  1.4 4.3 %collective-permute-start = (f32[8,128]{1,0:T(8,128)S(1)}, f32[8,128]{1,0:T(8,128)S(1)}, u32[]{:S(2)}, u32[]{:S(2)}) collective-permute-start(f32[8,128]{1,0:T(8,128)S(1)} %shard_map.114), channel_id=1, source_target_pairs={{0,4},{4,0},{8,12},{12,8},{16,20},{20,16},{24,28},{28,24},{1,5},{5... | collective-permute-start | bytes 12296 | tf_op jit(solution)/shard_map/ppermute | solution.py:538
  1.9 4.1 %collective-permute-start.1 = (f32[8,128]{1,0:T(8,128)S(1)}, f32[8,128]{1,0:T(8,128)S(1)}, u32[]{:S(2)}, u32[]{:S(2)}) collective-permute-start(f32[8,128]{1,0:T(8,128)S(1)} %shard_map.114), channel_id=1, source_target_pairs={{0,1},{1,0},{2,3},{3,2},{4,8},{5,9},{6,10},{7,11},{8,4},{9,5},{10,... | collective-permute-start | bytes 12296 | tf_op jit(solution)/shard_map/ppermute | solution.py:551
  6.6 1.4 %collective-permute-start.2 = (bf16[2,3,64,128]{3,2,1,0:T(8,128)(2,1)S(1)}, bf16[2,3,64,128]{3,2,1,0:T(8,128)(2,1)S(1)}, u32[]{:S(2)}, u32[]{:S(2)}) collective-permute-start(bf16[2,3,64,128]{3,2,1,0:T(8,128)(2,1)S(1)} %shard_map.115.total_ref), channel_id=1, source_target_pairs={{0,4},{4,0},{8,12},{12,8},{16,20},{20,16},{24,28},{28,24},{1,5},{5... | collective-permute-start | bytes 294920 | tf_op jit(solution)/shard_map/ppermute | solution.py:538
  8.6 4.4 %collective-permute-start.3 = (bf16[1,272,128]{2,1,0:T(8,128)(2,1)S(1)}, bf16[1,272,128]{2,1,0:T(8,128)(2,1)S(1)}, u32[]{:S(2)}, u32[]{:S(2)}) collective-permute-start(bf16[1,272,128]{2,1,0:T(8,128)(2,1)S(1)} %get-tuple-element.29), channel_id=1, source_target_pairs={{0,8},{4,12},{8,0},{12,4},{16,24},{20,28},{24,16},{28,20},{1,9},{5... | collective-permute-start | bytes 208904 | tf_op jit(solution)/shard_map/ppermute | solution.py:538
  13.6 5.0 %collective-permute-start.4 = (bf16[1,144,128]{2,1,0:T(8,128)(2,1)S(1)}, bf16[1,144,128]{2,1,0:T(8,128)(2,1)S(1)}, u32[]{:S(2)}, u32[]{:S(2)}) collective-permute-start(bf16[1,144,128]{2,1,0:T(8,128)(2,1)S(1)} %shard_map.119), channel_id=1, source_target_pairs={{0,16},{4,20},{8,24},{12,28},{16,0},{20,4},{24,8},{28,12},{1,17},{... | collective-permute-start | bytes 110600 | tf_op jit(solution)/shard_map/ppermute | solution.py:538
  16.4 6.3 %collective-permute-start.6 = (f32[1,3,2,256]{3,2,1,0:T(2,128)S(1)}, f32[1,3,2,256]{3,2,1,0:T(2,128)S(1)}, u32[]{:S(2)}, u32[]{:S(2)}) collective-permute-start(f32[1,3,2,256]{3,2,1,0:T(2,128)S(1)} %get-tuple-element.27.params_ref.had_ref), channel_id=1, source_target_pairs={{0,1},{1,0},{2,3},{3,2},{4,5},{5,4},{6,7},{7,6},{8,9},{9,8},{10,11... | collective-permute-start | bytes 18440 | tf_op jit(solution)/shard_map/ppermute | solution.py:538
  19.1 9.9 %collective-permute-start.9 = (bf16[1,64,128]{2,1,0:T(8,128)(2,1)S(1)}, bf16[1,64,128]{2,1,0:T(8,128)(2,1)S(1)}, u32[]{:S(2)}, u32[]{:S(2)}) collective-permute-start(bf16[1,64,128]{2,1,0:T(8,128)(2,1)S(1)} %get-tuple-element.31.lesser_ref), channel_id=1, source_target_pairs={{0,1},{1,0},{2,3},{3,2},{4,5},{5,4},{6,7},{7,6},{8,9},{9,8},{10,11... | collective-permute-start | bytes 49160 | tf_op jit(solution)/shard_map/ppermute | solution.py:538
  21.1 8.9 %collective-permute-start.8 = (bf16[1,64,128]{2,1,0:T(8,128)(2,1)S(1)}, bf16[1,64,128]{2,1,0:T(8,128)(2,1)S(1)}, u32[]{:S(2)}, u32[]{:S(2)}) collective-permute-start(bf16[1,64,128]{2,1,0:T(8,128)(2,1)S(1)} %get-tuple-element.31.lesser_ref), channel_id=1, source_target_pairs={{0,3},{1,2},{2,1},{3,0},{4,7},{5,6},{6,5},{7,4},{8,11},{9,10},{10,... | collective-permute-start | bytes 49160 | tf_op jit(solution)/shard_map/ppermute | solution.py:538
  22.6 8.3 %collective-permute-start.5 = (bf16[1,64,128]{2,1,0:T(8,128)(2,1)S(1)}, bf16[1,64,128]{2,1,0:T(8,128)(2,1)S(1)}, u32[]{:S(2)}, u32[]{:S(2)}) collective-permute-start(bf16[1,64,128]{2,1,0:T(8,128)(2,1)S(1)} %get-tuple-element.31.lesser_ref), channel_id=1, source_target_pairs={{0,2},{1,3},{2,0},{3,1},{4,6},{5,7},{6,4},{7,5},{8,10},{9,11},{10,... | collective-permute-start | bytes 49160 | tf_op jit(solution)/shard_map/ppermute | solution.py:538
  22.7 3.8 %collective-permute-start.7 = (f32[2,3,2,256]{3,2,1,0:T(2,128)S(1)}, f32[2,3,2,256]{3,2,1,0:T(2,128)S(1)}, u32[]{:S(2)}, u32[]{:S(2)}) collective-permute-start(f32[2,3,2,256]{3,2,1,0:T(2,128)S(1)} %shard_map.124), channel_id=1, source_target_pairs={{0,2},{1,3},{2,0},{3,1},{4,6},{5,7},{6,4},{7,5},{8,10},{9,11},{10,... | collective-permute-start | bytes 36872 | tf_op jit(solution)/shard_map/ppermute | solution.py:538

commit v11 on v10

--- a/solution.py
+++ b/solution.py
@@ -461,10 +461,10 @@
     copy.wait()
     height = 16
 
-    def out_copy(step):
+    def out_copy(step, part):
         rows = pl.ds(pl.multiple_of(step * height, height), height)
         return pltpu.make_async_copy(
-            refs[0].at[:, :, :, rows, :], out_hbm.at[:, :, :, rows, :], refs[1].at[step]
+            refs[0].at[0, part, :, rows, :], out_hbm.at[0, part, :, rows, :], refs[1].at[step, part]
         )
 
     def rows_of(step, _):
@@ -479,18 +479,20 @@
                 for part in range(3):
                     sums_ref[part, target, rows, :] += factors[part] * held[e][part]
         if last:
-            for e in range(overall):
-                common = sums_ref[0, reach + e, rows, :]
-                refs[0][0, 0, e, rows, :] = (-(common + sums_ref[2, reach + e, rows, :])).astype(bf16)
-                refs[0][0, 1, e, rows, :] = (common - sums_ref[1, reach + e, rows, :]).astype(bf16)
-            out_copy(step).start()
+            for part, turned in ((0, 2), (1, 1)):
+                for e in range(overall):
+                    common, other = sums_ref[0, reach + e, rows, :], sums_ref[turned, reach + e, rows, :]
+                    value = common - other if part else -(common + other)
+                    refs[0][0, part, e, rows, :] = value.astype(bf16)
+                out_copy(step, part).start()
         return 0
 
     steps = share // height
     lax.fori_loop(0, steps, rows_of, 0)
     if last:
         for step in range(steps):
-            out_copy(step).wait()
+            for part in range(2):
+                out_copy(step, part).wait()
 
 
 def in_hbm(x):
@@ -635,7 +637,7 @@
             outs, specs = outs + (density_shape,), specs + (VMEM,)
         if last:
             outs, specs = outs + (sigma_shape,), specs + (HBM,)
-            extra = [pltpu.VMEM(sigma_shape.shape, bf16), pltpu.SemaphoreType.DMA((share // 16,))]
+            extra = [pltpu.VMEM(sigma_shape.shape, bf16), pltpu.SemaphoreType.DMA((share // 16, 2))]
         sums, *rest = call(
             partial(convolve_kernel, reach, hop, last),
             outs,

time: 32.8 us -> 32.8 us (level)
  no operation moved by 1% of the time
where the time goes in v11:
time: 32.8 us; the launch traced here: 32.6 us
  starting transfers between devices  14.8 us (45%)
  Pallas kernels  11.6 us (35%)
  waiting for transfers between devices  4.74 us (14%)
  between operations  1.48 us (5%)
    ppermute x9, starting transfers between devices, swapped(): lax.ppermute(x, axis, [(i, i ^ distance) for i in range(lax.axis_size(axi...  12.2 us
    pallas_call x4, Pallas kernels, body(): call(partial(convolve_kernel, reach, hop, last), outs, [VMEM] * len(given...  4.94 us
    ppermute x9, waiting for transfers between devices, swapped(): lax.ppermute(x, axis, [(i, i ^ distance) for i in range(lax.axis_size(axi...  4.39 us
    ppermute x1, starting transfers between devices, body(): two = lax.ppermute(block, ('cell', 'energy'), route)  2.55 us
    pallas_call x3, Pallas kernels, body(): call(partial(rows_kernel, overall, share, count + slot, slot), (left_shap...  1.7 us
    pallas_call x1, Pallas kernels, body(): call(front_kernel, (sds((extent, orbitals), f32), sds(modes.shape, bf16),...  1.23 us
    pallas_call x2, Pallas kernels, body(): sent, *rest = call(partial(kernel, level), outs, [VMEM] * 2)(total, other)  1.16 us
  transfers between devices with their start and end apart: 10, of which 4 were waited for; matrix products, arithmetic and copies ran while one was open for 0% of the time, Pallas kernels for 25%

profile of v11, /device:TPU:0, one launch (start us, length us, event | category | flops | bytes accessed | tf_op | source)
XLA Modules:
  0.0 32.6 jit_solution(13635378706208998724)
XLA Ops:
  1.4 0.6 %collective-permute-start = (f32[8,128]{1,0:T(8,128)S(1)}, f32[8,128]{1,0:T(8,128)S(1)}, u32[]{:S(2)}, u32[]{:S(2)}) collective-permute-start(f32[8,128]{1,0:T(8,128)S(1)} %shard_map.114), channel_id=1, source_target_pairs={{0,4},{4,0},{8,12},{12,8},{16,20},{20,16},{24,28},{28,24},{1,5},{5... | collective-permute-start | bytes 12296 | tf_op jit(solution)/shard_map/ppermute | solution.py:540
  1.9 2.6 %collective-permute-start.1 = (f32[8,128]{1,0:T(8,128)S(1)}, f32[8,128]{1,0:T(8,128)S(1)}, u32[]{:S(2)}, u32[]{:S(2)}) collective-permute-start(f32[8,128]{1,0:T(8,128)S(1)} %shard_map.114), channel_id=1, source_target_pairs={{0,1},{1,0},{2,3},{3,2},{4,8},{5,9},{6,10},{7,11},{8,4},{9,5},{10,... | collective-permute-start | bytes 12296 | tf_op jit(solution)/shard_map/ppermute | solution.py:553
  4.5 1.2 %shard_map.113 = (f32[64,256]{1,0:T(8,128)S(1)}, bf16[1,256,256]{2,1,0:T(8,128)(2,1)S(1)}, f32[1,256]{1,0:T(1,128)S(1)}, f32[1,3,2,256]{3,2,1,0:T(2,128)S(1)}, s32[8]{0:T(128)S(1)}) custom-call(s32[1,4]{1,0:T(1,128)} %mask_hbm.1, bf16[1,256,256]{2,1,0:T(8,128)(2,1)} %modes_hbm.1, f32[1,256]{1,0:T(1,128)} %levels_hbm.1, bf16[1,64,256]{2,1,0:T(8,128)(2,1)} %bitcast.1, ...), custom_call_target="tpu_custom_call" | custom-call | flops 1000000 | bytes 1000000 | tf_op jit(solution)/shard_map/pallas_call | solution.py:555
  6.1 0.6 %shard_map.115.total_ref = bf16[2,3,64,128]{3,2,1,0:T(8,128)(2,1)S(1)} custom-call(f32[8,128]{1,0:T(8,128)S(1)} %collective-permute-done.one_ref, f32[8,128]{1,0:T(8,128)S(1)} %collective-permute-done.1.two_ref, bf16[1,256,256]{2,1,0:T(8,128)(2,1)S(1)} %get-tuple-element.25.modes_ref, f32[1,256]{1,0:T(1,128)S(1)} %get-tuple-element.26.levels_ref, ...), custom_call_target="tpu_custom_call" | custom-call | flops 1000000 | bytes 1000000 | tf_op jit(solution)/shard_map/pallas_call | solution.py:579
  6.8 1.2 %collective-permute-done.2.other_ref = bf16[2,3,64,128]{3,2,1,0:T(8,128)(2,1)S(1)} collective-permute-done((bf16[2,3,64,128]{3,2,1,0:T(8,128)(2,1)S(1)}, bf16[2,3,64,128]{3,2,1,0:T(8,128)(2,1)S(1)}, u32[]{:S(2)}, u32[]{:S(2)}) %collective-permute-start.2) | collective-permute-done | bytes 98336 | tf_op jit(solution)/shard_map/ppermute | solution.py:540
  8.0 0.5 %shard_map.116 = (bf16[1,272,128]{2,1,0:T(8,128)(2,1)S(1)}, bf16[2,3,64,128]{3,2,1,0:T(8,128)(2,1)S(1)}) custom-call(bf16[2,3,64,128]{3,2,1,0:T(8,128)(2,1)S(1)} %shard_map.115.total_ref, bf16[2,3,64,128]{3,2,1,0:T(8,128)(2,1)S(1)} %collective-permute-done.2.other_ref), custom_call_target="tpu_custom_call" | custom-call | flops 1000000 | bytes 1000000 | tf_op jit(solution)/shard_map/pallas_call | solution.py:611
  8.6 1.7 %collective-permute-start.3 = (bf16[1,272,128]{2,1,0:T(8,128)(2,1)S(1)}, bf16[1,272,128]{2,1,0:T(8,128)(2,1)S(1)}, u32[]{:S(2)}, u32[]{:S(2)}) collective-permute-start(bf16[1,272,128]{2,1,0:T(8,128)(2,1)S(1)} %get-tuple-element.29), channel_id=1, source_target_pairs={{0,8},{4,12},{8,0},{12,4},{16,24},{20,28},{24,16},{28,20},{1,9},{5... | collective-permute-start | bytes 208904 | tf_op jit(solution)/shard_map/ppermute | solution.py:540
  10.2 2.7 %collective-permute-done.3.other_ref = bf16[1,272,128]{2,1,0:T(8,128)(2,1)S(1)} collective-permute-done((bf16[1,272,128]{2,1,0:T(8,128)(2,1)S(1)}, bf16[1,272,128]{2,1,0:T(8,128)(2,1)S(1)}, u32[]{:S(2)}, u32[]{:S(2)}) %collective-permute-start.3) | collective-permute-done | bytes 69664 | tf_op jit(solution)/shard_map/ppermute | solution.py:540
  12.9 0.6 %shard_map.119 = bf16[1,144,128]{2,1,0:T(8,128)(2,1)S(1)} custom-call(bf16[2,3,64,128]{3,2,1,0:T(8,128)(2,1)S(1)} %get-tuple-element.30.total_ref, bf16[1,272,128]{2,1,0:T(8,128)(2,1)S(1)} %collective-permute-done.3.other_ref), custom_call_target="tpu_custom_call" | custom-call | flops 1000000 | bytes 1000000 | tf_op jit(solution)/shard_map/pallas_call | solution.py:611
  13.6 2.8 %collective-permute-start.4 = (bf16[1,144,128]{2,1,0:T(8,128)(2,1)S(1)}, bf16[1,144,128]{2,1,0:T(8,128)(2,1)S(1)}, u32[]{:S(2)}, u32[]{:S(2)}) collective-permute-start(bf16[1,144,128]{2,1,0:T(8,128)(2,1)S(1)} %shard_map.119), channel_id=1, source_target_pairs={{0,16},{4,20},{8,24},{12,28},{16,0},{20,4},{24,8},{28,12},{1,17},{... | collective-permute-start | bytes 110600 | tf_op jit(solution)/shard_map/ppermute | solution.py:540
  16.4 1.5 %collective-permute-start.6 = (f32[1,3,2,256]{3,2,1,0:T(2,128)S(1)}, f32[1,3,2,256]{3,2,1,0:T(2,128)S(1)}, u32[]{:S(2)}, u32[]{:S(2)}) collective-permute-start(f32[1,3,2,256]{3,2,1,0:T(2,128)S(1)} %get-tuple-element.27.params_ref.had_ref), channel_id=1, source_target_pairs={{0,1},{1,0},{2,3},{3,2},{4,5},{5,4},{6,7},{7,6},{8,9},{9,8},{10,11... | collective-permute-start | bytes 18440 | tf_op jit(solution)/shard_map/ppermute | solution.py:540
  17.9 0.6 %shard_map.118.enter_ref = bf16[2,3,64,128]{3,2,1,0:T(8,128)(2,1)S(1)} custom-call(bf16[1,272,128]{2,1,0:T(8,128)(2,1)S(1)} %collective-permute-done.3.other_ref, bf16[2,3,64,128]{3,2,1,0:T(8,128)(2,1)S(1)} %shard_map.117.refs_0_), custom_call_target="tpu_custom_call" | custom-call | flops 1000000 | bytes 1000000 | tf_op jit(solution)/shard_map/pallas_call | solution.py:614
  18.6 0.6 %shard_map.120 = (bf16[2,64,128]{2,1,0:T(8,128)(2,1)S(1)}, bf16[1,64,128]{2,1,0:T(8,128)(2,1)S(1)}) custom-call(bf16[2,3,64,128]{3,2,1,0:T(8,128)(2,1)S(1)} %shard_map.118.enter_ref, bf16[1,144,128]{2,1,0:T(8,128)(2,1)S(1)} %collective-permute-done.4.state_ref), custom_call_target="tpu_custom_call" | custom-call | flops 1000000 | bytes 1000000 | tf_op jit(solution)/shard_map/pallas_call | solution.py:616
  19.1 2.0 %collective-permute-start.9 = (bf16[1,64,128]{2,1,0:T(8,128)(2,1)S(1)}, bf16[1,64,128]{2,1,0:T(8,128)(2,1)S(1)}, u32[]{:S(2)}, u32[]{:S(2)}) collective-permute-start(bf16[1,64,128]{2,1,0:T(8,128)(2,1)S(1)} %get-tuple-element.31.lesser_ref), channel_id=1, source_target_pairs={{0,1},{1,0},{2,3},{3,2},{4,5},{5,4},{6,7},{7,6},{8,9},{9,8},{10,11... | collective-permute-start | bytes 49160 | tf_op jit(solution)/shard_map/ppermute | solution.py:540
  21.1 1.5 %collective-permute-start.8 = (bf16[1,64,128]{2,1,0:T(8,128)(2,1)S(1)}, bf16[1,64,128]{2,1,0:T(8,128)(2,1)S(1)}, u32[]{:S(2)}, u32[]{:S(2)}) collective-permute-start(bf16[1,64,128]{2,1,0:T(8,128)(2,1)S(1)} %get-tuple-element.31.lesser_ref), channel_id=1, source_target_pairs={{0,3},{1,2},{2,1},{3,0},{4,7},{5,6},{6,5},{7,4},{8,11},{9,10},{10,... | collective-permute-start | bytes 49160 | tf_op jit(solution)/shard_map/ppermute | solution.py:540
  22.7 2.0 %collective-permute-start.7 = (f32[2,3,2,256]{3,2,1,0:T(2,128)S(1)}, f32[2,3,2,256]{3,2,1,0:T(2,128)S(1)}, u32[]{:S(2)}, u32[]{:S(2)}) collective-permute-start(f32[2,3,2,256]{3,2,1,0:T(2,128)S(1)} %shard_map.124), channel_id=1, source_target_pairs={{0,2},{1,3},{2,0},{3,1},{4,6},{5,7},{6,4},{7,5},{8,10},{9,11},{10,... | collective-permute-start | bytes 36872 | tf_op jit(solution)/shard_map/ppermute | solution.py:540
  24.6 0.6 %shard_map.121 = (bf16[2,256,128]{2,1,0:T(8,128)(2,1)S(1)}, bf16[2,2,64,256]{3,2,1,0:T(8,128)(2,1)S(1)}) custom-call(bf16[1,256,256]{2,1,0:T(8,128)(2,1)S(1)} %get-tuple-element.25.modes_ref, f32[1,256]{1,0:T(1,128)S(1)} %get-tuple-element.26.levels_ref, f32[64,256]{1,0:T(8,128)S(1)} %get-tuple-element.28.mixed_ref, ...), custom_call_target="tpu_custom_call" | custom-call | flops 1000000 | bytes 1000000 | tf_op jit(solution)/shard_map/pallas_call | solution.py:574
  25.5 0.6 %shard_map.127 = (bf16[2,256,128]{2,1,0:T(8,128)(2,1)S(1)}, bf16[2,2,64,256]{3,2,1,0:T(8,128)(2,1)S(1)}) custom-call(bf16[1,256,256]{2,1,0:T(8,128)(2,1)S(1)} %get-tuple-element.25.modes_ref, f32[1,256]{1,0:T(1,128)S(1)} %get-tuple-element.26.levels_ref, f32[64,256]{1,0:T(8,128)S(1)} %get-tuple-element.28.mixed_ref, ...), custom_call_target="tpu_custom_call" | custom-call | flops 1000000 | bytes 1000000 | tf_op jit(solution)/shard_map/pallas_call | solution.py:596
  26.5 0.6 %shard_map.126 = (bf16[2,256,128]{2,1,0:T(8,128)(2,1)S(1)}, bf16[2,2,64,256]{3,2,1,0:T(8,128)(2,1)S(1)}) custom-call(bf16[1,256,256]{2,1,0:T(8,128)(2,1)S(1)} %get-tuple-element.25.modes_ref, f32[1,256]{1,0:T(1,128)S(1)} %get-tuple-element.26.levels_ref, f32[64,256]{1,0:T(8,128)S(1)} %get-tuple-element.28.mixed_ref, ...), custom_call_target="tpu_custom_call" | custom-call | flops 1000000 | bytes 1000000 | tf_op jit(solution)/shard_map/pallas_call | solution.py:596
  27.1 0.6 %shard_map.125 = (bf16[2,256,128]{2,1,0:T(8,128)(2,1)S(1)}, bf16[2,2,64,256]{3,2,1,0:T(8,128)(2,1)S(1)}) custom-call(bf16[1,256,256]{2,1,0:T(8,128)(2,1)S(1)} %get-tuple-element.25.modes_ref, f32[1,256]{1,0:T(1,128)S(1)} %get-tuple-element.26.levels_ref, f32[64,256]{1,0:T(8,128)S(1)} %get-tuple-element.28.mixed_ref, ...), custom_call_target="tpu_custom_call" | custom-call | flops 1000000 | bytes 1000000 | tf_op jit(solution)/shard_map/pallas_call | solution.py:596
  27.6 1.4 %shard_map.123 = (f32[3,12,64,256]{3,2,1,0:T(8,128)S(1)}, f32[1,2,256]{2,1,0:T(2,128)}) custom-call(s32[8]{0:T(128)S(1)} %get-tuple-element.24.offsets_ref, bf16[1,2,8,64,256]{4,3,2,1,0:T(8,128)(2,1)S(1)} %copy-done, bf16[1,64,128]{2,1,0:T(8,128)(2,1)S(1)} %get-tuple-element.31.lesser_ref, ...), custom_call_target="tpu_custom_call", output_to_operand_aliasing={{0}: (5, {})} | custom-call | flops 1000000 | bytes 1000000 | tf_op jit(solution)/shard_map/pallas_call | solution.py:641
  29.1 0.9 %shard_map.128._ = f32[3,12,64,256]{3,2,1,0:T(8,128)S(1)} custom-call(s32[8]{0:T(128)S(1)} %get-tuple-element.24.offsets_ref, bf16[1,2,8,64,256]{4,3,2,1,0:T(8,128)(2,1)S(1)} %copy-done, bf16[1,64,128]{2,1,0:T(8,128)(2,1)S(1)} %collective-permute-done.9.lesser_ref, ...), custom_call_target="tpu_custom_call", output_to_operand_aliasing={{}: (5, {})} | custom-call | flops 1000000 | bytes 1000000 | tf_op jit(solution)/shard_map/pallas_call | solution.py:641
  30.0 0.9 %shard_map.129._ = f32[3,12,64,256]{3,2,1,0:T(8,128)S(1)} custom-call(s32[8]{0:T(128)S(1)} %get-tuple-element.24.offsets_ref, bf16[1,2,8,64,256]{4,3,2,1,0:T(8,128)(2,1)S(1)} %copy-done, bf16[1,64,128]{2,1,0:T(8,128)(2,1)S(1)} %collective-permute-done.8.lesser_ref, ...), custom_call_target="tpu_custom_call", output_to_operand_aliasing={{}: (5, {})} | custom-call | flops 1000000 | bytes 1000000 | tf_op jit(solution)/shard_map/pallas_call | solution.py:641
  30.9 1.7 %shard_map.130 = (f32[3,12,64,256]{3,2,1,0:T(8,128)S(1)}, bf16[1,2,8,64,256]{4,3,2,1,0:T(8,128)(2,1)}) custom-call(s32[8]{0:T(128)S(1)} %get-tuple-element.24.offsets_ref, bf16[1,2,8,64,256]{4,3,2,1,0:T(8,128)(2,1)S(1)} %copy-done, bf16[1,64,128]{2,1,0:T(8,128)(2,1)S(1)} %collective-permute-done.5.lesser_ref, ...), custom_call_target="tpu_custom_call", output_to_operand_aliasing={{0}: (5, {})} | custom-call | flops 1000000 | bytes 1000000 | tf_op jit(solution)/shard_map/pallas_call | solution.py:641
  (16 shorter events, 1.4 us)
Async XLA Ops:
  0.6 27.0 %copy-start = (bf16[1,2,8,64,256]{4,3,2,1,0:T(8,128)(2,1)S(1)}, bf16[1,2,8,64,256]{4,3,2,1,0:T(8,128)(2,1)}, u32[]{:S(2)}) copy-start(bf16[1,2,8,64,256]{4,3,2,1,0:T(8,128)(2,1)} %screen_ref.7) | copy-start | bytes 1572868
  1.4 4.3 %collective-permute-start = (f32[8,128]{1,0:T(8,128)S(1)}, f32[8,128]{1,0:T(8,128)S(1)}, u32[]{:S(2)}, u32[]{:S(2)}) collective-permute-start(f32[8,128]{1,0:T(8,128)S(1)} %shard_map.114), channel_id=1, source_target_pairs={{0,4},{4,0},{8,12},{12,8},{16,20},{20,16},{24,28},{28,24},{1,5},{5... | collective-permute-start | bytes 12296 | tf_op jit(solution)/shard_map/ppermute | solution.py:540
  1.9 4.1 %collective-permute-start.1 = (f32[8,128]{1,0:T(8,128)S(1)}, f32[8,128]{1,0:T(8,128)S(1)}, u32[]{:S(2)}, u32[]{:S(2)}) collective-permute-start(f32[8,128]{1,0:T(8,128)S(1)} %shard_map.114), channel_id=1, source_target_pairs={{0,1},{1,0},{2,3},{3,2},{4,8},{5,9},{6,10},{7,11},{8,4},{9,5},{10,... | collective-permute-start | bytes 12296 | tf_op jit(solution)/shard_map/ppermute | solution.py:553
  6.6 1.4 %collective-permute-start.2 = (bf16[2,3,64,128]{3,2,1,0:T(8,128)(2,1)S(1)}, bf16[2,3,64,128]{3,2,1,0:T(8,128)(2,1)S(1)}, u32[]{:S(2)}, u32[]{:S(2)}) collective-permute-start(bf16[2,3,64,128]{3,2,1,0:T(8,128)(2,1)S(1)} %shard_map.115.total_ref), channel_id=1, source_target_pairs={{0,4},{4,0},{8,12},{12,8},{16,20},{20,16},{24,28},{28,24},{1,5},{5... | collective-permute-start | bytes 294920 | tf_op jit(solution)/shard_map/ppermute | solution.py:540
  8.6 4.4 %collective-permute-start.3 = (bf16[1,272,128]{2,1,0:T(8,128)(2,1)S(1)}, bf16[1,272,128]{2,1,0:T(8,128)(2,1)S(1)}, u32[]{:S(2)}, u32[]{:S(2)}) collective-permute-start(bf16[1,272,128]{2,1,0:T(8,128)(2,1)S(1)} %get-tuple-element.29), channel_id=1, source_target_pairs={{0,8},{4,12},{8,0},{12,4},{16,24},{20,28},{24,16},{28,20},{1,9},{5... | collective-permute-start | bytes 208904 | tf_op jit(solution)/shard_map/ppermute | solution.py:540
  13.6 5.0 %collective-permute-start.4 = (bf16[1,144,128]{2,1,0:T(8,128)(2,1)S(1)}, bf16[1,144,128]{2,1,0:T(8,128)(2,1)S(1)}, u32[]{:S(2)}, u32[]{:S(2)}) collective-permute-start(bf16[1,144,128]{2,1,0:T(8,128)(2,1)S(1)} %shard_map.119), channel_id=1, source_target_pairs={{0,16},{4,20},{8,24},{12,28},{16,0},{20,4},{24,8},{28,12},{1,17},{... | collective-permute-start | bytes 110600 | tf_op jit(solution)/shard_map/ppermute | solution.py:540
  16.4 6.3 %collective-permute-start.6 = (f32[1,3,2,256]{3,2,1,0:T(2,128)S(1)}, f32[1,3,2,256]{3,2,1,0:T(2,128)S(1)}, u32[]{:S(2)}, u32[]{:S(2)}) collective-permute-start(f32[1,3,2,256]{3,2,1,0:T(2,128)S(1)} %get-tuple-element.27.params_ref.had_ref), channel_id=1, source_target_pairs={{0,1},{1,0},{2,3},{3,2},{4,5},{5,4},{6,7},{7,6},{8,9},{9,8},{10,11... | collective-permute-start | bytes 18440 | tf_op jit(solution)/shard_map/ppermute | solution.py:540
  19.1 9.9 %collective-permute-start.9 = (bf16[1,64,128]{2,1,0:T(8,128)(2,1)S(1)}, bf16[1,64,128]{2,1,0:T(8,128)(2,1)S(1)}, u32[]{:S(2)}, u32[]{:S(2)}) collective-permute-start(bf16[1,64,128]{2,1,0:T(8,128)(2,1)S(1)} %get-tuple-element.31.lesser_ref), channel_id=1, source_target_pairs={{0,1},{1,0},{2,3},{3,2},{4,5},{5,4},{6,7},{7,6},{8,9},{9,8},{10,11... | collective-permute-start | bytes 49160 | tf_op jit(solution)/shard_map/ppermute | solution.py:540
  21.1 8.9 %collective-permute-start.8 = (bf16[1,64,128]{2,1,0:T(8,128)(2,1)S(1)}, bf16[1,64,128]{2,1,0:T(8,128)(2,1)S(1)}, u32[]{:S(2)}, u32[]{:S(2)}) collective-permute-start(bf16[1,64,128]{2,1,0:T(8,128)(2,1)S(1)} %get-tuple-element.31.lesser_ref), channel_id=1, source_target_pairs={{0,3},{1,2},{2,1},{3,0},{4,7},{5,6},{6,5},{7,4},{8,11},{9,10},{10,... | collective-permute-start | bytes 49160 | tf_op jit(solution)/shard_map/ppermute | solution.py:540
  22.6 8.3 %collective-permute-start.5 = (bf16[1,64,128]{2,1,0:T(8,128)(2,1)S(1)}, bf16[1,64,128]{2,1,0:T(8,128)(2,1)S(1)}, u32[]{:S(2)}, u32[]{:S(2)}) collective-permute-start(bf16[1,64,128]{2,1,0:T(8,128)(2,1)S(1)} %get-tuple-element.31.lesser_ref), channel_id=1, source_target_pairs={{0,2},{1,3},{2,0},{3,1},{4,6},{5,7},{6,4},{7,5},{8,10},{9,11},{10,... | collective-permute-start | bytes 49160 | tf_op jit(solution)/shard_map/ppermute | solution.py:540
  22.7 3.8 %collective-permute-start.7 = (f32[2,3,2,256]{3,2,1,0:T(2,128)S(1)}, f32[2,3,2,256]{3,2,1,0:T(2,128)S(1)}, u32[]{:S(2)}, u32[]{:S(2)}) collective-permute-start(f32[2,3,2,256]{3,2,1,0:T(2,128)S(1)} %shard_map.124), channel_id=1, source_target_pairs={{0,2},{1,3},{2,0},{3,1},{4,6},{5,7},{6,4},{7,5},{8,10},{9,11},{10,... | collective-permute-start | bytes 36872 | tf_op jit(solution)/shard_map/ppermute | solution.py:540
